TPU v7x, 128 devices: a whole 4x4x4 slice. The times are simulated.
128 devices in a mesh: blk: 32 (over y_hi, x, z), head: 4 (over y_lo, core).
Axes of the slice: x: 4, y: 4 (y_hi: 2, y_lo: 2; y = y_hi * 2 + y_lo), z: 4, core: 2. Of those that a mesh axis runs over, the one named last changes fastest.
Arguments:
- states_in: bfloat16 [8192, 2048], P('blk'), may hold values from -12 to 12
- w_qkv: bfloat16 [3, 2048, 2048], P(None, None, 'head'), may hold values from -0.35355339 to 0.35355339
- qk_gain: float32 [2, 2048], P(None, 'head'), may hold values from 0.8 to 7.8
- w_out: bfloat16 [2048, 2048], P('head'), may hold values from -0.125 to 0.125
- post_gain: float32 [2, 2048], replicated, may hold values from 0.5 to 1.5
- w_gate_up: bfloat16 [2, 2048, 8192], P(None, None, 'blk'), may hold values from -0.125 to 0.125
- w_down: bfloat16 [8192, 2048], P('blk'), may hold values from -0.0625 to 0.0625
- cache_keys: bfloat16 [32, 256, 2048], P('blk', None, 'head'), may hold values from -6 to 6
- cache_values: bfloat16 [32, 256, 2048], P('blk', None, 'head'), may hold values from -6 to 6
- slot_node: int32 [32], replicated, may hold values from 0 to 31, each once
- node_length: int32 [32], replicated, may hold values from 1 to 256, 5120 in all
- node_parent: int32 [28], replicated, may hold values from 0 to 3
- leaf_segment: int32 [32, 256], replicated, may hold values from 0 to 7, never falling along the last dimension, each value on 1 to 128 neighbouring positions
- leaf_node: int32 [32, 8], replicated, may hold values from 4 to 31
Outputs:
- layer_out: bfloat16 [8192, 2048], P(('blk', 'head'))
Inputs may be any that keep to these rules, and one draw needn't show every extreme that they name: Slot s holds node slot_node[s]; every node is held once. Rows 0 to node_length[n] - 1 of node n's slot are valid; the longest node has 256 rows. Nodes 0 to 3 are roots; middle node 4 + i hangs under root node_parent[i]. `leaf_segment`: never falls along a group; every leaf of a group has 1 to 128 tokens. `leaf_node`: every leaf hangs under a middle node.
All inputs are finite; a program needn't handle non-finite values.
Results may differ from a plain program's by a relative error of at most 0.025.
Values may be sent and summed in bfloat16 or wider, within the bound.
No kernel may reach another device: no remote copies, remote signals or barrier semaphores. Data moves between devices by JAX's collectives and lax.ppermute only.
A program may use at most 192 MiB of HBM per device.

v0:
```python
import functools

import jax
import jax.numpy as jnp
from jax import lax
from jax.experimental import pallas as pl
from jax.experimental.pallas import tpu as pltpu
from jax.sharding import Mesh, PartitionSpec as P

HD = 128
EPS = 1e-06
THETA = 500000.0
NEG = -1e30
LOG2E = 1.4426950408889634
BF = jnp.bfloat16
F32 = jnp.float32
BLK = ("yhi", "x", "z")
HEAD = ("ylo", "core")


def shift(values, axis, by):
    n = lax.axis_size(axis)
    return lax.ppermute(values, axis, [(i, (i + by) % n) for i in range(n)])


def select_row(table, row):
    return lax.dynamic_index_in_dim(table, row, 0, keepdims=False)


def tree_info(leaf_segment, leaf_node, node_parent, node_length):
    groups, tok_rows = leaf_segment.shape
    leaf_count = leaf_node.shape[1]
    middles = node_parent.shape[0]
    all_nodes = node_length.shape[0]
    tenant_count = all_nodes - middles
    leaf_ids = jnp.arange(leaf_count, dtype=jnp.int32)
    onehot = (leaf_segment[:, :, None] == leaf_ids[None, None, :]).astype(jnp.int32)
    middle = jnp.sum(onehot * leaf_node[:, None, :], axis=-1)
    counts = jnp.sum(onehot, axis=1)
    starts = jnp.sum(jnp.where(leaf_ids[None, :] < leaf_ids[:, None], counts[:, None, :], 0), axis=-1)
    first_at = jnp.sum(onehot * starts[:, None, :], axis=-1)
    middle_ids = jnp.arange(middles, dtype=jnp.int32) + tenant_count
    root_node = jnp.sum(jnp.where(middle[..., None] == middle_ids, node_parent, 0), axis=-1)
    node_ids = jnp.arange(all_nodes, dtype=jnp.int32)
    len_middle = jnp.sum(jnp.where(middle[..., None] == node_ids, node_length, 0), axis=-1)
    len_root = jnp.sum(jnp.where(root_node[..., None] == node_ids, node_length, 0), axis=-1)
    offsets = jnp.arange(tok_rows, dtype=jnp.int32)[None, :] - first_at
    return middle, root_node, len_root + len_middle + offsets


def rms_norm(values_in, gain):
    return (
        values_in * lax.rsqrt(jnp.mean(values_in * values_in, axis=-1, keepdims=True) + EPS) * gain
    )


def attention_body(
    nodes_ref, lengths_ref, lists_ref, counts_ref,
    *rest,
):
    out_ref, qkv_ref, k_all, v_all, held, sems, qkv_sems = rest[-7:]
    qkv_parts = rest[:4]
    info_ref, seg_ref = rest[4:6]
    parts = rest[6:-7]
    step = pl.program_id(0)
    group = step // 2
    tile = step % 2
    half_rows = out_ref.shape[1]
    rows = 2 * half_rows
    node_rows = k_all.shape[1]
    per_part = parts[0].shape[0]
    batch = held.shape[2] // node_rows

    def copies():
        for i, part in enumerate(qkv_parts):
            yield pltpu.make_async_copy(part, qkv_ref.at[i], qkv_sems.at[i])
        for i, part in enumerate(parts):
            for j in range(per_part):
                yield pltpu.make_async_copy(
                    part.at[j, 0], k_all.at[i * per_part + j], sems.at[0, i, j]
                )
                yield pltpu.make_async_copy(
                    part.at[j, 1], v_all.at[i * per_part + j], sems.at[1, i, j]
                )

    @pl.when(step == 0)
    def _():
        for copy in copies():
            copy.start()
        for copy in copies():
            copy.wait()

    scale = HD**-0.5 * LOG2E
    nt = (((1,), (1,)), ((), ()))
    count = counts_ref[group, tile]

    def work(first):
        q = qkv_ref[group, 0, first : first + half_rows, :]
        seen = first + half_rows
        middle = info_ref[0, first:seen, 0:1]
        root = info_ref[0, first:seen, 1:2]
        seg_col = info_ref[0, first:seen, 2:3]
        seg_row = seg_ref[0][:, :seen]
        row_at = lax.broadcasted_iota(jnp.int32, (half_rows, seen), 0) + first
        col_at = lax.broadcasted_iota(jnp.int32, (half_rows, seen), 1)
        key_at = lax.broadcasted_iota(jnp.int32, (1, node_rows), 1)
        near = lax.dot_general(q, qkv_ref[group, 1, :seen, :], nt, preferred_element_type=F32) * scale
        near = jnp.where((seg_col == seg_row) & (col_at <= row_at), near, NEG)
        top = jnp.max(near, axis=1, keepdims=True)

        def score(i, top):
            best = None
            for j in range(batch):
                slot = lists_ref[group, tile, i * batch + j]
                node = nodes_ref[slot]
                length = jnp.where(i * batch + j < count, lengths_ref[slot], 0)
                s = lax.dot_general(q, k_all[slot], nt, preferred_element_type=F32) * scale
                shown = ((middle == node) | (root == node)) & (key_at < length)
                s = jnp.where(shown, s, NEG)
                held[i, :, j * node_rows : (j + 1) * node_rows] = s
                best = s if best is None else jnp.maximum(best, s)
            return jnp.maximum(top, jnp.max(best, axis=1, keepdims=True))

        batches = (count + batch - 1) // batch
        top = lax.fori_loop(0, batches, score, top)
        weights = jnp.exp2(near - top)
        total = jnp.sum(weights, axis=1, keepdims=True)
        summed = jnp.dot(weights.astype(BF), qkv_ref[group, 2, :seen, :], preferred_element_type=F32)

        def gather(i, carry):
            total, summed = carry
            added = None
            for j in range(batch):
                slot = lists_ref[group, tile, i * batch + j]
                w = jnp.exp2(held[i, :, j * node_rows : (j + 1) * node_rows] - top)
                added = w if added is None else added + w
                summed = summed + jnp.dot(
                    w.astype(BF), v_all[slot], preferred_element_type=F32
                )
            return total + jnp.sum(added, axis=1, keepdims=True), summed

        total, summed = lax.fori_loop(0, batches, gather, (total, summed))
        out_ref[0] = (summed / total).astype(BF)

    for t in range(2):
        @pl.when(tile == t)
        def _(t=t):
            work(t * half_rows)


def attention(nodes, lengths, lists, counts, qkv_parts, row_info, seg_row, parts):
    rows = qkv_parts[0].shape[1]
    groups = len(qkv_parts)
    per_part, _, node_rows, _ = parts[0].shape
    slots = nodes.shape[0]
    batch = 4
    one = lambda shape: pl.BlockSpec((1,) + shape, lambda i, *_: (i // 2,) + (0,) * len(shape))
    return pl.pallas_call(
        attention_body,
        out_shape=jax.ShapeDtypeStruct((groups, rows, HD), BF),
        grid_spec=pltpu.PrefetchScalarGridSpec(
            num_scalar_prefetch=4,
            grid=(groups * 2,),
            in_specs=[pl.BlockSpec(memory_space=pl.ANY)] * groups
            + [one((rows, 3)), one((1, rows))]
            + [pl.BlockSpec(memory_space=pl.ANY)] * len(parts),
            out_specs=pl.BlockSpec((1, rows // 2, HD), lambda i, *_: (i // 2, i % 2, 0)),
            scratch_shapes=[
                pltpu.VMEM((groups, 3, rows, HD), BF),
                pltpu.VMEM((slots, node_rows, HD), BF),
                pltpu.VMEM((slots, node_rows, HD), BF),
                pltpu.VMEM((lists.shape[2] // batch, rows // 2, batch * node_rows), F32),
                pltpu.SemaphoreType.DMA((2, len(parts), per_part)),
                pltpu.SemaphoreType.DMA((groups,)),
            ],
        ),
        compiler_params=pltpu.CompilerParams(vmem_limit_bytes=32 << 20),
        cost_estimate=pl.CostEstimate(
            flops=2 * 10**9, transcendentals=4 * 10**6, bytes_accessed=6 * 10**6
        ),
    )(nodes, lengths, lists, counts, *qkv_parts, row_info, seg_row, *parts)


def feed_forward_body(*refs):
    token_refs = refs[:4]
    gu_ref, dn_ref, own_ref, other_ref, held, sems = refs[4:]

    def copy(i, j):
        return pltpu.make_async_copy(token_refs[j], held.at[i], sems.at[i])

    for i in range(4):
        copy(i, i).start()

    def one(i, carry):
        for side, target in ((0, own_ref), (2, other_ref)):
            copy(i + side, side).wait()
            tokens = held[i + side]
            gate = jnp.dot(tokens, gu_ref[0], preferred_element_type=F32)
            up = jnp.dot(tokens, gu_ref[1], preferred_element_type=F32)
            hidden = (gate / (1.0 + jnp.exp(-gate)) * up).astype(BF)
            target[i] = jnp.dot(hidden, dn_ref[...], preferred_element_type=F32).astype(BF)
        return carry

    lax.fori_loop(0, 2, one, 0)


def feed_forward(parts, w_gu, w_dn):
    rows, width = parts[0].shape
    units = w_dn.shape[0]
    space = pl.BlockSpec(memory_space=pltpu.VMEM)
    out = jax.ShapeDtypeStruct((2, rows, width), BF)
    return pl.pallas_call(
        feed_forward_body,
        out_shape=(out, out),
        in_specs=[pl.BlockSpec(memory_space=pl.ANY)] * 4 + [space] * 2,
        out_specs=(space, space),
        scratch_shapes=[pltpu.VMEM((4, rows, width), BF), pltpu.SemaphoreType.DMA((4,))],
        compiler_params=pltpu.CompilerParams(vmem_limit_bytes=40 << 20),
        cost_estimate=pl.CostEstimate(
            flops=4 * rows * width * units * 6,
            transcendentals=4 * rows * units,
            bytes_accessed=(8 * rows * width + 3 * width * units) * 2,
        ),
    )(*parts, w_gu, w_dn)


def on_device(
    states_in,
    w_qkv,
    qk_gain,
    w_out,
    post_gain,
    w_gate_up,
    w_down,
    cache_keys,
    cache_values,
    slot_node,
    node_length,
    node_parent,
    leaf_segment,
    leaf_node,
):
    yhi, x_at, z_at, ylo, core = (lax.axis_index(a) for a in ("yhi", "x", "z", "ylo", "core"))
    n_y, n_x, n_z = (lax.axis_size(a) for a in BLK)
    blk = (yhi * n_x + x_at) * n_z + z_at
    head_index = ylo * 2 + core
    rows = states_in.shape[0]
    heads_here = w_qkv.shape[2] // HD
    columns = w_qkv.shape[2] * 4

    corner = ("yhi", "z", "core")

    def across(values, s):
        pairs = [
            ((y * n_z + z) * 2 + c, (c * n_z + (z + s) % n_z) * 2 + y)
            for y in range(n_y) for z in range(n_z) for c in range(2)
        ]
        return lax.ppermute(values, corner, pairs)

    def head_piece(s):
        cut = ((z_at + s) % n_z) * HD
        return jnp.stack(
            [lax.dynamic_slice_in_dim(c[0], cut, HD, 1) for c in (cache_keys, cache_values)]
        )

    cached = jnp.stack([across(head_piece(s), s) for s in range(n_z)])
    cached_parts = [cached] + [shift(cached, "x", s) for s in (1, 3, 2)]
    cached_parts = cached_parts + [shift(part, "core", 1) for part in cached_parts]
    slot_from = jnp.stack(
        [
            (jnp.where(c == 0, core, 1 - core) * n_x + (x_at - sx) % n_x) * n_z + (z_at - sz) % n_z
            for c in range(2) for sx in (0, 1, 3, 2) for sz in range(n_z)
        ]
    ).astype(jnp.int32)

    def other_weights(weights):
        there = lax.ppermute(weights, ("yhi", "core"), [(3, 1), (0, 2)])
        return jnp.where(yhi == core, weights, there)

    w_gate_up, w_down, _ = lax.optimization_barrier((w_gate_up, w_down, cached))
    w_gu = other_weights(w_gate_up)
    w_dn = other_weights(w_down)
    w_out = lax.dynamic_slice_in_dim(jnp.concatenate([w_out, w_out]), z_at * HD, w_out.shape[0], 0)

    qkv_raw = jnp.einsum("td,cdw->ctw", states_in, w_qkv, preferred_element_type=F32)
    squares = lax.psum(jnp.sum(qkv_raw[:2] * qkv_raw[:2], axis=2), HEAD)
    group_from = jnp.stack(
        [blk] + [(core * n_x + x_at) * n_z + (z_at - g) % n_z for g in range(n_z)]
    ).astype(jnp.int32)
    segments = jnp.take(leaf_segment, group_from, axis=0)
    middle, root, position = tree_info(
        segments, jnp.take(leaf_node, group_from, axis=0), node_parent, node_length
    )
    position, middle, root, segments = position[0], middle[1:], root[1:], segments[1:]
    half = HD // 2
    frequency = THETA ** (-2.0 * jnp.arange(half, dtype=F32) / HD)
    angles = position.astype(F32)[:, None] * frequency[None, :]
    cosine, sine = jnp.cos(angles)[:, None, :], jnp.sin(angles)[:, None, :]

    def normed(c):
        scaled = qkv_raw[c] * lax.rsqrt(squares[c] / columns + EPS)[:, None] * qk_gain[c]
        scaled = scaled.reshape(rows, heads_here, HD)
        low, high = scaled[..., :half], scaled[..., half:]
        turned = jnp.concatenate([low * cosine - high * sine, high * cosine + low * sine], axis=-1)
        return turned.astype(BF)

    qkv = jnp.stack(
        [normed(0), normed(1), qkv_raw[2].astype(BF).reshape(rows, heads_here, HD)]
    ).transpose(2, 0, 1, 3)
    qkv_parts = [across(select_row(qkv, (z_at + s) % n_z), s) for s in range(n_z)]

    slots = slot_from.shape[0]
    slot_nodes = jnp.take(slot_node, slot_from)
    slot_lengths = jnp.take(node_length, slot_nodes)
    halves = (n_z, 2, rows // 2, 1)
    needed = jnp.any(
        (middle.reshape(halves) == slot_nodes) | (root.reshape(halves) == slot_nodes), axis=2
    )
    before = jnp.arange(slots)[:, None] < jnp.arange(slots)[None, :]
    rank = jnp.sum(jnp.where(needed[..., :, None] & before, 1, 0), axis=2)
    longest = leaf_node.shape[1] + 4
    places = jnp.arange(longest, dtype=jnp.int32)
    lists = jnp.sum(
        jnp.where(
            needed[..., :, None] & (rank[..., :, None] == places),
            jnp.arange(slots, dtype=jnp.int32)[:, None], 0,
        ),
        axis=2,
    )
    counts = jnp.sum(needed.astype(jnp.int32), axis=2)
    row_info = jnp.stack([middle, root, segments], axis=-1)
    attended = attention(
        slot_nodes, slot_lengths, lists, counts, qkv_parts, row_info, segments[:, None, :],
        cached_parts,
    )

    def back(values, s):
        pairs = [
            ((y * n_z + z) * 2 + c, (c * n_z + (z - s) % n_z) * 2 + y)
            for y in range(n_y) for z in range(n_z) for c in range(2)
        ]
        return lax.ppermute(values, corner, pairs)

    attended = jnp.concatenate([back(attended[s], s) for s in range(n_z)], axis=1)
    attn_part = jnp.dot(attended, w_out, preferred_element_type=F32)
    attn_part = attn_part.reshape(2, 2, rows // 4, -1)

    def of_core(c):
        return lax.dynamic_index_in_dim(attn_part, c, 1, keepdims=False)

    attn_part = of_core(core) + shift(of_core(1 - core).astype(BF), "core", 1).astype(F32)
    attn_proj = select_row(attn_part, ylo) + shift(
        select_row(attn_part, 1 - ylo).astype(BF), "ylo", 1
    ).astype(F32)
    own_rows = rows // 4
    state_rows = lax.dynamic_slice_in_dim(states_in, head_index * own_rows, own_rows, 0)
    mid_state = (state_rows.astype(F32) + rms_norm(attn_proj, post_gain[0])).astype(BF)

    cut = own_rows // 2
    upper, lower = mid_state[:cut], mid_state[cut:]
    upper4 = jnp.concatenate([upper] + [shift(upper, "x", s) for s in range(1, n_x)])
    lower4 = jnp.concatenate([lower] + [shift(lower, "z", s) for s in range(1, n_z)])

    upper_sum = lower_sum = 0.0
    for t in (0, 1, 3, 2):
        pair = (upper4, lower4)
        if t:
            pair = (shift(upper4, "z", t), shift(lower4, "x", t))
        own, other = feed_forward(
            pair + (shift(pair[0], "core", 1), shift(pair[1], "core", 1)), w_gu, w_dn
        )
        total = own.astype(F32) + shift(other, "core", 1).astype(F32)
        up_part, low_part = total[0], total[1]
        if t:
            up_part = shift(up_part.astype(BF), "z", n_z - t).astype(F32)
            low_part = shift(low_part.astype(BF), "x", n_x - t).astype(F32)
        upper_sum = upper_sum + up_part
        lower_sum = lower_sum + low_part
    upper_sum = upper_sum.reshape(n_x, cut, -1)
    lower_sum = lower_sum.reshape(n_z, cut, -1)
    upper_out, lower_out = upper_sum[0], lower_sum[0]
    for s in range(1, 4):
        upper_out = upper_out + shift(upper_sum[s].astype(BF), "x", n_x - s).astype(F32)
        lower_out = lower_out + shift(lower_sum[s].astype(BF), "z", n_z - s).astype(F32)
    mlp_proj = jnp.concatenate([upper_out, lower_out])
    return (mid_state.astype(F32) + rms_norm(mlp_proj, post_gain[1])).astype(BF)


def solution(mesh):
    fine = Mesh(mesh.devices.reshape(2, 4, 4, 2, 2), BLK + HEAD)
    placed = (
        P(BLK, None),
        P(None, None, HEAD),
        P(None, HEAD),
        P(HEAD, None),
        P(),
        P(None, None, BLK),
        P(BLK, None),
        P(BLK, None, HEAD),
        P(BLK, None, HEAD),
        P(),
        P(),
        P(),
        P(),
        P(),
    )
    return jax.shard_map(
        on_device, mesh=fine, in_specs=placed, out_specs=P(BLK + HEAD, None), check_vma=False
    )
```

profile of v0, /device:TPU:0, one launch (start us, length us, event | category | flops | bytes accessed | tf_op | source)
XLA Modules:
  0.0 245.6 jit_solution(16817349462299053234)
XLA Ops:
  0.0 4.9 %convolution_bitcast_fusion = f32[3,256,512]{1,2,0:T(8,128)S(1)} fusion(bf16[3,2048,512]{2,1,0:T(8,128)(2,1)} %param.17, bf16[256,2048]{1,0:T(8,128)(2,1)} %param.16), kind=kOutput, calls=%fused_computation.13 | convolution fusion | flops 1610612736 | bytes 8912896 | tf_op jit(solution)/shard_map/td,cdw->ctw/dot_general | solution.py:285
  7.4 7.1 %psum.7 = f32[2,256]{1,0:T(2,128)S(1)} all-reduce(f32[2,256]{1,0:T(2,128)S(1)} %fusion.9), channel_id=1, replica_groups=mesh['yhi'=2,'x'=4,'z'=4,'ylo'=2,'core'=2] {'ylo','core'}, use_global_device_ids=true, to_apply=%region_7.9 | all-reduce | flops 512 | bytes 4096 | tf_op jit(solution)/shard_map/psum | solution.py:286
  18.6 4.1 %collective-permute-start.7 = (bf16[2,256,128]{2,1,0:T(8,128)(2,1)S(1)}, bf16[2,256,128]{2,1,0:T(8,128)(2,1)S(1)}, u32[]{:S(2)}, u32[]{:S(2)}) collective-permute-start(bf16[2,256,128]{2,1,0:T(8,128)(2,1)S(1)} %pad_maximum_fusion.8), channel_id=1, source_target_pairs={{0,12},{1,76},{4,0},{5,64},{8,4},{9,68},{12,8},{13,72},{64,13},{65... | collective-permute-start | bytes 393224 | tf_op jit(solution)/shard_map/ppermute | solution.py:258
  22.9 1.3 collective-permute-start.5
  26.8 2.3 collective-permute-start.1
  30.6 1.6 collective-permute-start.8
  32.2 1.7 collective-permute-start.9
  33.9 1.8 collective-permute-start.10
  36.5 1.2 gather_fusion.3
  37.7 7.5 %collective-permute-start.11 = (bf16[4,2,256,128]{3,2,1,0:T(8,128)(2,1)S(1)}, bf16[4,2,256,128]{3,2,1,0:T(8,128)(2,1)S(1)}, u32[]{:S(2)}, u32[]{:S(2)}) collective-permute-start(bf16[4,2,256,128]{3,2,1,0:T(8,128)(2,1)S(1)} %pad_maximum_fusion.1.rest_6_), channel_id=1, source_target_pairs={{0,1},{1,0},{2,3},{3,2},{4,5},{5,4},{6,7},{7,6},{8,9},{9,8},{10,11... | collective-permute-start | bytes 1572872 | tf_op jit(solution)/shard_map/ppermute | solution.py:23
  45.3 7.9 %collective-permute-start.12 = (bf16[4,2,256,128]{3,2,1,0:T(8,128)(2,1)S(1)}, bf16[4,2,256,128]{3,2,1,0:T(8,128)(2,1)}, u32[]{:S(2)}, u32[]{:S(2)}) collective-permute-start(bf16[4,2,256,128]{3,2,1,0:T(8,128)(2,1)S(1)} %collective-permute-done.8.rest_7_), channel_id=1, source_target_pairs={{0,1},{1,0},{2,3},{3,2},{4,5},{5,4},{6,7},{7,6},{8,9},{9,8},{10,11... | collective-permute-start | bytes 1572872 | tf_op jit(solution)/shard_map/ppermute | solution.py:23
  53.1 5.6 %collective-permute-start.14 = (bf16[4,2,256,128]{3,2,1,0:T(8,128)(2,1)S(1)}, bf16[4,2,256,128]{3,2,1,0:T(8,128)(2,1)}, u32[]{:S(2)}, u32[]{:S(2)}) collective-permute-start(bf16[4,2,256,128]{3,2,1,0:T(8,128)(2,1)S(1)} %collective-permute-done.10.rest_9_), channel_id=1, source_target_pairs={{0,1},{1,0},{2,3},{3,2},{4,5},{5,4},{6,7},{7,6},{8,9},{9,8},{10,11... | collective-permute-start | bytes 1572872 | tf_op jit(solution)/shard_map/ppermute | solution.py:23
  58.9 1.4 collective-permute-start.2
  60.9 1.3 pad_add_fusion
  63.8 2.6 %collective-permute-done.2.rest_2_ = bf16[3,256,128]{2,1,0:T(8,128)(2,1)} collective-permute-done((bf16[3,256,128]{2,1,0:T(8,128)(2,1)}, bf16[3,256,128]{2,1,0:T(8,128)(2,1)}, u32[]{:S(2)}, u32[]{:S(2)}) %collective-permute-start.2) | collective-permute-done | bytes 196640 | tf_op jit(solution)/shard_map/ppermute | solution.py:258
  67.9 4.5 %collective-permute-done.3.rest_3_ = bf16[3,256,128]{2,1,0:T(8,128)(2,1)S(1)} collective-permute-done((bf16[3,256,128]{2,1,0:T(8,128)(2,1)}, bf16[3,256,128]{2,1,0:T(8,128)(2,1)S(1)}, u32[]{:S(2)}, u32[]{:S(2)}) %collective-permute-start.3) | collective-permute-done | bytes 196640 | tf_op jit(solution)/shard_map/ppermute | solution.py:258
  72.4 20.3 %shard_map.136 = bf16[4,256,128]{2,1,0:T(8,128)(2,1)S(1)} custom-call(s32[32]{0:T(128)S(1)} %get-tuple-element.37.nodes_ref, s32[32]{0:T(128)S(1)} %and_select_fusion.lengths_ref, s32[4,2,12]{2,1,0:T(2,128)S(1)} %copy.56.lists_ref, s32[4,2]{1,0:T(4,128)S(1)} %copy.57.counts_ref, bf16[3,256,128]{2,1,0:T(8,128)(2,1)S(1)} %collective-permute-done.rest_0_, ...), custom_call_target="tpu_custom_call" | custom-call | flops 2000000000 | bytes 6000000 | tf_op jit(solution)/shard_map/pallas_call | solution.py:158
  92.8 3.5 %collective-permute-start.17 = (bf16[256,128]{1,0:T(8,128)(2,1)S(1)}, bf16[256,128]{1,0:T(8,128)(2,1)S(1)}, u32[]{:S(2)}, u32[]{:S(2)}) collective-permute-start(bf16[256,128]{1,0:T(8,128)(2,1)S(1)} %get-tuple-element.66), channel_id=1, source_target_pairs={{0,8},{1,72},{4,12},{5,76},{8,0},{9,64},{12,4},{13,68},{64,9},{65,... | collective-permute-start | bytes 196616 | tf_op jit(solution)/shard_map/ppermute | solution.py:342
  99.2 1.3 collective-permute-done.16
  100.5 2.8 %fusion.1 = f32[256,2048]{1,0:T(8,128)S(1)} fusion(s32[]{:T(128)S(6)} %select_n.369, bf16[512,2048]{1,0:T(8,128)(2,1)} %param.19, bf16[256,128]{1,0:T(8,128)(2,1)S(1)} %collective-permute-done.18, bf16[256,128]{1,0:T(8,128)(2,1)S(1)} %collective-permute-done.17, bf16[256,128]{1,0:T(8,128)(2,1)S(1)} %collective-permute-done.16, ...), kind=kOutput, calls=%fused_computation.7 | convolution fusion | flops 542113792 | bytes 4456452 | tf_op jit(solution)/shard_map/dot_general | solution.py:345
  103.4 8.9 %collective-permute-start.19 = (bf16[2,64,2048]{2,1,0:T(8,128)(2,1)S(1)}, bf16[2,64,2048]{2,1,0:T(8,128)(2,1)S(1)}, u32[]{:S(2)}, u32[]{:S(2)}) collective-permute-start(bf16[2,64,2048]{2,1,0:T(8,128)(2,1)S(1)} %fusion.11), channel_id=1, source_target_pairs={{0,1},{1,0},{2,3},{3,2},{4,5},{5,4},{6,7},{7,6},{8,9},{9,8},{10,11... | collective-permute-start | bytes 1572872 | tf_op jit(solution)/shard_map/ppermute | solution.py:23
  112.3 1.5 collective-permute-done.19
  114.4 7.2 %collective-permute-start.29 = (bf16[2,2048,256]{2,1,0:T(8,128)(2,1)}, bf16[2,2048,256]{2,1,0:T(8,128)(2,1)}, u32[]{:S(2)}, u32[]{:S(2)}) collective-permute-start(bf16[2,2048,256]{2,1,0:T(8,128)(2,1)} %param.21), channel_id=1, source_target_pairs={{65,1},{0,64},{67,3},{2,66},{69,5},{4,68},{71,7},{6,70},{73,9},{8,... | collective-permute-start | bytes 6291464 | tf_op jit(solution)/shard_map/ppermute | solution.py:277
  124.0 5.1 %collective-permute-start.23 = (bf16[32,2048]{1,0:T(8,128)(2,1)S(1)}, bf16[32,2048]{1,0:T(8,128)(2,1)S(1)}, u32[]{:S(2)}, u32[]{:S(2)}) collective-permute-start(bf16[32,2048]{1,0:T(8,128)(2,1)S(1)} %get-tuple-element.63), channel_id=1, source_target_pairs={{0,48},{16,0},{32,16},{48,32},{1,49},{17,1},{33,17},{49,33},{2,50}... | collective-permute-start | bytes 393224 | tf_op jit(solution)/shard_map/ppermute | solution.py:23
  130.0 6.8 %collective-permute-start.30 = (bf16[256,2048]{1,0:T(8,128)(2,1)S(1)}, bf16[256,2048]{1,0:T(8,128)(2,1)}, u32[]{:S(2)}, u32[]{:S(2)}) collective-permute-start(bf16[256,2048]{1,0:T(8,128)(2,1)S(1)} %copy-done.4), channel_id=1, source_target_pairs={{65,1},{0,64},{67,3},{2,66},{69,5},{4,68},{71,7},{6,70},{73,9},{8,... | collective-permute-start | bytes 3145736 | tf_op jit(solution)/shard_map/ppermute | solution.py:277
  136.8 3.6 %collective-permute-start.25 = (bf16[32,2048]{1,0:T(8,128)(2,1)S(1)}, bf16[32,2048]{1,0:T(8,128)(2,1)S(1)}, u32[]{:S(2)}, u32[]{:S(2)}) collective-permute-start(bf16[32,2048]{1,0:T(8,128)(2,1)S(1)} %get-tuple-element.62), channel_id=1, source_target_pairs={{0,8},{4,12},{8,0},{12,4},{1,9},{5,13},{9,1},{13,5},{2,10},{6,14},... | collective-permute-start | bytes 393224 | tf_op jit(solution)/shard_map/ppermute | solution.py:23
  140.5 1.3 collective-permute-done.26
  141.8 2.2 collective-permute-start.44
  144.4 12.2 %collective-permute-done.24 = bf16[32,2048]{1,0:T(8,128)(2,1)S(1)} collective-permute-done((bf16[32,2048]{1,0:T(8,128)(2,1)S(1)}, bf16[32,2048]{1,0:T(8,128)(2,1)S(1)}, u32[]{:S(2)}, u32[]{:S(2)}) %collective-permute-start.24) | collective-permute-done | bytes 131104 | tf_op jit(solution)/shard_map/ppermute | solution.py:23
  157.6 9.7 %collective-permute-done.45.refs_1_ = bf16[128,2048]{1,0:T(8,128)(2,1)S(1)} collective-permute-done((bf16[128,2048]{1,0:T(8,128)(2,1)S(1)}, bf16[128,2048]{1,0:T(8,128)(2,1)S(1)}, u32[]{:S(2)}, u32[]{:S(2)}) %collective-permute-start.45) | collective-permute-done | bytes 524320 | tf_op jit(solution)/shard_map/ppermute | solution.py:23
  167.5 2.9 %collective-permute-start.39 = (bf16[128,2048]{1,0:T(8,128)(2,1)S(1)}, bf16[128,2048]{1,0:T(8,128)(2,1)S(1)}, u32[]{:S(2)}, u32[]{:S(2)}) collective-permute-start(bf16[128,2048]{1,0:T(8,128)(2,1)S(1)} %pad_maximum_fusion.3.refs_1_), channel_id=1, source_target_pairs={{0,48},{16,0},{32,16},{48,32},{1,49},{17,1},{33,17},{49,33},{2,50}... | collective-permute-start | bytes 1572872 | tf_op jit(solution)/shard_map/ppermute | solution.py:23
  170.5 1.5 collective-permute-start.27
  172.3 1.8 broadcast_select_fusion.refs_4_
  174.2 3.0 %shard_map.140 = (bf16[2,128,2048]{2,1,0:T(8,128)(2,1)S(1)}, bf16[2,128,2048]{2,1,0:T(8,128)(2,1)S(1)}) custom-call(bf16[128,2048]{1,0:T(8,128)(2,1)S(1)} %collective-permute-done.44.refs_0_, bf16[128,2048]{1,0:T(8,128)(2,1)S(1)} %collective-permute-done.45.refs_1_, bf16[128,2048]{1,0:T(8,128)(2,1)S(1)} %collective-permute-done.46.refs_2_, ...), custom_call_target="tpu_custom_call" | custom-call | flops 1610612736 | bytes 7340032 | tf_op jit(solution)/shard_map/pallas_call | solution.py:212
  177.2 4.8 %collective-permute-done.39.refs_1_ = bf16[128,2048]{1,0:T(8,128)(2,1)S(1)} collective-permute-done((bf16[128,2048]{1,0:T(8,128)(2,1)S(1)}, bf16[128,2048]{1,0:T(8,128)(2,1)S(1)}, u32[]{:S(2)}, u32[]{:S(2)}) %collective-permute-start.39) | collective-permute-done | bytes 524320 | tf_op jit(solution)/shard_map/ppermute | solution.py:23
  182.8 3.2 %collective-permute-done.32.refs_0_ = bf16[128,2048]{1,0:T(8,128)(2,1)S(1)} collective-permute-done((bf16[128,2048]{1,0:T(8,128)(2,1)S(1)}, bf16[128,2048]{1,0:T(8,128)(2,1)S(1)}, u32[]{:S(2)}, u32[]{:S(2)}) %collective-permute-start.32) | collective-permute-done | bytes 524320 | tf_op jit(solution)/shard_map/ppermute | solution.py:23
  187.0 3.0 %shard_map.137 = (bf16[2,128,2048]{2,1,0:T(8,128)(2,1)S(1)}, bf16[2,128,2048]{2,1,0:T(8,128)(2,1)S(1)}) custom-call(bf16[128,2048]{1,0:T(8,128)(2,1)S(1)} %pad_maximum_fusion.2.refs_0_, bf16[128,2048]{1,0:T(8,128)(2,1)S(1)} %pad_maximum_fusion.3.refs_1_, bf16[128,2048]{1,0:T(8,128)(2,1)S(1)} %collective-permute-done.27.refs_2_, ...), custom_call_target="tpu_custom_call" | custom-call | flops 1610612736 | bytes 7340032 | tf_op jit(solution)/shard_map/pallas_call | solution.py:212
  190.4 3.0 %shard_map.139 = (bf16[2,128,2048]{2,1,0:T(8,128)(2,1)S(1)}, bf16[2,128,2048]{2,1,0:T(8,128)(2,1)S(1)}) custom-call(bf16[128,2048]{1,0:T(8,128)(2,1)S(1)} %collective-permute-done.38.refs_0_, bf16[128,2048]{1,0:T(8,128)(2,1)S(1)} %collective-permute-done.39.refs_1_, bf16[128,2048]{1,0:T(8,128)(2,1)S(1)} %collective-permute-done.40.refs_2_, ...), custom_call_target="tpu_custom_call" | custom-call | flops 1610612736 | bytes 7340032 | tf_op jit(solution)/shard_map/pallas_call | solution.py:212
  193.8 3.0 %shard_map.138 = (bf16[2,128,2048]{2,1,0:T(8,128)(2,1)S(1)}, bf16[2,128,2048]{2,1,0:T(8,128)(2,1)S(1)}) custom-call(bf16[128,2048]{1,0:T(8,128)(2,1)S(1)} %collective-permute-done.32.refs_0_, bf16[128,2048]{1,0:T(8,128)(2,1)S(1)} %collective-permute-done.33.refs_1_, bf16[128,2048]{1,0:T(8,128)(2,1)S(1)} %collective-permute-done.34.refs_2_, ...), custom_call_target="tpu_custom_call" | custom-call | flops 1610612736 | bytes 7340032 | tf_op jit(solution)/shard_map/pallas_call | solution.py:212
  199.3 3.1 %collective-permute-start.43 = (bf16[128,2048]{1,0:T(8,128)(2,1)S(1)}, bf16[128,2048]{1,0:T(8,128)(2,1)S(1)}, u32[]{:S(2)}, u32[]{:S(2)}) collective-permute-start(bf16[128,2048]{1,0:T(8,128)(2,1)S(1)} %get-tuple-element.44), channel_id=1, source_target_pairs={{0,4},{4,8},{8,12},{12,0},{1,5},{5,9},{9,13},{13,1},{2,6},{6,10},{... | collective-permute-start | bytes 1572872 | tf_op jit(solution)/shard_map/ppermute | solution.py:23
  203.8 10.2 %collective-permute-done.49 = bf16[128,2048]{1,0:T(8,128)(2,1)S(1)} collective-permute-done((bf16[128,2048]{1,0:T(8,128)(2,1)S(1)}, bf16[128,2048]{1,0:T(8,128)(2,1)S(1)}, u32[]{:S(2)}, u32[]{:S(2)}) %collective-permute-start.49) | collective-permute-done | bytes 524320 | tf_op jit(solution)/shard_map/ppermute | solution.py:23
  214.5 10.1 %collective-permute-done.43 = bf16[128,2048]{1,0:T(8,128)(2,1)S(1)} collective-permute-done((bf16[128,2048]{1,0:T(8,128)(2,1)S(1)}, bf16[128,2048]{1,0:T(8,128)(2,1)S(1)}, u32[]{:S(2)}, u32[]{:S(2)}) %collective-permute-start.43) | collective-permute-done | bytes 524320 | tf_op jit(solution)/shard_map/ppermute | solution.py:23
  225.0 4.6 %collective-permute-done.54 = bf16[128,2048]{1,0:T(8,128)(2,1)S(1)} collective-permute-done((bf16[128,2048]{1,0:T(8,128)(2,1)S(1)}, bf16[128,2048]{1,0:T(8,128)(2,1)S(1)}, u32[]{:S(2)}, u32[]{:S(2)}) %collective-permute-start.54) | collective-permute-done | bytes 524320 | tf_op jit(solution)/shard_map/ppermute | solution.py:23
  232.3 2.0 collective-permute-start.56
  234.5 2.3 collective-permute-start.51
  236.8 2.8 %collective-permute-done.58 = bf16[32,2048]{1,0:T(8,128)(2,1)S(1)} collective-permute-done((bf16[32,2048]{1,0:T(8,128)(2,1)S(1)}, bf16[32,2048]{1,0:T(8,128)(2,1)S(1)}, u32[]{:S(2)}, u32[]{:S(2)}) %collective-permute-start.58) | collective-permute-done | bytes 131104 | tf_op jit(solution)/shard_map/ppermute | solution.py:23
  240.2 2.5 %collective-permute-done.52 = bf16[32,2048]{1,0:T(8,128)(2,1)S(1)} collective-permute-done((bf16[32,2048]{1,0:T(8,128)(2,1)S(1)}, bf16[32,2048]{1,0:T(8,128)(2,1)S(1)}, u32[]{:S(2)}, u32[]{:S(2)}) %collective-permute-start.52) | collective-permute-done | bytes 131104 | tf_op jit(solution)/shard_map/ppermute | solution.py:23
  242.8 1.8 collective-permute-done.50
  (194 shorter events, 35.6 us)
Async XLA Ops:
  17.7 20.1 %collective-permute-start = (bf16[3,256,128]{2,1,0:T(8,128)(2,1)S(1)}, bf16[3,256,128]{2,1,0:T(8,128)(2,1)S(1)}, u32[]{:S(2)}, u32[]{:S(2)}) collective-permute-start(bf16[3,256,128]{2,1,0:T(8,128)(2,1)S(1)} %get-tuple-element.51), channel_id=1, source_target_pairs={{0,0},{1,64},{4,4},{5,68},{8,8},{9,72},{12,12},{13,76},{64,1},{65,... | collective-permute-start | bytes 589832 | tf_op jit(solution)/shard_map/ppermute | solution.py:258
  18.6 8.1 %collective-permute-start.7 = (bf16[2,256,128]{2,1,0:T(8,128)(2,1)S(1)}, bf16[2,256,128]{2,1,0:T(8,128)(2,1)S(1)}, u32[]{:S(2)}, u32[]{:S(2)}) collective-permute-start(bf16[2,256,128]{2,1,0:T(8,128)(2,1)S(1)} %pad_maximum_fusion.8), channel_id=1, source_target_pairs={{0,12},{1,76},{4,0},{5,64},{8,4},{9,68},{12,8},{13,72},{64,13},{65... | collective-permute-start | bytes 393224 | tf_op jit(solution)/shard_map/ppermute | solution.py:258
  22.8 6.7 %collective-permute-start.6 = (bf16[2,256,128]{2,1,0:T(8,128)(2,1)S(1)}, bf16[2,256,128]{2,1,0:T(8,128)(2,1)S(1)}, u32[]{:S(2)}, u32[]{:S(2)}) collective-permute-start(bf16[2,256,128]{2,1,0:T(8,128)(2,1)S(1)} %pad_maximum_fusion.7), channel_id=1, source_target_pairs={{0,8},{1,72},{4,12},{5,76},{8,0},{9,64},{12,4},{13,68},{64,9},{65,... | collective-permute-start | bytes 393224 | tf_op jit(solution)/shard_map/ppermute | solution.py:258
  22.9 7.7 %collective-permute-start.5 = (bf16[2,256,128]{2,1,0:T(8,128)(2,1)S(1)}, bf16[2,256,128]{2,1,0:T(8,128)(2,1)S(1)}, u32[]{:S(2)}, u32[]{:S(2)}) collective-permute-start(bf16[2,256,128]{2,1,0:T(8,128)(2,1)S(1)} %pad_maximum_fusion.6), channel_id=1, source_target_pairs={{0,4},{1,68},{4,8},{5,72},{8,12},{9,76},{12,0},{13,64},{64,5},{65,... | collective-permute-start | bytes 393224 | tf_op jit(solution)/shard_map/ppermute | solution.py:258
  24.2 6.3 %collective-permute-start.4 = (bf16[2,256,128]{2,1,0:T(8,128)(2,1)S(1)}, bf16[2,256,128]{2,1,0:T(8,128)(2,1)S(1)}, u32[]{:S(2)}, u32[]{:S(2)}) collective-permute-start(bf16[2,256,128]{2,1,0:T(8,128)(2,1)S(1)} %pad_maximum_fusion.5), channel_id=1, source_target_pairs={{0,0},{1,64},{4,4},{5,68},{8,8},{9,72},{12,12},{13,76},{64,1},{65,... | collective-permute-start | bytes 393224 | tf_op jit(solution)/shard_map/ppermute | solution.py:258
  26.8 32.1 %collective-permute-start.1 = (bf16[3,256,128]{2,1,0:T(8,128)(2,1)S(1)}, bf16[3,256,128]{2,1,0:T(8,128)(2,1)S(1)}, u32[]{:S(2)}, u32[]{:S(2)}) collective-permute-start(bf16[3,256,128]{2,1,0:T(8,128)(2,1)S(1)} %get-tuple-element.50), channel_id=1, source_target_pairs={{0,4},{1,68},{4,8},{5,72},{8,12},{9,76},{12,0},{13,64},{64,5},{65,... | collective-permute-start | bytes 589832 | tf_op jit(solution)/shard_map/ppermute | solution.py:258
  30.6 14.6 %collective-permute-start.8 = (bf16[4,2,256,128]{3,2,1,0:T(8,128)(2,1)S(1)}, bf16[4,2,256,128]{3,2,1,0:T(8,128)(2,1)S(1)}, u32[]{:S(2)}, u32[]{:S(2)}) collective-permute-start(bf16[4,2,256,128]{3,2,1,0:T(8,128)(2,1)S(1)} %pad_maximum_fusion.1.rest_6_), channel_id=1, source_target_pairs={{0,16},{16,32},{32,48},{48,0},{1,17},{17,33},{33,49},{49,1},{2,18}... | collective-permute-start | bytes 1572872 | tf_op jit(solution)/shard_map/ppermute | solution.py:23
  32.2 21.0 %collective-permute-start.9 = (bf16[4,2,256,128]{3,2,1,0:T(8,128)(2,1)S(1)}, bf16[4,2,256,128]{3,2,1,0:T(8,128)(2,1)S(1)}, u32[]{:S(2)}, u32[]{:S(2)}) collective-permute-start(bf16[4,2,256,128]{3,2,1,0:T(8,128)(2,1)S(1)} %pad_maximum_fusion.1.rest_6_), channel_id=1, source_target_pairs={{0,48},{16,0},{32,16},{48,32},{1,49},{17,1},{33,17},{49,33},{2,50}... | collective-permute-start | bytes 1572872 | tf_op jit(solution)/shard_map/ppermute | solution.py:23
  33.9 19.2 %collective-permute-start.10 = (bf16[4,2,256,128]{3,2,1,0:T(8,128)(2,1)S(1)}, bf16[4,2,256,128]{3,2,1,0:T(8,128)(2,1)S(1)}, u32[]{:S(2)}, u32[]{:S(2)}) collective-permute-start(bf16[4,2,256,128]{3,2,1,0:T(8,128)(2,1)S(1)} %pad_maximum_fusion.1.rest_6_), channel_id=1, source_target_pairs={{0,32},{16,48},{32,0},{48,16},{1,33},{17,49},{33,1},{49,17},{2,34}... | collective-permute-start | bytes 1572872 | tf_op jit(solution)/shard_map/ppermute | solution.py:23
  37.7 34.6 %collective-permute-start.11 = (bf16[4,2,256,128]{3,2,1,0:T(8,128)(2,1)S(1)}, bf16[4,2,256,128]{3,2,1,0:T(8,128)(2,1)S(1)}, u32[]{:S(2)}, u32[]{:S(2)}) collective-permute-start(bf16[4,2,256,128]{3,2,1,0:T(8,128)(2,1)S(1)} %pad_maximum_fusion.1.rest_6_), channel_id=1, source_target_pairs={{0,1},{1,0},{2,3},{3,2},{4,5},{5,4},{6,7},{7,6},{8,9},{9,8},{10,11... | collective-permute-start | bytes 1572872 | tf_op jit(solution)/shard_map/ppermute | solution.py:23
  45.3 27.1 %collective-permute-start.12 = (bf16[4,2,256,128]{3,2,1,0:T(8,128)(2,1)S(1)}, bf16[4,2,256,128]{3,2,1,0:T(8,128)(2,1)}, u32[]{:S(2)}, u32[]{:S(2)}) collective-permute-start(bf16[4,2,256,128]{3,2,1,0:T(8,128)(2,1)S(1)} %collective-permute-done.8.rest_7_), channel_id=1, source_target_pairs={{0,1},{1,0},{2,3},{3,2},{4,5},{5,4},{6,7},{7,6},{8,9},{9,8},{10,11... | collective-permute-start | bytes 1572872 | tf_op jit(solution)/shard_map/ppermute | solution.py:23
  53.1 19.2 %collective-permute-start.13 = (bf16[4,2,256,128]{3,2,1,0:T(8,128)(2,1)S(1)}, bf16[4,2,256,128]{3,2,1,0:T(8,128)(2,1)}, u32[]{:S(2)}, u32[]{:S(2)}) collective-permute-start(bf16[4,2,256,128]{3,2,1,0:T(8,128)(2,1)S(1)} %collective-permute-done.9.rest_8_), channel_id=1, source_target_pairs={{0,1},{1,0},{2,3},{3,2},{4,5},{5,4},{6,7},{7,6},{8,9},{9,8},{10,11... | collective-permute-start | bytes 1572872 | tf_op jit(solution)/shard_map/ppermute | solution.py:23
  53.1 19.2 %collective-permute-start.14 = (bf16[4,2,256,128]{3,2,1,0:T(8,128)(2,1)S(1)}, bf16[4,2,256,128]{3,2,1,0:T(8,128)(2,1)}, u32[]{:S(2)}, u32[]{:S(2)}) collective-permute-start(bf16[4,2,256,128]{3,2,1,0:T(8,128)(2,1)S(1)} %collective-permute-done.10.rest_9_), channel_id=1, source_target_pairs={{0,1},{1,0},{2,3},{3,2},{4,5},{5,4},{6,7},{7,6},{8,9},{9,8},{10,11... | collective-permute-start | bytes 1572872 | tf_op jit(solution)/shard_map/ppermute | solution.py:23
  58.9 7.6 %collective-permute-start.2 = (bf16[3,256,128]{2,1,0:T(8,128)(2,1)}, bf16[3,256,128]{2,1,0:T(8,128)(2,1)}, u32[]{:S(2)}, u32[]{:S(2)}) collective-permute-start(bf16[3,256,128]{2,1,0:T(8,128)(2,1)} %get-tuple-element.49), channel_id=1, source_target_pairs={{0,8},{1,72},{4,12},{5,76},{8,0},{9,64},{12,4},{13,68},{64,9},{65,... | collective-permute-start | bytes 589832 | tf_op jit(solution)/shard_map/ppermute | solution.py:258
  92.8 6.4 %collective-permute-start.17 = (bf16[256,128]{1,0:T(8,128)(2,1)S(1)}, bf16[256,128]{1,0:T(8,128)(2,1)S(1)}, u32[]{:S(2)}, u32[]{:S(2)}) collective-permute-start(bf16[256,128]{1,0:T(8,128)(2,1)S(1)} %get-tuple-element.66), channel_id=1, source_target_pairs={{0,8},{1,72},{4,12},{5,76},{8,0},{9,64},{12,4},{13,68},{64,9},{65,... | collective-permute-start | bytes 196616 | tf_op jit(solution)/shard_map/ppermute | solution.py:342
  103.4 10.4 %collective-permute-start.19 = (bf16[2,64,2048]{2,1,0:T(8,128)(2,1)S(1)}, bf16[2,64,2048]{2,1,0:T(8,128)(2,1)S(1)}, u32[]{:S(2)}, u32[]{:S(2)}) collective-permute-start(bf16[2,64,2048]{2,1,0:T(8,128)(2,1)S(1)} %fusion.11), channel_id=1, source_target_pairs={{0,1},{1,0},{2,3},{3,2},{4,5},{5,4},{6,7},{7,6},{8,9},{9,8},{10,11... | collective-permute-start | bytes 1572872 | tf_op jit(solution)/shard_map/ppermute | solution.py:23
  114.0 8.7 %collective-permute-start.20 = (bf16[64,2048]{1,0:T(8,128)(2,1)S(1)}, bf16[64,2048]{1,0:T(8,128)(2,1)S(1)}, u32[]{:S(2)}, u32[]{:S(2)}) collective-permute-start(bf16[64,2048]{1,0:T(8,128)(2,1)S(1)} %fusion.16), channel_id=1, source_target_pairs={{0,2},{2,0},{1,3},{3,1},{4,6},{6,4},{5,7},{7,5},{8,10},{10,8},{9,1... | collective-permute-start | bytes 786440 | tf_op jit(solution)/shard_map/ppermute | solution.py:23
  114.4 56.0 %collective-permute-start.29 = (bf16[2,2048,256]{2,1,0:T(8,128)(2,1)}, bf16[2,2048,256]{2,1,0:T(8,128)(2,1)}, u32[]{:S(2)}, u32[]{:S(2)}) collective-permute-start(bf16[2,2048,256]{2,1,0:T(8,128)(2,1)} %param.21), channel_id=1, source_target_pairs={{65,1},{0,64},{67,3},{2,66},{69,5},{4,68},{71,7},{6,70},{73,9},{8,... | collective-permute-start | bytes 6291464 | tf_op jit(solution)/shard_map/ppermute | solution.py:277
  124.0 12.9 %collective-permute-start.23 = (bf16[32,2048]{1,0:T(8,128)(2,1)S(1)}, bf16[32,2048]{1,0:T(8,128)(2,1)S(1)}, u32[]{:S(2)}, u32[]{:S(2)}) collective-permute-start(bf16[32,2048]{1,0:T(8,128)(2,1)S(1)} %get-tuple-element.63), channel_id=1, source_target_pairs={{0,48},{16,0},{32,16},{48,32},{1,49},{17,1},{33,17},{49,33},{2,50}... | collective-permute-start | bytes 393224 | tf_op jit(solution)/shard_map/ppermute | solution.py:23
  129.1 7.8 %collective-permute-start.22 = (bf16[32,2048]{1,0:T(8,128)(2,1)S(1)}, bf16[32,2048]{1,0:T(8,128)(2,1)S(1)}, u32[]{:S(2)}, u32[]{:S(2)}) collective-permute-start(bf16[32,2048]{1,0:T(8,128)(2,1)S(1)} %get-tuple-element.63), channel_id=1, source_target_pairs={{0,32},{16,48},{32,0},{48,16},{1,33},{17,49},{33,1},{49,17},{2,34}... | collective-permute-start | bytes 393224 | tf_op jit(solution)/shard_map/ppermute | solution.py:23
  129.4 11.0 %collective-permute-start.21 = (bf16[32,2048]{1,0:T(8,128)(2,1)S(1)}, bf16[32,2048]{1,0:T(8,128)(2,1)S(1)}, u32[]{:S(2)}, u32[]{:S(2)}) collective-permute-start(bf16[32,2048]{1,0:T(8,128)(2,1)S(1)} %get-tuple-element.63), channel_id=1, source_target_pairs={{0,16},{16,32},{32,48},{48,0},{1,17},{17,33},{33,49},{49,1},{2,18}... | collective-permute-start | bytes 393224 | tf_op jit(solution)/shard_map/ppermute | solution.py:23
  130.0 37.3 %collective-permute-start.30 = (bf16[256,2048]{1,0:T(8,128)(2,1)S(1)}, bf16[256,2048]{1,0:T(8,128)(2,1)}, u32[]{:S(2)}, u32[]{:S(2)}) collective-permute-start(bf16[256,2048]{1,0:T(8,128)(2,1)S(1)} %copy-done.4), channel_id=1, source_target_pairs={{65,1},{0,64},{67,3},{2,66},{69,5},{4,68},{71,7},{6,70},{73,9},{8,... | collective-permute-start | bytes 3145736 | tf_op jit(solution)/shard_map/ppermute | solution.py:277
  136.8 7.5 %collective-permute-start.25 = (bf16[32,2048]{1,0:T(8,128)(2,1)S(1)}, bf16[32,2048]{1,0:T(8,128)(2,1)S(1)}, u32[]{:S(2)}, u32[]{:S(2)}) collective-permute-start(bf16[32,2048]{1,0:T(8,128)(2,1)S(1)} %get-tuple-element.62), channel_id=1, source_target_pairs={{0,8},{4,12},{8,0},{12,4},{1,9},{5,13},{9,1},{13,5},{2,10},{6,14},... | collective-permute-start | bytes 393224 | tf_op jit(solution)/shard_map/ppermute | solution.py:23
  140.4 16.1 %collective-permute-start.24 = (bf16[32,2048]{1,0:T(8,128)(2,1)S(1)}, bf16[32,2048]{1,0:T(8,128)(2,1)S(1)}, u32[]{:S(2)}, u32[]{:S(2)}) collective-permute-start(bf16[32,2048]{1,0:T(8,128)(2,1)S(1)} %get-tuple-element.62), channel_id=1, source_target_pairs={{0,4},{4,8},{8,12},{12,0},{1,5},{5,9},{9,13},{13,1},{2,6},{6,10},{... | collective-permute-start | bytes 393224 | tf_op jit(solution)/shard_map/ppermute | solution.py:23
  141.8 15.8 %collective-permute-start.44 = (bf16[128,2048]{1,0:T(8,128)(2,1)S(1)}, bf16[128,2048]{1,0:T(8,128)(2,1)S(1)}, u32[]{:S(2)}, u32[]{:S(2)}) collective-permute-start(bf16[128,2048]{1,0:T(8,128)(2,1)S(1)} %pad_maximum_fusion.2.refs_0_), channel_id=1, source_target_pairs={{0,8},{4,12},{8,0},{12,4},{1,9},{5,13},{9,1},{13,5},{2,10},{6,14},... | collective-permute-start | bytes 1572872 | tf_op jit(solution)/shard_map/ppermute | solution.py:23
  156.6 10.8 %collective-permute-start.45 = (bf16[128,2048]{1,0:T(8,128)(2,1)S(1)}, bf16[128,2048]{1,0:T(8,128)(2,1)S(1)}, u32[]{:S(2)}, u32[]{:S(2)}) collective-permute-start(bf16[128,2048]{1,0:T(8,128)(2,1)S(1)} %pad_maximum_fusion.3.refs_1_), channel_id=1, source_target_pairs={{0,32},{16,48},{32,0},{48,16},{1,33},{17,49},{33,1},{49,17},{2,34}... | collective-permute-start | bytes 1572872 | tf_op jit(solution)/shard_map/ppermute | solution.py:23
  157.6 12.8 %collective-permute-start.38 = (bf16[128,2048]{1,0:T(8,128)(2,1)S(1)}, bf16[128,2048]{1,0:T(8,128)(2,1)S(1)}, u32[]{:S(2)}, u32[]{:S(2)}) collective-permute-start(bf16[128,2048]{1,0:T(8,128)(2,1)S(1)} %pad_maximum_fusion.2.refs_0_), channel_id=1, source_target_pairs={{0,12},{4,0},{8,4},{12,8},{1,13},{5,1},{9,5},{13,9},{2,14},{6,2},{... | collective-permute-start | bytes 1572872 | tf_op jit(solution)/shard_map/ppermute | solution.py:23
  157.6 12.9 %collective-permute-start.46 = (bf16[128,2048]{1,0:T(8,128)(2,1)S(1)}, bf16[128,2048]{1,0:T(8,128)(2,1)S(1)}, u32[]{:S(2)}, u32[]{:S(2)}) collective-permute-start(bf16[128,2048]{1,0:T(8,128)(2,1)S(1)} %collective-permute-done.44.refs_0_), channel_id=1, source_target_pairs={{0,1},{1,0},{2,3},{3,2},{4,5},{5,4},{6,7},{7,6},{8,9},{9,8},{10,11... | collective-permute-start | bytes 1572872 | tf_op jit(solution)/shard_map/ppermute | solution.py:23
  167.5 14.5 %collective-permute-start.39 = (bf16[128,2048]{1,0:T(8,128)(2,1)S(1)}, bf16[128,2048]{1,0:T(8,128)(2,1)S(1)}, u32[]{:S(2)}, u32[]{:S(2)}) collective-permute-start(bf16[128,2048]{1,0:T(8,128)(2,1)S(1)} %pad_maximum_fusion.3.refs_1_), channel_id=1, source_target_pairs={{0,48},{16,0},{32,16},{48,32},{1,49},{17,1},{33,17},{49,33},{2,50}... | collective-permute-start | bytes 1572872 | tf_op jit(solution)/shard_map/ppermute | solution.py:23
  170.4 15.6 %collective-permute-start.32 = (bf16[128,2048]{1,0:T(8,128)(2,1)S(1)}, bf16[128,2048]{1,0:T(8,128)(2,1)S(1)}, u32[]{:S(2)}, u32[]{:S(2)}) collective-permute-start(bf16[128,2048]{1,0:T(8,128)(2,1)S(1)} %pad_maximum_fusion.2.refs_0_), channel_id=1, source_target_pairs={{0,4},{4,8},{8,12},{12,0},{1,5},{5,9},{9,13},{13,1},{2,6},{6,10},{... | collective-permute-start | bytes 1572872 | tf_op jit(solution)/shard_map/ppermute | solution.py:23
  170.4 15.8 %collective-permute-start.33 = (bf16[128,2048]{1,0:T(8,128)(2,1)S(1)}, bf16[128,2048]{1,0:T(8,128)(2,1)S(1)}, u32[]{:S(2)}, u32[]{:S(2)}) collective-permute-start(bf16[128,2048]{1,0:T(8,128)(2,1)S(1)} %pad_maximum_fusion.3.refs_1_), channel_id=1, source_target_pairs={{0,16},{16,32},{32,48},{48,0},{1,17},{17,33},{33,49},{49,1},{2,18}... | collective-permute-start | bytes 1572872 | tf_op jit(solution)/shard_map/ppermute | solution.py:23
  170.5 16.0 %collective-permute-start.27 = (bf16[128,2048]{1,0:T(8,128)(2,1)S(1)}, bf16[128,2048]{1,0:T(8,128)(2,1)S(1)}, u32[]{:S(2)}, u32[]{:S(2)}) collective-permute-start(bf16[128,2048]{1,0:T(8,128)(2,1)S(1)} %pad_maximum_fusion.2.refs_0_), channel_id=1, source_target_pairs={{0,1},{1,0},{2,3},{3,2},{4,5},{5,4},{6,7},{7,6},{8,9},{9,8},{10,11... | collective-permute-start | bytes 1572872 | tf_op jit(solution)/shard_map/ppermute | solution.py:23
  172.0 14.7 %collective-permute-start.28 = (bf16[128,2048]{1,0:T(8,128)(2,1)S(1)}, bf16[128,2048]{1,0:T(8,128)(2,1)S(1)}, u32[]{:S(2)}, u32[]{:S(2)}) collective-permute-start(bf16[128,2048]{1,0:T(8,128)(2,1)S(1)} %pad_maximum_fusion.3.refs_1_), channel_id=1, source_target_pairs={{0,1},{1,0},{2,3},{3,2},{4,5},{5,4},{6,7},{7,6},{8,9},{9,8},{10,11... | collective-permute-start | bytes 1572872 | tf_op jit(solution)/shard_map/ppermute | solution.py:23
  182.0 15.2 %collective-permute-start.48 = (bf16[2,128,2048]{2,1,0:T(8,128)(2,1)S(1)}, bf16[2,128,2048]{2,1,0:T(8,128)(2,1)S(1)}, u32[]{:S(2)}, u32[]{:S(2)}) collective-permute-start(bf16[2,128,2048]{2,1,0:T(8,128)(2,1)S(1)} %get-tuple-element.25), channel_id=1, source_target_pairs={{0,1},{1,0},{2,3},{3,2},{4,5},{5,4},{6,7},{7,6},{8,9},{9,8},{10,11... | collective-permute-start | bytes 3145736 | tf_op jit(solution)/shard_map/ppermute | solution.py:23
  186.5 7.3 %collective-permute-start.34 = (bf16[128,2048]{1,0:T(8,128)(2,1)S(1)}, bf16[128,2048]{1,0:T(8,128)(2,1)S(1)}, u32[]{:S(2)}, u32[]{:S(2)}) collective-permute-start(bf16[128,2048]{1,0:T(8,128)(2,1)S(1)} %collective-permute-done.32.refs_0_), channel_id=1, source_target_pairs={{0,1},{1,0},{2,3},{3,2},{4,5},{5,4},{6,7},{7,6},{8,9},{9,8},{10,11... | collective-permute-start | bytes 1572872 | tf_op jit(solution)/shard_map/ppermute | solution.py:23
  186.7 7.1 %collective-permute-start.35 = (bf16[128,2048]{1,0:T(8,128)(2,1)S(1)}, bf16[128,2048]{1,0:T(8,128)(2,1)S(1)}, u32[]{:S(2)}, u32[]{:S(2)}) collective-permute-start(bf16[128,2048]{1,0:T(8,128)(2,1)S(1)} %collective-permute-done.33.refs_1_), channel_id=1, source_target_pairs={{0,1},{1,0},{2,3},{3,2},{4,5},{5,4},{6,7},{7,6},{8,9},{9,8},{10,11... | collective-permute-start | bytes 1572872 | tf_op jit(solution)/shard_map/ppermute | solution.py:23
  190.1 13.2 %collective-permute-start.31 = (bf16[2,128,2048]{2,1,0:T(8,128)(2,1)S(1)}, bf16[2,128,2048]{2,1,0:T(8,128)(2,1)S(1)}, u32[]{:S(2)}, u32[]{:S(2)}) collective-permute-start(bf16[2,128,2048]{2,1,0:T(8,128)(2,1)S(1)} %get-tuple-element.19), channel_id=1, source_target_pairs={{0,1},{1,0},{2,3},{3,2},{4,5},{5,4},{6,7},{7,6},{8,9},{9,8},{10,11... | collective-permute-start | bytes 3145736 | tf_op jit(solution)/shard_map/ppermute | solution.py:23
  197.7 16.4 %collective-permute-start.49 = (bf16[128,2048]{1,0:T(8,128)(2,1)S(1)}, bf16[128,2048]{1,0:T(8,128)(2,1)S(1)}, u32[]{:S(2)}, u32[]{:S(2)}) collective-permute-start(bf16[128,2048]{1,0:T(8,128)(2,1)S(1)} %get-tuple-element.46), channel_id=1, source_target_pairs={{0,8},{4,12},{8,0},{12,4},{1,9},{5,13},{9,1},{13,5},{2,10},{6,14},... | collective-permute-start | bytes 1572872 | tf_op jit(solution)/shard_map/ppermute | solution.py:23
  199.3 25.3 %collective-permute-start.43 = (bf16[128,2048]{1,0:T(8,128)(2,1)S(1)}, bf16[128,2048]{1,0:T(8,128)(2,1)S(1)}, u32[]{:S(2)}, u32[]{:S(2)}) collective-permute-start(bf16[128,2048]{1,0:T(8,128)(2,1)S(1)} %get-tuple-element.44), channel_id=1, source_target_pairs={{0,4},{4,8},{8,12},{12,0},{1,5},{5,9},{9,13},{13,1},{2,6},{6,10},{... | collective-permute-start | bytes 1572872 | tf_op jit(solution)/shard_map/ppermute | solution.py:23
  202.9 22.1 %collective-permute-start.37 = (bf16[128,2048]{1,0:T(8,128)(2,1)S(1)}, bf16[128,2048]{1,0:T(8,128)(2,1)S(1)}, u32[]{:S(2)}, u32[]{:S(2)}) collective-permute-start(bf16[128,2048]{1,0:T(8,128)(2,1)S(1)} %get-tuple-element.42), channel_id=1, source_target_pairs={{0,12},{4,0},{8,4},{12,8},{1,13},{5,1},{9,5},{13,9},{2,14},{6,2},{... | collective-permute-start | bytes 1572872 | tf_op jit(solution)/shard_map/ppermute | solution.py:23
  203.3 21.8 %collective-permute-start.55 = (bf16[128,2048]{1,0:T(8,128)(2,1)S(1)}, bf16[128,2048]{1,0:T(8,128)(2,1)S(1)}, u32[]{:S(2)}, u32[]{:S(2)}) collective-permute-start(bf16[128,2048]{1,0:T(8,128)(2,1)S(1)} %get-tuple-element.47), channel_id=1, source_target_pairs={{0,32},{16,48},{32,0},{48,16},{1,33},{17,49},{33,1},{49,17},{2,34}... | collective-permute-start | bytes 1572872 | tf_op jit(solution)/shard_map/ppermute | solution.py:23
  203.3 26.4 %collective-permute-start.54 = (bf16[128,2048]{1,0:T(8,128)(2,1)S(1)}, bf16[128,2048]{1,0:T(8,128)(2,1)S(1)}, u32[]{:S(2)}, u32[]{:S(2)}) collective-permute-start(bf16[128,2048]{1,0:T(8,128)(2,1)S(1)} %get-tuple-element.45), channel_id=1, source_target_pairs={{0,16},{16,32},{32,48},{48,0},{1,17},{17,33},{33,49},{49,1},{2,18}... | collective-permute-start | bytes 1572872 | tf_op jit(solution)/shard_map/ppermute | solution.py:23
  214.1 15.6 %collective-permute-start.53 = (bf16[128,2048]{1,0:T(8,128)(2,1)S(1)}, bf16[128,2048]{1,0:T(8,128)(2,1)S(1)}, u32[]{:S(2)}, u32[]{:S(2)}) collective-permute-start(bf16[128,2048]{1,0:T(8,128)(2,1)S(1)} %get-tuple-element.43), channel_id=1, source_target_pairs={{0,48},{16,0},{32,16},{48,32},{1,49},{17,1},{33,17},{49,33},{2,50}... | collective-permute-start | bytes 1572872 | tf_op jit(solution)/shard_map/ppermute | solution.py:23
  230.4 9.2 %collective-permute-start.58 = (bf16[32,2048]{1,0:T(8,128)(2,1)S(1)}, bf16[32,2048]{1,0:T(8,128)(2,1)S(1)}, u32[]{:S(2)}, u32[]{:S(2)}) collective-permute-start(bf16[32,2048]{1,0:T(8,128)(2,1)S(1)} %get-tuple-element.60), channel_id=1, source_target_pairs={{0,4},{4,8},{8,12},{12,0},{1,5},{5,9},{9,13},{13,1},{2,6},{6,10},{... | collective-permute-start | bytes 393224 | tf_op jit(solution)/shard_map/ppermute | solution.py:23
  231.4 8.6 %collective-permute-start.57 = (bf16[32,2048]{1,0:T(8,128)(2,1)S(1)}, bf16[32,2048]{1,0:T(8,128)(2,1)S(1)}, u32[]{:S(2)}, u32[]{:S(2)}) collective-permute-start(bf16[32,2048]{1,0:T(8,128)(2,1)S(1)} %get-tuple-element.61), channel_id=1, source_target_pairs={{0,8},{4,12},{8,0},{12,4},{1,9},{5,13},{9,1},{13,5},{2,10},{6,14},... | collective-permute-start | bytes 393224 | tf_op jit(solution)/shard_map/ppermute | solution.py:23
  232.3 7.8 %collective-permute-start.56 = (bf16[32,2048]{1,0:T(8,128)(2,1)S(1)}, bf16[32,2048]{1,0:T(8,128)(2,1)S(1)}, u32[]{:S(2)}, u32[]{:S(2)}) collective-permute-start(bf16[32,2048]{1,0:T(8,128)(2,1)S(1)} %get-tuple-element.59), channel_id=1, source_target_pairs={{0,12},{4,0},{8,4},{12,8},{1,13},{5,1},{9,5},{13,9},{2,14},{6,2},{... | collective-permute-start | bytes 393224 | tf_op jit(solution)/shard_map/ppermute | solution.py:23
  234.4 8.4 %collective-permute-start.52 = (bf16[32,2048]{1,0:T(8,128)(2,1)S(1)}, bf16[32,2048]{1,0:T(8,128)(2,1)S(1)}, u32[]{:S(2)}, u32[]{:S(2)}) collective-permute-start(bf16[32,2048]{1,0:T(8,128)(2,1)S(1)} %get-tuple-element.57), channel_id=1, source_target_pairs={{0,16},{16,32},{32,48},{48,0},{1,17},{17,33},{33,49},{49,1},{2,18}... | collective-permute-start | bytes 393224 | tf_op jit(solution)/shard_map/ppermute | solution.py:23
  234.5 8.3 %collective-permute-start.51 = (bf16[32,2048]{1,0:T(8,128)(2,1)S(1)}, bf16[32,2048]{1,0:T(8,128)(2,1)S(1)}, u32[]{:S(2)}, u32[]{:S(2)}) collective-permute-start(bf16[32,2048]{1,0:T(8,128)(2,1)S(1)} %get-tuple-element.58), channel_id=1, source_target_pairs={{0,32},{16,48},{32,0},{48,16},{1,33},{17,49},{33,1},{49,17},{2,34}... | collective-permute-start | bytes 393224 | tf_op jit(solution)/shard_map/ppermute | solution.py:23
  (24 other events, 161.4 us)
where the time goes:
time: 245 us; the launch traced here: 246 us
  starting transfers between devices  98 us (40%)
  waiting for transfers between devices  78.6 us (32%)
  Pallas kernels  32.5 us (13%)
  other arithmetic  12.3 us (5%)
  local copies, waits for them, and re-layouts  8.61 us (4%)
  matrix products  7.69 us (3%)
  blocking collectives  7.07 us (3%)
    ppermute x45, starting transfers between devices, shift(): return lax.ppermute(values, axis, [(i, (i + by) % n) for i in range(n)])  67.9 us
    ppermute x45, waiting for transfers between devices, shift(): return lax.ppermute(values, axis, [(i, (i + by) % n) for i in range(n)])  66.8 us
    pallas_call x1, Pallas kernels, attention(): pl.pallas_call(attention_body, out_shape=jax.ShapeDtypeStruct((groups, ro...  20.3 us
    ppermute x2, starting transfers between devices, other_weights(): there = lax.ppermute(weights, ('yhi', 'core'), [(3, 1), (0, 2)])  14 us
    pallas_call x4, Pallas kernels, feed_forward(): pl.pallas_call(feed_forward_body, out_shape=(out, out), in_specs=[pl.Bloc...  12.2 us
    ppermute x8, starting transfers between devices, across(): return lax.ppermute(values, corner, pairs)  11.4 us
    ppermute x8, waiting for transfers between devices, across(): return lax.ppermute(values, corner, pairs)  8.59 us
    psum x1, blocking collectives, on_device(): squares = lax.psum(jnp.sum(qkv_raw[:2] * qkv_raw[:2], axis=2), HEAD)  7.07 us
  transfers between devices with their start and end apart: 59, of which 23 were waited for; matrix products, arithmetic and copies ran while one was open for 5% of the time, Pallas kernels for 5%

commit v1 on v0

--- a/solution.py
+++ b/solution.py
@@ -21,6 +21,14 @@
 def shift(values, axis, by):
     n = lax.axis_size(axis)
     return lax.ppermute(values, axis, [(i, (i + by) % n) for i in range(n)])
+
+
+def spread(values, axes):
+    n = 1
+    for axis in (axes,) if isinstance(axes, str) else axes:
+        n *= lax.axis_size(axis)
+    copies = lax.optimization_barrier(jnp.broadcast_to(values, (n,) + values.shape))
+    return lax.all_to_all(copies, axes, 0, 0, tiled=True)
 
 
 def select_row(table, row):
@@ -181,47 +189,44 @@
     )(nodes, lengths, lists, counts, *qkv_parts, row_info, seg_row, *parts)
 
 
-def feed_forward_body(*refs):
-    token_refs = refs[:4]
-    gu_ref, dn_ref, own_ref, other_ref, held, sems = refs[4:]
-
-    def copy(i, j):
-        return pltpu.make_async_copy(token_refs[j], held.at[i], sems.at[i])
-
-    for i in range(4):
-        copy(i, i).start()
+def feed_forward_body(
+    own_tokens, other_tokens, gu_a, dn_a, gu_b, dn_b, own_ref, other_ref
+):
+    rows = 128
 
     def one(i, carry):
-        for side, target in ((0, own_ref), (2, other_ref)):
-            copy(i + side, side).wait()
-            tokens = held[i + side]
-            gate = jnp.dot(tokens, gu_ref[0], preferred_element_type=F32)
-            up = jnp.dot(tokens, gu_ref[1], preferred_element_type=F32)
-            hidden = (gate / (1.0 + jnp.exp(-gate)) * up).astype(BF)
-            target[i] = jnp.dot(hidden, dn_ref[...], preferred_element_type=F32).astype(BF)
+        at = pl.ds(i * rows, rows)
+        for tokens_ref, target in ((own_tokens, own_ref), (other_tokens, other_ref)):
+            tokens = tokens_ref[at, :]
+            part = 0.0
+            for gu_ref, dn_ref in ((gu_a, dn_a), (gu_b, dn_b)):
+                gate = jnp.dot(tokens, gu_ref[0], preferred_element_type=F32)
+                up = jnp.dot(tokens, gu_ref[1], preferred_element_type=F32)
+                hidden = (gate / (1.0 + jnp.exp(-gate)) * up).astype(BF)
+                part = part + jnp.dot(hidden, dn_ref[...], preferred_element_type=F32)
+            target[at, :] = part.astype(BF)
         return carry
 
-    lax.fori_loop(0, 2, one, 0)
-
-
-def feed_forward(parts, w_gu, w_dn):
-    rows, width = parts[0].shape
-    units = w_dn.shape[0]
+    lax.fori_loop(0, own_tokens.shape[0] // rows, one, 0)
+
+
+def feed_forward(own, other, weights):
+    rows, width = own.shape
+    units = weights[1].shape[0]
     space = pl.BlockSpec(memory_space=pltpu.VMEM)
-    out = jax.ShapeDtypeStruct((2, rows, width), BF)
+    out = jax.ShapeDtypeStruct((rows, width), BF)
     return pl.pallas_call(
         feed_forward_body,
         out_shape=(out, out),
-        in_specs=[pl.BlockSpec(memory_space=pl.ANY)] * 4 + [space] * 2,
+        in_specs=[space] * 6,
         out_specs=(space, space),
-        scratch_shapes=[pltpu.VMEM((4, rows, width), BF), pltpu.SemaphoreType.DMA((4,))],
         compiler_params=pltpu.CompilerParams(vmem_limit_bytes=40 << 20),
         cost_estimate=pl.CostEstimate(
             flops=4 * rows * width * units * 6,
             transcendentals=4 * rows * units,
-            bytes_accessed=(8 * rows * width + 3 * width * units) * 2,
+            bytes_accessed=(4 * rows * width + 6 * width * units) * 2,
         ),
-    )(*parts, w_gu, w_dn)
+    )(own, other, *weights)
 
 
 def on_device(
@@ -264,22 +269,16 @@
         )
 
     cached = jnp.stack([across(head_piece(s), s) for s in range(n_z)])
-    cached_parts = [cached] + [shift(cached, "x", s) for s in (1, 3, 2)]
-    cached_parts = cached_parts + [shift(part, "core", 1) for part in cached_parts]
+    states_in, cached = lax.optimization_barrier((states_in, cached))
+    cached_own = spread(cached, "x").reshape((n_x * n_z,) + cached.shape[1:])
+    cached_parts = [cached_own, shift(cached_own, "core", 1)]
     slot_from = jnp.stack(
         [
-            (jnp.where(c == 0, core, 1 - core) * n_x + (x_at - sx) % n_x) * n_z + (z_at - sz) % n_z
-            for c in range(2) for sx in (0, 1, 3, 2) for sz in range(n_z)
+            (jnp.where(c == 0, core, 1 - core) * n_x + x) * n_z + (z_at - sz) % n_z
+            for c in range(2) for x in range(n_x) for sz in range(n_z)
         ]
     ).astype(jnp.int32)
 
-    def other_weights(weights):
-        there = lax.ppermute(weights, ("yhi", "core"), [(3, 1), (0, 2)])
-        return jnp.where(yhi == core, weights, there)
-
-    w_gate_up, w_down, _ = lax.optimization_barrier((w_gate_up, w_down, cached))
-    w_gu = other_weights(w_gate_up)
-    w_dn = other_weights(w_down)
     w_out = lax.dynamic_slice_in_dim(jnp.concatenate([w_out, w_out]), z_at * HD, w_out.shape[0], 0)
 
     qkv_raw = jnp.einsum("td,cdw->ctw", states_in, w_qkv, preferred_element_type=F32)
@@ -308,6 +307,21 @@
         [normed(0), normed(1), qkv_raw[2].astype(BF).reshape(rows, heads_here, HD)]
     ).transpose(2, 0, 1, 3)
     qkv_parts = [across(select_row(qkv, (z_at + s) % n_z), s) for s in range(n_z)]
+
+    w_gate_up, w_down, qkv_parts = lax.optimization_barrier((w_gate_up, w_down, qkv_parts))
+
+    def ring_weights(weights):
+        beside = lax.ppermute(
+            weights, ("z", "core"),
+            [(z * 2 + c, (z + 1 - 2 * c) % n_z * 2 + c) for z in range(n_z) for c in range(2)],
+        )
+        far = lax.ppermute(
+            weights, ("z", "core"), [(z * 2 + 1, (z + 2) % n_z * 2 + 1) for z in range(n_z)]
+        )
+        return beside, jnp.where(core == 0, weights, far)
+
+    gu_a, gu_b = ring_weights(w_gate_up)
+    dn_a, dn_b = ring_weights(w_down)
 
     slots = slot_from.shape[0]
     slot_nodes = jnp.take(slot_node, slot_from)
@@ -356,33 +370,18 @@
     state_rows = lax.dynamic_slice_in_dim(states_in, head_index * own_rows, own_rows, 0)
     mid_state = (state_rows.astype(F32) + rms_norm(attn_proj, post_gain[0])).astype(BF)
 
-    cut = own_rows // 2
-    upper, lower = mid_state[:cut], mid_state[cut:]
-    upper4 = jnp.concatenate([upper] + [shift(upper, "x", s) for s in range(1, n_x)])
-    lower4 = jnp.concatenate([lower] + [shift(lower, "z", s) for s in range(1, n_z)])
-
-    upper_sum = lower_sum = 0.0
-    for t in (0, 1, 3, 2):
-        pair = (upper4, lower4)
-        if t:
-            pair = (shift(upper4, "z", t), shift(lower4, "x", t))
-        own, other = feed_forward(
-            pair + (shift(pair[0], "core", 1), shift(pair[1], "core", 1)), w_gu, w_dn
-        )
-        total = own.astype(F32) + shift(other, "core", 1).astype(F32)
-        up_part, low_part = total[0], total[1]
-        if t:
-            up_part = shift(up_part.astype(BF), "z", n_z - t).astype(F32)
-            low_part = shift(low_part.astype(BF), "x", n_x - t).astype(F32)
-        upper_sum = upper_sum + up_part
-        lower_sum = lower_sum + low_part
-    upper_sum = upper_sum.reshape(n_x, cut, -1)
-    lower_sum = lower_sum.reshape(n_z, cut, -1)
-    upper_out, lower_out = upper_sum[0], lower_sum[0]
-    for s in range(1, 4):
-        upper_out = upper_out + shift(upper_sum[s].astype(BF), "x", n_x - s).astype(F32)
-        lower_out = lower_out + shift(lower_sum[s].astype(BF), "z", n_z - s).astype(F32)
-    mlp_proj = jnp.concatenate([upper_out, lower_out])
+    chunks = 2
+    cut = own_rows // chunks
+    plane = ("yhi", "x")
+    n_plane = n_y * n_x
+    mlp_parts = []
+    for i in range(chunks):
+        tokens = spread(mid_state[i * cut : (i + 1) * cut], plane).reshape(n_plane * cut, -1)
+        own, other = feed_forward(tokens, shift(tokens, "core", 1), (gu_a, dn_a, gu_b, dn_b))
+        total = (own.astype(F32) + shift(other, "core", 1).astype(F32)).astype(BF)
+        total = lax.all_to_all(total.reshape(n_plane, cut, -1), plane, 0, 0, tiled=True)
+        mlp_parts.append(jnp.sum(total.astype(F32), axis=0))
+    mlp_proj = jnp.concatenate(mlp_parts)
     return (mid_state.astype(F32) + rms_norm(mlp_proj, post_gain[1])).astype(BF)
 
 

time: 245 us -> 254 us (1.037); the launches traced: 246 us -> 252 us
  starting transfers between devices: 98 us -> 68 us
  waiting for transfers between devices: 78.6 us -> 105 us
  local copies, waits for them, and re-layouts: 8.61 us -> 14.1 us
    all_to_all x0 -> x5, waiting for transfers between devices: none -> 71.5 us  [the longest x3 38 us: spread(): return lax.all_to_all(copies, axes, 0, 0, tiled=True)]
    ppermute x45 -> x7, waiting for transfers between devices: 66.8 us -> 7.02 us  [shift(): return lax.ppermute(values, axis, [(i, (i + by) % n) for i in range(n)])]
    ppermute x45 -> x7, starting transfers between devices: 67.9 us -> 23.1 us  [shift(): return lax.ppermute(values, axis, [(i, (i + by) % n) for i in range(n)])]
    all_to_all x0 -> x5, starting transfers between devices: none -> 21 us  [the longest x3 12.8 us: spread(): return lax.all_to_all(copies, axes, 0, 0, tiled=True)]
    ppermute x2 -> x4, waiting for transfers between devices: 0.01 us -> 12.2 us  [the longest x2 12.2 us: ring_weights(): lax.ppermute(weights, ('z', 'core'), [(z * 2 + c, (z + 1 - 2 * c) % n_z *...]
    ppermute x2 -> x4, starting transfers between devices: 14 us -> 8.99 us  [the longest x2 5.35 us: ring_weights(): lax.ppermute(weights, ('z', 'core'), [(z * 2 + c, (z + 1 - 2 * c) % n_z *...]
    broadcast_in_dim x0 -> x3, local copies, waits for them, and re-layouts: none -> 4.03 us  [spread(): jnp.broadcast_to(values, (n,) + values.shape)]
    convert_element_type x0 -> x2, other arithmetic: none -> 2.79 us  [on_device(): total = (own.astype(F32) + shift(other, 'core', 1).astype(F32)).astype(BF)]
  transfers between devices with their start and end apart: 59 -> 28, of which waited for: 23 -> 13; matrix products, arithmetic and copies ran while one was open for 5% -> 12% of each run, Pallas kernels for 5% -> 5%
where the time goes in v1:
time: 254 us; the launch traced here: 252 us
  waiting for transfers between devices  105 us (41%)
  starting transfers between devices  68 us (27%)
  Pallas kernels  33.7 us (13%)
  other arithmetic  14.7 us (6%)
  local copies, waits for them, and re-layouts  14.1 us (6%)
  matrix products  8.87 us (3%)
  blocking collectives  6.95 us (3%)
    all_to_all x3, waiting for transfers between devices, spread(): return lax.all_to_all(copies, axes, 0, 0, tiled=True)  38 us
    all_to_all x2, waiting for transfers between devices, on_device(): lax.all_to_all(total.reshape(n_plane, cut, -1), plane, 0, 0, tiled=True)  33.5 us
    ppermute x7, starting transfers between devices, shift(): return lax.ppermute(values, axis, [(i, (i + by) % n) for i in range(n)])  23.1 us
    pallas_call x1, Pallas kernels, attention(): pl.pallas_call(attention_body, out_shape=jax.ShapeDtypeStruct((groups, ro...  20.3 us
    pallas_call x2, Pallas kernels, feed_forward(): pl.pallas_call(feed_forward_body, out_shape=(out, out), in_specs=[space]...  13.4 us
    all_to_all x3, starting transfers between devices, spread(): return lax.all_to_all(copies, axes, 0, 0, tiled=True)  12.8 us
    ppermute x2, waiting for transfers between devices, ring_weights(): lax.ppermute(weights, ('z', 'core'), [(z * 2 + c, (z + 1 - 2 * c) % n_z *...  12.2 us
    ppermute x8, starting transfers between devices, across(): return lax.ppermute(values, corner, pairs)  12 us
  transfers between devices with their start and end apart: 28, of which 13 were waited for; matrix products, arithmetic and copies ran while one was open for 12% of the time, Pallas kernels for 5%

profile of v1, /device:TPU:0, one launch (start us, length us, event | category | flops | bytes accessed | tf_op | source)
XLA Modules:
  0.0 251.7 jit_solution(12525080327535122387)
XLA Ops:
  0.1 1.1 constant_dynamic-slice_fusion.6
  1.9 2.1 collective-permute-start.1
  4.0 3.7 %collective-permute-start.2 = (bf16[2,256,128]{2,1,0:T(8,128)(2,1)S(1)}, bf16[2,256,128]{2,1,0:T(8,128)(2,1)S(1)}, u32[]{:S(2)}, u32[]{:S(2)}) collective-permute-start(bf16[2,256,128]{2,1,0:T(8,128)(2,1)S(1)} %pad_maximum_fusion.5), channel_id=1, source_target_pairs={{0,8},{1,72},{4,12},{5,76},{8,0},{9,64},{12,4},{13,68},{64,9},{65,... | collective-permute-start | bytes 393224 | tf_op jit(solution)/shard_map/ppermute | solution.py:263
  13.5 1.8 broadcast_in_dim.140
  15.4 4.4 %all-to-all-start = ((bf16[4,4,2,256,128]{4,3,2,1,0:T(8,128)(2,1)}), bf16[4,4,2,256,128]{4,3,2,1,0:T(8,128)(2,1)S(1)}, u32[]{:S(2)}, u32[]{:S(2)}) async-start(bf16[4,4,2,256,128]{4,3,2,1,0:T(8,128)(2,1)} %broadcast_in_dim.140), calls=%async_computation | async-start | bytes 4194304 | tf_op jit(solution)/shard_map/all_to_all | solution.py:31
  21.2 6.1 %convolution_bitcast_fusion = f32[3,256,512]{2,1,0:T(8,128)} fusion(bf16[3,2048,512]{2,1,0:T(8,128)(2,1)} %param.17, bf16[256,2048]{1,0:T(8,128)(2,1)} %param.16), kind=kOutput, calls=%fused_computation.13 | convolution fusion | flops 1610612736 | bytes 8912896 | tf_op jit(solution)/shard_map/td,cdw->ctw/dot_general | solution.py:284
  27.3 13.6 %all-to-all-done = bf16[4,4,2,256,128]{4,3,2,1,0:T(8,128)(2,1)S(1)} async-done(((bf16[4,4,2,256,128]{4,3,2,1,0:T(8,128)(2,1)}), bf16[4,4,2,256,128]{4,3,2,1,0:T(8,128)(2,1)S(1)}, u32[]{:S(2)}, u32[]{:S(2)}) %all-to-all-start) | async-done | bytes 2097184 | tf_op jit(solution)/shard_map/all_to_all | solution.py:31
  40.9 6.4 %collective-permute-start.8 = (bf16[16,2,256,128]{3,2,1,0:T(8,128)(2,1)S(1)}, bf16[16,2,256,128]{3,2,1,0:T(8,128)(2,1)}, u32[]{:S(2)}, u32[]{:S(2)}) collective-permute-start(bf16[16,2,256,128]{3,2,1,0:T(8,128)(2,1)S(1)} %bitcast.122), channel_id=1, source_target_pairs={{0,1},{1,0},{2,3},{3,2},{4,5},{5,4},{6,7},{7,6},{8,9},{9,8},{10,11... | collective-permute-start | bytes 6291464 | tf_op jit(solution)/shard_map/ppermute | solution.py:23
  47.4 2.0 fusion.31
  50.4 1.2 squeeze.53
  51.6 1.4 fusion.3
  53.0 7.0 %psum.7 = f32[2,256]{1,0:T(2,128)S(1)} all-reduce(f32[2,256]{1,0:T(2,128)S(1)} %fusion.3), channel_id=1, replica_groups=mesh['yhi'=2,'x'=4,'z'=4,'ylo'=2,'core'=2] {'ylo','core'}, use_global_device_ids=true, to_apply=%region_7.9 | all-reduce | flops 512 | bytes 4096 | tf_op jit(solution)/shard_map/psum | solution.py:285
  59.9 1.2 fusion.6
  64.9 1.9 collective-permute-start.6
  67.7 4.9 %collective-permute-done.5.rest_1_ = bf16[3,256,128]{2,1,0:T(8,128)(2,1)S(1)} collective-permute-done((bf16[3,256,128]{2,1,0:T(8,128)(2,1)S(1)}, bf16[3,256,128]{2,1,0:T(8,128)(2,1)S(1)}, u32[]{:S(2)}, u32[]{:S(2)}) %collective-permute-start.5) | collective-permute-done | bytes 196640 | tf_op jit(solution)/shard_map/ppermute | solution.py:263
  72.6 5.1 %collective-permute-done.6.rest_2_ = bf16[3,256,128]{2,1,0:T(8,128)(2,1)S(1)} collective-permute-done((bf16[3,256,128]{2,1,0:T(8,128)(2,1)S(1)}, bf16[3,256,128]{2,1,0:T(8,128)(2,1)S(1)}, u32[]{:S(2)}, u32[]{:S(2)}) %collective-permute-start.6) | collective-permute-done | bytes 196640 | tf_op jit(solution)/shard_map/ppermute | solution.py:263
  77.7 20.3 %shard_map.136 = bf16[4,256,128]{2,1,0:T(8,128)(2,1)S(1)} custom-call(s32[32]{0:T(128)S(1)} %get-tuple-element.37.nodes_ref, s32[32]{0:T(128)S(1)} %and_select_fusion.lengths_ref, s32[4,2,12]{2,1,0:T(2,128)S(1)} %copy.53.lists_ref, s32[4,2]{1,0:T(4,128)S(1)} %copy.54.counts_ref, bf16[3,256,128]{2,1,0:T(8,128)(2,1)S(1)} %collective-permute-done.4.rest_0_, ...), custom_call_target="tpu_custom_call" | custom-call | flops 2000000000 | bytes 6000000 | tf_op jit(solution)/shard_map/pallas_call | solution.py:166
  98.2 1.9 collective-permute-start.12
  101.0 1.4 collective-permute-done.10
  102.4 1.6 collective-permute-done.11
  105.0 2.8 %fusion.1 = f32[256,2048]{1,0:T(8,128)S(1)} fusion(s32[]{:T(128)S(6)} %select_n.293, bf16[512,2048]{1,0:T(8,128)(2,1)} %param.19, bf16[256,128]{1,0:T(8,128)(2,1)S(1)} %collective-permute-done.12, bf16[256,128]{1,0:T(8,128)(2,1)S(1)} %collective-permute-done.11, bf16[256,128]{1,0:T(8,128)(2,1)S(1)} %collective-permute-done.10, ...), kind=kOutput, calls=%fused_computation.7 | convolution fusion | flops 542113792 | bytes 4456452 | tf_op jit(solution)/shard_map/dot_general | solution.py:359
  107.9 7.3 %collective-permute-start.13 = (bf16[2,64,2048]{2,1,0:T(8,128)(2,1)S(1)}, bf16[2,64,2048]{2,1,0:T(8,128)(2,1)S(1)}, u32[]{:S(2)}, u32[]{:S(2)}) collective-permute-start(bf16[2,64,2048]{2,1,0:T(8,128)(2,1)S(1)} %fusion.5), channel_id=1, source_target_pairs={{0,1},{1,0},{2,3},{3,2},{4,5},{5,4},{6,7},{7,6},{8,9},{9,8},{10,11... | collective-permute-start | bytes 1572872 | tf_op jit(solution)/shard_map/ppermute | solution.py:23
  115.2 1.5 collective-permute-done.13
  116.9 1.2 collective-permute-start.14
  118.1 2.0 collective-permute-start.18
  120.1 5.5 %collective-permute-done.14 = bf16[64,2048]{1,0:T(8,128)(2,1)S(1)} collective-permute-done((bf16[64,2048]{1,0:T(8,128)(2,1)S(1)}, bf16[64,2048]{1,0:T(8,128)(2,1)S(1)}, u32[]{:S(2)}, u32[]{:S(2)}) %collective-permute-start.14) | collective-permute-done | bytes 262176 | tf_op jit(solution)/shard_map/ppermute | solution.py:23
  125.8 1.1 add_convert_fusion.3
  126.9 1.1 broadcast_in_dim.141
  128.0 4.8 %all-to-all-start.1 = ((bf16[8,32,2048]{2,1,0:T(8,128)(2,1)}), bf16[8,32,2048]{2,1,0:T(8,128)(2,1)S(1)}, u32[]{:S(2)}, u32[]{:S(2)}) async-start(bf16[8,32,2048]{2,1,0:T(8,128)(2,1)} %broadcast_in_dim.141), calls=%async_computation.1 | async-start | bytes 2097152 | tf_op jit(solution)/shard_map/all_to_all | solution.py:31
  132.8 1.7 collective-permute-start.19
  134.5 2.4 collective-permute-start.16
  136.9 1.1 broadcast_in_dim.142
  138.0 11.5 %all-to-all-done.1 = bf16[8,32,2048]{2,1,0:T(8,128)(2,1)S(1)} async-done(((bf16[8,32,2048]{2,1,0:T(8,128)(2,1)}), bf16[8,32,2048]{2,1,0:T(8,128)(2,1)S(1)}, u32[]{:S(2)}, u32[]{:S(2)}) %all-to-all-start.1) | async-done | bytes 1048608 | tf_op jit(solution)/shard_map/all_to_all | solution.py:31
  149.5 3.6 %all-to-all-start.3 = ((bf16[8,32,2048]{2,1,0:T(8,128)(2,1)}), bf16[8,32,2048]{2,1,0:T(8,128)(2,1)S(1)}, u32[]{:S(2)}, u32[]{:S(2)}) async-start(bf16[8,32,2048]{2,1,0:T(8,128)(2,1)} %broadcast_in_dim.142), calls=%async_computation.3 | async-start | bytes 2097152 | tf_op jit(solution)/shard_map/all_to_all | solution.py:31
  153.1 2.9 %collective-permute-start.17 = (bf16[256,2048]{1,0:T(8,128)(2,1)}, bf16[256,2048]{1,0:T(8,128)(2,1)}, u32[]{:S(2)}, u32[]{:S(2)}) collective-permute-start(bf16[256,2048]{1,0:T(8,128)(2,1)} %param.22), channel_id=1, source_target_pairs={{0,4},{1,13},{4,8},{5,1},{8,12},{9,5},{12,0},{13,9},{2,6},{3,15},{... | collective-permute-start | bytes 3145736 | tf_op jit(solution)/shard_map/ppermute | solution.py:314
  156.0 1.4 broadcast_select_fusion.1.dn_b
  157.4 12.9 %all-to-all-done.3 = bf16[8,32,2048]{2,1,0:T(8,128)(2,1)S(1)} async-done(((bf16[8,32,2048]{2,1,0:T(8,128)(2,1)}), bf16[8,32,2048]{2,1,0:T(8,128)(2,1)S(1)}, u32[]{:S(2)}, u32[]{:S(2)}) %all-to-all-start.3) | async-done | bytes 1048608 | tf_op jit(solution)/shard_map/all_to_all | solution.py:31
  170.3 7.6 %collective-permute-start.21 = (bf16[256,2048]{1,0:T(8,128)(2,1)S(1)}, bf16[256,2048]{1,0:T(8,128)(2,1)S(1)}, u32[]{:S(2)}, u32[]{:S(2)}) collective-permute-start(bf16[256,2048]{1,0:T(8,128)(2,1)S(1)} %bitcast.126), channel_id=1, source_target_pairs={{0,1},{1,0},{2,3},{3,2},{4,5},{5,4},{6,7},{7,6},{8,9},{9,8},{10,11... | collective-permute-start | bytes 3145736 | tf_op jit(solution)/shard_map/ppermute | solution.py:23
  177.9 1.8 broadcast_select_fusion.gu_b
  179.8 12.2 %collective-permute-done.17.dn_a = bf16[256,2048]{1,0:T(8,128)(2,1)} collective-permute-done((bf16[256,2048]{1,0:T(8,128)(2,1)}, bf16[256,2048]{1,0:T(8,128)(2,1)}, u32[]{:S(2)}, u32[]{:S(2)}) %collective-permute-start.17) | collective-permute-done | bytes 1048608 | tf_op jit(solution)/shard_map/ppermute | solution.py:314
  191.9 6.4 %shard_map.137 = (bf16[256,2048]{1,0:T(8,128)(2,1)S(1)}, bf16[256,2048]{1,0:T(8,128)(2,1)S(1)}) custom-call(bf16[256,2048]{1,0:T(8,128)(2,1)S(1)} %bitcast.125, bf16[256,2048]{1,0:T(8,128)(2,1)} %collective-permute-done.15.other_tokens, bf16[2,2048,256]{2,1,0:T(8,128)(2,1)} %collective-permute-done.16.gu_a, bf16[256,2048]{1,0:T(8,128)(2,1)} %collective-permute-done.17.dn_a, ...), custom_call_target="tpu_custom_call" | custom-call | flops 3221225472 | bytes 10485760 | tf_op jit(solution)/shard_map/pallas_call | solution.py:218
  198.9 7.0 %shard_map.138 = (bf16[256,2048]{1,0:T(8,128)(2,1)S(1)}, bf16[256,2048]{1,0:T(8,128)(2,1)}) custom-call(bf16[256,2048]{1,0:T(8,128)(2,1)S(1)} %bitcast.127, bf16[256,2048]{1,0:T(8,128)(2,1)S(1)} %collective-permute-done.21.other_tokens, bf16[2,2048,256]{2,1,0:T(8,128)(2,1)} %collective-permute-done.16.gu_a, bf16[256,2048]{1,0:T(8,128)(2,1)} %collective-permute-done.17.dn_a, ...), custom_call_target="tpu_custom_call" | custom-call | flops 3221225472 | bytes 10485760 | tf_op jit(solution)/shard_map/pallas_call | solution.py:218
  206.0 1.4 add_convert_fusion.1
  207.3 4.6 %all-to-all-start.2 = ((bf16[8,32,2048]{2,1,0:T(8,128)(2,1)}), bf16[8,32,2048]{2,1,0:T(8,128)(2,1)S(1)}, u32[]{:S(2)}, u32[]{:S(2)}) async-start(bf16[8,32,2048]{2,1,0:T(8,128)(2,1)} %bitcast.79), calls=%async_computation.2 | async-start | bytes 2097152 | tf_op jit(solution)/shard_map/all_to_all | solution.py:382
  211.9 1.4 add_convert_fusion
  213.4 16.3 %all-to-all-done.2 = bf16[8,32,2048]{2,1,0:T(8,128)(2,1)S(1)} async-done(((bf16[8,32,2048]{2,1,0:T(8,128)(2,1)}), bf16[8,32,2048]{2,1,0:T(8,128)(2,1)S(1)}, u32[]{:S(2)}, u32[]{:S(2)}) %all-to-all-start.2) | async-done | bytes 1048608 | tf_op jit(solution)/shard_map/all_to_all | solution.py:382
  229.6 3.6 %all-to-all-start.4 = ((bf16[8,32,2048]{2,1,0:T(8,128)(2,1)}), bf16[8,32,2048]{2,1,0:T(8,128)(2,1)S(1)}, u32[]{:S(2)}, u32[]{:S(2)}) async-start(bf16[8,32,2048]{2,1,0:T(8,128)(2,1)} %bitcast.81), calls=%async_computation.4 | async-start | bytes 2097152 | tf_op jit(solution)/shard_map/all_to_all | solution.py:382
  233.3 17.2 %all-to-all-done.4 = bf16[8,32,2048]{2,1,0:T(8,128)(2,1)S(1)} async-done(((bf16[8,32,2048]{2,1,0:T(8,128)(2,1)}), bf16[8,32,2048]{2,1,0:T(8,128)(2,1)S(1)}, u32[]{:S(2)}, u32[]{:S(2)}) %all-to-all-start.4) | async-done | bytes 1048608 | tf_op jit(solution)/shard_map/all_to_all | solution.py:382
  (111 shorter events, 17.8 us)
Async XLA Ops:
  0.0 9.0 %copy-start = (s32[32,256]{1,0:T(8,128)S(1)}, s32[32,256]{1,0:T(8,128)}, u32[]{:S(2)}) copy-start(s32[32,256]{1,0:T(8,128)} %param.28) | copy-start | bytes 98308
  0.0 9.9 %copy-start.4 = (s32[32,8]{0,1:T(8,128)S(1)}, s32[32,8]{0,1:T(8,128)}, u32[]{:S(2)}) copy-start(s32[32,8]{0,1:T(8,128)} %param.29) | copy-start | bytes 3076
  0.0 10.9 %copy-start.6 = (s32[28]{0:T(128)S(1)}, s32[28]{0:T(128)}, u32[]{:S(2)}) copy-start(s32[28]{0:T(128)} %param.27) | copy-start | bytes 340
  0.0 11.2 %copy-start.2 = (s32[32]{0:T(128)S(1)}, s32[32]{0:T(128)}, u32[]{:S(2)}) copy-start(s32[32]{0:T(128)} %param.25) | copy-start | bytes 388
  1.2 12.2 %collective-permute-start = (bf16[2,256,128]{2,1,0:T(8,128)(2,1)S(1)}, bf16[2,256,128]{2,1,0:T(8,128)(2,1)S(1)}, u32[]{:S(2)}, u32[]{:S(2)}) collective-permute-start(bf16[2,256,128]{2,1,0:T(8,128)(2,1)S(1)} %pad_maximum_fusion.3), channel_id=1, source_target_pairs={{0,0},{1,64},{4,4},{5,68},{8,8},{9,72},{12,12},{13,76},{64,1},{65,... | collective-permute-start | bytes 393224 | tf_op jit(solution)/shard_map/ppermute | solution.py:263
  1.9 11.5 %collective-permute-start.1 = (bf16[2,256,128]{2,1,0:T(8,128)(2,1)S(1)}, bf16[2,256,128]{2,1,0:T(8,128)(2,1)S(1)}, u32[]{:S(2)}, u32[]{:S(2)}) collective-permute-start(bf16[2,256,128]{2,1,0:T(8,128)(2,1)S(1)} %pad_maximum_fusion.4), channel_id=1, source_target_pairs={{0,4},{1,68},{4,8},{5,72},{8,12},{9,76},{12,0},{13,64},{64,5},{65,... | collective-permute-start | bytes 393224 | tf_op jit(solution)/shard_map/ppermute | solution.py:263
  4.0 9.4 %collective-permute-start.2 = (bf16[2,256,128]{2,1,0:T(8,128)(2,1)S(1)}, bf16[2,256,128]{2,1,0:T(8,128)(2,1)S(1)}, u32[]{:S(2)}, u32[]{:S(2)}) collective-permute-start(bf16[2,256,128]{2,1,0:T(8,128)(2,1)S(1)} %pad_maximum_fusion.5), channel_id=1, source_target_pairs={{0,8},{1,72},{4,12},{5,76},{8,0},{9,64},{12,4},{13,68},{64,9},{65,... | collective-permute-start | bytes 393224 | tf_op jit(solution)/shard_map/ppermute | solution.py:263
  7.7 5.7 %collective-permute-start.3 = (bf16[2,256,128]{2,1,0:T(8,128)(2,1)S(1)}, bf16[2,256,128]{2,1,0:T(8,128)(2,1)S(1)}, u32[]{:S(2)}, u32[]{:S(2)}) collective-permute-start(bf16[2,256,128]{2,1,0:T(8,128)(2,1)S(1)} %pad_maximum_fusion.6), channel_id=1, source_target_pairs={{0,12},{1,76},{4,0},{5,64},{8,4},{9,68},{12,8},{13,72},{64,13},{65... | collective-permute-start | bytes 393224 | tf_op jit(solution)/shard_map/ppermute | solution.py:263
  15.4 4.4 %copy-start.1 = (s32[32]{0:T(128)S(1)}, s32[32]{0:T(128)}, u32[]{:S(2)}) copy-start(s32[32]{0:T(128)} %param.26) | copy-start | bytes 388
  15.4 5.3 %copy-start.5 = (f32[2,512]{1,0:T(2,128)S(1)}, f32[2,512]{1,0:T(2,128)}, u32[]{:S(2)}) copy-start(f32[2,512]{1,0:T(2,128)} %param.18) | copy-start | bytes 12292
  15.4 25.6 %all-to-all-start = ((bf16[4,4,2,256,128]{4,3,2,1,0:T(8,128)(2,1)}), bf16[4,4,2,256,128]{4,3,2,1,0:T(8,128)(2,1)S(1)}, u32[]{:S(2)}, u32[]{:S(2)}) async-start(bf16[4,4,2,256,128]{4,3,2,1,0:T(8,128)(2,1)} %broadcast_in_dim.140), calls=%async_computation | async-start | bytes 4194304 | tf_op jit(solution)/shard_map/all_to_all | solution.py:31
  40.9 36.8 %collective-permute-start.8 = (bf16[16,2,256,128]{3,2,1,0:T(8,128)(2,1)S(1)}, bf16[16,2,256,128]{3,2,1,0:T(8,128)(2,1)}, u32[]{:S(2)}, u32[]{:S(2)}) collective-permute-start(bf16[16,2,256,128]{3,2,1,0:T(8,128)(2,1)S(1)} %bitcast.122), channel_id=1, source_target_pairs={{0,1},{1,0},{2,3},{3,2},{4,5},{5,4},{6,7},{7,6},{8,9},{9,8},{10,11... | collective-permute-start | bytes 6291464 | tf_op jit(solution)/shard_map/ppermute | solution.py:23
  63.1 4.5 %collective-permute-start.4 = (bf16[3,256,128]{2,1,0:T(8,128)(2,1)S(1)}, bf16[3,256,128]{2,1,0:T(8,128)(2,1)S(1)}, u32[]{:S(2)}, u32[]{:S(2)}) collective-permute-start(bf16[3,256,128]{2,1,0:T(8,128)(2,1)S(1)} %get-tuple-element.43), channel_id=1, source_target_pairs={{0,0},{1,64},{4,4},{5,68},{8,8},{9,72},{12,12},{13,76},{64,1},{65,... | collective-permute-start | bytes 589832 | tf_op jit(solution)/shard_map/ppermute | solution.py:263
  63.8 8.8 %collective-permute-start.5 = (bf16[3,256,128]{2,1,0:T(8,128)(2,1)S(1)}, bf16[3,256,128]{2,1,0:T(8,128)(2,1)S(1)}, u32[]{:S(2)}, u32[]{:S(2)}) collective-permute-start(bf16[3,256,128]{2,1,0:T(8,128)(2,1)S(1)} %get-tuple-element.42), channel_id=1, source_target_pairs={{0,4},{1,68},{4,8},{5,72},{8,12},{9,76},{12,0},{13,64},{64,5},{65,... | collective-permute-start | bytes 589832 | tf_op jit(solution)/shard_map/ppermute | solution.py:263
  64.9 12.8 %collective-permute-start.6 = (bf16[3,256,128]{2,1,0:T(8,128)(2,1)S(1)}, bf16[3,256,128]{2,1,0:T(8,128)(2,1)S(1)}, u32[]{:S(2)}, u32[]{:S(2)}) collective-permute-start(bf16[3,256,128]{2,1,0:T(8,128)(2,1)S(1)} %get-tuple-element.41), channel_id=1, source_target_pairs={{0,8},{1,72},{4,12},{5,76},{8,0},{9,64},{12,4},{13,68},{64,9},{65,... | collective-permute-start | bytes 589832 | tf_op jit(solution)/shard_map/ppermute | solution.py:263
  66.8 10.9 %collective-permute-start.7 = (bf16[3,256,128]{2,1,0:T(8,128)(2,1)S(1)}, bf16[3,256,128]{2,1,0:T(8,128)(2,1)S(1)}, u32[]{:S(2)}, u32[]{:S(2)}) collective-permute-start(bf16[3,256,128]{2,1,0:T(8,128)(2,1)S(1)} %get-tuple-element.40), channel_id=1, source_target_pairs={{0,12},{1,76},{4,0},{5,64},{8,4},{9,68},{12,8},{13,72},{64,13},{65... | collective-permute-start | bytes 589832 | tf_op jit(solution)/shard_map/ppermute | solution.py:263
  98.0 4.3 %collective-permute-start.10 = (bf16[256,128]{1,0:T(8,128)(2,1)S(1)}, bf16[256,128]{1,0:T(8,128)(2,1)S(1)}, u32[]{:S(2)}, u32[]{:S(2)}) collective-permute-start(bf16[256,128]{1,0:T(8,128)(2,1)S(1)} %get-tuple-element.53), channel_id=1, source_target_pairs={{0,12},{1,76},{4,0},{5,64},{8,4},{9,68},{12,8},{13,72},{64,13},{65... | collective-permute-start | bytes 196616 | tf_op jit(solution)/shard_map/ppermute | solution.py:356
  98.1 5.8 %collective-permute-start.11 = (bf16[256,128]{1,0:T(8,128)(2,1)S(1)}, bf16[256,128]{1,0:T(8,128)(2,1)S(1)}, u32[]{:S(2)}, u32[]{:S(2)}) collective-permute-start(bf16[256,128]{1,0:T(8,128)(2,1)S(1)} %get-tuple-element.52), channel_id=1, source_target_pairs={{0,8},{1,72},{4,12},{5,76},{8,0},{9,64},{12,4},{13,68},{64,9},{65,... | collective-permute-start | bytes 196616 | tf_op jit(solution)/shard_map/ppermute | solution.py:356
  98.2 6.8 %collective-permute-start.12 = (bf16[256,128]{1,0:T(8,128)(2,1)S(1)}, bf16[256,128]{1,0:T(8,128)(2,1)S(1)}, u32[]{:S(2)}, u32[]{:S(2)}) collective-permute-start(bf16[256,128]{1,0:T(8,128)(2,1)S(1)} %get-tuple-element.51), channel_id=1, source_target_pairs={{0,4},{1,68},{4,8},{5,72},{8,12},{9,76},{12,0},{13,64},{64,5},{65,... | collective-permute-start | bytes 196616 | tf_op jit(solution)/shard_map/ppermute | solution.py:356
  100.1 4.9 %collective-permute-start.9 = (bf16[256,128]{1,0:T(8,128)(2,1)S(1)}, bf16[256,128]{1,0:T(8,128)(2,1)S(1)}, u32[]{:S(2)}, u32[]{:S(2)}) collective-permute-start(bf16[256,128]{1,0:T(8,128)(2,1)S(1)} %get-tuple-element.50), channel_id=1, source_target_pairs={{0,0},{1,64},{4,4},{5,68},{8,8},{9,72},{12,12},{13,76},{64,1},{65,... | collective-permute-start | bytes 196616 | tf_op jit(solution)/shard_map/ppermute | solution.py:356
  107.9 10.3 %copy-start.3 = (f32[2,2048]{1,0:T(2,128)S(1)}, f32[2,2048]{1,0:T(2,128)}, u32[]{:S(2)}) copy-start(f32[2,2048]{1,0:T(2,128)} %param.20) | copy-start | bytes 49156
  107.9 8.8 %collective-permute-start.13 = (bf16[2,64,2048]{2,1,0:T(8,128)(2,1)S(1)}, bf16[2,64,2048]{2,1,0:T(8,128)(2,1)S(1)}, u32[]{:S(2)}, u32[]{:S(2)}) collective-permute-start(bf16[2,64,2048]{2,1,0:T(8,128)(2,1)S(1)} %fusion.5), channel_id=1, source_target_pairs={{0,1},{1,0},{2,3},{3,2},{4,5},{5,4},{6,7},{7,6},{8,9},{9,8},{10,11... | collective-permute-start | bytes 1572872 | tf_op jit(solution)/shard_map/ppermute | solution.py:23
  116.9 8.7 %collective-permute-start.14 = (bf16[64,2048]{1,0:T(8,128)(2,1)S(1)}, bf16[64,2048]{1,0:T(8,128)(2,1)S(1)}, u32[]{:S(2)}, u32[]{:S(2)}) collective-permute-start(bf16[64,2048]{1,0:T(8,128)(2,1)S(1)} %fusion.12), channel_id=1, source_target_pairs={{0,2},{2,0},{1,3},{3,1},{4,6},{6,4},{5,7},{7,5},{8,10},{10,8},{9,1... | collective-permute-start | bytes 786440 | tf_op jit(solution)/shard_map/ppermute | solution.py:23
  118.1 59.8 %collective-permute-start.18 = (bf16[2,2048,256]{2,1,0:T(8,128)(2,1)}, bf16[2,2048,256]{2,1,0:T(8,128)(2,1)}, u32[]{:S(2)}, u32[]{:S(2)}) collective-permute-start(bf16[2,2048,256]{2,1,0:T(8,128)(2,1)} %param.21), channel_id=1, source_target_pairs={{1,9},{5,13},{9,1},{13,5},{3,11},{7,15},{11,3},{15,7},{17,25},{21,... | collective-permute-start | bytes 6291464 | tf_op jit(solution)/shard_map/ppermute | solution.py:318
  128.0 21.5 %all-to-all-start.1 = ((bf16[8,32,2048]{2,1,0:T(8,128)(2,1)}), bf16[8,32,2048]{2,1,0:T(8,128)(2,1)S(1)}, u32[]{:S(2)}, u32[]{:S(2)}) async-start(bf16[8,32,2048]{2,1,0:T(8,128)(2,1)} %broadcast_in_dim.141), calls=%async_computation.1 | async-start | bytes 2097152 | tf_op jit(solution)/shard_map/all_to_all | solution.py:31
  132.8 23.2 %collective-permute-start.19 = (bf16[256,2048]{1,0:T(8,128)(2,1)}, bf16[256,2048]{1,0:T(8,128)(2,1)}, u32[]{:S(2)}, u32[]{:S(2)}) collective-permute-start(bf16[256,2048]{1,0:T(8,128)(2,1)} %param.22), channel_id=1, source_target_pairs={{1,9},{5,13},{9,1},{13,5},{3,11},{7,15},{11,3},{15,7},{17,25},{21,... | collective-permute-start | bytes 3145736 | tf_op jit(solution)/shard_map/ppermute | solution.py:318
  134.5 57.4 %collective-permute-start.16 = (bf16[2,2048,256]{2,1,0:T(8,128)(2,1)}, bf16[2,2048,256]{2,1,0:T(8,128)(2,1)}, u32[]{:S(2)}, u32[]{:S(2)}) collective-permute-start(bf16[2,2048,256]{2,1,0:T(8,128)(2,1)} %param.21), channel_id=1, source_target_pairs={{0,4},{1,13},{4,8},{5,1},{8,12},{9,5},{12,0},{13,9},{2,6},{3,15},{... | collective-permute-start | bytes 6291464 | tf_op jit(solution)/shard_map/ppermute | solution.py:314
  149.5 20.8 %all-to-all-start.3 = ((bf16[8,32,2048]{2,1,0:T(8,128)(2,1)}), bf16[8,32,2048]{2,1,0:T(8,128)(2,1)S(1)}, u32[]{:S(2)}, u32[]{:S(2)}) async-start(bf16[8,32,2048]{2,1,0:T(8,128)(2,1)} %broadcast_in_dim.142), calls=%async_computation.3 | async-start | bytes 2097152 | tf_op jit(solution)/shard_map/all_to_all | solution.py:31
  153.1 38.8 %collective-permute-start.17 = (bf16[256,2048]{1,0:T(8,128)(2,1)}, bf16[256,2048]{1,0:T(8,128)(2,1)}, u32[]{:S(2)}, u32[]{:S(2)}) collective-permute-start(bf16[256,2048]{1,0:T(8,128)(2,1)} %param.22), channel_id=1, source_target_pairs={{0,4},{1,13},{4,8},{5,1},{8,12},{9,5},{12,0},{13,9},{2,6},{3,15},{... | collective-permute-start | bytes 3145736 | tf_op jit(solution)/shard_map/ppermute | solution.py:314
  156.0 35.9 %collective-permute-start.15 = (bf16[256,2048]{1,0:T(8,128)(2,1)S(1)}, bf16[256,2048]{1,0:T(8,128)(2,1)}, u32[]{:S(2)}, u32[]{:S(2)}) collective-permute-start(bf16[256,2048]{1,0:T(8,128)(2,1)S(1)} %bitcast.124), channel_id=1, source_target_pairs={{0,1},{1,0},{2,3},{3,2},{4,5},{5,4},{6,7},{7,6},{8,9},{9,8},{10,11... | collective-permute-start | bytes 3145736 | tf_op jit(solution)/shard_map/ppermute | solution.py:23
  170.3 28.5 %collective-permute-start.21 = (bf16[256,2048]{1,0:T(8,128)(2,1)S(1)}, bf16[256,2048]{1,0:T(8,128)(2,1)S(1)}, u32[]{:S(2)}, u32[]{:S(2)}) collective-permute-start(bf16[256,2048]{1,0:T(8,128)(2,1)S(1)} %bitcast.126), channel_id=1, source_target_pairs={{0,1},{1,0},{2,3},{3,2},{4,5},{5,4},{6,7},{7,6},{8,9},{9,8},{10,11... | collective-permute-start | bytes 3145736 | tf_op jit(solution)/shard_map/ppermute | solution.py:23
  198.3 7.7 %collective-permute-start.20 = (bf16[256,2048]{1,0:T(8,128)(2,1)S(1)}, bf16[256,2048]{1,0:T(8,128)(2,1)S(1)}, u32[]{:S(2)}, u32[]{:S(2)}) collective-permute-start(bf16[256,2048]{1,0:T(8,128)(2,1)S(1)} %get-tuple-element.27), channel_id=1, source_target_pairs={{0,1},{1,0},{2,3},{3,2},{4,5},{5,4},{6,7},{7,6},{8,9},{9,8},{10,11... | collective-permute-start | bytes 3145736 | tf_op jit(solution)/shard_map/ppermute | solution.py:23
  205.9 6.0 %collective-permute-start.22 = (bf16[256,2048]{1,0:T(8,128)(2,1)}, bf16[256,2048]{1,0:T(8,128)(2,1)S(1)}, u32[]{:S(2)}, u32[]{:S(2)}) collective-permute-start(bf16[256,2048]{1,0:T(8,128)(2,1)} %get-tuple-element.29), channel_id=1, source_target_pairs={{0,1},{1,0},{2,3},{3,2},{4,5},{5,4},{6,7},{7,6},{8,9},{9,8},{10,11... | collective-permute-start | bytes 3145736 | tf_op jit(solution)/shard_map/ppermute | solution.py:23
  207.3 22.3 %all-to-all-start.2 = ((bf16[8,32,2048]{2,1,0:T(8,128)(2,1)}), bf16[8,32,2048]{2,1,0:T(8,128)(2,1)S(1)}, u32[]{:S(2)}, u32[]{:S(2)}) async-start(bf16[8,32,2048]{2,1,0:T(8,128)(2,1)} %bitcast.79), calls=%async_computation.2 | async-start | bytes 2097152 | tf_op jit(solution)/shard_map/all_to_all | solution.py:382
  229.6 20.9 %all-to-all-start.4 = ((bf16[8,32,2048]{2,1,0:T(8,128)(2,1)}), bf16[8,32,2048]{2,1,0:T(8,128)(2,1)S(1)}, u32[]{:S(2)}, u32[]{:S(2)}) async-start(bf16[8,32,2048]{2,1,0:T(8,128)(2,1)} %bitcast.81), calls=%async_computation.4 | async-start | bytes 2097152 | tf_op jit(solution)/shard_map/all_to_all | solution.py:382

commit v2 on v1

--- a/solution.py
+++ b/solution.py
@@ -269,9 +269,6 @@
         )
 
     cached = jnp.stack([across(head_piece(s), s) for s in range(n_z)])
-    states_in, cached = lax.optimization_barrier((states_in, cached))
-    cached_own = spread(cached, "x").reshape((n_x * n_z,) + cached.shape[1:])
-    cached_parts = [cached_own, shift(cached_own, "core", 1)]
     slot_from = jnp.stack(
         [
             (jnp.where(c == 0, core, 1 - core) * n_x + x) * n_z + (z_at - sz) % n_z
@@ -283,6 +280,8 @@
 
     qkv_raw = jnp.einsum("td,cdw->ctw", states_in, w_qkv, preferred_element_type=F32)
     squares = lax.psum(jnp.sum(qkv_raw[:2] * qkv_raw[:2], axis=2), HEAD)
+    squares, cached = lax.optimization_barrier((squares, cached))
+    cached_own = spread(cached, "x").reshape((n_x * n_z,) + cached.shape[1:])
     group_from = jnp.stack(
         [blk] + [(core * n_x + x_at) * n_z + (z_at - g) % n_z for g in range(n_z)]
     ).astype(jnp.int32)
@@ -308,20 +307,27 @@
     ).transpose(2, 0, 1, 3)
     qkv_parts = [across(select_row(qkv, (z_at + s) % n_z), s) for s in range(n_z)]
 
-    w_gate_up, w_down, qkv_parts = lax.optimization_barrier((w_gate_up, w_down, qkv_parts))
-
-    def ring_weights(weights):
-        beside = lax.ppermute(
+    cached_own, qkv_parts = lax.optimization_barrier((cached_own, qkv_parts))
+    cached_parts = [cached_own, shift(cached_own, "core", 1)]
+
+    def beside(weights):
+        return lax.ppermute(
             weights, ("z", "core"),
             [(z * 2 + c, (z + 1 - 2 * c) % n_z * 2 + c) for z in range(n_z) for c in range(2)],
         )
+
+    def beyond(weights):
         far = lax.ppermute(
             weights, ("z", "core"), [(z * 2 + 1, (z + 2) % n_z * 2 + 1) for z in range(n_z)]
         )
-        return beside, jnp.where(core == 0, weights, far)
-
-    gu_a, gu_b = ring_weights(w_gate_up)
-    dn_a, dn_b = ring_weights(w_down)
+        return jnp.where(core == 0, weights, far)
+
+    w_gate_up, w_down, _ = lax.optimization_barrier((w_gate_up, w_down, cached))
+    gu_a, dn_a = beside(w_gate_up), beside(w_down)
+    w_gate_up, w_down, gu_a, dn_a, qkv_parts = lax.optimization_barrier(
+        (w_gate_up, w_down, gu_a, dn_a, qkv_parts)
+    )
+    gu_b, dn_b = beyond(w_gate_up), beyond(w_down)
 
     slots = slot_from.shape[0]
     slot_nodes = jnp.take(slot_node, slot_from)
@@ -356,6 +362,7 @@
         return lax.ppermute(values, corner, pairs)
 
     attended = jnp.concatenate([back(attended[s], s) for s in range(n_z)], axis=1)
+    attended, gu_b, dn_b = lax.optimization_barrier((attended, gu_b, dn_b))
     attn_part = jnp.dot(attended, w_out, preferred_element_type=F32)
     attn_part = attn_part.reshape(2, 2, rows // 4, -1)
 

time: 254 us -> 247 us (0.972)
  blocking collectives: 6.95 us -> 53.8 us
  starting transfers between devices: 68 us -> 42.9 us
  waiting for transfers between devices: 105 us -> 81.3 us
  matrix products: 8.87 us -> 6.09 us
    all_to_all x0 -> x2, blocking collectives: none -> 41.6 us  [spread(): return lax.all_to_all(copies, axes, 0, 0, tiled=True)]
    all_to_all x3 -> x1, waiting for transfers between devices: 38 us -> 0.01 us  [spread(): return lax.all_to_all(copies, axes, 0, 0, tiled=True)]
    ppermute x7, starting transfers between devices: 23.1 us -> 8.67 us  [shift(): return lax.ppermute(values, axis, [(i, (i + by) % n) for i in range(n)])]
    ppermute x8, waiting for transfers between devices: 10.1 us -> 20.7 us  [across(): return lax.ppermute(values, corner, pairs)]
    all_to_all x3 -> x1, starting transfers between devices: 12.8 us -> 4.29 us  [spread(): return lax.all_to_all(copies, axes, 0, 0, tiled=True)]
    psum x1, blocking collectives: 6.95 us -> 12.1 us  [on_device(): squares = lax.psum(jnp.sum(qkv_raw[:2] * qkv_raw[:2], axis=2), HEAD)]
    unnamed x15 -> x29, local copies, waits for them, and re-layouts: 0.11 us -> 3.62 us
    ppermute x4, waiting for transfers between devices: 4.07 us -> 7.54 us  [back(): return lax.ppermute(values, corner, pairs)]
  transfers between devices with their start and end apart: 28 -> 26, of which waited for: 13 -> 8; matrix products, arithmetic and copies ran while one was open for 12% -> 8% of each run, Pallas kernels for 5% -> 14%
where the time goes in v2:
time: 247 us; the launch traced here: 246 us
  waiting for transfers between devices  81.3 us (33%)
  blocking collectives  53.8 us (22%)
  starting transfers between devices  42.9 us (17%)
  Pallas kernels  33.8 us (14%)
  other arithmetic  15.6 us (6%)
  local copies, waits for them, and re-layouts  11.8 us (5%)
  matrix products  6.09 us (2%)
    all_to_all x2, blocking collectives, spread(): return lax.all_to_all(copies, axes, 0, 0, tiled=True)  41.6 us
    all_to_all x2, waiting for transfers between devices, on_device(): lax.all_to_all(total.reshape(n_plane, cut, -1), plane, 0, 0, tiled=True)  33.9 us
    pallas_call x1, Pallas kernels, attention(): pl.pallas_call(attention_body, out_shape=jax.ShapeDtypeStruct((groups, ro...  20.8 us
    ppermute x8, waiting for transfers between devices, across(): return lax.ppermute(values, corner, pairs)  20.7 us
    pallas_call x2, Pallas kernels, feed_forward(): pl.pallas_call(feed_forward_body, out_shape=(out, out), in_specs=[space]...  13 us
    psum x1, blocking collectives, on_device(): squares = lax.psum(jnp.sum(qkv_raw[:2] * qkv_raw[:2], axis=2), HEAD)  12.1 us
    ppermute x8, starting transfers between devices, across(): return lax.ppermute(values, corner, pairs)  11.4 us
    ppermute x2, waiting for transfers between devices, beside(): lax.ppermute(weights, ('z', 'core'), [(z * 2 + c, (z + 1 - 2 * c) % n_z *...  9.85 us
  transfers between devices with their start and end apart: 26, of which 8 were waited for; matrix products, arithmetic and copies ran while one was open for 8% of the time, Pallas kernels for 14%

profile of v2, /device:TPU:0, one launch (start us, length us, event | category | flops | bytes accessed | tf_op | source)
XLA Modules:
  0.0 245.9 jit_solution(10671444259591461327)
XLA Ops:
  0.0 1.2 constant_dynamic-slice_fusion.6
  1.2 4.2 %collective-permute-start.3 = (bf16[2,256,128]{2,1,0:T(8,128)(2,1)S(1)}, bf16[2,256,128]{2,1,0:T(8,128)(2,1)S(1)}, u32[]{:S(2)}, u32[]{:S(2)}) collective-permute-start(bf16[2,256,128]{2,1,0:T(8,128)(2,1)S(1)} %pad_maximum_fusion.7), channel_id=1, source_target_pairs={{0,12},{1,76},{4,0},{5,64},{8,4},{9,68},{12,8},{13,72},{64,13},{65... | collective-permute-start | bytes 393224 | tf_op jit(solution)/shard_map/ppermute | solution.py:263
  5.6 1.3 collective-permute-start.1
  6.9 1.3 collective-permute-start
  8.2 4.7 %convolution_bitcast_fusion = f32[3,256,512]{1,2,0:T(8,128)S(1)} fusion(bf16[3,2048,512]{2,1,0:T(8,128)(2,1)} %param.17, bf16[256,2048]{1,0:T(8,128)(2,1)S(1)} %copy-done.8), kind=kOutput, calls=%fused_computation.13 | convolution fusion | flops 1610612736 | bytes 8912896 | tf_op jit(solution)/shard_map/td,cdw->ctw/dot_general | solution.py:281
  15.0 12.1 %psum.7 = f32[2,256]{1,0:T(2,128)S(1)} all-reduce(f32[2,256]{1,0:T(2,128)S(1)} %fusion.3), channel_id=1, replica_groups=mesh['yhi'=2,'x'=4,'z'=4,'ylo'=2,'core'=2] {'ylo','core'}, use_global_device_ids=true, to_apply=%region_7.9 | all-reduce | flops 512 | bytes 4096 | tf_op jit(solution)/shard_map/psum | solution.py:282
  28.3 1.2 multiply_cosine_fusion
  29.5 1.1 pad_maximum_fusion.1
  30.6 2.3 collective-permute-start.4
  32.9 1.8 broadcast_in_dim.134
  34.7 4.3 %all-to-all-start = ((bf16[4,4,2,256,128]{4,3,2,1,0:T(8,128)(2,1)}), bf16[4,4,2,256,128]{4,3,2,1,0:T(8,128)(2,1)S(1)}, u32[]{:S(2)}, u32[]{:S(2)}) async-start(bf16[4,4,2,256,128]{4,3,2,1,0:T(8,128)(2,1)} %broadcast_in_dim.134), calls=%async_computation | async-start | bytes 4194304 | tf_op jit(solution)/shard_map/all_to_all | solution.py:31
  41.6 2.5 %collective-permute-start.8 = (bf16[3,256,128]{2,1,0:T(8,128)(2,1)S(1)}, bf16[3,256,128]{2,1,0:T(8,128)(2,1)S(1)}, u32[]{:S(2)}, u32[]{:S(2)}) collective-permute-start(bf16[3,256,128]{2,1,0:T(8,128)(2,1)S(1)} %get-tuple-element.65), channel_id=1, source_target_pairs={{0,8},{1,72},{4,12},{5,76},{8,0},{9,64},{12,4},{13,68},{64,9},{65,... | collective-permute-start | bytes 589832 | tf_op jit(solution)/shard_map/ppermute | solution.py:263
  44.1 1.3 collective-permute-start.9
  45.4 0.7 collective-permute-start.5
  46.1 18.4 %collective-permute-done.7.rest_1_ = bf16[3,256,128]{2,1,0:T(8,128)(2,1)S(1)} collective-permute-done((bf16[3,256,128]{2,1,0:T(8,128)(2,1)S(1)}, bf16[3,256,128]{2,1,0:T(8,128)(2,1)S(1)}, u32[]{:S(2)}, u32[]{:S(2)}) %collective-permute-start.7) | collective-permute-done | bytes 196640 | tf_op jit(solution)/shard_map/ppermute | solution.py:263
  64.5 2.4 collective-permute-done.8.rest_2_
  67.1 0.7 gather_fusion.2
  68.1 9.8 %collective-permute-done.5.dn_a = bf16[256,2048]{1,0:T(8,128)(2,1)} collective-permute-done((bf16[256,2048]{1,0:T(8,128)(2,1)}, bf16[256,2048]{1,0:T(8,128)(2,1)}, u32[]{:S(2)}, u32[]{:S(2)}) %collective-permute-start.5) | collective-permute-done | bytes 1048608 | tf_op jit(solution)/shard_map/ppermute | solution.py:314
  77.9 2.0 collective-permute-start.15
  80.9 1.7 collective-permute-start.16
  83.5 20.8 %shard_map.136 = bf16[4,256,128]{2,1,0:T(8,128)(2,1)S(1)} custom-call(s32[32]{0:T(128)S(1)} %get-tuple-element.61.nodes_ref, s32[32]{0:T(128)S(1)} %and_select_fusion.lengths_ref, s32[4,2,12]{2,1,0:T(2,128)S(1)} %copy.57.lists_ref, s32[4,2]{1,0:T(4,128)S(1)} %copy.58.counts_ref, bf16[3,256,128]{2,1,0:T(8,128)(2,1)S(1)} %collective-permute-done.6.rest_0_, ...), custom_call_target="tpu_custom_call" | custom-call | flops 2000000000 | bytes 6000000 | tf_op jit(solution)/shard_map/pallas_call | solution.py:166
  104.4 1.3 collective-permute-start.14
  105.7 1.2 collective-permute-start.13
  106.9 1.6 collective-permute-start.12
  109.2 1.3 broadcast_select_fusion.1.dn_b
  110.5 7.5 %collective-permute-done.14 = bf16[256,128]{1,0:T(8,128)(2,1)S(1)} collective-permute-done((bf16[256,128]{1,0:T(8,128)(2,1)S(1)}, bf16[256,128]{1,0:T(8,128)(2,1)S(1)}, u32[]{:S(2)}, u32[]{:S(2)}) %collective-permute-start.14) | collective-permute-done | bytes 65568 | tf_op jit(solution)/shard_map/ppermute | solution.py:362
  118.1 2.0 broadcast_select_fusion.gu_b
  120.3 1.4 fusion.1
  121.8 1.3 copy-done.5
  123.1 0.9 fusion.5
  123.9 6.7 %collective-permute-start.17 = (bf16[2,64,2048]{2,1,0:T(8,128)(2,1)}, bf16[2,64,2048]{2,1,0:T(8,128)(2,1)}, u32[]{:S(2)}, u32[]{:S(2)}) collective-permute-start(bf16[2,64,2048]{2,1,0:T(8,128)(2,1)} %fusion.5), channel_id=1, source_target_pairs={{0,1},{1,0},{2,3},{3,2},{4,5},{5,4},{6,7},{7,6},{8,9},{9,8},{10,11... | collective-permute-start | bytes 1572872 | tf_op jit(solution)/shard_map/ppermute | solution.py:23
  130.7 1.9 collective-permute-done.17
  132.6 1.5 bitcast_add_fusion
  134.1 1.3 collective-permute-start.18
  135.4 7.3 %collective-permute-done.18 = bf16[64,2048]{1,0:T(8,128)(2,1)S(1)} collective-permute-done((bf16[64,2048]{1,0:T(8,128)(2,1)S(1)}, bf16[64,2048]{1,0:T(8,128)(2,1)S(1)}, u32[]{:S(2)}, u32[]{:S(2)}) %collective-permute-start.18) | collective-permute-done | bytes 262176 | tf_op jit(solution)/shard_map/ppermute | solution.py:23
  143.0 1.1 add_convert_fusion.3
  144.2 21.0 %all_to_all.25 = bf16[8,32,2048]{2,1,0:T(8,128)(2,1)S(1)} all-to-all(bf16[8,32,2048]{2,1,0:T(8,128)(2,1)S(1)} %broadcast_in_dim.142), channel_id=1, replica_groups=mesh['yhi'=2,'x'=4,'z'=4,'ylo'=2,'core'=2] {'yhi','x'}, dimensions={0} | all-to-all | bytes 2097152 | tf_op jit(solution)/shard_map/all_to_all | solution.py:31
  165.4 20.6 %all_to_all.26 = bf16[8,32,2048]{2,1,0:T(8,128)(2,1)S(1)} all-to-all(bf16[8,32,2048]{2,1,0:T(8,128)(2,1)S(1)} %broadcast_in_dim.141), channel_id=1, replica_groups=mesh['yhi'=2,'x'=4,'z'=4,'ylo'=2,'core'=2] {'yhi','x'}, dimensions={0} | all-to-all | bytes 2097152 | tf_op jit(solution)/shard_map/all_to_all | solution.py:31
  186.0 6.0 %shard_map.138 = (bf16[256,2048]{1,0:T(8,128)(2,1)S(1)}, bf16[256,2048]{1,0:T(8,128)(2,1)S(1)}) custom-call(bf16[256,2048]{1,0:T(8,128)(2,1)S(1)} %bitcast.126, bf16[256,2048]{1,0:T(8,128)(2,1)S(1)} %collective-permute-done.21.other_tokens, bf16[2,2048,256]{2,1,0:T(8,128)(2,1)} %collective-permute-done.4.gu_a, ...), custom_call_target="tpu_custom_call" | custom-call | flops 3221225472 | bytes 10485760 | tf_op jit(solution)/shard_map/pallas_call | solution.py:218
  192.6 1.2 copy-done.2
  193.8 7.0 %shard_map.137 = (bf16[256,2048]{1,0:T(8,128)(2,1)S(1)}, bf16[256,2048]{1,0:T(8,128)(2,1)}) custom-call(bf16[256,2048]{1,0:T(8,128)(2,1)S(1)} %bitcast.124, bf16[256,2048]{1,0:T(8,128)(2,1)S(1)} %collective-permute-done.19.other_tokens, bf16[2,2048,256]{2,1,0:T(8,128)(2,1)} %collective-permute-done.4.gu_a, bf16[256,2048]{1,0:T(8,128)(2,1)} %collective-permute-done.5.dn_a, ...), custom_call_target="tpu_custom_call" | custom-call | flops 3221225472 | bytes 10485760 | tf_op jit(solution)/shard_map/pallas_call | solution.py:218
  200.8 1.4 add_convert_fusion
  202.2 3.6 %all-to-all-start.4 = ((bf16[8,32,2048]{2,1,0:T(8,128)(2,1)}), bf16[8,32,2048]{2,1,0:T(8,128)(2,1)S(1)}, u32[]{:S(2)}, u32[]{:S(2)}) async-start(bf16[8,32,2048]{2,1,0:T(8,128)(2,1)} %bitcast.84), calls=%async_computation.4 | async-start | bytes 2097152 | tf_op jit(solution)/shard_map/all_to_all | solution.py:389
  205.8 1.4 add_convert_fusion.1
  207.2 16.6 %all-to-all-done.4 = bf16[8,32,2048]{2,1,0:T(8,128)(2,1)S(1)} async-done(((bf16[8,32,2048]{2,1,0:T(8,128)(2,1)}), bf16[8,32,2048]{2,1,0:T(8,128)(2,1)S(1)}, u32[]{:S(2)}, u32[]{:S(2)}) %all-to-all-start.4) | async-done | bytes 1048608 | tf_op jit(solution)/shard_map/all_to_all | solution.py:389
  223.8 3.6 %all-to-all-start.2 = ((bf16[8,32,2048]{2,1,0:T(8,128)(2,1)}), bf16[8,32,2048]{2,1,0:T(8,128)(2,1)S(1)}, u32[]{:S(2)}, u32[]{:S(2)}) async-start(bf16[8,32,2048]{2,1,0:T(8,128)(2,1)} %bitcast.82), calls=%async_computation.2 | async-start | bytes 2097152 | tf_op jit(solution)/shard_map/all_to_all | solution.py:389
  227.5 17.2 %all-to-all-done.2 = bf16[8,32,2048]{2,1,0:T(8,128)(2,1)S(1)} async-done(((bf16[8,32,2048]{2,1,0:T(8,128)(2,1)}), bf16[8,32,2048]{2,1,0:T(8,128)(2,1)S(1)}, u32[]{:S(2)}, u32[]{:S(2)}) %all-to-all-start.2) | async-done | bytes 1048608 | tf_op jit(solution)/shard_map/all_to_all | solution.py:389
  245.1 0.9 add_convert_fusion.2
  (125 shorter events, 10.6 us)
Async XLA Ops:
  0.0 13.5 %copy-start = (s32[32,256]{1,0:T(8,128)S(1)}, s32[32,256]{1,0:T(8,128)}, u32[]{:S(2)}) copy-start(s32[32,256]{1,0:T(8,128)} %param.28) | copy-start | bytes 98308
  0.0 8.2 %copy-start.8 = (bf16[256,2048]{1,0:T(8,128)(2,1)S(1)}, bf16[256,2048]{1,0:T(8,128)(2,1)}, u32[]{:S(2)}) copy-start(bf16[256,2048]{1,0:T(8,128)(2,1)} %param.16) | copy-start | bytes 3145732
  1.2 28.3 %collective-permute-start.3 = (bf16[2,256,128]{2,1,0:T(8,128)(2,1)S(1)}, bf16[2,256,128]{2,1,0:T(8,128)(2,1)S(1)}, u32[]{:S(2)}, u32[]{:S(2)}) collective-permute-start(bf16[2,256,128]{2,1,0:T(8,128)(2,1)S(1)} %pad_maximum_fusion.7), channel_id=1, source_target_pairs={{0,12},{1,76},{4,0},{5,64},{8,4},{9,68},{12,8},{13,72},{64,13},{65... | collective-permute-start | bytes 393224 | tf_op jit(solution)/shard_map/ppermute | solution.py:263
  5.4 24.1 %collective-permute-start.2 = (bf16[2,256,128]{2,1,0:T(8,128)(2,1)S(1)}, bf16[2,256,128]{2,1,0:T(8,128)(2,1)}, u32[]{:S(2)}, u32[]{:S(2)}) collective-permute-start(bf16[2,256,128]{2,1,0:T(8,128)(2,1)S(1)} %pad_maximum_fusion.6), channel_id=1, source_target_pairs={{0,8},{1,72},{4,12},{5,76},{8,0},{9,64},{12,4},{13,68},{64,9},{65,... | collective-permute-start | bytes 393224 | tf_op jit(solution)/shard_map/ppermute | solution.py:263
  5.6 24.0 %collective-permute-start.1 = (bf16[2,256,128]{2,1,0:T(8,128)(2,1)S(1)}, bf16[2,256,128]{2,1,0:T(8,128)(2,1)}, u32[]{:S(2)}, u32[]{:S(2)}) collective-permute-start(bf16[2,256,128]{2,1,0:T(8,128)(2,1)S(1)} %pad_maximum_fusion.5), channel_id=1, source_target_pairs={{0,4},{1,68},{4,8},{5,72},{8,12},{9,76},{12,0},{13,64},{64,5},{65,... | collective-permute-start | bytes 393224 | tf_op jit(solution)/shard_map/ppermute | solution.py:263
  6.9 22.6 %collective-permute-start = (bf16[2,256,128]{2,1,0:T(8,128)(2,1)S(1)}, bf16[2,256,128]{2,1,0:T(8,128)(2,1)}, u32[]{:S(2)}, u32[]{:S(2)}) collective-permute-start(bf16[2,256,128]{2,1,0:T(8,128)(2,1)S(1)} %pad_maximum_fusion.4), channel_id=1, source_target_pairs={{0,0},{1,64},{4,4},{5,68},{8,8},{9,72},{12,12},{13,76},{64,1},{65,... | collective-permute-start | bytes 393224 | tf_op jit(solution)/shard_map/ppermute | solution.py:263
  12.9 1.4 copy-start.10
  13.0 14.9 %copy-start.12 = (s32[28]{0:T(128)S(1)}, s32[28]{0:T(128)}, u32[]{:S(2)}) copy-start(s32[28]{0:T(128)} %param.27) | copy-start | bytes 340
  13.1 15.0 %copy-start.3 = (s32[32]{0:T(128)S(1)}, s32[32]{0:T(128)}, u32[]{:S(2)}) copy-start(s32[32]{0:T(128)} %param.26) | copy-start | bytes 388
  13.2 16.3 %copy-start.11 = (f32[2,512]{1,0:T(2,128)S(1)}, f32[2,512]{1,0:T(2,128)}, u32[]{:S(2)}) copy-start(f32[2,512]{1,0:T(2,128)} %param.18) | copy-start | bytes 12292
  30.6 47.3 %collective-permute-start.4 = (bf16[2,2048,256]{2,1,0:T(8,128)(2,1)}, bf16[2,2048,256]{2,1,0:T(8,128)(2,1)}, u32[]{:S(2)}, u32[]{:S(2)}) collective-permute-start(bf16[2,2048,256]{2,1,0:T(8,128)(2,1)} %param.21), channel_id=1, source_target_pairs={{0,4},{1,13},{4,8},{5,1},{8,12},{9,5},{12,0},{13,9},{2,6},{3,15},{... | collective-permute-start | bytes 6291464 | tf_op jit(solution)/shard_map/ppermute | solution.py:314
  34.7 32.1 %all-to-all-start = ((bf16[4,4,2,256,128]{4,3,2,1,0:T(8,128)(2,1)}), bf16[4,4,2,256,128]{4,3,2,1,0:T(8,128)(2,1)S(1)}, u32[]{:S(2)}, u32[]{:S(2)}) async-start(bf16[4,4,2,256,128]{4,3,2,1,0:T(8,128)(2,1)} %broadcast_in_dim.134), calls=%async_computation | async-start | bytes 4194304 | tf_op jit(solution)/shard_map/all_to_all | solution.py:31
  39.0 0.9 copy-start.6
  39.0 1.0 copy-start.7
  40.4 26.6 %copy-start.4 = (s32[32]{0:T(128)S(1)}, s32[32]{0:T(128)}, u32[]{:S(2)}) copy-start(s32[32]{0:T(128)} %param.25) | copy-start | bytes 388
  40.9 4.5 %collective-permute-start.6 = (bf16[3,256,128]{2,1,0:T(8,128)(2,1)S(1)}, bf16[3,256,128]{2,1,0:T(8,128)(2,1)S(1)}, u32[]{:S(2)}, u32[]{:S(2)}) collective-permute-start(bf16[3,256,128]{2,1,0:T(8,128)(2,1)S(1)} %get-tuple-element.67), channel_id=1, source_target_pairs={{0,0},{1,64},{4,4},{5,68},{8,8},{9,72},{12,12},{13,76},{64,1},{65,... | collective-permute-start | bytes 589832 | tf_op jit(solution)/shard_map/ppermute | solution.py:263
  41.5 22.9 %collective-permute-start.7 = (bf16[3,256,128]{2,1,0:T(8,128)(2,1)S(1)}, bf16[3,256,128]{2,1,0:T(8,128)(2,1)S(1)}, u32[]{:S(2)}, u32[]{:S(2)}) collective-permute-start(bf16[3,256,128]{2,1,0:T(8,128)(2,1)S(1)} %get-tuple-element.66), channel_id=1, source_target_pairs={{0,4},{1,68},{4,8},{5,72},{8,12},{9,76},{12,0},{13,64},{64,5},{65,... | collective-permute-start | bytes 589832 | tf_op jit(solution)/shard_map/ppermute | solution.py:263
  41.6 25.2 %collective-permute-start.8 = (bf16[3,256,128]{2,1,0:T(8,128)(2,1)S(1)}, bf16[3,256,128]{2,1,0:T(8,128)(2,1)S(1)}, u32[]{:S(2)}, u32[]{:S(2)}) collective-permute-start(bf16[3,256,128]{2,1,0:T(8,128)(2,1)S(1)} %get-tuple-element.65), channel_id=1, source_target_pairs={{0,8},{1,72},{4,12},{5,76},{8,0},{9,64},{12,4},{13,68},{64,9},{65,... | collective-permute-start | bytes 589832 | tf_op jit(solution)/shard_map/ppermute | solution.py:263
  44.1 22.8 %collective-permute-start.9 = (bf16[3,256,128]{2,1,0:T(8,128)(2,1)S(1)}, bf16[3,256,128]{2,1,0:T(8,128)(2,1)S(1)}, u32[]{:S(2)}, u32[]{:S(2)}) collective-permute-start(bf16[3,256,128]{2,1,0:T(8,128)(2,1)S(1)} %get-tuple-element.64), channel_id=1, source_target_pairs={{0,12},{1,76},{4,0},{5,64},{8,4},{9,68},{12,8},{13,72},{64,13},{65... | collective-permute-start | bytes 589832 | tf_op jit(solution)/shard_map/ppermute | solution.py:263
  45.4 32.5 %collective-permute-start.5 = (bf16[256,2048]{1,0:T(8,128)(2,1)}, bf16[256,2048]{1,0:T(8,128)(2,1)}, u32[]{:S(2)}, u32[]{:S(2)}) collective-permute-start(bf16[256,2048]{1,0:T(8,128)(2,1)} %param.22), channel_id=1, source_target_pairs={{0,4},{1,13},{4,8},{5,1},{8,12},{9,5},{12,0},{13,9},{2,6},{3,15},{... | collective-permute-start | bytes 3145736 | tf_op jit(solution)/shard_map/ppermute | solution.py:314
  66.9 16.7 %collective-permute-start.10 = (bf16[16,2,256,128]{3,2,1,0:T(8,128)(2,1)S(1)}, bf16[16,2,256,128]{3,2,1,0:T(8,128)(2,1)}, u32[]{:S(2)}, u32[]{:S(2)}) collective-permute-start(bf16[16,2,256,128]{3,2,1,0:T(8,128)(2,1)S(1)} %bitcast.121), channel_id=1, source_target_pairs={{0,1},{1,0},{2,3},{3,2},{4,5},{5,4},{6,7},{7,6},{8,9},{9,8},{10,11... | collective-permute-start | bytes 6291464 | tf_op jit(solution)/shard_map/ppermute | solution.py:23
  77.9 40.2 %collective-permute-start.15 = (bf16[2,2048,256]{2,1,0:T(8,128)(2,1)}, bf16[2,2048,256]{2,1,0:T(8,128)(2,1)}, u32[]{:S(2)}, u32[]{:S(2)}) collective-permute-start(bf16[2,2048,256]{2,1,0:T(8,128)(2,1)} %param.21), channel_id=1, source_target_pairs={{1,9},{5,13},{9,1},{13,5},{3,11},{7,15},{11,3},{15,7},{17,25},{21,... | collective-permute-start | bytes 6291464 | tf_op jit(solution)/shard_map/ppermute | solution.py:320
  80.9 27.6 %collective-permute-start.16 = (bf16[256,2048]{1,0:T(8,128)(2,1)}, bf16[256,2048]{1,0:T(8,128)(2,1)}, u32[]{:S(2)}, u32[]{:S(2)}) collective-permute-start(bf16[256,2048]{1,0:T(8,128)(2,1)} %param.22), channel_id=1, source_target_pairs={{1,9},{5,13},{9,1},{13,5},{3,11},{7,15},{11,3},{15,7},{17,25},{21,... | collective-permute-start | bytes 3145736 | tf_op jit(solution)/shard_map/ppermute | solution.py:320
  104.4 13.6 %collective-permute-start.14 = (bf16[256,128]{1,0:T(8,128)(2,1)S(1)}, bf16[256,128]{1,0:T(8,128)(2,1)S(1)}, u32[]{:S(2)}, u32[]{:S(2)}) collective-permute-start(bf16[256,128]{1,0:T(8,128)(2,1)S(1)} %get-tuple-element.75), channel_id=1, source_target_pairs={{0,4},{1,68},{4,8},{5,72},{8,12},{9,76},{12,0},{13,64},{64,5},{65,... | collective-permute-start | bytes 196616 | tf_op jit(solution)/shard_map/ppermute | solution.py:362
  105.7 12.3 %collective-permute-start.13 = (bf16[256,128]{1,0:T(8,128)(2,1)S(1)}, bf16[256,128]{1,0:T(8,128)(2,1)S(1)}, u32[]{:S(2)}, u32[]{:S(2)}) collective-permute-start(bf16[256,128]{1,0:T(8,128)(2,1)S(1)} %get-tuple-element.76), channel_id=1, source_target_pairs={{0,8},{1,72},{4,12},{5,76},{8,0},{9,64},{12,4},{13,68},{64,9},{65,... | collective-permute-start | bytes 196616 | tf_op jit(solution)/shard_map/ppermute | solution.py:362
  106.9 11.2 %collective-permute-start.12 = (bf16[256,128]{1,0:T(8,128)(2,1)S(1)}, bf16[256,128]{1,0:T(8,128)(2,1)S(1)}, u32[]{:S(2)}, u32[]{:S(2)}) collective-permute-start(bf16[256,128]{1,0:T(8,128)(2,1)S(1)} %get-tuple-element.77), channel_id=1, source_target_pairs={{0,12},{1,76},{4,0},{5,64},{8,4},{9,68},{12,8},{13,72},{64,13},{65... | collective-permute-start | bytes 196616 | tf_op jit(solution)/shard_map/ppermute | solution.py:362
  108.5 9.6 %collective-permute-start.11 = (bf16[256,128]{1,0:T(8,128)(2,1)S(1)}, bf16[256,128]{1,0:T(8,128)(2,1)S(1)}, u32[]{:S(2)}, u32[]{:S(2)}) collective-permute-start(bf16[256,128]{1,0:T(8,128)(2,1)S(1)} %get-tuple-element.74), channel_id=1, source_target_pairs={{0,0},{1,64},{4,4},{5,68},{8,8},{9,72},{12,12},{13,76},{64,1},{65,... | collective-permute-start | bytes 196616 | tf_op jit(solution)/shard_map/ppermute | solution.py:362
  110.5 75.5 %copy-start.1 = (bf16[256,2048]{1,0:T(8,128)(2,1)}, bf16[256,2048]{1,0:T(8,128)(2,1)S(1)}, u32[]{:S(2)}) copy-start(bf16[256,2048]{1,0:T(8,128)(2,1)S(1)} %broadcast_select_fusion.1.dn_b) | copy-start | bytes 3145732
  118.1 2.2 copy-start.13
  121.8 1.3 copy-start.5
  123.1 12.3 %copy-start.9 = (f32[2,2048]{1,0:T(2,128)S(1)}, f32[2,2048]{1,0:T(2,128)}, u32[]{:S(2)}) copy-start(f32[2,2048]{1,0:T(2,128)} %param.20) | copy-start | bytes 49156
  123.9 8.6 %collective-permute-start.17 = (bf16[2,64,2048]{2,1,0:T(8,128)(2,1)}, bf16[2,64,2048]{2,1,0:T(8,128)(2,1)}, u32[]{:S(2)}, u32[]{:S(2)}) collective-permute-start(bf16[2,64,2048]{2,1,0:T(8,128)(2,1)} %fusion.5), channel_id=1, source_target_pairs={{0,1},{1,0},{2,3},{3,2},{4,5},{5,4},{6,7},{7,6},{8,9},{9,8},{10,11... | collective-permute-start | bytes 1572872 | tf_op jit(solution)/shard_map/ppermute | solution.py:23
  134.1 8.7 %collective-permute-start.18 = (bf16[64,2048]{1,0:T(8,128)(2,1)S(1)}, bf16[64,2048]{1,0:T(8,128)(2,1)S(1)}, u32[]{:S(2)}, u32[]{:S(2)}) collective-permute-start(bf16[64,2048]{1,0:T(8,128)(2,1)S(1)} %fusion.10), channel_id=1, source_target_pairs={{0,2},{2,0},{1,3},{3,1},{4,6},{6,4},{5,7},{7,5},{8,10},{10,8},{9,1... | collective-permute-start | bytes 786440 | tf_op jit(solution)/shard_map/ppermute | solution.py:23
  165.2 20.7 %collective-permute-start.21 = (bf16[256,2048]{1,0:T(8,128)(2,1)S(1)}, bf16[256,2048]{1,0:T(8,128)(2,1)S(1)}, u32[]{:S(2)}, u32[]{:S(2)}) collective-permute-start(bf16[256,2048]{1,0:T(8,128)(2,1)S(1)} %bitcast.125), channel_id=1, source_target_pairs={{0,1},{1,0},{2,3},{3,2},{4,5},{5,4},{6,7},{7,6},{8,9},{9,8},{10,11... | collective-permute-start | bytes 3145736 | tf_op jit(solution)/shard_map/ppermute | solution.py:23
  186.0 6.6 %collective-permute-start.19 = (bf16[256,2048]{1,0:T(8,128)(2,1)S(1)}, bf16[256,2048]{1,0:T(8,128)(2,1)S(1)}, u32[]{:S(2)}, u32[]{:S(2)}) collective-permute-start(bf16[256,2048]{1,0:T(8,128)(2,1)S(1)} %bitcast.123), channel_id=1, source_target_pairs={{0,1},{1,0},{2,3},{3,2},{4,5},{5,4},{6,7},{7,6},{8,9},{9,8},{10,11... | collective-permute-start | bytes 3145736 | tf_op jit(solution)/shard_map/ppermute | solution.py:23
  192.0 8.8 %collective-permute-start.22 = (bf16[256,2048]{1,0:T(8,128)(2,1)S(1)}, bf16[256,2048]{1,0:T(8,128)(2,1)S(1)}, u32[]{:S(2)}, u32[]{:S(2)}) collective-permute-start(bf16[256,2048]{1,0:T(8,128)(2,1)S(1)} %get-tuple-element.53), channel_id=1, source_target_pairs={{0,1},{1,0},{2,3},{3,2},{4,5},{5,4},{6,7},{7,6},{8,9},{9,8},{10,11... | collective-permute-start | bytes 3145736 | tf_op jit(solution)/shard_map/ppermute | solution.py:23
  192.6 1.2 copy-start.2
  200.8 5.0 %collective-permute-start.20 = (bf16[256,2048]{1,0:T(8,128)(2,1)}, bf16[256,2048]{1,0:T(8,128)(2,1)S(1)}, u32[]{:S(2)}, u32[]{:S(2)}) collective-permute-start(bf16[256,2048]{1,0:T(8,128)(2,1)} %get-tuple-element.51), channel_id=1, source_target_pairs={{0,1},{1,0},{2,3},{3,2},{4,5},{5,4},{6,7},{7,6},{8,9},{9,8},{10,11... | collective-permute-start | bytes 3145736 | tf_op jit(solution)/shard_map/ppermute | solution.py:23
  202.2 21.6 %all-to-all-start.4 = ((bf16[8,32,2048]{2,1,0:T(8,128)(2,1)}), bf16[8,32,2048]{2,1,0:T(8,128)(2,1)S(1)}, u32[]{:S(2)}, u32[]{:S(2)}) async-start(bf16[8,32,2048]{2,1,0:T(8,128)(2,1)} %bitcast.84), calls=%async_computation.4 | async-start | bytes 2097152 | tf_op jit(solution)/shard_map/all_to_all | solution.py:389
  223.8 21.0 %all-to-all-start.2 = ((bf16[8,32,2048]{2,1,0:T(8,128)(2,1)}), bf16[8,32,2048]{2,1,0:T(8,128)(2,1)S(1)}, u32[]{:S(2)}, u32[]{:S(2)}) async-start(bf16[8,32,2048]{2,1,0:T(8,128)(2,1)} %bitcast.82), calls=%async_computation.2 | async-start | bytes 2097152 | tf_op jit(solution)/shard_map/all_to_all | solution.py:389

commit v3 on v2

--- a/solution.py
+++ b/solution.py
@@ -189,44 +189,50 @@
     )(nodes, lengths, lists, counts, *qkv_parts, row_info, seg_row, *parts)
 
 
-def feed_forward_body(
-    own_tokens, other_tokens, gu_a, dn_a, gu_b, dn_b, own_ref, other_ref
-):
-    rows = 128
+def feed_forward_body(core_ref, tokens_ref, gu_own, gu_got, dn_own, dn_got, out_ref):
+    rows = 256
+    first = core_ref[0] == 0
+    cut = dn_own.shape[1]
 
     def one(i, carry):
         at = pl.ds(i * rows, rows)
-        for tokens_ref, target in ((own_tokens, own_ref), (other_tokens, other_ref)):
-            tokens = tokens_ref[at, :]
-            part = 0.0
-            for gu_ref, dn_ref in ((gu_a, dn_a), (gu_b, dn_b)):
-                gate = jnp.dot(tokens, gu_ref[0], preferred_element_type=F32)
-                up = jnp.dot(tokens, gu_ref[1], preferred_element_type=F32)
-                hidden = (gate / (1.0 + jnp.exp(-gate)) * up).astype(BF)
-                part = part + jnp.dot(hidden, dn_ref[...], preferred_element_type=F32)
-            target[at, :] = part.astype(BF)
+        tokens = tokens_ref[at, :]
+        part = 0.0
+        for share in range(gu_own.shape[0]):
+            one_side = jnp.dot(tokens, gu_own[share], preferred_element_type=F32)
+            other_side = jnp.dot(tokens, gu_got[share], preferred_element_type=F32)
+            gate = jnp.where(first, one_side, other_side)
+            up = jnp.where(first, other_side, one_side)
+            hidden = gate / (1.0 + jnp.exp(-gate)) * up
+            low, high = hidden[:, :cut], hidden[:, cut:]
+            part = part + jnp.dot(
+                jnp.where(first, low, high).astype(BF), dn_own[share], preferred_element_type=F32
+            )
+            part = part + jnp.dot(
+                jnp.where(first, high, low).astype(BF), dn_got[share], preferred_element_type=F32
+            )
+        out_ref[at, :] = part.astype(BF)
         return carry
 
-    lax.fori_loop(0, own_tokens.shape[0] // rows, one, 0)
-
-
-def feed_forward(own, other, weights):
-    rows, width = own.shape
-    units = weights[1].shape[0]
+    lax.fori_loop(0, tokens_ref.shape[0] // rows, one, 0)
+
+
+def feed_forward(core, tokens, weights):
+    rows, width = tokens.shape
+    units = weights[0].shape[2] * 2
     space = pl.BlockSpec(memory_space=pltpu.VMEM)
-    out = jax.ShapeDtypeStruct((rows, width), BF)
     return pl.pallas_call(
         feed_forward_body,
-        out_shape=(out, out),
-        in_specs=[space] * 6,
-        out_specs=(space, space),
-        compiler_params=pltpu.CompilerParams(vmem_limit_bytes=40 << 20),
+        out_shape=jax.ShapeDtypeStruct((rows, width), BF),
+        in_specs=[pl.BlockSpec(memory_space=pltpu.SMEM)] + [space] * 5,
+        out_specs=space,
+        compiler_params=pltpu.CompilerParams(vmem_limit_bytes=48 << 20),
         cost_estimate=pl.CostEstimate(
-            flops=4 * rows * width * units * 6,
-            transcendentals=4 * rows * units,
-            bytes_accessed=(4 * rows * width + 6 * width * units) * 2,
+            flops=2 * rows * width * units * 3,
+            transcendentals=rows * units,
+            bytes_accessed=(2 * rows * width + 3 * width * units) * 2,
         ),
-    )(own, other, *weights)
+    )(core, tokens, *weights)
 
 
 def on_device(
@@ -278,9 +284,14 @@
 
     w_out = lax.dynamic_slice_in_dim(jnp.concatenate([w_out, w_out]), z_at * HD, w_out.shape[0], 0)
 
+    half_units = w_down.shape[0] // 2
+    gu_ring = lax.all_gather(select_row(w_gate_up, core), "z")
+    dn_ring = lax.all_gather(
+        lax.dynamic_slice_in_dim(w_down, core * half_units, half_units, 0), "z"
+    )
+
     qkv_raw = jnp.einsum("td,cdw->ctw", states_in, w_qkv, preferred_element_type=F32)
     squares = lax.psum(jnp.sum(qkv_raw[:2] * qkv_raw[:2], axis=2), HEAD)
-    squares, cached = lax.optimization_barrier((squares, cached))
     cached_own = spread(cached, "x").reshape((n_x * n_z,) + cached.shape[1:])
     group_from = jnp.stack(
         [blk] + [(core * n_x + x_at) * n_z + (z_at - g) % n_z for g in range(n_z)]
@@ -309,25 +320,6 @@
 
     cached_own, qkv_parts = lax.optimization_barrier((cached_own, qkv_parts))
     cached_parts = [cached_own, shift(cached_own, "core", 1)]
-
-    def beside(weights):
-        return lax.ppermute(
-            weights, ("z", "core"),
-            [(z * 2 + c, (z + 1 - 2 * c) % n_z * 2 + c) for z in range(n_z) for c in range(2)],
-        )
-
-    def beyond(weights):
-        far = lax.ppermute(
-            weights, ("z", "core"), [(z * 2 + 1, (z + 2) % n_z * 2 + 1) for z in range(n_z)]
-        )
-        return jnp.where(core == 0, weights, far)
-
-    w_gate_up, w_down, _ = lax.optimization_barrier((w_gate_up, w_down, cached))
-    gu_a, dn_a = beside(w_gate_up), beside(w_down)
-    w_gate_up, w_down, gu_a, dn_a, qkv_parts = lax.optimization_barrier(
-        (w_gate_up, w_down, gu_a, dn_a, qkv_parts)
-    )
-    gu_b, dn_b = beyond(w_gate_up), beyond(w_down)
 
     slots = slot_from.shape[0]
     slot_nodes = jnp.take(slot_node, slot_from)
@@ -362,7 +354,6 @@
         return lax.ppermute(values, corner, pairs)
 
     attended = jnp.concatenate([back(attended[s], s) for s in range(n_z)], axis=1)
-    attended, gu_b, dn_b = lax.optimization_barrier((attended, gu_b, dn_b))
     attn_part = jnp.dot(attended, w_out, preferred_element_type=F32)
     attn_part = attn_part.reshape(2, 2, rows // 4, -1)
 
@@ -377,18 +368,22 @@
     state_rows = lax.dynamic_slice_in_dim(states_in, head_index * own_rows, own_rows, 0)
     mid_state = (state_rows.astype(F32) + rms_norm(attn_proj, post_gain[0])).astype(BF)
 
-    chunks = 2
-    cut = own_rows // chunks
+    mid_state, gu_ring, dn_ring = lax.optimization_barrier((mid_state, gu_ring, dn_ring))
     plane = ("yhi", "x")
-    n_plane = n_y * n_x
-    mlp_parts = []
-    for i in range(chunks):
-        tokens = spread(mid_state[i * cut : (i + 1) * cut], plane).reshape(n_plane * cut, -1)
-        own, other = feed_forward(tokens, shift(tokens, "core", 1), (gu_a, dn_a, gu_b, dn_b))
-        total = (own.astype(F32) + shift(other, "core", 1).astype(F32)).astype(BF)
-        total = lax.all_to_all(total.reshape(n_plane, cut, -1), plane, 0, 0, tiled=True)
-        mlp_parts.append(jnp.sum(total.astype(F32), axis=0))
-    mlp_proj = jnp.concatenate(mlp_parts)
+
+    def shares(ring, c):
+        return lax.dynamic_slice_in_dim(ring, c * 2, 2, 0)
+
+    weights = []
+    for ring in (gu_ring, dn_ring):
+        weights += [shares(ring, core), shift(shares(ring, 1 - core), "core", 1)]
+    core_at = core.astype(jnp.int32).reshape(1)
+    tokens = spread(mid_state, plane)
+    flat = tokens.reshape(-1, tokens.shape[2])
+    other = feed_forward(core_at, shift(flat, "core", 1), weights)
+    total = feed_forward(core_at, flat, weights).astype(F32) + shift(other, "core", 1).astype(F32)
+    total = lax.all_to_all(total.astype(BF).reshape(tokens.shape), plane, 0, 0, tiled=True)
+    mlp_proj = jnp.sum(total.astype(F32), axis=0)
     return (mid_state.astype(F32) + rms_norm(mlp_proj, post_gain[1])).astype(BF)
 
 

time: 247 us -> 235 us (0.951)
  waiting for transfers between devices: 81.3 us -> 60 us
  between operations: 0.66 us -> 14.2 us
  local copies, waits for them, and re-layouts: 11.8 us -> 21.8 us
  blocking collectives: 53.8 us -> 44.9 us
  other arithmetic: 15.6 us -> 10.9 us
  starting transfers between devices: 42.9 us -> 38.2 us
  Pallas kernels: 33.8 us -> 37 us
    all_to_all x2 -> x0, waiting for transfers between devices: 33.9 us -> none  [on_device(): lax.all_to_all(total.reshape(n_plane, cut, -1), plane, 0, 0, tiled=True)]
    all_to_all x1 -> x2, waiting for transfers between devices: 0.01 us -> 24.1 us  [spread(): return lax.all_to_all(copies, axes, 0, 0, tiled=True)]
    ppermute x4 -> x0, waiting for transfers between devices: 9.85 us -> none  [the longest x2 9.85 us: beside(): lax.ppermute(weights, ('z', 'core'), [(z * 2 + c, (z + 1 - 2 * c) % n_z *...]
    all_to_all x2 -> x1, blocking collectives: 41.6 us -> 32.6 us  [on_device(): lax.all_to_all(total.astype(BF).reshape(tokens.shape), plane, 0, 0, tiled...]
    dynamic_slice x0 -> x4, local copies, waits for them, and re-layouts: none -> 8.82 us  [the longest x2 5.66 us: shares(): return lax.dynamic_slice_in_dim(ring, c * 2, 2, 0)]
    all_to_all x2 -> x0, starting transfers between devices: 7.11 us -> none  [on_device(): lax.all_to_all(total.reshape(n_plane, cut, -1), plane, 0, 0, tiled=True)]
    ppermute x4 -> x0, starting transfers between devices: 6.7 us -> none  [the longest x2 3.68 us: beyond(): lax.ppermute(weights, ('z', 'core'), [(z * 2 + 1, (z + 2) % n_z * 2 + 1)...]
    all_to_all x1 -> x2, starting transfers between devices: 4.29 us -> 10.8 us  [spread(): return lax.all_to_all(copies, axes, 0, 0, tiled=True)]
  transfers between devices with their start and end apart: 26 -> 23, of which waited for: 8 -> 10; matrix products, arithmetic and copies ran while one was open for 8% -> 14% of each run, Pallas kernels for 14% -> 12%
where the time goes in v3:
time: 235 us; the launch traced here: 234 us
  waiting for transfers between devices  60 us (26%)
  blocking collectives  44.9 us (19%)
  starting transfers between devices  38.2 us (16%)
  Pallas kernels  37 us (16%)
  local copies, waits for them, and re-layouts  21.8 us (9%)
  between operations  14.2 us (6%)
  other arithmetic  10.9 us (5%)
  matrix products  7.44 us (3%)
    all_to_all x1, blocking collectives, on_device(): lax.all_to_all(total.astype(BF).reshape(tokens.shape), plane, 0, 0, tiled...  32.6 us
    all_to_all x2, waiting for transfers between devices, spread(): return lax.all_to_all(copies, axes, 0, 0, tiled=True)  24.1 us
    pallas_call x1, Pallas kernels, attention(): pl.pallas_call(attention_body, out_shape=jax.ShapeDtypeStruct((groups, ro...  20.9 us
    ppermute x8, waiting for transfers between devices, across(): return lax.ppermute(values, corner, pairs)  18.8 us
    pallas_call x2, Pallas kernels, feed_forward(): pl.pallas_call(feed_forward_body, out_shape=jax.ShapeDtypeStruct((rows, w...  16.1 us
    ppermute x7, waiting for transfers between devices, shift(): return lax.ppermute(values, axis, [(i, (i + by) % n) for i in range(n)])  13.9 us
    psum x1, blocking collectives, on_device(): squares = lax.psum(jnp.sum(qkv_raw[:2] * qkv_raw[:2], axis=2), HEAD)  12.3 us
    ppermute x8, starting transfers between devices, across(): return lax.ppermute(values, corner, pairs)  12 us
  transfers between devices with their start and end apart: 23, of which 10 were waited for; matrix products, arithmetic and copies ran while one was open for 14% of the time, Pallas kernels for 12%

profile of v3, /device:TPU:0, one launch (start us, length us, event | category | flops | bytes accessed | tf_op | source)
XLA Modules:
  0.0 234.4 jit_solution(14156870055051308831)
XLA Ops:
  6.5 2.0 constant_dynamic-slice_fusion.1
  8.7 1.1 constant_dynamic-slice_fusion.9
  9.9 4.0 %collective-permute-start.2 = (bf16[2,256,128]{2,1,0:T(8,128)(2,1)S(1)}, bf16[2,256,128]{2,1,0:T(8,128)(2,1)}, u32[]{:S(2)}, u32[]{:S(2)}) collective-permute-start(bf16[2,256,128]{2,1,0:T(8,128)(2,1)S(1)} %pad_maximum_fusion.4), channel_id=1, source_target_pairs={{0,8},{1,72},{4,12},{5,76},{8,0},{9,64},{12,4},{13,68},{64,9},{65,... | collective-permute-start | bytes 393224 | tf_op jit(solution)/shard_map/ppermute | solution.py:269
  14.6 0.7 collective-permute-start.3
  15.3 0.7 pad_maximum_fusion.3
  16.0 1.3 collective-permute-start.1
  18.0 2.1 collective-permute-start
  20.1 1.1 constant_dynamic-slice_fusion.2
  23.7 4.6 %convolution_bitcast_fusion = f32[3,256,512]{1,2,0:T(8,128)S(1)} fusion(bf16[3,2048,512]{2,1,0:T(8,128)(2,1)} %param.17, bf16[256,2048]{1,0:T(8,128)(2,1)S(1)} %copy-done.8), kind=kOutput, calls=%fused_computation.10 | convolution fusion | flops 1610612736 | bytes 8912896 | tf_op jit(solution)/shard_map/td,cdw->ctw/dot_general | solution.py:293
  29.9 0.7 slice.176
  31.8 12.3 %psum.7 = f32[2,256]{1,0:T(2,128)} all-reduce(f32[2,256]{1,0:T(2,128)S(1)} %fusion.3), channel_id=1, replica_groups=mesh['yhi'=2,'x'=4,'z'=4,'ylo'=2,'core'=2] {'ylo','core'}, use_global_device_ids=true, to_apply=%region_7.9 | all-reduce | flops 512 | bytes 4096 | tf_op jit(solution)/shard_map/psum | solution.py:294
  44.2 1.2 pad_maximum_fusion.1
  45.3 1.8 broadcast_in_dim.131
  47.2 4.4 %all-to-all-start = ((bf16[4,4,2,256,128]{4,3,2,1,0:T(8,128)(2,1)}), bf16[4,4,2,256,128]{4,3,2,1,0:T(8,128)(2,1)S(1)}, u32[]{:S(2)}, u32[]{:S(2)}) async-start(bf16[4,4,2,256,128]{4,3,2,1,0:T(8,128)(2,1)} %broadcast_in_dim.131), calls=%async_computation | async-start | bytes 4194304 | tf_op jit(solution)/shard_map/all_to_all | solution.py:31
  53.2 0.8 dynamic-slice_bitcast_fusion
  54.0 1.9 collective-permute-start.7
  55.9 1.2 collective-permute-start.6
  57.1 0.7 collective-permute-start.4
  57.9 9.9 %collective-permute-done.7.rest_3_ = bf16[3,256,128]{2,1,0:T(8,128)(2,1)S(1)} collective-permute-done((bf16[3,256,128]{2,1,0:T(8,128)(2,1)}, bf16[3,256,128]{2,1,0:T(8,128)(2,1)S(1)}, u32[]{:S(2)}, u32[]{:S(2)}) %collective-permute-start.7) | collective-permute-done | bytes 196640 | tf_op jit(solution)/shard_map/ppermute | solution.py:269
  67.8 3.9 %collective-permute-done.6.rest_2_ = bf16[3,256,128]{2,1,0:T(8,128)(2,1)S(1)} collective-permute-done((bf16[3,256,128]{2,1,0:T(8,128)(2,1)}, bf16[3,256,128]{2,1,0:T(8,128)(2,1)S(1)}, u32[]{:S(2)}, u32[]{:S(2)}) %collective-permute-start.6) | collective-permute-done | bytes 196640 | tf_op jit(solution)/shard_map/ppermute | solution.py:269
  71.7 5.0 %collective-permute-done.5.rest_1_ = bf16[3,256,128]{2,1,0:T(8,128)(2,1)S(1)} collective-permute-done((bf16[3,256,128]{2,1,0:T(8,128)(2,1)S(1)}, bf16[3,256,128]{2,1,0:T(8,128)(2,1)S(1)}, u32[]{:S(2)}, u32[]{:S(2)}) %collective-permute-start.5) | collective-permute-done | bytes 196640 | tf_op jit(solution)/shard_map/ppermute | solution.py:269
  76.8 0.7 gather_fusion.2
  77.5 0.7 gather_fusion.3
  79.8 1.2 collective-permute-done.8.rest_7_
  81.0 20.9 %shard_map.136 = bf16[4,256,128]{2,1,0:T(8,128)(2,1)S(1)} custom-call(s32[32]{0:T(128)S(1)} %get-tuple-element.29.nodes_ref, s32[32]{0:T(128)S(1)} %and_select_fusion.lengths_ref, s32[4,2,12]{2,1,0:T(2,128)S(1)} %copy.66.lists_ref, s32[4,2]{1,0:T(4,128)S(1)} %copy.67.counts_ref, bf16[3,256,128]{2,1,0:T(8,128)(2,1)S(1)} %collective-permute-done.4.rest_0_, ...), custom_call_target="tpu_custom_call" | custom-call | flops 2000000000 | bytes 6000000 | tf_op jit(solution)/shard_map/pallas_call | solution.py:166
  101.9 0.7 collective-permute-start.9
  102.6 2.5 %collective-permute-start.12 = (bf16[256,128]{1,0:T(8,128)(2,1)S(1)}, bf16[256,128]{1,0:T(8,128)(2,1)S(1)}, u32[]{:S(2)}, u32[]{:S(2)}) collective-permute-start(bf16[256,128]{1,0:T(8,128)(2,1)S(1)} %get-tuple-element.45), channel_id=1, source_target_pairs={{0,4},{1,68},{4,8},{5,72},{8,12},{9,76},{12,0},{13,64},{64,5},{65,... | collective-permute-start | bytes 196616 | tf_op jit(solution)/shard_map/ppermute | solution.py:354
  105.1 0.8 collective-permute-start.11
  106.0 1.9 collective-permute-start.10
  108.1 2.8 %collective-permute-done.11 = bf16[256,128]{1,0:T(8,128)(2,1)S(1)} collective-permute-done((bf16[256,128]{1,0:T(8,128)(2,1)S(1)}, bf16[256,128]{1,0:T(8,128)(2,1)S(1)}, u32[]{:S(2)}, u32[]{:S(2)}) %collective-permute-start.11) | collective-permute-done | bytes 65568 | tf_op jit(solution)/shard_map/ppermute | solution.py:354
  110.9 2.8 %fusion.1 = f32[256,2048]{1,0:T(8,128)S(1)} fusion(s32[]{:T(128)S(6)} %select_n.290, bf16[512,2048]{1,0:T(8,128)(2,1)} %param.19, bf16[256,128]{1,0:T(8,128)(2,1)S(1)} %collective-permute-done.12, bf16[256,128]{1,0:T(8,128)(2,1)S(1)} %collective-permute-done.11, bf16[256,128]{1,0:T(8,128)(2,1)S(1)} %collective-permute-done.10, ...), kind=kOutput, calls=%fused_computation.9 | convolution fusion | flops 542113792 | bytes 4456452 | tf_op jit(solution)/shard_map/dot_general | solution.py:357
  113.8 7.8 %collective-permute-start.13 = (bf16[2,64,2048]{2,1,0:T(8,128)(2,1)S(1)}, bf16[2,64,2048]{2,1,0:T(8,128)(2,1)S(1)}, u32[]{:S(2)}, u32[]{:S(2)}) collective-permute-start(bf16[2,64,2048]{2,1,0:T(8,128)(2,1)S(1)} %fusion.5), channel_id=1, source_target_pairs={{0,1},{1,0},{2,3},{3,2},{4,5},{5,4},{6,7},{7,6},{8,9},{9,8},{10,11... | collective-permute-start | bytes 1572872 | tf_op jit(solution)/shard_map/ppermute | solution.py:23
  121.6 1.5 collective-permute-done.13
  123.3 0.8 collective-permute-start.14
  124.1 7.9 %collective-permute-done.14 = bf16[64,2048]{1,0:T(8,128)(2,1)S(1)} collective-permute-done((bf16[64,2048]{1,0:T(8,128)(2,1)S(1)}, bf16[64,2048]{1,0:T(8,128)(2,1)S(1)}, u32[]{:S(2)}, u32[]{:S(2)}) %collective-permute-start.14) | collective-permute-done | bytes 262176 | tf_op jit(solution)/shard_map/ppermute | solution.py:23
  132.2 1.1 add_convert_fusion.2
  133.3 1.6 broadcast_in_dim.138
  134.9 6.3 %all-to-all-start.1 = ((bf16[8,64,2048]{2,1,0:T(8,128)(2,1)}), bf16[8,64,2048]{2,1,0:T(8,128)(2,1)}, u32[]{:S(2)}, u32[]{:S(2)}) async-start(bf16[8,64,2048]{2,1,0:T(8,128)(2,1)} %broadcast_in_dim.138), calls=%async_computation.1 | async-start | bytes 4194304 | tf_op jit(solution)/shard_map/all_to_all | solution.py:31
  141.3 3.9 %constant_dynamic-slice_fusion.11 = (bf16[2,2048,256]{2,1,0:T(8,128)(2,1)S(1)}, bf16[2,2048,256]{2,1,0:T(8,128)(2,1)}) fusion(bf16[4,2048,256]{2,1,0:T(8,128)(2,1)} %all-gather.4.cloned.1.call-done, s32[]{:T(128)S(6)} %select_n.297, s32[]{:T(128)S(6)} %select_n.296), kind=kLoop, calls=%fused_computation.88 | loop fusion | bytes 8388616 | tf_op jit(solution)/shard_map/dynamic_slice | solution.py:375
  145.1 24.1 %all-to-all-done.1 = bf16[8,64,2048]{2,1,0:T(8,128)(2,1)} async-done(((bf16[8,64,2048]{2,1,0:T(8,128)(2,1)}), bf16[8,64,2048]{2,1,0:T(8,128)(2,1)}, u32[]{:S(2)}, u32[]{:S(2)}) %all-to-all-start.1) | async-done | bytes 2097184 | tf_op jit(solution)/shard_map/all_to_all | solution.py:31
  169.3 1.8 constant_dynamic-slice_fusion.13
  171.7 3.3 %collective-permute-done.16.dn_got = bf16[2,128,2048]{2,1,0:T(8,128)(2,1)S(1)} collective-permute-done((bf16[2,128,2048]{2,1,0:T(8,128)(2,1)S(1)}, bf16[2,128,2048]{2,1,0:T(8,128)(2,1)S(1)}, u32[]{:S(2)}, u32[]{:S(2)}) %collective-permute-start.16) | collective-permute-done | bytes 1048608 | tf_op jit(solution)/shard_map/ppermute | solution.py:23
  175.0 1.3 copy-done.19
  176.3 8.1 %shard_map.138 = bf16[512,2048]{1,0:T(8,128)(2,1)S(1)} custom-call(s32[1]{0:T(128)} %bitcast.82.core_ref, bf16[512,2048]{1,0:T(8,128)(2,1)} %copy-done.19, bf16[2,2048,256]{2,1,0:T(8,128)(2,1)} %get-tuple-element.31.gu_own, bf16[2,2048,256]{2,1,0:T(8,128)(2,1)} %collective-permute-done.15.gu_got, bf16[2,128,2048]{2,1,0:T(8,128)(2,1)S(1)} %get-tuple-element.33.dn_own, ...), custom_call_target="tpu_custom_call" | custom-call | flops 3221225472 | bytes 10485760 | tf_op jit(solution)/shard_map/pallas_call | solution.py:224
  184.5 8.1 %shard_map.137 = bf16[512,2048]{1,0:T(8,128)(2,1)S(1)} custom-call(s32[1]{0:T(128)} %bitcast.82.core_ref, bf16[512,2048]{1,0:T(8,128)(2,1)} %bitcast.83.tokens_ref, bf16[2,2048,256]{2,1,0:T(8,128)(2,1)} %get-tuple-element.31.gu_own, bf16[2,2048,256]{2,1,0:T(8,128)(2,1)} %collective-permute-done.15.gu_got, ...), custom_call_target="tpu_custom_call" | custom-call | flops 3221225472 | bytes 10485760 | tf_op jit(solution)/shard_map/pallas_call | solution.py:224
  192.6 0.9 add_convert_fusion
  193.6 32.6 %all_to_all.15 = bf16[8,64,2048]{2,1,0:T(8,128)(2,1)S(1)} all-to-all(bf16[8,64,2048]{2,1,0:T(8,128)(2,1)S(1)} %bitcast.122), channel_id=1, replica_groups=mesh['yhi'=2,'x'=4,'z'=4,'ylo'=2,'core'=2] {'yhi','x'}, dimensions={0} | all-to-all | bytes 4194304 | tf_op jit(solution)/shard_map/all_to_all | solution.py:385
  226.7 0.9 add_convert_fusion.1
  (128 shorter events, 11.5 us)
Async XLA Ops:
  6.5 13.6 %copy-start = (bf16[2,2048,256]{2,1,0:T(8,128)(2,1)S(1)}, bf16[2,2048,256]{2,1,0:T(8,128)(2,1)}, u32[]{:S(2)}) copy-start(bf16[2,2048,256]{2,1,0:T(8,128)(2,1)} %param.21) | copy-start | bytes 6291460
  6.5 126.7 %all-gather.6.cloned.1.call-start = ((), (), s32[]{:S(2)}) async-start(), calls=%async_computation.4 | async-start | bytes 2621440 | tf_op jit(solution)/shard_map/all_gather | solution.py:289
  8.6 124.7 %all-gather.4.cloned.1.call-start = ((), (), s32[]{:S(2)}) async-start(), calls=%async_computation.3 | async-start | bytes 5242880 | tf_op jit(solution)/shard_map/all_gather | solution.py:288
  9.9 11.7 %copy-start.17 = (f32[2,512]{1,0:T(2,128)S(1)}, f32[2,512]{1,0:T(2,128)}, u32[]{:S(2)}) copy-start(f32[2,512]{1,0:T(2,128)} %param.18) | copy-start | bytes 12292
  9.9 12.3 %copy-start.5 = (s32[32,256]{1,0:T(8,128)S(1)}, s32[32,256]{1,0:T(8,128)}, u32[]{:S(2)}) copy-start(s32[32,256]{1,0:T(8,128)} %param.28) | copy-start | bytes 98308
  9.9 34.2 %collective-permute-start.2 = (bf16[2,256,128]{2,1,0:T(8,128)(2,1)S(1)}, bf16[2,256,128]{2,1,0:T(8,128)(2,1)}, u32[]{:S(2)}, u32[]{:S(2)}) collective-permute-start(bf16[2,256,128]{2,1,0:T(8,128)(2,1)S(1)} %pad_maximum_fusion.4), channel_id=1, source_target_pairs={{0,8},{1,72},{4,12},{5,76},{8,0},{9,64},{12,4},{13,68},{64,9},{65,... | collective-permute-start | bytes 393224 | tf_op jit(solution)/shard_map/ppermute | solution.py:269
  13.9 9.1 %copy-start.16 = (s32[32,8]{0,1:T(8,128)S(1)}, s32[32,8]{0,1:T(8,128)}, u32[]{:S(2)}) copy-start(s32[32,8]{0,1:T(8,128)} %param.29) | copy-start | bytes 3076
  13.9 9.8 %copy-start.8 = (bf16[256,2048]{1,0:T(8,128)(2,1)S(1)}, bf16[256,2048]{1,0:T(8,128)(2,1)}, u32[]{:S(2)}) copy-start(bf16[256,2048]{1,0:T(8,128)(2,1)} %param.16) | copy-start | bytes 3145732
  14.6 29.5 %collective-permute-start.3 = (bf16[2,256,128]{2,1,0:T(8,128)(2,1)}, bf16[2,256,128]{2,1,0:T(8,128)(2,1)}, u32[]{:S(2)}, u32[]{:S(2)}) collective-permute-start(bf16[2,256,128]{2,1,0:T(8,128)(2,1)} %pad_maximum_fusion.5), channel_id=1, source_target_pairs={{0,12},{1,76},{4,0},{5,64},{8,4},{9,68},{12,8},{13,72},{64,13},{65... | collective-permute-start | bytes 393224 | tf_op jit(solution)/shard_map/ppermute | solution.py:269
  16.0 28.2 %collective-permute-start.1 = (bf16[2,256,128]{2,1,0:T(8,128)(2,1)}, bf16[2,256,128]{2,1,0:T(8,128)(2,1)}, u32[]{:S(2)}, u32[]{:S(2)}) collective-permute-start(bf16[2,256,128]{2,1,0:T(8,128)(2,1)} %pad_maximum_fusion.3), channel_id=1, source_target_pairs={{0,4},{1,68},{4,8},{5,72},{8,12},{9,76},{12,0},{13,64},{64,5},{65,... | collective-permute-start | bytes 393224 | tf_op jit(solution)/shard_map/ppermute | solution.py:269
  18.0 26.2 %collective-permute-start = (bf16[2,256,128]{2,1,0:T(8,128)(2,1)}, bf16[2,256,128]{2,1,0:T(8,128)(2,1)}, u32[]{:S(2)}, u32[]{:S(2)}) collective-permute-start(bf16[2,256,128]{2,1,0:T(8,128)(2,1)} %pad_maximum_fusion.2), channel_id=1, source_target_pairs={{0,0},{1,64},{4,4},{5,68},{8,8},{9,72},{12,12},{13,76},{64,1},{65,... | collective-permute-start | bytes 393224 | tf_op jit(solution)/shard_map/ppermute | solution.py:269
  28.4 0.7 copy-start.18
  28.4 0.8 copy-start.2
  28.7 2.3 copy-start.6
  29.1 2.0 copy-start.9
  30.7 0.9 copy-start.4
  47.2 4.4 %copy-start.14 = (f32[2,256]{1,0:T(2,128)S(1)}, f32[2,256]{1,0:T(2,128)}, u32[]{:S(2)}) copy-start(f32[2,256]{1,0:T(2,128)} %psum.7) | copy-start | bytes 6148
  47.2 4.5 %copy-start.15 = (f32[1,256]{1,0:T(1,128)S(1)}, f32[1,256]{1,0:T(1,128)}, u32[]{:S(2)}) copy-start(f32[1,256]{1,0:T(1,128)} %fusion.25) | copy-start | bytes 3076
  47.2 5.0 %copy-start.12 = (f32[1,512]{1,0:T(1,128)S(1)}, f32[1,512]{1,0:T(1,128)}, u32[]{:S(2)}) copy-start(f32[1,512]{1,0:T(1,128)} %get-tuple-element.66) | copy-start | bytes 6148
  47.2 5.0 %copy-start.13 = (f32[1,512]{1,0:T(1,128)S(1)}, f32[1,512]{1,0:T(1,128)}, u32[]{:S(2)}) copy-start(f32[1,512]{1,0:T(1,128)} %get-tuple-element.67) | copy-start | bytes 6148
  47.2 29.5 %all-to-all-start = ((bf16[4,4,2,256,128]{4,3,2,1,0:T(8,128)(2,1)}), bf16[4,4,2,256,128]{4,3,2,1,0:T(8,128)(2,1)S(1)}, u32[]{:S(2)}, u32[]{:S(2)}) async-start(bf16[4,4,2,256,128]{4,3,2,1,0:T(8,128)(2,1)} %broadcast_in_dim.131), calls=%async_computation | async-start | bytes 4194304 | tf_op jit(solution)/shard_map/all_to_all | solution.py:31
  52.8 24.0 %copy-start.3 = (s32[32]{0:T(128)S(1)}, s32[32]{0:T(128)}, u32[]{:S(2)}) copy-start(s32[32]{0:T(128)} %param.25) | copy-start | bytes 388
  53.0 25.2 %copy-start.7 = (s32[5,256]{1,0:T(8,128)S(1)}, s32[5,256]{1,0:T(8,128)}, u32[]{:S(2)}) copy-start(s32[5,256]{1,0:T(8,128)} %copy-done.6) | copy-start | bytes 15364
  53.0 25.2 %copy-start.10 = (s32[5,256]{1,0:T(8,128)S(1)}, s32[5,256]{1,0:T(8,128)}, u32[]{:S(2)}) copy-start(s32[5,256]{1,0:T(8,128)} %copy-done.9) | copy-start | bytes 15364
  54.0 13.8 %collective-permute-start.7 = (bf16[3,256,128]{2,1,0:T(8,128)(2,1)}, bf16[3,256,128]{2,1,0:T(8,128)(2,1)S(1)}, u32[]{:S(2)}, u32[]{:S(2)}) collective-permute-start(bf16[3,256,128]{2,1,0:T(8,128)(2,1)} %get-tuple-element.36), channel_id=1, source_target_pairs={{0,12},{1,76},{4,0},{5,64},{8,4},{9,68},{12,8},{13,72},{64,13},{65... | collective-permute-start | bytes 589832 | tf_op jit(solution)/shard_map/ppermute | solution.py:269
  55.9 15.8 %collective-permute-start.6 = (bf16[3,256,128]{2,1,0:T(8,128)(2,1)}, bf16[3,256,128]{2,1,0:T(8,128)(2,1)S(1)}, u32[]{:S(2)}, u32[]{:S(2)}) collective-permute-start(bf16[3,256,128]{2,1,0:T(8,128)(2,1)} %get-tuple-element.37), channel_id=1, source_target_pairs={{0,8},{1,72},{4,12},{5,76},{8,0},{9,64},{12,4},{13,68},{64,9},{65,... | collective-permute-start | bytes 589832 | tf_op jit(solution)/shard_map/ppermute | solution.py:269
  57.1 19.6 %collective-permute-start.5 = (bf16[3,256,128]{2,1,0:T(8,128)(2,1)S(1)}, bf16[3,256,128]{2,1,0:T(8,128)(2,1)S(1)}, u32[]{:S(2)}, u32[]{:S(2)}) collective-permute-start(bf16[3,256,128]{2,1,0:T(8,128)(2,1)S(1)} %get-tuple-element.38), channel_id=1, source_target_pairs={{0,4},{1,68},{4,8},{5,72},{8,12},{9,76},{12,0},{13,64},{64,5},{65,... | collective-permute-start | bytes 589832 | tf_op jit(solution)/shard_map/ppermute | solution.py:269
  57.1 19.6 %collective-permute-start.4 = (bf16[3,256,128]{2,1,0:T(8,128)(2,1)S(1)}, bf16[3,256,128]{2,1,0:T(8,128)(2,1)S(1)}, u32[]{:S(2)}, u32[]{:S(2)}) collective-permute-start(bf16[3,256,128]{2,1,0:T(8,128)(2,1)S(1)} %get-tuple-element.39), channel_id=1, source_target_pairs={{0,0},{1,64},{4,4},{5,68},{8,8},{9,72},{12,12},{13,76},{64,1},{65,... | collective-permute-start | bytes 589832 | tf_op jit(solution)/shard_map/ppermute | solution.py:269
  76.7 4.3 %collective-permute-start.8 = (bf16[16,2,256,128]{3,2,1,0:T(8,128)(2,1)S(1)}, bf16[16,2,256,128]{3,2,1,0:T(8,128)(2,1)}, u32[]{:S(2)}, u32[]{:S(2)}) collective-permute-start(bf16[16,2,256,128]{3,2,1,0:T(8,128)(2,1)S(1)} %bitcast.120), channel_id=1, source_target_pairs={{0,1},{1,0},{2,3},{3,2},{4,5},{5,4},{6,7},{7,6},{8,9},{9,8},{10,11... | collective-permute-start | bytes 6291464 | tf_op jit(solution)/shard_map/ppermute | solution.py:23
  101.9 6.0 %collective-permute-start.9 = (bf16[256,128]{1,0:T(8,128)(2,1)S(1)}, bf16[256,128]{1,0:T(8,128)(2,1)S(1)}, u32[]{:S(2)}, u32[]{:S(2)}) collective-permute-start(bf16[256,128]{1,0:T(8,128)(2,1)S(1)} %get-tuple-element.44), channel_id=1, source_target_pairs={{0,0},{1,64},{4,4},{5,68},{8,8},{9,72},{12,12},{13,76},{64,1},{65,... | collective-permute-start | bytes 196616 | tf_op jit(solution)/shard_map/ppermute | solution.py:354
  102.6 5.5 %collective-permute-start.12 = (bf16[256,128]{1,0:T(8,128)(2,1)S(1)}, bf16[256,128]{1,0:T(8,128)(2,1)S(1)}, u32[]{:S(2)}, u32[]{:S(2)}) collective-permute-start(bf16[256,128]{1,0:T(8,128)(2,1)S(1)} %get-tuple-element.45), channel_id=1, source_target_pairs={{0,4},{1,68},{4,8},{5,72},{8,12},{9,76},{12,0},{13,64},{64,5},{65,... | collective-permute-start | bytes 196616 | tf_op jit(solution)/shard_map/ppermute | solution.py:354
  105.1 5.8 %collective-permute-start.11 = (bf16[256,128]{1,0:T(8,128)(2,1)S(1)}, bf16[256,128]{1,0:T(8,128)(2,1)S(1)}, u32[]{:S(2)}, u32[]{:S(2)}) collective-permute-start(bf16[256,128]{1,0:T(8,128)(2,1)S(1)} %get-tuple-element.46), channel_id=1, source_target_pairs={{0,8},{1,72},{4,12},{5,76},{8,0},{9,64},{12,4},{13,68},{64,9},{65,... | collective-permute-start | bytes 196616 | tf_op jit(solution)/shard_map/ppermute | solution.py:354
  106.0 4.9 %collective-permute-start.10 = (bf16[256,128]{1,0:T(8,128)(2,1)S(1)}, bf16[256,128]{1,0:T(8,128)(2,1)S(1)}, u32[]{:S(2)}, u32[]{:S(2)}) collective-permute-start(bf16[256,128]{1,0:T(8,128)(2,1)S(1)} %get-tuple-element.47), channel_id=1, source_target_pairs={{0,12},{1,76},{4,0},{5,64},{8,4},{9,68},{12,8},{13,72},{64,13},{65... | collective-permute-start | bytes 196616 | tf_op jit(solution)/shard_map/ppermute | solution.py:354
  113.7 10.4 %copy-start.11 = (f32[2,2048]{1,0:T(2,128)S(1)}, f32[2,2048]{1,0:T(2,128)}, u32[]{:S(2)}) copy-start(f32[2,2048]{1,0:T(2,128)} %param.20) | copy-start | bytes 49156
  113.8 9.4 %collective-permute-start.13 = (bf16[2,64,2048]{2,1,0:T(8,128)(2,1)S(1)}, bf16[2,64,2048]{2,1,0:T(8,128)(2,1)S(1)}, u32[]{:S(2)}, u32[]{:S(2)}) collective-permute-start(bf16[2,64,2048]{2,1,0:T(8,128)(2,1)S(1)} %fusion.5), channel_id=1, source_target_pairs={{0,1},{1,0},{2,3},{3,2},{4,5},{5,4},{6,7},{7,6},{8,9},{9,8},{10,11... | collective-permute-start | bytes 1572872 | tf_op jit(solution)/shard_map/ppermute | solution.py:23
  123.3 8.7 %collective-permute-start.14 = (bf16[64,2048]{1,0:T(8,128)(2,1)S(1)}, bf16[64,2048]{1,0:T(8,128)(2,1)S(1)}, u32[]{:S(2)}, u32[]{:S(2)}) collective-permute-start(bf16[64,2048]{1,0:T(8,128)(2,1)S(1)} %fusion.10), channel_id=1, source_target_pairs={{0,2},{2,0},{1,3},{3,1},{4,6},{6,4},{5,7},{7,5},{8,10},{10,8},{9,1... | collective-permute-start | bytes 786440 | tf_op jit(solution)/shard_map/ppermute | solution.py:23
  134.9 34.4 %all-to-all-start.1 = ((bf16[8,64,2048]{2,1,0:T(8,128)(2,1)}), bf16[8,64,2048]{2,1,0:T(8,128)(2,1)}, u32[]{:S(2)}, u32[]{:S(2)}) async-start(bf16[8,64,2048]{2,1,0:T(8,128)(2,1)} %broadcast_in_dim.138), calls=%async_computation.1 | async-start | bytes 4194304 | tf_op jit(solution)/shard_map/all_to_all | solution.py:31
  145.1 29.8 %collective-permute-start.15 = (bf16[2,2048,256]{2,1,0:T(8,128)(2,1)S(1)}, bf16[2,2048,256]{2,1,0:T(8,128)(2,1)}, u32[]{:S(2)}, u32[]{:S(2)}) collective-permute-start(bf16[2,2048,256]{2,1,0:T(8,128)(2,1)S(1)} %get-tuple-element.30), channel_id=1, source_target_pairs={{0,1},{1,0},{2,3},{3,2},{4,5},{5,4},{6,7},{7,6},{8,9},{9,8},{10,11... | collective-permute-start | bytes 6291464 | tf_op jit(solution)/shard_map/ppermute | solution.py:23
  169.3 5.7 %collective-permute-start.17 = (bf16[512,2048]{1,0:T(8,128)(2,1)}, bf16[512,2048]{1,0:T(8,128)(2,1)S(1)}, u32[]{:S(2)}, u32[]{:S(2)}) collective-permute-start(bf16[512,2048]{1,0:T(8,128)(2,1)} %bitcast.83.tokens_ref), channel_id=1, source_target_pairs={{0,1},{1,0},{2,3},{3,2},{4,5},{5,4},{6,7},{7,6},{8,9},{9,8},{10,11... | collective-permute-start | bytes 6291464 | tf_op jit(solution)/shard_map/ppermute | solution.py:23
  171.1 3.9 %collective-permute-start.16 = (bf16[2,128,2048]{2,1,0:T(8,128)(2,1)S(1)}, bf16[2,128,2048]{2,1,0:T(8,128)(2,1)S(1)}, u32[]{:S(2)}, u32[]{:S(2)}) collective-permute-start(bf16[2,128,2048]{2,1,0:T(8,128)(2,1)S(1)} %get-tuple-element.32), channel_id=1, source_target_pairs={{0,1},{1,0},{2,3},{3,2},{4,5},{5,4},{6,7},{7,6},{8,9},{9,8},{10,11... | collective-permute-start | bytes 3145736 | tf_op jit(solution)/shard_map/ppermute | solution.py:23
  174.9 1.3 copy-start.19
  184.3 8.3 %collective-permute-start.18 = (bf16[512,2048]{1,0:T(8,128)(2,1)S(1)}, bf16[512,2048]{1,0:T(8,128)(2,1)S(1)}, u32[]{:S(2)}, u32[]{:S(2)}) collective-permute-start(bf16[512,2048]{1,0:T(8,128)(2,1)S(1)} %shard_map.138), channel_id=1, source_target_pairs={{0,1},{1,0},{2,3},{3,2},{4,5},{5,4},{6,7},{7,6},{8,9},{9,8},{10,11... | collective-permute-start | bytes 6291464 | tf_op jit(solution)/shard_map/ppermute | solution.py:23
  193.5 34.0 %copy-start.1 = (bf16[2,2048,256]{2,1,0:T(8,128)(2,1)S(1)}, bf16[2,2048,256]{2,1,0:T(8,128)(2,1)}, u32[]{:S(2)}) copy-start(bf16[2,2048,256]{2,1,0:T(8,128)(2,1)} %param.21) | copy-start | bytes 6291460
Sparse Core Ops, SparseCore 0:
  9.0 34.7 all-gather.5
  45.5 55.9 all-gather.3

commit v4 on v3

--- a/solution.py
+++ b/solution.py
@@ -68,8 +68,8 @@
 ):
     out_ref, qkv_ref, k_all, v_all, held, sems, qkv_sems = rest[-7:]
     qkv_parts = rest[:4]
-    info_ref, seg_ref = rest[4:6]
-    parts = rest[6:-7]
+    info_ref, seg_ref, factor_ref, key_factor_ref = rest[4:8]
+    parts = rest[8:-7]
     step = pl.program_id(0)
     group = step // 2
     tile = step % 2
@@ -98,7 +98,6 @@
         for copy in copies():
             copy.wait()
 
-    scale = HD**-0.5 * LOG2E
     nt = (((1,), (1,)), ((), ()))
     count = counts_ref[group, tile]
 
@@ -112,7 +111,9 @@
         row_at = lax.broadcasted_iota(jnp.int32, (half_rows, seen), 0) + first
         col_at = lax.broadcasted_iota(jnp.int32, (half_rows, seen), 1)
         key_at = lax.broadcasted_iota(jnp.int32, (1, node_rows), 1)
-        near = lax.dot_general(q, qkv_ref[group, 1, :seen, :], nt, preferred_element_type=F32) * scale
+        scale = factor_ref[0, first:seen, 0:1] * (HD**-0.5 * LOG2E)
+        near = lax.dot_general(q, qkv_ref[group, 1, :seen, :], nt, preferred_element_type=F32)
+        near = near * scale * key_factor_ref[0][:, :seen]
         near = jnp.where((seg_col == seg_row) & (col_at <= row_at), near, NEG)
         top = jnp.max(near, axis=1, keepdims=True)
 
@@ -156,7 +157,9 @@
             work(t * half_rows)
 
 
-def attention(nodes, lengths, lists, counts, qkv_parts, row_info, seg_row, parts):
+def attention(
+    nodes, lengths, lists, counts, qkv_parts, row_info, seg_row, factors, key_factors, parts
+):
     rows = qkv_parts[0].shape[1]
     groups = len(qkv_parts)
     per_part, _, node_rows, _ = parts[0].shape
@@ -170,11 +173,11 @@
             num_scalar_prefetch=4,
             grid=(groups * 2,),
             in_specs=[pl.BlockSpec(memory_space=pl.ANY)] * groups
-            + [one((rows, 3)), one((1, rows))]
+            + [one((rows, 3)), one((1, rows)), one((rows, 2)), one((1, rows))]
             + [pl.BlockSpec(memory_space=pl.ANY)] * len(parts),
             out_specs=pl.BlockSpec((1, rows // 2, HD), lambda i, *_: (i // 2, i % 2, 0)),
             scratch_shapes=[
-                pltpu.VMEM((groups, 3, rows, HD), BF),
+                pltpu.VMEM((groups, 4, rows, HD), BF),
                 pltpu.VMEM((slots, node_rows, HD), BF),
                 pltpu.VMEM((slots, node_rows, HD), BF),
                 pltpu.VMEM((lists.shape[2] // batch, rows // 2, batch * node_rows), F32),
@@ -186,45 +189,35 @@
         cost_estimate=pl.CostEstimate(
             flops=2 * 10**9, transcendentals=4 * 10**6, bytes_accessed=6 * 10**6
         ),
-    )(nodes, lengths, lists, counts, *qkv_parts, row_info, seg_row, *parts)
-
-
-def feed_forward_body(core_ref, tokens_ref, gu_own, gu_got, dn_own, dn_got, out_ref):
+    )(nodes, lengths, lists, counts, *qkv_parts, row_info, seg_row, factors, key_factors, *parts)
+
+
+def feed_forward_body(tokens_ref, gu_a, dn_a, gu_b, dn_b, out_ref):
     rows = 256
-    first = core_ref[0] == 0
-    cut = dn_own.shape[1]
 
     def one(i, carry):
         at = pl.ds(i * rows, rows)
         tokens = tokens_ref[at, :]
         part = 0.0
-        for share in range(gu_own.shape[0]):
-            one_side = jnp.dot(tokens, gu_own[share], preferred_element_type=F32)
-            other_side = jnp.dot(tokens, gu_got[share], preferred_element_type=F32)
-            gate = jnp.where(first, one_side, other_side)
-            up = jnp.where(first, other_side, one_side)
-            hidden = gate / (1.0 + jnp.exp(-gate)) * up
-            low, high = hidden[:, :cut], hidden[:, cut:]
-            part = part + jnp.dot(
-                jnp.where(first, low, high).astype(BF), dn_own[share], preferred_element_type=F32
-            )
-            part = part + jnp.dot(
-                jnp.where(first, high, low).astype(BF), dn_got[share], preferred_element_type=F32
-            )
+        for gu_ref, dn_ref in ((gu_a, dn_a), (gu_b, dn_b)):
+            gate = jnp.dot(tokens, gu_ref[0], preferred_element_type=F32)
+            up = jnp.dot(tokens, gu_ref[1], preferred_element_type=F32)
+            hidden = (gate / (1.0 + jnp.exp(-gate)) * up).astype(BF)
+            part = part + jnp.dot(hidden, dn_ref[...], preferred_element_type=F32)
         out_ref[at, :] = part.astype(BF)
         return carry
 
     lax.fori_loop(0, tokens_ref.shape[0] // rows, one, 0)
 
 
-def feed_forward(core, tokens, weights):
+def feed_forward(tokens, weights):
     rows, width = tokens.shape
-    units = weights[0].shape[2] * 2
+    units = weights[1].shape[0] * 2
     space = pl.BlockSpec(memory_space=pltpu.VMEM)
     return pl.pallas_call(
         feed_forward_body,
         out_shape=jax.ShapeDtypeStruct((rows, width), BF),
-        in_specs=[pl.BlockSpec(memory_space=pltpu.SMEM)] + [space] * 5,
+        in_specs=[space] * 5,
         out_specs=space,
         compiler_params=pltpu.CompilerParams(vmem_limit_bytes=48 << 20),
         cost_estimate=pl.CostEstimate(
@@ -232,7 +225,7 @@
             transcendentals=rows * units,
             bytes_accessed=(2 * rows * width + 3 * width * units) * 2,
         ),
-    )(core, tokens, *weights)
+    )(tokens, *weights)
 
 
 def on_device(
@@ -284,14 +277,8 @@
 
     w_out = lax.dynamic_slice_in_dim(jnp.concatenate([w_out, w_out]), z_at * HD, w_out.shape[0], 0)
 
-    half_units = w_down.shape[0] // 2
-    gu_ring = lax.all_gather(select_row(w_gate_up, core), "z")
-    dn_ring = lax.all_gather(
-        lax.dynamic_slice_in_dim(w_down, core * half_units, half_units, 0), "z"
-    )
-
     qkv_raw = jnp.einsum("td,cdw->ctw", states_in, w_qkv, preferred_element_type=F32)
-    squares = lax.psum(jnp.sum(qkv_raw[:2] * qkv_raw[:2], axis=2), HEAD)
+    squares = jnp.sum(qkv_raw[:2] * qkv_raw[:2], axis=2)
     cached_own = spread(cached, "x").reshape((n_x * n_z,) + cached.shape[1:])
     group_from = jnp.stack(
         [blk] + [(core * n_x + x_at) * n_z + (z_at - g) % n_z for g in range(n_z)]
@@ -306,20 +293,46 @@
     angles = position.astype(F32)[:, None] * frequency[None, :]
     cosine, sine = jnp.cos(angles)[:, None, :], jnp.sin(angles)[:, None, :]
 
-    def normed(c):
-        scaled = qkv_raw[c] * lax.rsqrt(squares[c] / columns + EPS)[:, None] * qk_gain[c]
-        scaled = scaled.reshape(rows, heads_here, HD)
+    def turned(c):
+        scaled = (qkv_raw[c] * qk_gain[c]).reshape(rows, heads_here, HD)
         low, high = scaled[..., :half], scaled[..., half:]
-        turned = jnp.concatenate([low * cosine - high * sine, high * cosine + low * sine], axis=-1)
-        return turned.astype(BF)
-
+        both = jnp.concatenate([low * cosine - high * sine, high * cosine + low * sine], axis=-1)
+        return both.astype(BF)
+
+    terms = []
+    left = squares
+    for _ in range(3):
+        terms.append(lax.reduce_precision(left, 8, 7))
+        left = left - terms[-1]
+    terms = jnp.stack(terms).reshape(6, rows).astype(BF).T
+    terms = jnp.pad(terms, ((0, 0), (0, HD - 6)))
     qkv = jnp.stack(
-        [normed(0), normed(1), qkv_raw[2].astype(BF).reshape(rows, heads_here, HD)]
+        [
+            turned(0), turned(1), qkv_raw[2].astype(BF).reshape(rows, heads_here, HD),
+            jnp.broadcast_to(terms[:, None], (rows, heads_here, HD)),
+        ]
     ).transpose(2, 0, 1, 3)
     qkv_parts = [across(select_row(qkv, (z_at + s) % n_z), s) for s in range(n_z)]
-
-    cached_own, qkv_parts = lax.optimization_barrier((cached_own, qkv_parts))
+    terms = jnp.stack([part[3, :, :6] for part in qkv_parts]).astype(F32)
+    squares = jnp.sum(terms.reshape(n_z, rows, 3, 2), axis=2)
+    factors = lax.rsqrt(lax.psum(squares, ("yhi", "ylo")) / columns + EPS)
+    cached_own, factors = lax.optimization_barrier((cached_own, factors))
     cached_parts = [cached_own, shift(cached_own, "core", 1)]
+
+    def beside(weights):
+        return lax.ppermute(
+            weights, ("z", "core"),
+            [(z * 2 + c, (z + 1 - 2 * c) % n_z * 2 + c) for z in range(n_z) for c in range(2)],
+        )
+
+    def beyond(weights):
+        far = lax.ppermute(
+            weights, ("z", "core"), [(z * 2 + 1, (z + 2) % n_z * 2 + 1) for z in range(n_z)]
+        )
+        return jnp.where(core == 0, weights, far)
+
+    w_gate_up, w_down, factors = lax.optimization_barrier((w_gate_up, w_down, factors))
+    gu_a, dn_a = beside(w_gate_up), beside(w_down)
 
     slots = slot_from.shape[0]
     slot_nodes = jnp.take(slot_node, slot_from)
@@ -343,7 +356,7 @@
     row_info = jnp.stack([middle, root, segments], axis=-1)
     attended = attention(
         slot_nodes, slot_lengths, lists, counts, qkv_parts, row_info, segments[:, None, :],
-        cached_parts,
+        factors, factors[:, None, :, 1], cached_parts,
     )
 
     def back(values, s):
@@ -354,6 +367,10 @@
         return lax.ppermute(values, corner, pairs)
 
     attended = jnp.concatenate([back(attended[s], s) for s in range(n_z)], axis=1)
+    attended, gu_a, dn_a, w_gate_up, w_down = lax.optimization_barrier(
+        (attended, gu_a, dn_a, w_gate_up, w_down)
+    )
+    gu_b, dn_b = beyond(w_gate_up), beyond(w_down)
     attn_part = jnp.dot(attended, w_out, preferred_element_type=F32)
     attn_part = attn_part.reshape(2, 2, rows // 4, -1)
 
@@ -368,20 +385,12 @@
     state_rows = lax.dynamic_slice_in_dim(states_in, head_index * own_rows, own_rows, 0)
     mid_state = (state_rows.astype(F32) + rms_norm(attn_proj, post_gain[0])).astype(BF)
 
-    mid_state, gu_ring, dn_ring = lax.optimization_barrier((mid_state, gu_ring, dn_ring))
     plane = ("yhi", "x")
-
-    def shares(ring, c):
-        return lax.dynamic_slice_in_dim(ring, c * 2, 2, 0)
-
-    weights = []
-    for ring in (gu_ring, dn_ring):
-        weights += [shares(ring, core), shift(shares(ring, 1 - core), "core", 1)]
-    core_at = core.astype(jnp.int32).reshape(1)
+    weights = (gu_a, dn_a, gu_b, dn_b)
     tokens = spread(mid_state, plane)
     flat = tokens.reshape(-1, tokens.shape[2])
-    other = feed_forward(core_at, shift(flat, "core", 1), weights)
-    total = feed_forward(core_at, flat, weights).astype(F32) + shift(other, "core", 1).astype(F32)
+    other = feed_forward(shift(flat, "core", 1), weights)
+    total = feed_forward(flat, weights).astype(F32) + shift(other, "core", 1).astype(F32)
     total = lax.all_to_all(total.astype(BF).reshape(tokens.shape), plane, 0, 0, tiled=True)
     mlp_proj = jnp.sum(total.astype(F32), axis=0)
     return (mid_state.astype(F32) + rms_norm(mlp_proj, post_gain[1])).astype(BF)

time: 235 us -> 227 us (0.966)
  between operations: 14.2 us -> 0.75 us
  blocking collectives: 44.9 us -> 55.4 us
  starting transfers between devices: 38.2 us -> 45.7 us
  local copies, waits for them, and re-layouts: 21.8 us -> 15.2 us
  waiting for transfers between devices: 60 us -> 55.2 us
  Pallas kernels: 37 us -> 32.3 us
  other arithmetic: 10.9 us -> 14 us
    ppermute x8, waiting for transfers between devices: 18.8 us -> 7.78 us  [across(): return lax.ppermute(values, corner, pairs)]
    dynamic_slice x4 -> x0, local copies, waits for them, and re-layouts: 8.82 us -> none  [the longest x2 5.66 us: shares(): return lax.dynamic_slice_in_dim(ring, c * 2, 2, 0)]
    psum x1, blocking collectives: 12.3 us -> 20.1 us  [on_device(): factors = lax.rsqrt(lax.psum(squares, ('yhi', 'ylo')) / columns + EPS)]
    ppermute x4, waiting for transfers between devices: 3 us -> 10.1 us  [back(): return lax.ppermute(values, corner, pairs)]
    ppermute x0 -> x4, starting transfers between devices: none -> 4.8 us  [the longest x2 3.64 us: beyond(): lax.ppermute(weights, ('z', 'core'), [(z * 2 + 1, (z + 2) % n_z * 2 + 1)...]
    all_to_all x1, blocking collectives: 32.6 us -> 35.3 us  [on_device(): lax.all_to_all(total.astype(BF).reshape(tokens.shape), plane, 0, 0, tiled...]
    pallas_call x1, Pallas kernels: 20.9 us -> 18.4 us  [attention(): pl.pallas_call(attention_body, out_shape=jax.ShapeDtypeStruct((groups, ro...]
    ppermute x7 -> x5, starting transfers between devices: 9.41 us -> 11 us  [shift(): return lax.ppermute(values, axis, [(i, (i + by) % n) for i in range(n)])]
  transfers between devices with their start and end apart: 23 -> 23, of which waited for: 10 -> 8; matrix products, arithmetic and copies ran while one was open for 14% -> 9% of each run, Pallas kernels for 12% -> 11%
where the time goes in v4:
time: 227 us; the launch traced here: 226 us
  blocking collectives  55.4 us (24%)
  waiting for transfers between devices  55.2 us (24%)
  starting transfers between devices  45.7 us (20%)
  Pallas kernels  32.3 us (14%)
  local copies, waits for them, and re-layouts  15.2 us (7%)
  other arithmetic  14 us (6%)
  matrix products  7.47 us (3%)
    all_to_all x1, blocking collectives, on_device(): lax.all_to_all(total.astype(BF).reshape(tokens.shape), plane, 0, 0, tiled...  35.3 us
    all_to_all x2, waiting for transfers between devices, spread(): return lax.all_to_all(copies, axes, 0, 0, tiled=True)  24.4 us
    psum x1, blocking collectives, on_device(): factors = lax.rsqrt(lax.psum(squares, ('yhi', 'ylo')) / columns + EPS)  20.1 us
    pallas_call x1, Pallas kernels, attention(): pl.pallas_call(attention_body, out_shape=jax.ShapeDtypeStruct((groups, ro...  18.4 us
    pallas_call x2, Pallas kernels, feed_forward(): pl.pallas_call(feed_forward_body, out_shape=jax.ShapeDtypeStruct((rows, w...  13.9 us
    ppermute x5, waiting for transfers between devices, shift(): return lax.ppermute(values, axis, [(i, (i + by) % n) for i in range(n)])  13 us
    ppermute x8, starting transfers between devices, across(): return lax.ppermute(values, corner, pairs)  12.9 us
    ppermute x5, starting transfers between devices, shift(): return lax.ppermute(values, axis, [(i, (i + by) % n) for i in range(n)])  11 us
  transfers between devices with their start and end apart: 23, of which 8 were waited for; matrix products, arithmetic and copies ran while one was open for 9% of the time, Pallas kernels for 11%

profile of v4, /device:TPU:0, one launch (start us, length us, event | category | flops | bytes accessed | tf_op | source)
XLA Modules:
  0.0 226.2 jit_solution(10130089152992053330)
XLA Ops:
  0.0 1.2 constant_dynamic-slice_fusion.6
  1.2 4.0 %collective-permute-start.6 = (bf16[2,256,128]{2,1,0:T(8,128)(2,1)S(1)}, bf16[2,256,128]{2,1,0:T(8,128)(2,1)}, u32[]{:S(2)}, u32[]{:S(2)}) collective-permute-start(bf16[2,256,128]{2,1,0:T(8,128)(2,1)S(1)} %pad_maximum_fusion.5), channel_id=1, source_target_pairs={{0,8},{1,72},{4,12},{5,76},{8,0},{9,64},{12,4},{13,68},{64,9},{65,... | collective-permute-start | bytes 393224 | tf_op jit(solution)/shard_map/ppermute | solution.py:262
  5.9 0.7 collective-permute-start.7
  7.3 1.3 collective-permute-start.5
  9.3 2.2 collective-permute-start.4
  11.5 4.6 %convolution_bitcast_fusion = f32[3,256,512]{1,2,0:T(8,128)S(1)} fusion(bf16[3,2048,512]{2,1,0:T(8,128)(2,1)} %param.17, bf16[256,2048]{1,0:T(8,128)(2,1)S(1)} %copy-done.13), kind=kOutput, calls=%fused_computation.11 | convolution fusion | flops 1610612736 | bytes 8912896 | tf_op jit(solution)/shard_map/td,cdw->ctw/dot_general | solution.py:280
  18.4 1.0 copy.65
  19.4 1.0 copy.66
  21.2 1.2 multiply_cosine_fusion
  22.4 1.2 pad_maximum_fusion.1
  23.6 1.9 broadcast_in_dim.136
  25.5 4.4 %all-to-all-start = ((bf16[4,4,2,256,128]{4,3,2,1,0:T(8,128)(2,1)}), bf16[4,4,2,256,128]{4,3,2,1,0:T(8,128)(2,1)S(1)}, u32[]{:S(2)}, u32[]{:S(2)}) async-start(bf16[4,4,2,256,128]{4,3,2,1,0:T(8,128)(2,1)} %broadcast_in_dim.136), calls=%async_computation | async-start | bytes 4194304 | tf_op jit(solution)/shard_map/all_to_all | solution.py:31
  29.9 1.3 broadcast_multiply_fusion
  32.1 1.0 dynamic-slice_bitcast_fusion
  33.1 1.9 collective-permute-start.3
  35.1 1.2 collective-permute-start.2
  36.2 1.6 collective-permute-start
  38.0 4.2 %collective-permute-done.3.rest_3_ = bf16[4,256,128]{2,1,0:T(8,128)(2,1)S(1)} collective-permute-done((bf16[4,256,128]{2,1,0:T(8,128)(2,1)}, bf16[4,256,128]{2,1,0:T(8,128)(2,1)S(1)}, u32[]{:S(2)}, u32[]{:S(2)}) %collective-permute-start.3) | collective-permute-done | bytes 262176 | tf_op jit(solution)/shard_map/ppermute | solution.py:262
  42.2 1.0 collective-permute-done.2.rest_2_
  43.4 2.6 %collective-permute-done.1.rest_1_ = bf16[4,256,128]{2,1,0:T(8,128)(2,1)S(1)} collective-permute-done((bf16[4,256,128]{2,1,0:T(8,128)(2,1)}, bf16[4,256,128]{2,1,0:T(8,128)(2,1)S(1)}, u32[]{:S(2)}, u32[]{:S(2)}) %collective-permute-start.1) | collective-permute-done | bytes 262176 | tf_op jit(solution)/shard_map/ppermute | solution.py:262
  46.3 20.1 %psum.7 = f32[4,256,2]{1,2,0:T(2,128)S(1)} all-reduce(f32[4,256,2]{1,2,0:T(2,128)S(1)} %convert_reduce_fusion.2), channel_id=1, replica_groups=mesh['yhi'=2,'x'=4,'z'=4,'ylo'=2,'core'=2] {'yhi','ylo'}, use_global_device_ids=true, to_apply=%region_13.15 | all-reduce | flops 2048 | bytes 16384 | tf_op jit(solution)/shard_map/psum | solution.py:318
  66.5 0.7 gather_fusion.2
  67.3 0.7 gather_fusion.3
  71.0 0.9 copy-done.2
  71.9 0.9 copy-done.4
  72.8 0.9 copy-done.6
  73.8 18.4 %shard_map.136 = bf16[4,256,128]{2,1,0:T(8,128)(2,1)S(1)} custom-call(s32[32]{0:T(128)S(1)} %get-tuple-element.33.nodes_ref, s32[32]{0:T(128)S(1)} %and_select_fusion.lengths_ref, s32[4,2,12]{2,1,0:T(2,128)S(1)} %copy.75.lists_ref, s32[4,2]{1,0:T(4,128)S(1)} %copy.76.counts_ref, bf16[4,256,128]{2,1,0:T(8,128)(2,1)S(1)} %copy-done.6, ...), custom_call_target="tpu_custom_call" | custom-call | flops 2000000000 | bytes 6000000 | tf_op jit(solution)/shard_map/pallas_call | solution.py:169
  92.9 1.5 collective-permute-start.12
  94.4 2.9 %collective-permute-start.11 = (bf16[256,128]{1,0:T(8,128)(2,1)S(1)}, bf16[256,128]{1,0:T(8,128)(2,1)S(1)}, u32[]{:S(2)}, u32[]{:S(2)}) collective-permute-start(bf16[256,128]{1,0:T(8,128)(2,1)S(1)} %get-tuple-element.46), channel_id=1, source_target_pairs={{0,8},{1,72},{4,12},{5,76},{8,0},{9,64},{12,4},{13,68},{64,9},{65,... | collective-permute-start | bytes 196616 | tf_op jit(solution)/shard_map/ppermute | solution.py:367
  97.2 2.2 collective-permute-start.10
  99.5 10.1 %collective-permute-done.12 = bf16[256,128]{1,0:T(8,128)(2,1)S(1)} collective-permute-done((bf16[256,128]{1,0:T(8,128)(2,1)S(1)}, bf16[256,128]{1,0:T(8,128)(2,1)S(1)}, u32[]{:S(2)}, u32[]{:S(2)}) %collective-permute-start.12) | collective-permute-done | bytes 65568 | tf_op jit(solution)/shard_map/ppermute | solution.py:367
  109.6 2.8 %fusion.1 = f32[256,2048]{1,0:T(8,128)S(1)} fusion(bf16[256,512]{1,0:T(8,128)(2,1)S(1)} %pad_maximum_fusion.2, s32[]{:T(128)S(6)} %select_n.293, bf16[512,2048]{1,0:T(8,128)(2,1)} %param.19), kind=kOutput, calls=%fused_computation.9 | convolution fusion | flops 541065216 | bytes 4456452 | tf_op jit(solution)/shard_map/dot_general | solution.py:374
  112.6 1.9 collective-permute-done.15
  114.8 8.3 %collective-permute-done.16 = bf16[64,2048]{1,0:T(8,128)(2,1)S(1)} collective-permute-done((bf16[64,2048]{1,0:T(8,128)(2,1)S(1)}, bf16[64,2048]{1,0:T(8,128)(2,1)S(1)}, u32[]{:S(2)}, u32[]{:S(2)}) %collective-permute-start.16) | collective-permute-done | bytes 262176 | tf_op jit(solution)/shard_map/ppermute | solution.py:23
  123.3 1.1 add_convert_fusion.2
  124.4 1.6 broadcast_in_dim.137
  126.0 5.4 %all-to-all-start.1 = ((bf16[8,64,2048]{2,1,0:T(8,128)(2,1)}), bf16[8,64,2048]{2,1,0:T(8,128)(2,1)}, u32[]{:S(2)}, u32[]{:S(2)}) async-start(bf16[8,64,2048]{2,1,0:T(8,128)(2,1)} %broadcast_in_dim.137), calls=%async_computation.1 | async-start | bytes 4194304 | tf_op jit(solution)/shard_map/all_to_all | solution.py:31
  131.4 2.0 collective-permute-start.17
  133.4 1.7 collective-permute-start.18
  135.1 24.4 %all-to-all-done.1 = bf16[8,64,2048]{2,1,0:T(8,128)(2,1)} async-done(((bf16[8,64,2048]{2,1,0:T(8,128)(2,1)}), bf16[8,64,2048]{2,1,0:T(8,128)(2,1)}, u32[]{:S(2)}, u32[]{:S(2)}) %all-to-all-start.1) | async-done | bytes 2097184 | tf_op jit(solution)/shard_map/all_to_all | solution.py:31
  159.6 1.6 broadcast_select_fusion.gu_b
  161.2 2.8 %collective-permute-done.19.tokens_ref = bf16[512,2048]{1,0:T(8,128)(2,1)} collective-permute-done((bf16[512,2048]{1,0:T(8,128)(2,1)}, bf16[512,2048]{1,0:T(8,128)(2,1)}, u32[]{:S(2)}, u32[]{:S(2)}) %collective-permute-start.19) | collective-permute-done | bytes 2097184 | tf_op jit(solution)/shard_map/ppermute | solution.py:23
  163.9 7.0 %shard_map.138 = bf16[512,2048]{1,0:T(8,128)(2,1)S(1)} custom-call(bf16[512,2048]{1,0:T(8,128)(2,1)} %collective-permute-done.19.tokens_ref, bf16[2,2048,256]{2,1,0:T(8,128)(2,1)} %collective-permute-done.13.gu_a, bf16[256,2048]{1,0:T(8,128)(2,1)} %collective-permute-done.14.dn_a, bf16[2,2048,256]{2,1,0:T(8,128)(2,1)} %broadcast_select_fusion.gu_b, ...), custom_call_target="tpu_custom_call" | custom-call | flops 3221225472 | bytes 10485760 | tf_op jit(solution)/shard_map/pallas_call | solution.py:217
  170.9 10.7 %collective-permute-start.20 = (bf16[512,2048]{1,0:T(8,128)(2,1)S(1)}, bf16[512,2048]{1,0:T(8,128)(2,1)S(1)}, u32[]{:S(2)}, u32[]{:S(2)}) collective-permute-start(bf16[512,2048]{1,0:T(8,128)(2,1)S(1)} %shard_map.138), channel_id=1, source_target_pairs={{0,1},{1,0},{2,3},{3,2},{4,5},{5,4},{6,7},{7,6},{8,9},{9,8},{10,11... | collective-permute-start | bytes 6291464 | tf_op jit(solution)/shard_map/ppermute | solution.py:23
  181.7 7.0 %shard_map.137 = bf16[512,2048]{1,0:T(8,128)(2,1)S(1)} custom-call(bf16[512,2048]{1,0:T(8,128)(2,1)} %bitcast.82.tokens_ref, bf16[2,2048,256]{2,1,0:T(8,128)(2,1)} %collective-permute-done.13.gu_a, bf16[256,2048]{1,0:T(8,128)(2,1)} %collective-permute-done.14.dn_a, bf16[2,2048,256]{2,1,0:T(8,128)(2,1)} %broadcast_select_fusion.gu_b, ...), custom_call_target="tpu_custom_call" | custom-call | flops 3221225472 | bytes 10485760 | tf_op jit(solution)/shard_map/pallas_call | solution.py:217
  188.6 0.9 add_convert_fusion
  189.5 35.3 %all_to_all.15 = bf16[8,64,2048]{2,1,0:T(8,128)(2,1)S(1)} all-to-all(bf16[8,64,2048]{2,1,0:T(8,128)(2,1)S(1)} %bitcast.137), channel_id=1, replica_groups=mesh['yhi'=2,'x'=4,'z'=4,'ylo'=2,'core'=2] {'yhi','x'}, dimensions={0} | all-to-all | bytes 4194304 | tf_op jit(solution)/shard_map/all_to_all | solution.py:394
  225.4 0.9 add_convert_fusion.1
  (142 shorter events, 11.3 us)
Async XLA Ops:
  0.0 16.7 %copy-start = (s32[32,256]{1,0:T(8,128)S(1)}, s32[32,256]{1,0:T(8,128)}, u32[]{:S(2)}) copy-start(s32[32,256]{1,0:T(8,128)} %param.28) | copy-start | bytes 98308
  0.0 11.5 %copy-start.13 = (bf16[256,2048]{1,0:T(8,128)(2,1)S(1)}, bf16[256,2048]{1,0:T(8,128)(2,1)}, u32[]{:S(2)}) copy-start(bf16[256,2048]{1,0:T(8,128)(2,1)} %param.16) | copy-start | bytes 3145732
  1.2 21.2 %collective-permute-start.6 = (bf16[2,256,128]{2,1,0:T(8,128)(2,1)S(1)}, bf16[2,256,128]{2,1,0:T(8,128)(2,1)}, u32[]{:S(2)}, u32[]{:S(2)}) collective-permute-start(bf16[2,256,128]{2,1,0:T(8,128)(2,1)S(1)} %pad_maximum_fusion.5), channel_id=1, source_target_pairs={{0,8},{1,72},{4,12},{5,76},{8,0},{9,64},{12,4},{13,68},{64,9},{65,... | collective-permute-start | bytes 393224 | tf_op jit(solution)/shard_map/ppermute | solution.py:262
  5.9 16.5 %collective-permute-start.7 = (bf16[2,256,128]{2,1,0:T(8,128)(2,1)}, bf16[2,256,128]{2,1,0:T(8,128)(2,1)}, u32[]{:S(2)}, u32[]{:S(2)}) collective-permute-start(bf16[2,256,128]{2,1,0:T(8,128)(2,1)} %pad_maximum_fusion.6), channel_id=1, source_target_pairs={{0,12},{1,76},{4,0},{5,64},{8,4},{9,68},{12,8},{13,72},{64,13},{65... | collective-permute-start | bytes 393224 | tf_op jit(solution)/shard_map/ppermute | solution.py:262
  7.3 15.1 %collective-permute-start.5 = (bf16[2,256,128]{2,1,0:T(8,128)(2,1)}, bf16[2,256,128]{2,1,0:T(8,128)(2,1)}, u32[]{:S(2)}, u32[]{:S(2)}) collective-permute-start(bf16[2,256,128]{2,1,0:T(8,128)(2,1)} %pad_maximum_fusion.4), channel_id=1, source_target_pairs={{0,4},{1,68},{4,8},{5,72},{8,12},{9,76},{12,0},{13,64},{64,5},{65,... | collective-permute-start | bytes 393224 | tf_op jit(solution)/shard_map/ppermute | solution.py:262
  9.3 13.1 %collective-permute-start.4 = (bf16[2,256,128]{2,1,0:T(8,128)(2,1)}, bf16[2,256,128]{2,1,0:T(8,128)(2,1)}, u32[]{:S(2)}, u32[]{:S(2)}) collective-permute-start(bf16[2,256,128]{2,1,0:T(8,128)(2,1)} %pad_maximum_fusion.3), channel_id=1, source_target_pairs={{0,0},{1,64},{4,4},{5,68},{8,8},{9,72},{12,12},{13,76},{64,1},{65,... | collective-permute-start | bytes 393224 | tf_op jit(solution)/shard_map/ppermute | solution.py:262
  16.2 1.3 copy-start.15
  16.3 4.6 %copy-start.17 = (s32[28]{0:T(128)S(1)}, s32[28]{0:T(128)}, u32[]{:S(2)}) copy-start(s32[28]{0:T(128)} %param.27) | copy-start | bytes 340
  16.3 4.7 %copy-start.7 = (s32[32]{0:T(128)S(1)}, s32[32]{0:T(128)}, u32[]{:S(2)}) copy-start(s32[32]{0:T(128)} %param.26) | copy-start | bytes 388
  25.5 4.4 %copy-start.16 = (f32[2,512]{1,0:T(2,128)S(1)}, f32[2,512]{1,0:T(2,128)}, u32[]{:S(2)}) copy-start(f32[2,512]{1,0:T(2,128)} %param.18) | copy-start | bytes 12292
  25.5 40.9 %all-to-all-start = ((bf16[4,4,2,256,128]{4,3,2,1,0:T(8,128)(2,1)}), bf16[4,4,2,256,128]{4,3,2,1,0:T(8,128)(2,1)S(1)}, u32[]{:S(2)}, u32[]{:S(2)}) async-start(bf16[4,4,2,256,128]{4,3,2,1,0:T(8,128)(2,1)} %broadcast_in_dim.136), calls=%async_computation | async-start | bytes 4194304 | tf_op jit(solution)/shard_map/all_to_all | solution.py:31
  29.9 1.4 copy-start.11
  29.9 1.4 copy-start.12
  32.1 34.4 %copy-start.8 = (s32[32]{0:T(128)S(1)}, s32[32]{0:T(128)}, u32[]{:S(2)}) copy-start(s32[32]{0:T(128)} %param.25) | copy-start | bytes 388
  33.1 9.0 %collective-permute-start.3 = (bf16[4,256,128]{2,1,0:T(8,128)(2,1)}, bf16[4,256,128]{2,1,0:T(8,128)(2,1)S(1)}, u32[]{:S(2)}, u32[]{:S(2)}) collective-permute-start(bf16[4,256,128]{2,1,0:T(8,128)(2,1)} %get-tuple-element.36), channel_id=1, source_target_pairs={{0,12},{1,76},{4,0},{5,64},{8,4},{9,68},{12,8},{13,72},{64,13},{65... | collective-permute-start | bytes 786440 | tf_op jit(solution)/shard_map/ppermute | solution.py:262
  35.1 8.2 %collective-permute-start.2 = (bf16[4,256,128]{2,1,0:T(8,128)(2,1)}, bf16[4,256,128]{2,1,0:T(8,128)(2,1)S(1)}, u32[]{:S(2)}, u32[]{:S(2)}) collective-permute-start(bf16[4,256,128]{2,1,0:T(8,128)(2,1)} %get-tuple-element.37), channel_id=1, source_target_pairs={{0,8},{1,72},{4,12},{5,76},{8,0},{9,64},{12,4},{13,68},{64,9},{65,... | collective-permute-start | bytes 786440 | tf_op jit(solution)/shard_map/ppermute | solution.py:262
  36.2 9.7 %collective-permute-start.1 = (bf16[4,256,128]{2,1,0:T(8,128)(2,1)}, bf16[4,256,128]{2,1,0:T(8,128)(2,1)S(1)}, u32[]{:S(2)}, u32[]{:S(2)}) collective-permute-start(bf16[4,256,128]{2,1,0:T(8,128)(2,1)} %get-tuple-element.38), channel_id=1, source_target_pairs={{0,4},{1,68},{4,8},{5,72},{8,12},{9,76},{12,0},{13,64},{64,5},{65,... | collective-permute-start | bytes 786440 | tf_op jit(solution)/shard_map/ppermute | solution.py:262
  36.2 9.9 %collective-permute-start = (bf16[4,256,128]{2,1,0:T(8,128)(2,1)}, bf16[4,256,128]{2,1,0:T(8,128)(2,1)S(1)}, u32[]{:S(2)}, u32[]{:S(2)}) collective-permute-start(bf16[4,256,128]{2,1,0:T(8,128)(2,1)} %get-tuple-element.39), channel_id=1, source_target_pairs={{0,0},{1,64},{4,4},{5,68},{8,8},{9,72},{12,12},{13,76},{64,1},{65,... | collective-permute-start | bytes 786440 | tf_op jit(solution)/shard_map/ppermute | solution.py:262
  43.3 26.5 %copy-start.1 = (bf16[4,256,128]{2,1,0:T(8,128)(2,1)}, bf16[4,256,128]{2,1,0:T(8,128)(2,1)S(1)}, u32[]{:S(2)}) copy-start(bf16[4,256,128]{2,1,0:T(8,128)(2,1)S(1)} %collective-permute-done.2.rest_2_) | copy-start | bytes 786436
  46.0 23.8 %copy-start.3 = (bf16[4,256,128]{2,1,0:T(8,128)(2,1)}, bf16[4,256,128]{2,1,0:T(8,128)(2,1)S(1)}, u32[]{:S(2)}) copy-start(bf16[4,256,128]{2,1,0:T(8,128)(2,1)S(1)} %collective-permute-done.1.rest_1_) | copy-start | bytes 786436
  46.1 24.6 %copy-start.5 = (bf16[4,256,128]{2,1,0:T(8,128)(2,1)}, bf16[4,256,128]{2,1,0:T(8,128)(2,1)S(1)}, u32[]{:S(2)}) copy-start(bf16[4,256,128]{2,1,0:T(8,128)(2,1)S(1)} %collective-permute-done.rest_0_) | copy-start | bytes 786436
  66.4 4.5 %collective-permute-start.8 = (bf16[16,2,256,128]{3,2,1,0:T(8,128)(2,1)S(1)}, bf16[16,2,256,128]{3,2,1,0:T(8,128)(2,1)}, u32[]{:S(2)}, u32[]{:S(2)}) collective-permute-start(bf16[16,2,256,128]{3,2,1,0:T(8,128)(2,1)S(1)} %bitcast.135), channel_id=1, source_target_pairs={{0,1},{1,0},{2,3},{3,2},{4,5},{5,4},{6,7},{7,6},{8,9},{9,8},{10,11... | collective-permute-start | bytes 6291464 | tf_op jit(solution)/shard_map/ppermute | solution.py:23
  68.0 41.6 %collective-permute-start.13 = (bf16[2,2048,256]{2,1,0:T(8,128)(2,1)}, bf16[2,2048,256]{2,1,0:T(8,128)(2,1)}, u32[]{:S(2)}, u32[]{:S(2)}) collective-permute-start(bf16[2,2048,256]{2,1,0:T(8,128)(2,1)} %param.21), channel_id=1, source_target_pairs={{0,4},{1,13},{4,8},{5,1},{8,12},{9,5},{12,0},{13,9},{2,6},{3,15},{... | collective-permute-start | bytes 6291464 | tf_op jit(solution)/shard_map/ppermute | solution.py:323
  70.0 39.6 %collective-permute-start.14 = (bf16[256,2048]{1,0:T(8,128)(2,1)}, bf16[256,2048]{1,0:T(8,128)(2,1)}, u32[]{:S(2)}, u32[]{:S(2)}) collective-permute-start(bf16[256,2048]{1,0:T(8,128)(2,1)} %param.22), channel_id=1, source_target_pairs={{0,4},{1,13},{4,8},{5,1},{8,12},{9,5},{12,0},{13,9},{2,6},{3,15},{... | collective-permute-start | bytes 3145736 | tf_op jit(solution)/shard_map/ppermute | solution.py:323
  70.9 1.0 copy-start.2
  71.9 0.9 copy-start.4
  72.8 0.9 copy-start.6
  92.2 5.0 %collective-permute-start.9 = (bf16[256,128]{1,0:T(8,128)(2,1)S(1)}, bf16[256,128]{1,0:T(8,128)(2,1)S(1)}, u32[]{:S(2)}, u32[]{:S(2)}) collective-permute-start(bf16[256,128]{1,0:T(8,128)(2,1)S(1)} %get-tuple-element.44), channel_id=1, source_target_pairs={{0,0},{1,64},{4,4},{5,68},{8,8},{9,72},{12,12},{13,76},{64,1},{65,... | collective-permute-start | bytes 196616 | tf_op jit(solution)/shard_map/ppermute | solution.py:367
  92.9 16.6 %collective-permute-start.12 = (bf16[256,128]{1,0:T(8,128)(2,1)S(1)}, bf16[256,128]{1,0:T(8,128)(2,1)S(1)}, u32[]{:S(2)}, u32[]{:S(2)}) collective-permute-start(bf16[256,128]{1,0:T(8,128)(2,1)S(1)} %get-tuple-element.45), channel_id=1, source_target_pairs={{0,4},{1,68},{4,8},{5,72},{8,12},{9,76},{12,0},{13,64},{64,5},{65,... | collective-permute-start | bytes 196616 | tf_op jit(solution)/shard_map/ppermute | solution.py:367
  94.4 15.2 %collective-permute-start.11 = (bf16[256,128]{1,0:T(8,128)(2,1)S(1)}, bf16[256,128]{1,0:T(8,128)(2,1)S(1)}, u32[]{:S(2)}, u32[]{:S(2)}) collective-permute-start(bf16[256,128]{1,0:T(8,128)(2,1)S(1)} %get-tuple-element.46), channel_id=1, source_target_pairs={{0,8},{1,72},{4,12},{5,76},{8,0},{9,64},{12,4},{13,68},{64,9},{65,... | collective-permute-start | bytes 196616 | tf_op jit(solution)/shard_map/ppermute | solution.py:367
  97.2 12.3 %collective-permute-start.10 = (bf16[256,128]{1,0:T(8,128)(2,1)S(1)}, bf16[256,128]{1,0:T(8,128)(2,1)S(1)}, u32[]{:S(2)}, u32[]{:S(2)}) collective-permute-start(bf16[256,128]{1,0:T(8,128)(2,1)S(1)} %get-tuple-element.47), channel_id=1, source_target_pairs={{0,12},{1,76},{4,0},{5,64},{8,4},{9,68},{12,8},{13,72},{64,13},{65... | collective-permute-start | bytes 196616 | tf_op jit(solution)/shard_map/ppermute | solution.py:367
  112.5 2.3 %copy-start.14 = (f32[2,2048]{1,0:T(2,128)S(1)}, f32[2,2048]{1,0:T(2,128)}, u32[]{:S(2)}) copy-start(f32[2,2048]{1,0:T(2,128)} %param.20) | copy-start | bytes 49156
  112.5 2.0 collective-permute-start.15
  114.7 8.4 %collective-permute-start.16 = (bf16[64,2048]{1,0:T(8,128)(2,1)S(1)}, bf16[64,2048]{1,0:T(8,128)(2,1)S(1)}, u32[]{:S(2)}, u32[]{:S(2)}) collective-permute-start(bf16[64,2048]{1,0:T(8,128)(2,1)S(1)} %fusion.10), channel_id=1, source_target_pairs={{0,2},{2,0},{1,3},{3,1},{4,6},{6,4},{5,7},{7,5},{8,10},{10,8},{9,1... | collective-permute-start | bytes 786440 | tf_op jit(solution)/shard_map/ppermute | solution.py:23
  126.0 5.4 %copy-start.9 = (bf16[2,2048,256]{2,1,0:T(8,128)(2,1)S(1)}, bf16[2,2048,256]{2,1,0:T(8,128)(2,1)}, u32[]{:S(2)}) copy-start(bf16[2,2048,256]{2,1,0:T(8,128)(2,1)} %param.21) | copy-start | bytes 6291460
  126.0 7.4 %copy-start.10 = (bf16[256,2048]{1,0:T(8,128)(2,1)S(1)}, bf16[256,2048]{1,0:T(8,128)(2,1)}, u32[]{:S(2)}) copy-start(bf16[256,2048]{1,0:T(8,128)(2,1)} %param.22) | copy-start | bytes 3145732
  126.0 33.4 %all-to-all-start.1 = ((bf16[8,64,2048]{2,1,0:T(8,128)(2,1)}), bf16[8,64,2048]{2,1,0:T(8,128)(2,1)}, u32[]{:S(2)}, u32[]{:S(2)}) async-start(bf16[8,64,2048]{2,1,0:T(8,128)(2,1)} %broadcast_in_dim.137), calls=%async_computation.1 | async-start | bytes 4194304 | tf_op jit(solution)/shard_map/all_to_all | solution.py:31
  131.4 28.1 %collective-permute-start.17 = (bf16[2,2048,256]{2,1,0:T(8,128)(2,1)S(1)}, bf16[2,2048,256]{2,1,0:T(8,128)(2,1)}, u32[]{:S(2)}, u32[]{:S(2)}) collective-permute-start(bf16[2,2048,256]{2,1,0:T(8,128)(2,1)S(1)} %copy-done.9), channel_id=1, source_target_pairs={{1,9},{5,13},{9,1},{13,5},{3,11},{7,15},{11,3},{15,7},{17,25},{21,... | collective-permute-start | bytes 6291464 | tf_op jit(solution)/shard_map/ppermute | solution.py:329
  133.4 26.0 %collective-permute-start.18 = (bf16[256,2048]{1,0:T(8,128)(2,1)S(1)}, bf16[256,2048]{1,0:T(8,128)(2,1)}, u32[]{:S(2)}, u32[]{:S(2)}) collective-permute-start(bf16[256,2048]{1,0:T(8,128)(2,1)S(1)} %copy-done.10), channel_id=1, source_target_pairs={{1,9},{5,13},{9,1},{13,5},{3,11},{7,15},{11,3},{15,7},{17,25},{21,... | collective-permute-start | bytes 3145736 | tf_op jit(solution)/shard_map/ppermute | solution.py:329
  159.4 4.5 %collective-permute-start.19 = (bf16[512,2048]{1,0:T(8,128)(2,1)}, bf16[512,2048]{1,0:T(8,128)(2,1)}, u32[]{:S(2)}, u32[]{:S(2)}) collective-permute-start(bf16[512,2048]{1,0:T(8,128)(2,1)} %bitcast.82.tokens_ref), channel_id=1, source_target_pairs={{0,1},{1,0},{2,3},{3,2},{4,5},{5,4},{6,7},{7,6},{8,9},{9,8},{10,11... | collective-permute-start | bytes 6291464 | tf_op jit(solution)/shard_map/ppermute | solution.py:23
  170.9 17.7 %collective-permute-start.20 = (bf16[512,2048]{1,0:T(8,128)(2,1)S(1)}, bf16[512,2048]{1,0:T(8,128)(2,1)S(1)}, u32[]{:S(2)}, u32[]{:S(2)}) collective-permute-start(bf16[512,2048]{1,0:T(8,128)(2,1)S(1)} %shard_map.138), channel_id=1, source_target_pairs={{0,1},{1,0},{2,3},{3,2},{4,5},{5,4},{6,7},{7,6},{8,9},{9,8},{10,11... | collective-permute-start | bytes 6291464 | tf_op jit(solution)/shard_map/ppermute | solution.py:23

commit v5 on v4

--- a/solution.py
+++ b/solution.py
@@ -102,7 +102,7 @@
     count = counts_ref[group, tile]
 
     def work(first):
-        q = qkv_ref[group, 0, first : first + half_rows, :]
+        q = qkv_ref[group, first : first + half_rows, :]
         seen = first + half_rows
         middle = info_ref[0, first:seen, 0:1]
         root = info_ref[0, first:seen, 1:2]
@@ -112,7 +112,7 @@
         col_at = lax.broadcasted_iota(jnp.int32, (half_rows, seen), 1)
         key_at = lax.broadcasted_iota(jnp.int32, (1, node_rows), 1)
         scale = factor_ref[0, first:seen, 0:1] * (HD**-0.5 * LOG2E)
-        near = lax.dot_general(q, qkv_ref[group, 1, :seen, :], nt, preferred_element_type=F32)
+        near = lax.dot_general(q, qkv_ref[group, rows : rows + seen, :], nt, preferred_element_type=F32)
         near = near * scale * key_factor_ref[0][:, :seen]
         near = jnp.where((seg_col == seg_row) & (col_at <= row_at), near, NEG)
         top = jnp.max(near, axis=1, keepdims=True)
@@ -134,7 +134,7 @@
         top = lax.fori_loop(0, batches, score, top)
         weights = jnp.exp2(near - top)
         total = jnp.sum(weights, axis=1, keepdims=True)
-        summed = jnp.dot(weights.astype(BF), qkv_ref[group, 2, :seen, :], preferred_element_type=F32)
+        summed = jnp.dot(weights.astype(BF), qkv_ref[group, 2 * rows : 2 * rows + seen, :], preferred_element_type=F32)
 
         def gather(i, carry):
             total, summed = carry
@@ -160,7 +160,7 @@
 def attention(
     nodes, lengths, lists, counts, qkv_parts, row_info, seg_row, factors, key_factors, parts
 ):
-    rows = qkv_parts[0].shape[1]
+    rows = row_info.shape[1]
     groups = len(qkv_parts)
     per_part, _, node_rows, _ = parts[0].shape
     slots = nodes.shape[0]
@@ -177,7 +177,7 @@
             + [pl.BlockSpec(memory_space=pl.ANY)] * len(parts),
             out_specs=pl.BlockSpec((1, rows // 2, HD), lambda i, *_: (i // 2, i % 2, 0)),
             scratch_shapes=[
-                pltpu.VMEM((groups, 4, rows, HD), BF),
+                pltpu.VMEM((groups,) + qkv_parts[0].shape, BF),
                 pltpu.VMEM((slots, node_rows, HD), BF),
                 pltpu.VMEM((slots, node_rows, HD), BF),
                 pltpu.VMEM((lists.shape[2] // batch, rows // 2, batch * node_rows), F32),
@@ -192,38 +192,68 @@
     )(nodes, lengths, lists, counts, *qkv_parts, row_info, seg_row, factors, key_factors, *parts)
 
 
-def feed_forward_body(tokens_ref, gu_a, dn_a, gu_b, dn_b, out_ref):
+def feed_forward_body(tokens_ref, gu_a, dn_a, gu_b, dn_b, out_ref, tokens, gu, dn, made, sems):
     rows = 256
-
-    def one(i, carry):
-        at = pl.ds(i * rows, rows)
-        tokens = tokens_ref[at, :]
+    blocks = tokens.shape[0] // rows
+
+    def block(ref, i):
+        return ref.at[pl.ds(i * rows, rows)]
+
+    def fetch(i):
+        return pltpu.make_async_copy(block(tokens_ref, i), block(tokens, i), sems.at[0, i])
+
+    def store(i):
+        return pltpu.make_async_copy(block(made, i), block(out_ref, i), sems.at[1, i])
+
+    loads = [
+        pltpu.make_async_copy(source, target, sems.at[2 + j, k])
+        for k, pair in enumerate(((gu_a, dn_a), (gu_b, dn_b)))
+        for j, (source, target) in enumerate(((pair[0], gu.at[k]), (pair[1], dn.at[k])))
+    ]
+    fetch(0).start()
+    for load in loads:
+        load.start()
+    for i in range(1, blocks):
+        fetch(i).start()
+    for i in range(blocks):
+        fetch(i).wait()
         part = 0.0
-        for gu_ref, dn_ref in ((gu_a, dn_a), (gu_b, dn_b)):
-            gate = jnp.dot(tokens, gu_ref[0], preferred_element_type=F32)
-            up = jnp.dot(tokens, gu_ref[1], preferred_element_type=F32)
+        for k in range(2):
+            if i == 0:
+                loads[2 * k].wait()
+            values = tokens[i * rows : (i + 1) * rows, :]
+            gate = jnp.dot(values, gu[k, 0], preferred_element_type=F32)
+            up = jnp.dot(values, gu[k, 1], preferred_element_type=F32)
             hidden = (gate / (1.0 + jnp.exp(-gate)) * up).astype(BF)
-            part = part + jnp.dot(hidden, dn_ref[...], preferred_element_type=F32)
-        out_ref[at, :] = part.astype(BF)
-        return carry
-
-    lax.fori_loop(0, tokens_ref.shape[0] // rows, one, 0)
+            if i == 0:
+                loads[2 * k + 1].wait()
+            part = part + jnp.dot(hidden, dn[k], preferred_element_type=F32)
+        made[i * rows : (i + 1) * rows, :] = part.astype(BF)
+        store(i).start()
+    for i in range(blocks):
+        store(i).wait()
 
 
 def feed_forward(tokens, weights):
     rows, width = tokens.shape
-    units = weights[1].shape[0] * 2
-    space = pl.BlockSpec(memory_space=pltpu.VMEM)
+    units = weights[1].shape[0]
     return pl.pallas_call(
         feed_forward_body,
         out_shape=jax.ShapeDtypeStruct((rows, width), BF),
-        in_specs=[space] * 5,
-        out_specs=space,
+        in_specs=[pl.BlockSpec(memory_space=pl.ANY)] * 5,
+        out_specs=pl.BlockSpec(memory_space=pl.ANY),
+        scratch_shapes=[
+            pltpu.VMEM((rows, width), BF),
+            pltpu.VMEM((2, 2, width, units), BF),
+            pltpu.VMEM((2, units, width), BF),
+            pltpu.VMEM((rows, width), BF),
+            pltpu.SemaphoreType.DMA((4, 2)),
+        ],
         compiler_params=pltpu.CompilerParams(vmem_limit_bytes=48 << 20),
         cost_estimate=pl.CostEstimate(
-            flops=2 * rows * width * units * 3,
-            transcendentals=rows * units,
-            bytes_accessed=(2 * rows * width + 3 * width * units) * 2,
+            flops=2 * rows * width * units * 6,
+            transcendentals=2 * rows * units,
+            bytes_accessed=(2 * rows * width + 6 * width * units) * 2,
         ),
     )(tokens, *weights)
 
@@ -277,6 +307,19 @@
 
     w_out = lax.dynamic_slice_in_dim(jnp.concatenate([w_out, w_out]), z_at * HD, w_out.shape[0], 0)
 
+    def beside(weights):
+        return lax.ppermute(
+            weights, ("z", "core"),
+            [(z * 2 + c, (z + 1 - 2 * c) % n_z * 2 + c) for z in range(n_z) for c in range(2)],
+        )
+
+    def beyond(weights):
+        return lax.ppermute(
+            weights, ("z", "core"), [(z * 2 + 1, (z + 2) % n_z * 2 + 1) for z in range(n_z)]
+        )
+
+    gu_a = beside(w_gate_up)
+
     qkv_raw = jnp.einsum("td,cdw->ctw", states_in, w_qkv, preferred_element_type=F32)
     squares = jnp.sum(qkv_raw[:2] * qkv_raw[:2], axis=2)
     cached_own = spread(cached, "x").reshape((n_x * n_z,) + cached.shape[1:])
@@ -304,35 +347,23 @@
     for _ in range(3):
         terms.append(lax.reduce_precision(left, 8, 7))
         left = left - terms[-1]
-    terms = jnp.stack(terms).reshape(6, rows).astype(BF).T
-    terms = jnp.pad(terms, ((0, 0), (0, HD - 6)))
+    terms = jnp.stack(terms).reshape(-1, HD).astype(BF)
+    term_rows = terms.shape[0]
+    terms = jnp.pad(terms, ((0, -term_rows % 16), (0, 0)))
     qkv = jnp.stack(
-        [
-            turned(0), turned(1), qkv_raw[2].astype(BF).reshape(rows, heads_here, HD),
-            jnp.broadcast_to(terms[:, None], (rows, heads_here, HD)),
-        ]
-    ).transpose(2, 0, 1, 3)
+        [turned(0), turned(1), qkv_raw[2].astype(BF).reshape(rows, heads_here, HD)]
+    ).transpose(2, 0, 1, 3).reshape(heads_here, 3 * rows, HD)
+    qkv = jnp.concatenate([qkv, jnp.broadcast_to(terms, (heads_here,) + terms.shape)], axis=1)
+    qkv, gu_a = lax.optimization_barrier((qkv, gu_a))
     qkv_parts = [across(select_row(qkv, (z_at + s) % n_z), s) for s in range(n_z)]
-    terms = jnp.stack([part[3, :, :6] for part in qkv_parts]).astype(F32)
-    squares = jnp.sum(terms.reshape(n_z, rows, 3, 2), axis=2)
+    terms = jnp.stack([part[3 * rows : 3 * rows + term_rows] for part in qkv_parts]).astype(F32)
+    squares = jnp.sum(terms.reshape(n_z, 3, 2, rows), axis=1).transpose(0, 2, 1)
     factors = lax.rsqrt(lax.psum(squares, ("yhi", "ylo")) / columns + EPS)
-    cached_own, factors = lax.optimization_barrier((cached_own, factors))
+    w_gate_up, w_down, qkv_parts = lax.optimization_barrier((w_gate_up, w_down, qkv_parts))
+    cached_own, qkv_parts = lax.optimization_barrier((cached_own, qkv_parts))
     cached_parts = [cached_own, shift(cached_own, "core", 1)]
 
-    def beside(weights):
-        return lax.ppermute(
-            weights, ("z", "core"),
-            [(z * 2 + c, (z + 1 - 2 * c) % n_z * 2 + c) for z in range(n_z) for c in range(2)],
-        )
-
-    def beyond(weights):
-        far = lax.ppermute(
-            weights, ("z", "core"), [(z * 2 + 1, (z + 2) % n_z * 2 + 1) for z in range(n_z)]
-        )
-        return jnp.where(core == 0, weights, far)
-
-    w_gate_up, w_down, factors = lax.optimization_barrier((w_gate_up, w_down, factors))
-    gu_a, dn_a = beside(w_gate_up), beside(w_down)
+    dn_a, gu_b, dn_b = beside(w_down), beyond(w_gate_up), beyond(w_down)
 
     slots = slot_from.shape[0]
     slot_nodes = jnp.take(slot_node, slot_from)
@@ -367,10 +398,7 @@
         return lax.ppermute(values, corner, pairs)
 
     attended = jnp.concatenate([back(attended[s], s) for s in range(n_z)], axis=1)
-    attended, gu_a, dn_a, w_gate_up, w_down = lax.optimization_barrier(
-        (attended, gu_a, dn_a, w_gate_up, w_down)
-    )
-    gu_b, dn_b = beyond(w_gate_up), beyond(w_down)
+    attended, dn_a, gu_b, dn_b = lax.optimization_barrier((attended, dn_a, gu_b, dn_b))
     attn_part = jnp.dot(attended, w_out, preferred_element_type=F32)
     attn_part = attn_part.reshape(2, 2, rows // 4, -1)
 
@@ -386,7 +414,9 @@
     mid_state = (state_rows.astype(F32) + rms_norm(attn_proj, post_gain[0])).astype(BF)
 
     plane = ("yhi", "x")
-    weights = (gu_a, dn_a, gu_b, dn_b)
+    weights = (
+        gu_a, dn_a, jnp.where(core == 0, w_gate_up, gu_b), jnp.where(core == 0, w_down, dn_b)
+    )
     tokens = spread(mid_state, plane)
     flat = tokens.reshape(-1, tokens.shape[2])
     other = feed_forward(shift(flat, "core", 1), weights)

time: 227 us -> 221 us (0.974)
  waiting for transfers between devices: 55.2 us -> 34.5 us
  blocking collectives: 55.4 us -> 74.6 us
  starting transfers between devices: 45.7 us -> 42 us
  other arithmetic: 14 us -> 11.7 us
    all_to_all x0 -> x1, blocking collectives: none -> 34.7 us  [spread(): return lax.all_to_all(copies, axes, 0, 0, tiled=True)]
    all_to_all x2 -> x1, waiting for transfers between devices: 24.4 us -> 0.01 us  [spread(): return lax.all_to_all(copies, axes, 0, 0, tiled=True)]
    psum x1, blocking collectives: 20.1 us -> 8.52 us  [on_device(): factors = lax.rsqrt(lax.psum(squares, ('yhi', 'ylo')) / columns + EPS)]
    ppermute x2, waiting for transfers between devices: 0.01 us -> 8.58 us  [beside(): lax.ppermute(weights, ('z', 'core'), [(z * 2 + c, (z + 1 - 2 * c) % n_z *...]
    all_to_all x2 -> x1, starting transfers between devices: 9.8 us -> 4.29 us  [spread(): return lax.all_to_all(copies, axes, 0, 0, tiled=True)]
    ppermute x5, starting transfers between devices: 11 us -> 15.8 us  [shift(): return lax.ppermute(values, axis, [(i, (i + by) % n) for i in range(n)])]
    all_to_all x1, blocking collectives: 35.3 us -> 31.4 us  [on_device(): lax.all_to_all(total.astype(BF).reshape(tokens.shape), plane, 0, 0, tiled...]
    ppermute x4, starting transfers between devices: 7.23 us -> 3.44 us  [back(): return lax.ppermute(values, corner, pairs)]
  transfers between devices with their start and end apart: 23 -> 22, of which waited for: 8 -> 9; matrix products, arithmetic and copies ran while one was open for 9% -> 11% of each run, Pallas kernels for 11% -> 12%
where the time goes in v5:
time: 221 us; the launch traced here: 220 us
  blocking collectives  74.6 us (34%)
  starting transfers between devices  42 us (19%)
  waiting for transfers between devices  34.5 us (16%)
  Pallas kernels  33.7 us (15%)
  local copies, waits for them, and re-layouts  15 us (7%)
  other arithmetic  11.7 us (5%)
  matrix products  7.75 us (4%)
    all_to_all x1, blocking collectives, spread(): return lax.all_to_all(copies, axes, 0, 0, tiled=True)  34.7 us
    all_to_all x1, blocking collectives, on_device(): lax.all_to_all(total.astype(BF).reshape(tokens.shape), plane, 0, 0, tiled...  31.4 us
    pallas_call x1, Pallas kernels, attention(): pl.pallas_call(attention_body, out_shape=jax.ShapeDtypeStruct((groups, ro...  20.8 us
    ppermute x5, starting transfers between devices, shift(): return lax.ppermute(values, axis, [(i, (i + by) % n) for i in range(n)])  15.8 us
    pallas_call x2, Pallas kernels, feed_forward(): pl.pallas_call(feed_forward_body, out_shape=jax.ShapeDtypeStruct((rows, w...  12.9 us
    ppermute x4, waiting for transfers between devices, back(): return lax.ppermute(values, corner, pairs)  11.7 us
    ppermute x8, starting transfers between devices, across(): return lax.ppermute(values, corner, pairs)  11.6 us
    ppermute x5, waiting for transfers between devices, shift(): return lax.ppermute(values, axis, [(i, (i + by) % n) for i in range(n)])  9.36 us
  transfers between devices with their start and end apart: 22, of which 9 were waited for; matrix products, arithmetic and copies ran while one was open for 11% of the time, Pallas kernels for 12%

profile of v5, /device:TPU:0, one launch (start us, length us, event | category | flops | bytes accessed | tf_op | source)
XLA Modules:
  0.0 219.9 jit_solution(8477709637929112515)
XLA Ops:
  0.0 1.1 constant_dynamic-slice_fusion.6
  1.2 4.1 %collective-permute-start.2 = (bf16[2,256,128]{2,1,0:T(8,128)(2,1)S(1)}, bf16[2,256,128]{2,1,0:T(8,128)(2,1)S(1)}, u32[]{:S(2)}, u32[]{:S(2)}) collective-permute-start(bf16[2,256,128]{2,1,0:T(8,128)(2,1)S(1)} %pad_maximum_fusion.5), channel_id=1, source_target_pairs={{0,8},{1,72},{4,12},{5,76},{8,0},{9,64},{12,4},{13,68},{64,9},{65,... | collective-permute-start | bytes 393224 | tf_op jit(solution)/shard_map/ppermute | solution.py:292
  5.3 0.8 collective-permute-start.3
  6.1 1.4 collective-permute-start.1
  8.2 1.1 collective-permute-start.4
  11.1 4.9 %convolution_bitcast_fusion = f32[3,256,512]{1,2,0:T(8,128)S(1)} fusion(bf16[3,2048,512]{2,1,0:T(8,128)(2,1)} %param.17, bf16[256,2048]{1,0:T(8,128)(2,1)} %param.16), kind=kOutput, calls=%fused_computation.11 | convolution fusion | flops 1610612736 | bytes 8912896 | tf_op jit(solution)/shard_map/td,cdw->ctw/dot_general | solution.py:323
  17.1 1.8 broadcast_in_dim.132
  19.0 4.3 %all-to-all-start = ((bf16[4,4,2,256,128]{4,3,2,1,0:T(8,128)(2,1)}), bf16[4,4,2,256,128]{4,3,2,1,0:T(8,128)(2,1)S(1)}, u32[]{:S(2)}, u32[]{:S(2)}) async-start(bf16[4,4,2,256,128]{4,3,2,1,0:T(8,128)(2,1)} %broadcast_in_dim.132), calls=%async_computation | async-start | bytes 4194304 | tf_op jit(solution)/shard_map/all_to_all | solution.py:31
  23.3 1.1 slice.182
  24.4 1.3 fusion.19
  26.1 1.2 copy.43
  27.4 1.2 pad_maximum_fusion
  28.6 8.6 %collective-permute-done.4.gu_a = bf16[2,2048,256]{2,1,0:T(8,128)(2,1)} collective-permute-done((bf16[2,2048,256]{2,1,0:T(8,128)(2,1)}, bf16[2,2048,256]{2,1,0:T(8,128)(2,1)}, u32[]{:S(2)}, u32[]{:S(2)}) %collective-permute-start.4) | collective-permute-done | bytes 2097184 | tf_op jit(solution)/shard_map/ppermute | solution.py:311
  37.2 0.9 dynamic-slice_bitcast_fusion
  38.1 0.7 collective-permute-start.8
  38.8 1.6 collective-permute-start.7
  40.4 0.8 collective-permute-start.6
  41.2 1.6 collective-permute-start.5
  42.8 0.7 gather_fusion.2
  44.0 2.3 %collective-permute-done.7.rest_2_ = bf16[784,128]{1,0:T(8,128)(2,1)S(1)} collective-permute-done((bf16[784,128]{1,0:T(8,128)(2,1)}, bf16[784,128]{1,0:T(8,128)(2,1)S(1)}, u32[]{:S(2)}, u32[]{:S(2)}) %collective-permute-start.7) | collective-permute-done | bytes 200736 | tf_op jit(solution)/shard_map/ppermute | solution.py:292
  46.3 2.1 collective-permute-done.6.rest_1_
  48.4 10.1 %collective-permute-start.9 = (bf16[16,2,256,128]{3,2,1,0:T(8,128)(2,1)S(1)}, bf16[16,2,256,128]{3,2,1,0:T(8,128)(2,1)}, u32[]{:S(2)}, u32[]{:S(2)}) collective-permute-start(bf16[16,2,256,128]{3,2,1,0:T(8,128)(2,1)S(1)} %bitcast.126), channel_id=1, source_target_pairs={{0,1},{1,0},{2,3},{3,2},{4,5},{5,4},{6,7},{7,6},{8,9},{9,8},{10,11... | collective-permute-start | bytes 6291464 | tf_op jit(solution)/shard_map/ppermute | solution.py:23
  58.5 2.0 collective-permute-start.15
  62.7 1.7 collective-permute-start.16
  64.4 2.1 collective-permute-start.14
  67.3 8.5 %psum.7 = f32[4,256,2]{1,2,0:T(2,128)S(1)} all-reduce(f32[4,256,2]{1,2,0:T(2,128)S(1)} %bitcast.143), channel_id=1, replica_groups=mesh['yhi'=2,'x'=4,'z'=4,'ylo'=2,'core'=2] {'yhi','ylo'}, use_global_device_ids=true, to_apply=%region_13.15 | all-reduce | flops 2048 | bytes 16384 | tf_op jit(solution)/shard_map/psum | solution.py:361
  76.1 0.9 copy-done.2
  77.0 0.9 copy-done.4
  78.0 0.9 copy-done.6
  78.9 20.8 %shard_map.136 = bf16[4,256,128]{2,1,0:T(8,128)(2,1)S(1)} custom-call(s32[32]{0:T(128)S(1)} %get-tuple-element.47.nodes_ref, s32[32]{0:T(128)S(1)} %and_select_fusion.lengths_ref, s32[4,2,12]{2,1,0:T(2,128)S(1)} %copy.44.lists_ref, s32[4,2]{1,0:T(4,128)S(1)} %copy.45.counts_ref, bf16[784,128]{1,0:T(8,128)(2,1)S(1)} %copy-done.6, ...), custom_call_target="tpu_custom_call" | custom-call | flops 2000000000 | bytes 6000000 | tf_op jit(solution)/shard_map/pallas_call | solution.py:169
  100.4 2.1 collective-permute-start.13
  102.5 0.7 collective-permute-start.12
  103.2 7.4 %collective-permute-done.13 = bf16[256,128]{1,0:T(8,128)(2,1)S(1)} collective-permute-done((bf16[256,128]{1,0:T(8,128)(2,1)S(1)}, bf16[256,128]{1,0:T(8,128)(2,1)S(1)}, u32[]{:S(2)}, u32[]{:S(2)}) %collective-permute-start.13) | collective-permute-done | bytes 65568 | tf_op jit(solution)/shard_map/ppermute | solution.py:398
  110.6 4.3 %collective-permute-done.11 = bf16[256,128]{1,0:T(8,128)(2,1)S(1)} collective-permute-done((bf16[256,128]{1,0:T(8,128)(2,1)S(1)}, bf16[256,128]{1,0:T(8,128)(2,1)S(1)}, u32[]{:S(2)}, u32[]{:S(2)}) %collective-permute-start.11) | collective-permute-done | bytes 65568 | tf_op jit(solution)/shard_map/ppermute | solution.py:398
  114.9 2.8 %fusion.1 = f32[256,2048]{1,0:T(8,128)S(1)} fusion(bf16[256,512]{1,0:T(8,128)(2,1)S(1)} %pad_maximum_fusion.2, s32[]{:T(128)S(6)} %select_n.293, bf16[512,2048]{1,0:T(8,128)(2,1)} %param.19), kind=kOutput, calls=%fused_computation.9 | convolution fusion | flops 541065216 | bytes 4456452 | tf_op jit(solution)/shard_map/dot_general | solution.py:402
  117.9 3.8 %collective-permute-start.17 = (bf16[2,64,2048]{2,1,0:T(8,128)(2,1)S(1)}, bf16[2,64,2048]{2,1,0:T(8,128)(2,1)S(1)}, u32[]{:S(2)}, u32[]{:S(2)}) collective-permute-start(bf16[2,64,2048]{2,1,0:T(8,128)(2,1)S(1)} %fusion.5), channel_id=1, source_target_pairs={{0,1},{1,0},{2,3},{3,2},{4,5},{5,4},{6,7},{7,6},{8,9},{9,8},{10,11... | collective-permute-start | bytes 1572872 | tf_op jit(solution)/shard_map/ppermute | solution.py:23
  121.6 1.5 collective-permute-done.17
  123.3 1.2 collective-permute-start.18
  124.5 7.4 %collective-permute-done.18 = bf16[64,2048]{1,0:T(8,128)(2,1)S(1)} collective-permute-done((bf16[64,2048]{1,0:T(8,128)(2,1)S(1)}, bf16[64,2048]{1,0:T(8,128)(2,1)S(1)}, u32[]{:S(2)}, u32[]{:S(2)}) %collective-permute-start.18) | collective-permute-done | bytes 262176 | tf_op jit(solution)/shard_map/ppermute | solution.py:23
  132.2 1.1 add_convert_fusion.2
  133.5 34.7 %all_to_all.15 = bf16[8,64,2048]{2,1,0:T(8,128)(2,1)S(1)} all-to-all(bf16[8,64,2048]{2,1,0:T(8,128)(2,1)S(1)} %broadcast_in_dim.140), channel_id=1, replica_groups=mesh['yhi'=2,'x'=4,'z'=4,'ylo'=2,'core'=2] {'yhi','x'}, dimensions={0} | all-to-all | bytes 4194304 | tf_op jit(solution)/shard_map/all_to_all | solution.py:31
  168.4 3.8 %broadcast_select_fusion.gu_b = bf16[2,2048,256]{2,1,0:T(8,128)(2,1)} fusion(bf16[2,2048,256]{2,1,0:T(8,128)(2,1)} %param.21, bf16[2,2048,256]{2,1,0:T(8,128)(2,1)} %collective-permute-done.15, pred[]{:T(512)S(6)} %eq.164), kind=kLoop, calls=%fused_computation.10 | loop fusion | flops 1048576 | bytes 6291457 | tf_op jit(solution)/shard_map/jit(_where)/select_n | solution.py:418
  172.6 6.4 %shard_map.138 = bf16[512,2048]{1,0:T(8,128)(2,1)S(1)} custom-call(bf16[512,2048]{1,0:T(8,128)(2,1)} %collective-permute-done.19.tokens_ref, bf16[2,2048,256]{2,1,0:T(8,128)(2,1)} %collective-permute-done.4.gu_a, bf16[256,2048]{1,0:T(8,128)(2,1)} %collective-permute-done.14.dn_a, bf16[2,2048,256]{2,1,0:T(8,128)(2,1)} %broadcast_select_fusion.gu_b, ...), custom_call_target="tpu_custom_call" | custom-call | flops 3221225472 | bytes 10485760 | tf_op jit(solution)/shard_map/pallas_call | solution.py:240
  179.0 0.8 collective-permute-start.20
  179.8 6.4 %shard_map.137 = bf16[512,2048]{1,0:T(8,128)(2,1)S(1)} custom-call(bf16[512,2048]{1,0:T(8,128)(2,1)} %bitcast.131, bf16[2,2048,256]{2,1,0:T(8,128)(2,1)} %collective-permute-done.4.gu_a, bf16[256,2048]{1,0:T(8,128)(2,1)} %collective-permute-done.14.dn_a, bf16[2,2048,256]{2,1,0:T(8,128)(2,1)} %broadcast_select_fusion.gu_b, ...), custom_call_target="tpu_custom_call" | custom-call | flops 3221225472 | bytes 10485760 | tf_op jit(solution)/shard_map/pallas_call | solution.py:240
  186.3 0.9 add_convert_fusion
  187.2 31.4 %all_to_all.16 = bf16[8,64,2048]{2,1,0:T(8,128)(2,1)S(1)} all-to-all(bf16[8,64,2048]{2,1,0:T(8,128)(2,1)S(1)} %bitcast.128), channel_id=1, replica_groups=mesh['yhi'=2,'x'=4,'z'=4,'ylo'=2,'core'=2] {'yhi','x'}, dimensions={0} | all-to-all | bytes 4194304 | tf_op jit(solution)/shard_map/all_to_all | solution.py:424
  219.0 0.9 add_convert_fusion.1
  (130 shorter events, 10.3 us)
Async XLA Ops:
  0.0 9.6 %copy-start = (s32[32,256]{1,0:T(8,128)S(1)}, s32[32,256]{1,0:T(8,128)}, u32[]{:S(2)}) copy-start(s32[32,256]{1,0:T(8,128)} %param.28) | copy-start | bytes 98308
  0.0 9.5 %copy-start.14 = (f32[2,512]{1,0:T(2,128)S(1)}, f32[2,512]{1,0:T(2,128)}, u32[]{:S(2)}) copy-start(f32[2,512]{1,0:T(2,128)} %param.18) | copy-start | bytes 12292
  0.0 10.4 %copy-start.13 = (s32[32,8]{0,1:T(8,128)S(1)}, s32[32,8]{0,1:T(8,128)}, u32[]{:S(2)}) copy-start(s32[32,8]{0,1:T(8,128)} %param.29) | copy-start | bytes 3076
  1.2 15.8 %collective-permute-start.2 = (bf16[2,256,128]{2,1,0:T(8,128)(2,1)S(1)}, bf16[2,256,128]{2,1,0:T(8,128)(2,1)S(1)}, u32[]{:S(2)}, u32[]{:S(2)}) collective-permute-start(bf16[2,256,128]{2,1,0:T(8,128)(2,1)S(1)} %pad_maximum_fusion.5), channel_id=1, source_target_pairs={{0,8},{1,72},{4,12},{5,76},{8,0},{9,64},{12,4},{13,68},{64,9},{65,... | collective-permute-start | bytes 393224 | tf_op jit(solution)/shard_map/ppermute | solution.py:292
  5.3 11.8 %collective-permute-start.3 = (bf16[2,256,128]{2,1,0:T(8,128)(2,1)S(1)}, bf16[2,256,128]{2,1,0:T(8,128)(2,1)S(1)}, u32[]{:S(2)}, u32[]{:S(2)}) collective-permute-start(bf16[2,256,128]{2,1,0:T(8,128)(2,1)S(1)} %pad_maximum_fusion.6), channel_id=1, source_target_pairs={{0,12},{1,76},{4,0},{5,64},{8,4},{9,68},{12,8},{13,72},{64,13},{65... | collective-permute-start | bytes 393224 | tf_op jit(solution)/shard_map/ppermute | solution.py:292
  6.1 11.0 %collective-permute-start.1 = (bf16[2,256,128]{2,1,0:T(8,128)(2,1)S(1)}, bf16[2,256,128]{2,1,0:T(8,128)(2,1)S(1)}, u32[]{:S(2)}, u32[]{:S(2)}) collective-permute-start(bf16[2,256,128]{2,1,0:T(8,128)(2,1)S(1)} %pad_maximum_fusion.4), channel_id=1, source_target_pairs={{0,4},{1,68},{4,8},{5,72},{8,12},{9,76},{12,0},{13,64},{64,5},{65,... | collective-permute-start | bytes 393224 | tf_op jit(solution)/shard_map/ppermute | solution.py:292
  7.5 9.6 %collective-permute-start = (bf16[2,256,128]{2,1,0:T(8,128)(2,1)S(1)}, bf16[2,256,128]{2,1,0:T(8,128)(2,1)S(1)}, u32[]{:S(2)}, u32[]{:S(2)}) collective-permute-start(bf16[2,256,128]{2,1,0:T(8,128)(2,1)S(1)} %pad_maximum_fusion.3), channel_id=1, source_target_pairs={{0,0},{1,64},{4,4},{5,68},{8,8},{9,72},{12,12},{13,76},{64,1},{65,... | collective-permute-start | bytes 393224 | tf_op jit(solution)/shard_map/ppermute | solution.py:292
  8.2 29.0 %collective-permute-start.4 = (bf16[2,2048,256]{2,1,0:T(8,128)(2,1)}, bf16[2,2048,256]{2,1,0:T(8,128)(2,1)}, u32[]{:S(2)}, u32[]{:S(2)}) collective-permute-start(bf16[2,2048,256]{2,1,0:T(8,128)(2,1)} %param.21), channel_id=1, source_target_pairs={{0,4},{1,13},{4,8},{5,1},{8,12},{9,5},{12,0},{13,9},{2,6},{3,15},{... | collective-permute-start | bytes 6291464 | tf_op jit(solution)/shard_map/ppermute | solution.py:311
  11.1 5.3 %copy-start.15 = (s32[28]{0:T(128)S(1)}, s32[28]{0:T(128)}, u32[]{:S(2)}) copy-start(s32[28]{0:T(128)} %param.27) | copy-start | bytes 340
  11.1 5.4 %copy-start.7 = (s32[32]{0:T(128)S(1)}, s32[32]{0:T(128)}, u32[]{:S(2)}) copy-start(s32[32]{0:T(128)} %param.26) | copy-start | bytes 388
  16.0 2.9 %copy-start.9 = (f32[3,256,512]{1,2,0:T(8,128)}, f32[3,256,512]{1,2,0:T(8,128)S(1)}, u32[]{:S(2)}) copy-start(f32[3,256,512]{1,2,0:T(8,128)S(1)} %convolution_bitcast_fusion) | copy-start | bytes 4718596
  19.0 29.4 %all-to-all-start = ((bf16[4,4,2,256,128]{4,3,2,1,0:T(8,128)(2,1)}), bf16[4,4,2,256,128]{4,3,2,1,0:T(8,128)(2,1)S(1)}, u32[]{:S(2)}, u32[]{:S(2)}) async-start(bf16[4,4,2,256,128]{4,3,2,1,0:T(8,128)(2,1)} %broadcast_in_dim.132), calls=%async_computation | async-start | bytes 4194304 | tf_op jit(solution)/shard_map/all_to_all | solution.py:31
  26.1 16.7 %copy-start.8 = (s32[32]{0:T(128)S(1)}, s32[32]{0:T(128)}, u32[]{:S(2)}) copy-start(s32[32]{0:T(128)} %param.25) | copy-start | bytes 388
  38.1 5.9 %collective-permute-start.8 = (bf16[784,128]{1,0:T(8,128)(2,1)}, bf16[784,128]{1,0:T(8,128)(2,1)S(1)}, u32[]{:S(2)}, u32[]{:S(2)}) collective-permute-start(bf16[784,128]{1,0:T(8,128)(2,1)} %get-tuple-element.50), channel_id=1, source_target_pairs={{0,12},{1,76},{4,0},{5,64},{8,4},{9,68},{12,8},{13,72},{64,13},{65... | collective-permute-start | bytes 602120 | tf_op jit(solution)/shard_map/ppermute | solution.py:292
  38.8 7.5 %collective-permute-start.7 = (bf16[784,128]{1,0:T(8,128)(2,1)}, bf16[784,128]{1,0:T(8,128)(2,1)S(1)}, u32[]{:S(2)}, u32[]{:S(2)}) collective-permute-start(bf16[784,128]{1,0:T(8,128)(2,1)} %get-tuple-element.51), channel_id=1, source_target_pairs={{0,8},{1,72},{4,12},{5,76},{8,0},{9,64},{12,4},{13,68},{64,9},{65,... | collective-permute-start | bytes 602120 | tf_op jit(solution)/shard_map/ppermute | solution.py:292
  40.4 8.0 %collective-permute-start.6 = (bf16[784,128]{1,0:T(8,128)(2,1)}, bf16[784,128]{1,0:T(8,128)(2,1)S(1)}, u32[]{:S(2)}, u32[]{:S(2)}) collective-permute-start(bf16[784,128]{1,0:T(8,128)(2,1)} %get-tuple-element.52), channel_id=1, source_target_pairs={{0,4},{1,68},{4,8},{5,72},{8,12},{9,76},{12,0},{13,64},{64,5},{65,... | collective-permute-start | bytes 602120 | tf_op jit(solution)/shard_map/ppermute | solution.py:292
  41.2 7.2 %collective-permute-start.5 = (bf16[784,128]{1,0:T(8,128)(2,1)}, bf16[784,128]{1,0:T(8,128)(2,1)S(1)}, u32[]{:S(2)}, u32[]{:S(2)}) collective-permute-start(bf16[784,128]{1,0:T(8,128)(2,1)} %get-tuple-element.53), channel_id=1, source_target_pairs={{0,0},{1,64},{4,4},{5,68},{8,8},{9,72},{12,12},{13,76},{64,1},{65,... | collective-permute-start | bytes 602120 | tf_op jit(solution)/shard_map/ppermute | solution.py:292
  46.3 29.5 %copy-start.1 = (bf16[784,128]{1,0:T(8,128)(2,1)}, bf16[784,128]{1,0:T(8,128)(2,1)S(1)}, u32[]{:S(2)}) copy-start(bf16[784,128]{1,0:T(8,128)(2,1)S(1)} %collective-permute-done.7.rest_2_) | copy-start | bytes 602116
  48.4 27.5 %copy-start.3 = (bf16[784,128]{1,0:T(8,128)(2,1)}, bf16[784,128]{1,0:T(8,128)(2,1)S(1)}, u32[]{:S(2)}) copy-start(bf16[784,128]{1,0:T(8,128)(2,1)S(1)} %collective-permute-done.6.rest_1_) | copy-start | bytes 602116
  48.4 14.1 %copy-start.5 = (bf16[784,128]{1,0:T(8,128)(2,1)}, bf16[784,128]{1,0:T(8,128)(2,1)S(1)}, u32[]{:S(2)}) copy-start(bf16[784,128]{1,0:T(8,128)(2,1)S(1)} %collective-permute-done.5.rest_0_) | copy-start | bytes 602116
  48.4 27.7 %collective-permute-start.9 = (bf16[16,2,256,128]{3,2,1,0:T(8,128)(2,1)S(1)}, bf16[16,2,256,128]{3,2,1,0:T(8,128)(2,1)}, u32[]{:S(2)}, u32[]{:S(2)}) collective-permute-start(bf16[16,2,256,128]{3,2,1,0:T(8,128)(2,1)S(1)} %bitcast.126), channel_id=1, source_target_pairs={{0,1},{1,0},{2,3},{3,2},{4,5},{5,4},{6,7},{7,6},{8,9},{9,8},{10,11... | collective-permute-start | bytes 6291464 | tf_op jit(solution)/shard_map/ppermute | solution.py:23
  58.5 56.4 %collective-permute-start.15 = (bf16[2,2048,256]{2,1,0:T(8,128)(2,1)}, bf16[2,2048,256]{2,1,0:T(8,128)(2,1)}, u32[]{:S(2)}, u32[]{:S(2)}) collective-permute-start(bf16[2,2048,256]{2,1,0:T(8,128)(2,1)} %param.21), channel_id=1, source_target_pairs={{1,9},{5,13},{9,1},{13,5},{3,11},{7,15},{11,3},{15,7},{17,25},{21,... | collective-permute-start | bytes 6291464 | tf_op jit(solution)/shard_map/ppermute | solution.py:317
  62.7 52.2 %collective-permute-start.16 = (bf16[256,2048]{1,0:T(8,128)(2,1)}, bf16[256,2048]{1,0:T(8,128)(2,1)}, u32[]{:S(2)}, u32[]{:S(2)}) collective-permute-start(bf16[256,2048]{1,0:T(8,128)(2,1)} %param.22), channel_id=1, source_target_pairs={{1,9},{5,13},{9,1},{13,5},{3,11},{7,15},{11,3},{15,7},{17,25},{21,... | collective-permute-start | bytes 3145736 | tf_op jit(solution)/shard_map/ppermute | solution.py:317
  64.4 50.5 %collective-permute-start.14 = (bf16[256,2048]{1,0:T(8,128)(2,1)}, bf16[256,2048]{1,0:T(8,128)(2,1)}, u32[]{:S(2)}, u32[]{:S(2)}) collective-permute-start(bf16[256,2048]{1,0:T(8,128)(2,1)} %param.22), channel_id=1, source_target_pairs={{0,4},{1,13},{4,8},{5,1},{8,12},{9,5},{12,0},{13,9},{2,6},{3,15},{... | collective-permute-start | bytes 3145736 | tf_op jit(solution)/shard_map/ppermute | solution.py:311
  76.1 0.9 copy-start.2
  77.0 0.9 copy-start.4
  78.0 0.9 copy-start.6
  99.7 2.7 %collective-permute-start.10 = (bf16[256,128]{1,0:T(8,128)(2,1)S(1)}, bf16[256,128]{1,0:T(8,128)(2,1)S(1)}, u32[]{:S(2)}, u32[]{:S(2)}) collective-permute-start(bf16[256,128]{1,0:T(8,128)(2,1)S(1)} %get-tuple-element.58), channel_id=1, source_target_pairs={{0,0},{1,64},{4,4},{5,68},{8,8},{9,72},{12,12},{13,76},{64,1},{65,... | collective-permute-start | bytes 196616 | tf_op jit(solution)/shard_map/ppermute | solution.py:398
  100.4 10.2 %collective-permute-start.13 = (bf16[256,128]{1,0:T(8,128)(2,1)S(1)}, bf16[256,128]{1,0:T(8,128)(2,1)S(1)}, u32[]{:S(2)}, u32[]{:S(2)}) collective-permute-start(bf16[256,128]{1,0:T(8,128)(2,1)S(1)} %get-tuple-element.59), channel_id=1, source_target_pairs={{0,4},{1,68},{4,8},{5,72},{8,12},{9,76},{12,0},{13,64},{64,5},{65,... | collective-permute-start | bytes 196616 | tf_op jit(solution)/shard_map/ppermute | solution.py:398
  102.5 8.1 %collective-permute-start.12 = (bf16[256,128]{1,0:T(8,128)(2,1)S(1)}, bf16[256,128]{1,0:T(8,128)(2,1)S(1)}, u32[]{:S(2)}, u32[]{:S(2)}) collective-permute-start(bf16[256,128]{1,0:T(8,128)(2,1)S(1)} %get-tuple-element.60), channel_id=1, source_target_pairs={{0,8},{1,72},{4,12},{5,76},{8,0},{9,64},{12,4},{13,68},{64,9},{65,... | collective-permute-start | bytes 196616 | tf_op jit(solution)/shard_map/ppermute | solution.py:398
  110.6 4.3 %collective-permute-start.11 = (bf16[256,128]{1,0:T(8,128)(2,1)S(1)}, bf16[256,128]{1,0:T(8,128)(2,1)S(1)}, u32[]{:S(2)}, u32[]{:S(2)}) collective-permute-start(bf16[256,128]{1,0:T(8,128)(2,1)S(1)} %get-tuple-element.61), channel_id=1, source_target_pairs={{0,12},{1,76},{4,0},{5,64},{8,4},{9,68},{12,8},{13,72},{64,13},{65... | collective-permute-start | bytes 196616 | tf_op jit(solution)/shard_map/ppermute | solution.py:398
  117.8 6.8 %copy-start.12 = (f32[2,2048]{1,0:T(2,128)S(1)}, f32[2,2048]{1,0:T(2,128)}, u32[]{:S(2)}) copy-start(f32[2,2048]{1,0:T(2,128)} %param.20) | copy-start | bytes 49156
  117.9 5.3 %collective-permute-start.17 = (bf16[2,64,2048]{2,1,0:T(8,128)(2,1)S(1)}, bf16[2,64,2048]{2,1,0:T(8,128)(2,1)S(1)}, u32[]{:S(2)}, u32[]{:S(2)}) collective-permute-start(bf16[2,64,2048]{2,1,0:T(8,128)(2,1)S(1)} %fusion.5), channel_id=1, source_target_pairs={{0,1},{1,0},{2,3},{3,2},{4,5},{5,4},{6,7},{7,6},{8,9},{9,8},{10,11... | collective-permute-start | bytes 1572872 | tf_op jit(solution)/shard_map/ppermute | solution.py:23
  123.3 8.7 %collective-permute-start.18 = (bf16[64,2048]{1,0:T(8,128)(2,1)S(1)}, bf16[64,2048]{1,0:T(8,128)(2,1)S(1)}, u32[]{:S(2)}, u32[]{:S(2)}) collective-permute-start(bf16[64,2048]{1,0:T(8,128)(2,1)S(1)} %fusion.6), channel_id=1, source_target_pairs={{0,2},{2,0},{1,3},{3,1},{4,6},{6,4},{5,7},{7,5},{8,10},{10,8},{9,1... | collective-permute-start | bytes 786440 | tf_op jit(solution)/shard_map/ppermute | solution.py:23
  133.5 34.7 %copy-start.11 = (bf16[256,2048]{1,0:T(8,128)(2,1)S(1)}, bf16[256,2048]{1,0:T(8,128)(2,1)}, u32[]{:S(2)}) copy-start(bf16[256,2048]{1,0:T(8,128)(2,1)} %param.22) | copy-start | bytes 3145732
  168.3 3.9 %copy-start.10 = (bf16[8,64,2048]{2,1,0:T(8,128)(2,1)}, bf16[8,64,2048]{2,1,0:T(8,128)(2,1)S(1)}, u32[]{:S(2)}) copy-start(bf16[8,64,2048]{2,1,0:T(8,128)(2,1)S(1)} %all_to_all.15) | copy-start | bytes 6291460
  168.3 4.3 %collective-permute-start.19 = (bf16[512,2048]{1,0:T(8,128)(2,1)S(1)}, bf16[512,2048]{1,0:T(8,128)(2,1)}, u32[]{:S(2)}, u32[]{:S(2)}) collective-permute-start(bf16[512,2048]{1,0:T(8,128)(2,1)S(1)} %bitcast.130), channel_id=1, source_target_pairs={{0,1},{1,0},{2,3},{3,2},{4,5},{5,4},{6,7},{7,6},{8,9},{9,8},{10,11... | collective-permute-start | bytes 6291464 | tf_op jit(solution)/shard_map/ppermute | solution.py:23
  179.0 7.3 %collective-permute-start.20 = (bf16[512,2048]{1,0:T(8,128)(2,1)S(1)}, bf16[512,2048]{1,0:T(8,128)(2,1)S(1)}, u32[]{:S(2)}, u32[]{:S(2)}) collective-permute-start(bf16[512,2048]{1,0:T(8,128)(2,1)S(1)} %shard_map.138), channel_id=1, source_target_pairs={{0,1},{1,0},{2,3},{3,2},{4,5},{5,4},{6,7},{7,6},{8,9},{9,8},{10,11... | collective-permute-start | bytes 6291464 | tf_op jit(solution)/shard_map/ppermute | solution.py:23

commit v6 on v5

--- a/solution.py
+++ b/solution.py
@@ -192,43 +192,54 @@
     )(nodes, lengths, lists, counts, *qkv_parts, row_info, seg_row, factors, key_factors, *parts)
 
 
-def feed_forward_body(tokens_ref, gu_a, dn_a, gu_b, dn_b, out_ref, tokens, gu, dn, made, sems):
-    rows = 256
-    blocks = tokens.shape[0] // rows
-
-    def block(ref, i):
-        return ref.at[pl.ds(i * rows, rows)]
-
-    def fetch(i):
-        return pltpu.make_async_copy(block(tokens_ref, i), block(tokens, i), sems.at[0, i])
+def feed_forward_body(
+    tokens_ref, gu_a, dn_a, gate_b, up_b, dn_b, out_ref, tokens, gu, dn, made, sems
+):
+    rows, width = tokens.shape
+    units = dn.shape[0] // 2
+    blocks = 2
+
+    def fetch():
+        return pltpu.make_async_copy(tokens_ref, tokens, sems.at[0])
+
+    gu_loads, dn_loads = [], []
+    pairs = ((gu_a.at[0], gu_a.at[1]), (gate_b, up_b))
+    for k, (pair, dn_ref) in enumerate(zip(pairs, (dn_a, dn_b))):
+        for j in range(2):
+            gu_loads.append(
+                pltpu.make_async_copy(
+                    pair[j],
+                    gu.at[:, pl.ds((2 * k + j) * units, units)],
+                    sems.at[1 + 2 * k + j],
+                )
+            )
+        dn_loads.append(
+            pltpu.make_async_copy(dn_ref, dn.at[pl.ds(k * units, units)], sems.at[5 + k])
+        )
 
     def store(i):
-        return pltpu.make_async_copy(block(made, i), block(out_ref, i), sems.at[1, i])
-
-    loads = [
-        pltpu.make_async_copy(source, target, sems.at[2 + j, k])
-        for k, pair in enumerate(((gu_a, dn_a), (gu_b, dn_b)))
-        for j, (source, target) in enumerate(((pair[0], gu.at[k]), (pair[1], dn.at[k])))
-    ]
-    fetch(0).start()
-    for load in loads:
+        part = pl.ds(i * (width // blocks), width // blocks)
+        return pltpu.make_async_copy(made.at[:, part], out_ref.at[:, part], sems.at[7 + i])
+
+    fetch().start()
+    for load in gu_loads + dn_loads:
         load.start()
-    for i in range(1, blocks):
-        fetch(i).start()
+    fetch().wait()
+    hidden = []
+    for k in range(2):
+        for load in gu_loads[2 * k : 2 * k + 2]:
+            load.wait()
+        both = jnp.dot(
+            tokens[...], gu[:, 2 * k * units : (2 * k + 2) * units], preferred_element_type=F32
+        )
+        gate, up = both[:, :units], both[:, units:]
+        hidden.append((gate / (1.0 + jnp.exp(-gate)) * up).astype(BF))
+    hidden = jnp.concatenate(hidden, axis=1)
+    for load in dn_loads:
+        load.wait()
     for i in range(blocks):
-        fetch(i).wait()
-        part = 0.0
-        for k in range(2):
-            if i == 0:
-                loads[2 * k].wait()
-            values = tokens[i * rows : (i + 1) * rows, :]
-            gate = jnp.dot(values, gu[k, 0], preferred_element_type=F32)
-            up = jnp.dot(values, gu[k, 1], preferred_element_type=F32)
-            hidden = (gate / (1.0 + jnp.exp(-gate)) * up).astype(BF)
-            if i == 0:
-                loads[2 * k + 1].wait()
-            part = part + jnp.dot(hidden, dn[k], preferred_element_type=F32)
-        made[i * rows : (i + 1) * rows, :] = part.astype(BF)
+        part = slice(i * (width // blocks), (i + 1) * (width // blocks))
+        made[:, part] = jnp.dot(hidden, dn[:, part], preferred_element_type=F32).astype(BF)
         store(i).start()
     for i in range(blocks):
         store(i).wait()
@@ -240,14 +251,14 @@
     return pl.pallas_call(
         feed_forward_body,
         out_shape=jax.ShapeDtypeStruct((rows, width), BF),
-        in_specs=[pl.BlockSpec(memory_space=pl.ANY)] * 5,
+        in_specs=[pl.BlockSpec(memory_space=pl.ANY)] * 6,
         out_specs=pl.BlockSpec(memory_space=pl.ANY),
         scratch_shapes=[
             pltpu.VMEM((rows, width), BF),
-            pltpu.VMEM((2, 2, width, units), BF),
-            pltpu.VMEM((2, units, width), BF),
+            pltpu.VMEM((width, 4 * units), BF),
+            pltpu.VMEM((2 * units, width), BF),
             pltpu.VMEM((rows, width), BF),
-            pltpu.SemaphoreType.DMA((4, 2)),
+            pltpu.SemaphoreType.DMA((9,)),
         ],
         compiler_params=pltpu.CompilerParams(vmem_limit_bytes=48 << 20),
         cost_estimate=pl.CostEstimate(
@@ -318,19 +329,17 @@
             weights, ("z", "core"), [(z * 2 + 1, (z + 2) % n_z * 2 + 1) for z in range(n_z)]
         )
 
-    gu_a = beside(w_gate_up)
-
     qkv_raw = jnp.einsum("td,cdw->ctw", states_in, w_qkv, preferred_element_type=F32)
     squares = jnp.sum(qkv_raw[:2] * qkv_raw[:2], axis=2)
+    for axis in ("core", "ylo"):
+        squares = squares + shift(squares, axis, 1)
     cached_own = spread(cached, "x").reshape((n_x * n_z,) + cached.shape[1:])
-    group_from = jnp.stack(
-        [blk] + [(core * n_x + x_at) * n_z + (z_at - g) % n_z for g in range(n_z)]
-    ).astype(jnp.int32)
-    segments = jnp.take(leaf_segment, group_from, axis=0)
-    middle, root, position = tree_info(
-        segments, jnp.take(leaf_node, group_from, axis=0), node_parent, node_length
-    )
-    position, middle, root, segments = position[0], middle[1:], root[1:], segments[1:]
+    def own_group(table):
+        return lax.dynamic_slice_in_dim(table, blk, 1, 0)
+
+    position = tree_info(
+        own_group(leaf_segment), own_group(leaf_node), node_parent, node_length
+    )[2][0]
     half = HD // 2
     frequency = THETA ** (-2.0 * jnp.arange(half, dtype=F32) / HD)
     angles = position.astype(F32)[:, None] * frequency[None, :]
@@ -354,17 +363,20 @@
         [turned(0), turned(1), qkv_raw[2].astype(BF).reshape(rows, heads_here, HD)]
     ).transpose(2, 0, 1, 3).reshape(heads_here, 3 * rows, HD)
     qkv = jnp.concatenate([qkv, jnp.broadcast_to(terms, (heads_here,) + terms.shape)], axis=1)
-    qkv, gu_a = lax.optimization_barrier((qkv, gu_a))
+    qkv, slot_node, node_length, node_parent, leaf_segment, leaf_node = (
+        lax.optimization_barrier(
+            (qkv, slot_node, node_length, node_parent, leaf_segment, leaf_node)
+        )
+    )
     qkv_parts = [across(select_row(qkv, (z_at + s) % n_z), s) for s in range(n_z)]
-    terms = jnp.stack([part[3 * rows : 3 * rows + term_rows] for part in qkv_parts]).astype(F32)
-    squares = jnp.sum(terms.reshape(n_z, 3, 2, rows), axis=1).transpose(0, 2, 1)
-    factors = lax.rsqrt(lax.psum(squares, ("yhi", "ylo")) / columns + EPS)
-    w_gate_up, w_down, qkv_parts = lax.optimization_barrier((w_gate_up, w_down, qkv_parts))
-    cached_own, qkv_parts = lax.optimization_barrier((cached_own, qkv_parts))
-    cached_parts = [cached_own, shift(cached_own, "core", 1)]
-
-    dn_a, gu_b, dn_b = beside(w_down), beyond(w_gate_up), beyond(w_down)
-
+
+    group_from = jnp.stack(
+        [(core * n_x + x_at) * n_z + (z_at - g) % n_z for g in range(n_z)]
+    ).astype(jnp.int32)
+    segments = jnp.take(leaf_segment, group_from, axis=0)
+    middle, root, _ = tree_info(
+        segments, jnp.take(leaf_node, group_from, axis=0), node_parent, node_length
+    )
     slots = slot_from.shape[0]
     slot_nodes = jnp.take(slot_node, slot_from)
     slot_lengths = jnp.take(node_length, slot_nodes)
@@ -385,10 +397,29 @@
     )
     counts = jnp.sum(needed.astype(jnp.int32), axis=2)
     row_info = jnp.stack([middle, root, segments], axis=-1)
+
+    terms = jnp.stack([part[3 * rows : 3 * rows + term_rows] for part in qkv_parts]).astype(F32)
+    squares = jnp.sum(terms.reshape(n_z, 3, 2, rows), axis=1).transpose(0, 2, 1)
+    factors = lax.rsqrt(squares / columns + EPS)
+    w_gate_up, w_down, qkv_parts = lax.optimization_barrier((w_gate_up, w_down, qkv_parts))
+    cached_own, qkv_parts, slot_nodes, slot_lengths, lists, counts, row_info, factors = (
+        lax.optimization_barrier(
+            (cached_own, qkv_parts, slot_nodes, slot_lengths, lists, counts, row_info, factors)
+        )
+    )
+    cached_parts = [cached_own, shift(cached_own, "core", 1)]
+
+    gu_a = beside(w_gate_up)
+
     attended = attention(
         slot_nodes, slot_lengths, lists, counts, qkv_parts, row_info, segments[:, None, :],
         factors, factors[:, None, :, 1], cached_parts,
     )
+
+    attended, gu_a, w_gate_up, w_down = lax.optimization_barrier(
+        (attended, gu_a, w_gate_up, w_down)
+    )
+    gate_b = beyond(w_gate_up[0])
 
     def back(values, s):
         pairs = [
@@ -398,7 +429,6 @@
         return lax.ppermute(values, corner, pairs)
 
     attended = jnp.concatenate([back(attended[s], s) for s in range(n_z)], axis=1)
-    attended, dn_a, gu_b, dn_b = lax.optimization_barrier((attended, dn_a, gu_b, dn_b))
     attn_part = jnp.dot(attended, w_out, preferred_element_type=F32)
     attn_part = attn_part.reshape(2, 2, rows // 4, -1)
 
@@ -414,10 +444,19 @@
     mid_state = (state_rows.astype(F32) + rms_norm(attn_proj, post_gain[0])).astype(BF)
 
     plane = ("yhi", "x")
+    mid_state, gate_b, w_gate_up, w_down = lax.optimization_barrier(
+        (mid_state, gate_b, w_gate_up, w_down)
+    )
+    up_b, dn_a, dn_b = beyond(w_gate_up[1]), beside(w_down), beyond(w_down)
+    tokens = spread(mid_state, plane)
+    tokens, up_b, dn_a, dn_b = lax.optimization_barrier((tokens, up_b, dn_a, dn_b))
+
+    def second(own, far):
+        return jnp.where(core == 0, own, far)
+
     weights = (
-        gu_a, dn_a, jnp.where(core == 0, w_gate_up, gu_b), jnp.where(core == 0, w_down, dn_b)
-    )
-    tokens = spread(mid_state, plane)
+        gu_a, dn_a, second(w_gate_up[0], gate_b), second(w_gate_up[1], up_b), second(w_down, dn_b)
+    )
     flat = tokens.reshape(-1, tokens.shape[2])
     other = feed_forward(shift(flat, "core", 1), weights)
     total = feed_forward(flat, weights).astype(F32) + shift(other, "core", 1).astype(F32)

time: 221 us -> 232 us (1.050)
  blocking collectives: 74.6 us -> 35.4 us
  starting transfers between devices: 42 us -> 59.3 us
  waiting for transfers between devices: 34.5 us -> 51.8 us
  local copies, waits for them, and re-layouts: 15 us -> 23.3 us
  other arithmetic: 11.7 us -> 19.3 us
    all_to_all x1 -> x0, blocking collectives: 34.7 us -> none  [spread(): return lax.all_to_all(copies, axes, 0, 0, tiled=True)]
    ppermute x5 -> x7, starting transfers between devices: 15.8 us -> 30.5 us  [shift(): return lax.ppermute(values, axis, [(i, (i + by) % n) for i in range(n)])]
    ppermute x2, waiting for transfers between devices: 8.58 us -> 22.3 us  [beside(): lax.ppermute(weights, ('z', 'core'), [(z * 2 + c, (z + 1 - 2 * c) % n_z *...]
    all_to_all x1 -> x2, waiting for transfers between devices: 0.01 us -> 12.6 us  [spread(): return lax.all_to_all(copies, axes, 0, 0, tiled=True)]
    psum x1 -> x0, blocking collectives: 8.52 us -> none  [on_device(): factors = lax.rsqrt(lax.psum(squares, ('yhi', 'ylo')) / columns + EPS)]
    ppermute x4, waiting for transfers between devices: 11.7 us -> 3.28 us  [back(): return lax.ppermute(values, corner, pairs)]
    unnamed x33 -> x50, local copies, waits for them, and re-layouts: 2.91 us -> 9.36 us
    ppermute x8, waiting for transfers between devices: 4.9 us -> 0.5 us  [across(): return lax.ppermute(values, corner, pairs)]
  transfers between devices with their start and end apart: 22 -> 26, of which waited for: 9 -> 11; matrix products, arithmetic and copies ran while one was open for 11% -> 12% of each run, Pallas kernels for 12% -> 11%
where the time goes in v6:
time: 232 us; the launch traced here: 230 us
  starting transfers between devices  59.3 us (26%)
  waiting for transfers between devices  51.8 us (22%)
  blocking collectives  35.4 us (15%)
  Pallas kernels  33.1 us (14%)
  local copies, waits for them, and re-layouts  23.3 us (10%)
  other arithmetic  19.3 us (8%)
  matrix products  7.52 us (3%)
    all_to_all x1, blocking collectives, on_device(): lax.all_to_all(total.astype(BF).reshape(tokens.shape), plane, 0, 0, tiled...  35.4 us
    ppermute x7, starting transfers between devices, shift(): return lax.ppermute(values, axis, [(i, (i + by) % n) for i in range(n)])  30.5 us
    ppermute x2, waiting for transfers between devices, beside(): lax.ppermute(weights, ('z', 'core'), [(z * 2 + c, (z + 1 - 2 * c) % n_z *...  22.3 us
    pallas_call x1, Pallas kernels, attention(): pl.pallas_call(attention_body, out_shape=jax.ShapeDtypeStruct((groups, ro...  19 us
    pallas_call x2, Pallas kernels, feed_forward(): pl.pallas_call(feed_forward_body, out_shape=jax.ShapeDtypeStruct((rows, w...  14.1 us
    ppermute x7, waiting for transfers between devices, shift(): return lax.ppermute(values, axis, [(i, (i + by) % n) for i in range(n)])  13.1 us
    all_to_all x2, waiting for transfers between devices, spread(): return lax.all_to_all(copies, axes, 0, 0, tiled=True)  12.6 us
    ppermute x8, starting transfers between devices, across(): return lax.ppermute(values, corner, pairs)  11.3 us
  transfers between devices with their start and end apart: 26, of which 11 were waited for; matrix products, arithmetic and copies ran while one was open for 12% of the time, Pallas kernels for 11%

profile of v6, /device:TPU:0, one launch (start us, length us, event | category | flops | bytes accessed | tf_op | source)
XLA Modules:
  0.0 230.3 jit_solution(6628776894292506990)
XLA Ops:
  0.0 1.2 constant_dynamic-slice_fusion.8
  1.2 4.0 %collective-permute-start.2 = (bf16[2,256,128]{2,1,0:T(8,128)(2,1)S(1)}, bf16[2,256,128]{2,1,0:T(8,128)(2,1)}, u32[]{:S(2)}, u32[]{:S(2)}) collective-permute-start(bf16[2,256,128]{2,1,0:T(8,128)(2,1)S(1)} %pad_maximum_fusion.4), channel_id=1, source_target_pairs={{0,8},{1,72},{4,12},{5,76},{8,0},{9,64},{12,4},{13,68},{64,9},{65,... | collective-permute-start | bytes 393224 | tf_op jit(solution)/shard_map/ppermute | solution.py:303
  6.1 1.4 collective-permute-start.1
  7.5 1.3 collective-permute-start
  8.8 4.7 %convolution_bitcast_fusion = f32[3,256,512]{1,2,0:T(8,128)S(1)} fusion(bf16[3,2048,512]{2,1,0:T(8,128)(2,1)} %param.17, bf16[256,2048]{1,0:T(8,128)(2,1)S(1)} %copy-done.18), kind=kOutput, calls=%fused_computation.10 | convolution fusion | flops 1610612736 | bytes 8912896 | tf_op jit(solution)/shard_map/td,cdw->ctw/dot_general | solution.py:332
  13.7 5.6 %collective-permute-start.4 = (f32[2,256]{1,0:T(2,128)S(1)}, f32[2,256]{1,0:T(2,128)S(1)}, u32[]{:S(2)}, u32[]{:S(2)}) collective-permute-start(f32[2,256]{1,0:T(2,128)S(1)} %fusion.3), channel_id=1, source_target_pairs={{0,1},{1,0},{2,3},{3,2},{4,5},{5,4},{6,7},{7,6},{8,9},{9,8},{10,11... | collective-permute-start | bytes 6152 | tf_op jit(solution)/shard_map/ppermute | solution.py:23
  21.2 1.4 collective-permute-start.5
  23.2 1.8 collective-permute-done.5
  27.9 1.2 pad_maximum_fusion.1
  29.1 1.8 broadcast_in_dim.141
  30.9 4.3 %all-to-all-start = ((bf16[4,4,2,256,128]{4,3,2,1,0:T(8,128)(2,1)}), bf16[4,4,2,256,128]{4,3,2,1,0:T(8,128)(2,1)S(1)}, u32[]{:S(2)}, u32[]{:S(2)}) async-start(bf16[4,4,2,256,128]{4,3,2,1,0:T(8,128)(2,1)} %broadcast_in_dim.141), calls=%async_computation | async-start | bytes 4194304 | tf_op jit(solution)/shard_map/all_to_all | solution.py:31
  37.4 1.9 collective-permute-start.9
  39.3 1.1 collective-permute-start.8
  41.2 1.2 pad_clamp_fusion.1
  42.4 1.4 gather_fusion.3
  45.1 1.4 convert_reduce_fusion.3
  46.5 1.8 select_reduce_fusion.2
  51.6 9.2 %all-to-all-done = bf16[4,4,2,256,128]{4,3,2,1,0:T(8,128)(2,1)S(1)} async-done(((bf16[4,4,2,256,128]{4,3,2,1,0:T(8,128)(2,1)}), bf16[4,4,2,256,128]{4,3,2,1,0:T(8,128)(2,1)S(1)}, u32[]{:S(2)}, u32[]{:S(2)}) %all-to-all-start) | async-done | bytes 2097184 | tf_op jit(solution)/shard_map/all_to_all | solution.py:31
  60.8 1.0 collective-permute-start.11
  64.4 0.9 copy.53.rest_4_
  66.3 0.9 copy-done.4
  67.2 0.9 copy-done.6
  68.1 19.0 %shard_map.136 = bf16[4,256,128]{2,1,0:T(8,128)(2,1)S(1)} custom-call(s32[32]{0:T(128)S(1)} %get-tuple-element.51.nodes_ref, s32[32]{0:T(128)S(1)} %and_select_fusion.lengths_ref, s32[4,2,12]{2,1,0:T(2,128)S(1)} %copy.51.lists_ref, s32[4,2]{1,0:T(4,128)S(1)} %copy.52.counts_ref, bf16[784,128]{1,0:T(8,128)(2,1)S(1)} %copy-done.6, ...), custom_call_target="tpu_custom_call" | custom-call | flops 2000000000 | bytes 6000000 | tf_op jit(solution)/shard_map/pallas_call | solution.py:169
  87.1 1.3 collective-permute-done.11.gu_a
  89.2 2.4 %collective-permute-start.14 = (bf16[256,128]{1,0:T(8,128)(2,1)S(1)}, bf16[256,128]{1,0:T(8,128)(2,1)S(1)}, u32[]{:S(2)}, u32[]{:S(2)}) collective-permute-start(bf16[256,128]{1,0:T(8,128)(2,1)S(1)} %get-tuple-element.98), channel_id=1, source_target_pairs={{0,8},{1,72},{4,12},{5,76},{8,0},{9,64},{12,4},{13,68},{64,9},{65,... | collective-permute-start | bytes 196616 | tf_op jit(solution)/shard_map/ppermute | solution.py:429
  91.6 1.4 collective-permute-start.13
  92.9 2.4 %collective-permute-done.15 = bf16[256,128]{1,0:T(8,128)(2,1)S(1)} collective-permute-done((bf16[256,128]{1,0:T(8,128)(2,1)S(1)}, bf16[256,128]{1,0:T(8,128)(2,1)S(1)}, u32[]{:S(2)}, u32[]{:S(2)}) %collective-permute-start.15) | collective-permute-done | bytes 65568 | tf_op jit(solution)/shard_map/ppermute | solution.py:429
  96.2 2.8 %fusion.1 = f32[256,2048]{1,0:T(8,128)S(1)} fusion(s32[]{:T(128)S(6)} %select_n.356, bf16[512,2048]{1,0:T(8,128)(2,1)} %param.19, bf16[256,128]{1,0:T(8,128)(2,1)S(1)} %collective-permute-done.15, bf16[256,128]{1,0:T(8,128)(2,1)S(1)} %collective-permute-done.14, bf16[256,128]{1,0:T(8,128)(2,1)S(1)} %collective-permute-done.13, ...), kind=kOutput, calls=%fused_computation.9 | convolution fusion | flops 542113792 | bytes 4456452 | tf_op jit(solution)/shard_map/dot_general | solution.py:432
  99.0 1.3 copy-done.10
  101.2 8.3 %collective-permute-start.16 = (bf16[2,64,2048]{2,1,0:T(8,128)(2,1)}, bf16[2,64,2048]{2,1,0:T(8,128)(2,1)}, u32[]{:S(2)}, u32[]{:S(2)}) collective-permute-start(bf16[2,64,2048]{2,1,0:T(8,128)(2,1)} %fusion.5), channel_id=1, source_target_pairs={{0,1},{1,0},{2,3},{3,2},{4,5},{5,4},{6,7},{7,6},{8,9},{9,8},{10,11... | collective-permute-start | bytes 1572872 | tf_op jit(solution)/shard_map/ppermute | solution.py:23
  110.4 0.9 collective-permute-done.16
  111.4 1.1 bitcast_add_fusion
  113.3 8.4 %collective-permute-done.17 = bf16[64,2048]{1,0:T(8,128)(2,1)S(1)} collective-permute-done((bf16[64,2048]{1,0:T(8,128)(2,1)S(1)}, bf16[64,2048]{1,0:T(8,128)(2,1)S(1)}, u32[]{:S(2)}, u32[]{:S(2)}) %collective-permute-start.17) | collective-permute-done | bytes 262176 | tf_op jit(solution)/shard_map/ppermute | solution.py:23
  121.9 1.1 add_convert_fusion.2
  123.0 1.6 broadcast_in_dim.164
  124.7 4.3 %all-to-all-start.1 = ((bf16[8,64,2048]{2,1,0:T(8,128)(2,1)}), bf16[8,64,2048]{2,1,0:T(8,128)(2,1)}, u32[]{:S(2)}, u32[]{:S(2)}) async-start(bf16[8,64,2048]{2,1,0:T(8,128)(2,1)} %broadcast_in_dim.164), calls=%async_computation.1 | async-start | bytes 4194304 | tf_op jit(solution)/shard_map/all_to_all | solution.py:31
  131.0 1.0 collective-permute-start.20
  132.0 1.0 copy-done.14
  133.0 1.1 copy-done.17
  134.0 21.0 %collective-permute-done.20.dn_a = bf16[256,2048]{1,0:T(8,128)(2,1)S(1)} collective-permute-done((bf16[256,2048]{1,0:T(8,128)(2,1)S(1)}, bf16[256,2048]{1,0:T(8,128)(2,1)S(1)}, u32[]{:S(2)}, u32[]{:S(2)}) %collective-permute-start.20) | collective-permute-done | bytes 1048608 | tf_op jit(solution)/shard_map/ppermute | solution.py:322
  155.1 3.4 %all-to-all-done.1 = bf16[8,64,2048]{2,1,0:T(8,128)(2,1)} async-done(((bf16[8,64,2048]{2,1,0:T(8,128)(2,1)}), bf16[8,64,2048]{2,1,0:T(8,128)(2,1)}, u32[]{:S(2)}, u32[]{:S(2)}) %all-to-all-start.1) | async-done | bytes 2097184 | tf_op jit(solution)/shard_map/all_to_all | solution.py:31
  158.4 13.9 %collective-permute-start.22 = (bf16[512,2048]{1,0:T(8,128)(2,1)}, bf16[512,2048]{1,0:T(8,128)(2,1)}, u32[]{:S(2)}, u32[]{:S(2)}) collective-permute-start(bf16[512,2048]{1,0:T(8,128)(2,1)} %bitcast.84.tokens_ref), channel_id=1, source_target_pairs={{0,1},{1,0},{2,3},{3,2},{4,5},{5,4},{6,7},{7,6},{8,9},{9,8},{10,11... | collective-permute-start | bytes 6291464 | tf_op jit(solution)/shard_map/ppermute | solution.py:23
  172.4 1.5 broadcast_select_fusion.dn_b
  174.4 2.1 collective-permute-done.22.tokens_ref
  176.5 7.1 %shard_map.138 = bf16[512,2048]{1,0:T(8,128)(2,1)} custom-call(bf16[512,2048]{1,0:T(8,128)(2,1)} %collective-permute-done.22.tokens_ref, bf16[2,2048,256]{2,1,0:T(8,128)(2,1)} %collective-permute-done.11.gu_a, bf16[256,2048]{1,0:T(8,128)(2,1)S(1)} %collective-permute-done.20.dn_a, bf16[2048,256]{1,0:T(8,128)(2,1)S(1)} %get-tuple-element.85.gate_b, ...), custom_call_target="tpu_custom_call" | custom-call | flops 3221225472 | bytes 10485760 | tf_op jit(solution)/shard_map/pallas_call | solution.py:251
  184.0 7.0 %shard_map.137 = bf16[512,2048]{1,0:T(8,128)(2,1)} custom-call(bf16[512,2048]{1,0:T(8,128)(2,1)} %bitcast.84.tokens_ref, bf16[2,2048,256]{2,1,0:T(8,128)(2,1)} %collective-permute-done.11.gu_a, bf16[256,2048]{1,0:T(8,128)(2,1)S(1)} %collective-permute-done.20.dn_a, bf16[2048,256]{1,0:T(8,128)(2,1)S(1)} %get-tuple-element.85.gate_b, ...), custom_call_target="tpu_custom_call" | custom-call | flops 3221225472 | bytes 10485760 | tf_op jit(solution)/shard_map/pallas_call | solution.py:251
  191.1 2.5 %add_convert_fusion = bf16[512,2048]{1,0:T(8,128)(2,1)S(1)} fusion(bf16[512,2048]{1,0:T(8,128)(2,1)S(1)} %collective-permute-done.23, bf16[512,2048]{1,0:T(8,128)(2,1)} %shard_map.137), kind=kLoop, calls=%fused_computation.7 | loop fusion | flops 4194304 | bytes 6291456 | tf_op jit(solution)/shard_map/convert_element_type | solution.py:463
  193.6 35.4 %all_to_all.15 = bf16[8,64,2048]{2,1,0:T(8,128)(2,1)S(1)} all-to-all(bf16[8,64,2048]{2,1,0:T(8,128)(2,1)S(1)} %bitcast.131), channel_id=1, replica_groups=mesh['yhi'=2,'x'=4,'z'=4,'ylo'=2,'core'=2] {'yhi','x'}, dimensions={0} | all-to-all | bytes 4194304 | tf_op jit(solution)/shard_map/all_to_all | solution.py:463
  (156 shorter events, 25.9 us)
Async XLA Ops:
  0.0 19.6 %copy-start = (s32[32,256]{1,0:T(8,128)S(1)}, s32[32,256]{1,0:T(8,128)}, u32[]{:S(2)}) copy-start(s32[32,256]{1,0:T(8,128)} %param.28) | copy-start | bytes 98308
  0.0 8.8 %copy-start.18 = (bf16[256,2048]{1,0:T(8,128)(2,1)S(1)}, bf16[256,2048]{1,0:T(8,128)(2,1)}, u32[]{:S(2)}) copy-start(bf16[256,2048]{1,0:T(8,128)(2,1)} %param.16) | copy-start | bytes 3145732
  1.2 26.7 %collective-permute-start.2 = (bf16[2,256,128]{2,1,0:T(8,128)(2,1)S(1)}, bf16[2,256,128]{2,1,0:T(8,128)(2,1)}, u32[]{:S(2)}, u32[]{:S(2)}) collective-permute-start(bf16[2,256,128]{2,1,0:T(8,128)(2,1)S(1)} %pad_maximum_fusion.4), channel_id=1, source_target_pairs={{0,8},{1,72},{4,12},{5,76},{8,0},{9,64},{12,4},{13,68},{64,9},{65,... | collective-permute-start | bytes 393224 | tf_op jit(solution)/shard_map/ppermute | solution.py:303
  5.3 22.6 %collective-permute-start.3 = (bf16[2,256,128]{2,1,0:T(8,128)(2,1)S(1)}, bf16[2,256,128]{2,1,0:T(8,128)(2,1)}, u32[]{:S(2)}, u32[]{:S(2)}) collective-permute-start(bf16[2,256,128]{2,1,0:T(8,128)(2,1)S(1)} %pad_maximum_fusion.5), channel_id=1, source_target_pairs={{0,12},{1,76},{4,0},{5,64},{8,4},{9,68},{12,8},{13,72},{64,13},{65... | collective-permute-start | bytes 393224 | tf_op jit(solution)/shard_map/ppermute | solution.py:303
  6.1 21.8 %collective-permute-start.1 = (bf16[2,256,128]{2,1,0:T(8,128)(2,1)S(1)}, bf16[2,256,128]{2,1,0:T(8,128)(2,1)}, u32[]{:S(2)}, u32[]{:S(2)}) collective-permute-start(bf16[2,256,128]{2,1,0:T(8,128)(2,1)S(1)} %pad_maximum_fusion.3), channel_id=1, source_target_pairs={{0,4},{1,68},{4,8},{5,72},{8,12},{9,76},{12,0},{13,64},{64,5},{65,... | collective-permute-start | bytes 393224 | tf_op jit(solution)/shard_map/ppermute | solution.py:303
  7.5 20.4 %collective-permute-start = (bf16[2,256,128]{2,1,0:T(8,128)(2,1)S(1)}, bf16[2,256,128]{2,1,0:T(8,128)(2,1)}, u32[]{:S(2)}, u32[]{:S(2)}) collective-permute-start(bf16[2,256,128]{2,1,0:T(8,128)(2,1)S(1)} %pad_maximum_fusion.2), channel_id=1, source_target_pairs={{0,0},{1,64},{4,4},{5,68},{8,8},{9,72},{12,12},{13,76},{64,1},{65,... | collective-permute-start | bytes 393224 | tf_op jit(solution)/shard_map/ppermute | solution.py:303
  13.5 5.9 %copy-start.20 = (s32[32,8]{0,1:T(8,128)S(1)}, s32[32,8]{0,1:T(8,128)}, u32[]{:S(2)}) copy-start(s32[32,8]{0,1:T(8,128)} %param.29) | copy-start | bytes 3076
  13.5 6.6 %copy-start.23 = (f32[2,512]{1,0:T(2,128)S(1)}, f32[2,512]{1,0:T(2,128)}, u32[]{:S(2)}) copy-start(f32[2,512]{1,0:T(2,128)} %param.18) | copy-start | bytes 12292
  13.5 6.7 %copy-start.24 = (s32[28]{0:T(128)S(1)}, s32[28]{0:T(128)}, u32[]{:S(2)}) copy-start(s32[28]{0:T(128)} %param.27) | copy-start | bytes 340
  13.5 6.8 %copy-start.7 = (s32[32]{0:T(128)S(1)}, s32[32]{0:T(128)}, u32[]{:S(2)}) copy-start(s32[32]{0:T(128)} %param.26) | copy-start | bytes 388
  13.7 7.6 %collective-permute-start.4 = (f32[2,256]{1,0:T(2,128)S(1)}, f32[2,256]{1,0:T(2,128)S(1)}, u32[]{:S(2)}, u32[]{:S(2)}) collective-permute-start(f32[2,256]{1,0:T(2,128)S(1)} %fusion.3), channel_id=1, source_target_pairs={{0,1},{1,0},{2,3},{3,2},{4,5},{5,4},{6,7},{7,6},{8,9},{9,8},{10,11... | collective-permute-start | bytes 6152 | tf_op jit(solution)/shard_map/ppermute | solution.py:23
  21.1 5.5 %copy-start.8 = (s32[32]{0:T(128)S(1)}, s32[32]{0:T(128)}, u32[]{:S(2)}) copy-start(s32[32]{0:T(128)} %param.25) | copy-start | bytes 388
  21.2 3.7 %collective-permute-start.5 = (f32[2,256]{1,0:T(2,128)S(1)}, f32[2,256]{1,0:T(2,128)S(1)}, u32[]{:S(2)}, u32[]{:S(2)}) collective-permute-start(f32[2,256]{1,0:T(2,128)S(1)} %add.413), channel_id=1, source_target_pairs={{0,2},{2,0},{1,3},{3,1},{4,6},{6,4},{5,7},{7,5},{8,10},{10,8},{9,1... | collective-permute-start | bytes 6152 | tf_op jit(solution)/shard_map/ppermute | solution.py:23
  22.7 3.7 %copy-start.22 = (pred[4]{0:T(512)(128)(4,1)}, pred[4]{0:T(512)(128)(4,1)S(1)}, u32[]{:S(2)}) copy-start(pred[4]{0:T(512)(128)(4,1)S(1)} %compare_and_fusion) | copy-start | bytes 16
  30.9 29.9 %all-to-all-start = ((bf16[4,4,2,256,128]{4,3,2,1,0:T(8,128)(2,1)}), bf16[4,4,2,256,128]{4,3,2,1,0:T(8,128)(2,1)S(1)}, u32[]{:S(2)}, u32[]{:S(2)}) async-start(bf16[4,4,2,256,128]{4,3,2,1,0:T(8,128)(2,1)} %broadcast_in_dim.141), calls=%async_computation | async-start | bytes 4194304 | tf_op jit(solution)/shard_map/all_to_all | solution.py:31
  37.4 12.0 %collective-permute-start.9 = (bf16[784,128]{1,0:T(8,128)(2,1)}, bf16[784,128]{1,0:T(8,128)(2,1)S(1)}, u32[]{:S(2)}, u32[]{:S(2)}) collective-permute-start(bf16[784,128]{1,0:T(8,128)(2,1)} %get-tuple-element.88), channel_id=1, source_target_pairs={{0,12},{1,76},{4,0},{5,64},{8,4},{9,68},{12,8},{13,72},{64,13},{65... | collective-permute-start | bytes 602120 | tf_op jit(solution)/shard_map/ppermute | solution.py:303
  39.3 10.1 %collective-permute-start.8 = (bf16[784,128]{1,0:T(8,128)(2,1)S(1)}, bf16[784,128]{1,0:T(8,128)(2,1)S(1)}, u32[]{:S(2)}, u32[]{:S(2)}) collective-permute-start(bf16[784,128]{1,0:T(8,128)(2,1)S(1)} %get-tuple-element.89), channel_id=1, source_target_pairs={{0,8},{1,72},{4,12},{5,76},{8,0},{9,64},{12,4},{13,68},{64,9},{65,... | collective-permute-start | bytes 602120 | tf_op jit(solution)/shard_map/ppermute | solution.py:303
  40.5 9.6 %collective-permute-start.7 = (bf16[784,128]{1,0:T(8,128)(2,1)S(1)}, bf16[784,128]{1,0:T(8,128)(2,1)S(1)}, u32[]{:S(2)}, u32[]{:S(2)}) collective-permute-start(bf16[784,128]{1,0:T(8,128)(2,1)S(1)} %get-tuple-element.90), channel_id=1, source_target_pairs={{0,4},{1,68},{4,8},{5,72},{8,12},{9,76},{12,0},{13,64},{64,5},{65,... | collective-permute-start | bytes 602120 | tf_op jit(solution)/shard_map/ppermute | solution.py:303
  40.5 10.3 %collective-permute-start.6 = (bf16[784,128]{1,0:T(8,128)(2,1)S(1)}, bf16[784,128]{1,0:T(8,128)(2,1)S(1)}, u32[]{:S(2)}, u32[]{:S(2)}) collective-permute-start(bf16[784,128]{1,0:T(8,128)(2,1)S(1)} %get-tuple-element.91), channel_id=1, source_target_pairs={{0,0},{1,64},{4,4},{5,68},{8,8},{9,72},{12,12},{13,76},{64,1},{65,... | collective-permute-start | bytes 602120 | tf_op jit(solution)/shard_map/ppermute | solution.py:303
  49.4 0.7 copy-start.1
  60.8 4.5 %collective-permute-start.10 = (bf16[16,2,256,128]{3,2,1,0:T(8,128)(2,1)S(1)}, bf16[16,2,256,128]{3,2,1,0:T(8,128)(2,1)}, u32[]{:S(2)}, u32[]{:S(2)}) collective-permute-start(bf16[16,2,256,128]{3,2,1,0:T(8,128)(2,1)S(1)} %bitcast.129), channel_id=1, source_target_pairs={{0,1},{1,0},{2,3},{3,2},{4,5},{5,4},{6,7},{7,6},{8,9},{9,8},{10,11... | collective-permute-start | bytes 6291464 | tf_op jit(solution)/shard_map/ppermute | solution.py:23
  60.8 27.6 %collective-permute-start.11 = (bf16[2,2048,256]{2,1,0:T(8,128)(2,1)}, bf16[2,2048,256]{2,1,0:T(8,128)(2,1)}, u32[]{:S(2)}, u32[]{:S(2)}) collective-permute-start(bf16[2,2048,256]{2,1,0:T(8,128)(2,1)} %param.21), channel_id=1, source_target_pairs={{0,4},{1,13},{4,8},{5,1},{8,12},{9,5},{12,0},{13,9},{2,6},{3,15},{... | collective-permute-start | bytes 6291464 | tf_op jit(solution)/shard_map/ppermute | solution.py:322
  65.3 0.9 copy-start.2
  66.3 0.9 copy-start.4
  67.2 0.9 copy-start.6
  88.4 4.5 %collective-permute-start.12 = (bf16[256,128]{1,0:T(8,128)(2,1)S(1)}, bf16[256,128]{1,0:T(8,128)(2,1)S(1)}, u32[]{:S(2)}, u32[]{:S(2)}) collective-permute-start(bf16[256,128]{1,0:T(8,128)(2,1)S(1)} %get-tuple-element.96), channel_id=1, source_target_pairs={{0,0},{1,64},{4,4},{5,68},{8,8},{9,72},{12,12},{13,76},{64,1},{65,... | collective-permute-start | bytes 196616 | tf_op jit(solution)/shard_map/ppermute | solution.py:429
  89.1 6.2 %collective-permute-start.15 = (bf16[256,128]{1,0:T(8,128)(2,1)S(1)}, bf16[256,128]{1,0:T(8,128)(2,1)S(1)}, u32[]{:S(2)}, u32[]{:S(2)}) collective-permute-start(bf16[256,128]{1,0:T(8,128)(2,1)S(1)} %get-tuple-element.97), channel_id=1, source_target_pairs={{0,4},{1,68},{4,8},{5,72},{8,12},{9,76},{12,0},{13,64},{64,5},{65,... | collective-permute-start | bytes 196616 | tf_op jit(solution)/shard_map/ppermute | solution.py:429
  89.2 6.2 %collective-permute-start.14 = (bf16[256,128]{1,0:T(8,128)(2,1)S(1)}, bf16[256,128]{1,0:T(8,128)(2,1)S(1)}, u32[]{:S(2)}, u32[]{:S(2)}) collective-permute-start(bf16[256,128]{1,0:T(8,128)(2,1)S(1)} %get-tuple-element.98), channel_id=1, source_target_pairs={{0,8},{1,72},{4,12},{5,76},{8,0},{9,64},{12,4},{13,68},{64,9},{65,... | collective-permute-start | bytes 196616 | tf_op jit(solution)/shard_map/ppermute | solution.py:429
  91.6 4.6 %collective-permute-start.13 = (bf16[256,128]{1,0:T(8,128)(2,1)S(1)}, bf16[256,128]{1,0:T(8,128)(2,1)S(1)}, u32[]{:S(2)}, u32[]{:S(2)}) collective-permute-start(bf16[256,128]{1,0:T(8,128)(2,1)S(1)} %get-tuple-element.99), channel_id=1, source_target_pairs={{0,12},{1,76},{4,0},{5,64},{8,4},{9,68},{12,8},{13,72},{64,13},{65... | collective-permute-start | bytes 196616 | tf_op jit(solution)/shard_map/ppermute | solution.py:429
  92.9 16.6 %copy-start.9 = (bf16[2,2048,256]{2,1,0:T(8,128)(2,1)S(1)}, bf16[2,2048,256]{2,1,0:T(8,128)(2,1)}, u32[]{:S(2)}) copy-start(bf16[2,2048,256]{2,1,0:T(8,128)(2,1)} %param.21) | copy-start | bytes 6291460
  99.0 1.3 copy-start.10
  101.2 10.2 %collective-permute-start.16 = (bf16[2,64,2048]{2,1,0:T(8,128)(2,1)}, bf16[2,64,2048]{2,1,0:T(8,128)(2,1)}, u32[]{:S(2)}, u32[]{:S(2)}) collective-permute-start(bf16[2,64,2048]{2,1,0:T(8,128)(2,1)} %fusion.5), channel_id=1, source_target_pairs={{0,1},{1,0},{2,3},{3,2},{4,5},{5,4},{6,7},{7,6},{8,9},{9,8},{10,11... | collective-permute-start | bytes 1572872 | tf_op jit(solution)/shard_map/ppermute | solution.py:23
  109.5 1.9 copy-start.11
  109.5 3.8 %copy-start.21 = (f32[2,2048]{1,0:T(2,128)S(1)}, f32[2,2048]{1,0:T(2,128)}, u32[]{:S(2)}) copy-start(f32[2,2048]{1,0:T(2,128)} %param.20) | copy-start | bytes 49156
  109.6 13.5 %collective-permute-start.18 = (bf16[2048,256]{1,0:T(8,128)(2,1)S(1)}, bf16[2048,256]{1,0:T(8,128)(2,1)S(1)}, u32[]{:S(2)}, u32[]{:S(2)}) collective-permute-start(bf16[2048,256]{1,0:T(8,128)(2,1)S(1)} %slice_bitcast_fusion.1), channel_id=1, source_target_pairs={{1,9},{5,13},{9,1},{13,5},{3,11},{7,15},{11,3},{15,7},{17,25},{21,... | collective-permute-start | bytes 3145736 | tf_op jit(solution)/shard_map/ppermute | solution.py:328
  112.6 9.2 %collective-permute-start.17 = (bf16[64,2048]{1,0:T(8,128)(2,1)S(1)}, bf16[64,2048]{1,0:T(8,128)(2,1)S(1)}, u32[]{:S(2)}, u32[]{:S(2)}) collective-permute-start(bf16[64,2048]{1,0:T(8,128)(2,1)S(1)} %fusion.6), channel_id=1, source_target_pairs={{0,2},{2,0},{1,3},{3,1},{4,6},{6,4},{5,7},{7,5},{8,10},{10,8},{9,1... | collective-permute-start | bytes 786440 | tf_op jit(solution)/shard_map/ppermute | solution.py:23
  123.0 1.6 copy-start.12
  124.7 33.8 %all-to-all-start.1 = ((bf16[8,64,2048]{2,1,0:T(8,128)(2,1)}), bf16[8,64,2048]{2,1,0:T(8,128)(2,1)}, u32[]{:S(2)}, u32[]{:S(2)}) async-start(bf16[8,64,2048]{2,1,0:T(8,128)(2,1)} %broadcast_in_dim.164), calls=%async_computation.1 | async-start | bytes 4194304 | tf_op jit(solution)/shard_map/all_to_all | solution.py:31
  129.0 1.2 copy-start.16
  129.1 2.9 %collective-permute-start.19 = (bf16[2048,256]{1,0:T(8,128)(2,1)S(1)}, bf16[2048,256]{1,0:T(8,128)(2,1)S(1)}, u32[]{:S(2)}, u32[]{:S(2)}) collective-permute-start(bf16[2048,256]{1,0:T(8,128)(2,1)S(1)} %slice_bitcast_fusion), channel_id=1, source_target_pairs={{1,9},{5,13},{9,1},{13,5},{3,11},{7,15},{11,3},{15,7},{17,25},{21,... | collective-permute-start | bytes 3145736 | tf_op jit(solution)/shard_map/ppermute | solution.py:328
  130.2 2.7 %collective-permute-start.21 = (bf16[256,2048]{1,0:T(8,128)(2,1)S(1)}, bf16[256,2048]{1,0:T(8,128)(2,1)S(1)}, u32[]{:S(2)}, u32[]{:S(2)}) collective-permute-start(bf16[256,2048]{1,0:T(8,128)(2,1)S(1)} %copy-done.16), channel_id=1, source_target_pairs={{1,9},{5,13},{9,1},{13,5},{3,11},{7,15},{11,3},{15,7},{17,25},{21,... | collective-permute-start | bytes 3145736 | tf_op jit(solution)/shard_map/ppermute | solution.py:328
  131.0 24.1 %collective-permute-start.20 = (bf16[256,2048]{1,0:T(8,128)(2,1)S(1)}, bf16[256,2048]{1,0:T(8,128)(2,1)S(1)}, u32[]{:S(2)}, u32[]{:S(2)}) collective-permute-start(bf16[256,2048]{1,0:T(8,128)(2,1)S(1)} %copy-done.16), channel_id=1, source_target_pairs={{0,4},{1,13},{4,8},{5,1},{8,12},{9,5},{12,0},{13,9},{2,6},{3,15},{... | collective-permute-start | bytes 3145736 | tf_op jit(solution)/shard_map/ppermute | solution.py:322
  132.0 1.0 copy-start.14
  133.0 1.1 copy-start.17
  158.4 18.1 %collective-permute-start.22 = (bf16[512,2048]{1,0:T(8,128)(2,1)}, bf16[512,2048]{1,0:T(8,128)(2,1)}, u32[]{:S(2)}, u32[]{:S(2)}) collective-permute-start(bf16[512,2048]{1,0:T(8,128)(2,1)} %bitcast.84.tokens_ref), channel_id=1, source_target_pairs={{0,1},{1,0},{2,3},{3,2},{4,5},{5,4},{6,7},{7,6},{8,9},{9,8},{10,11... | collective-permute-start | bytes 6291464 | tf_op jit(solution)/shard_map/ppermute | solution.py:23
  172.4 1.5 copy-start.13
  172.4 1.9 copy-start.15
  183.6 7.5 %collective-permute-start.23 = (bf16[512,2048]{1,0:T(8,128)(2,1)}, bf16[512,2048]{1,0:T(8,128)(2,1)S(1)}, u32[]{:S(2)}, u32[]{:S(2)}) collective-permute-start(bf16[512,2048]{1,0:T(8,128)(2,1)} %shard_map.138), channel_id=1, source_target_pairs={{0,1},{1,0},{2,3},{3,2},{4,5},{5,4},{6,7},{7,6},{8,9},{9,8},{10,11... | collective-permute-start | bytes 6291464 | tf_op jit(solution)/shard_map/ppermute | solution.py:23
  (3 other events, 1.9 us)

commit v7 on v5

--- a/solution.py
+++ b/solution.py
@@ -318,19 +318,17 @@
             weights, ("z", "core"), [(z * 2 + 1, (z + 2) % n_z * 2 + 1) for z in range(n_z)]
         )
 
-    gu_a = beside(w_gate_up)
-
     qkv_raw = jnp.einsum("td,cdw->ctw", states_in, w_qkv, preferred_element_type=F32)
     squares = jnp.sum(qkv_raw[:2] * qkv_raw[:2], axis=2)
+    for axis in ("core", "ylo"):
+        squares = squares + shift(squares, axis, 1)
     cached_own = spread(cached, "x").reshape((n_x * n_z,) + cached.shape[1:])
-    group_from = jnp.stack(
-        [blk] + [(core * n_x + x_at) * n_z + (z_at - g) % n_z for g in range(n_z)]
-    ).astype(jnp.int32)
-    segments = jnp.take(leaf_segment, group_from, axis=0)
-    middle, root, position = tree_info(
-        segments, jnp.take(leaf_node, group_from, axis=0), node_parent, node_length
-    )
-    position, middle, root, segments = position[0], middle[1:], root[1:], segments[1:]
+    def own_group(table):
+        return lax.dynamic_slice_in_dim(table, blk, 1, 0)
+
+    position = tree_info(
+        own_group(leaf_segment), own_group(leaf_node), node_parent, node_length
+    )[2][0]
     half = HD // 2
     frequency = THETA ** (-2.0 * jnp.arange(half, dtype=F32) / HD)
     angles = position.astype(F32)[:, None] * frequency[None, :]
@@ -354,17 +352,20 @@
         [turned(0), turned(1), qkv_raw[2].astype(BF).reshape(rows, heads_here, HD)]
     ).transpose(2, 0, 1, 3).reshape(heads_here, 3 * rows, HD)
     qkv = jnp.concatenate([qkv, jnp.broadcast_to(terms, (heads_here,) + terms.shape)], axis=1)
-    qkv, gu_a = lax.optimization_barrier((qkv, gu_a))
+    qkv, slot_node, node_length, node_parent, leaf_segment, leaf_node = (
+        lax.optimization_barrier(
+            (qkv, slot_node, node_length, node_parent, leaf_segment, leaf_node)
+        )
+    )
     qkv_parts = [across(select_row(qkv, (z_at + s) % n_z), s) for s in range(n_z)]
-    terms = jnp.stack([part[3 * rows : 3 * rows + term_rows] for part in qkv_parts]).astype(F32)
-    squares = jnp.sum(terms.reshape(n_z, 3, 2, rows), axis=1).transpose(0, 2, 1)
-    factors = lax.rsqrt(lax.psum(squares, ("yhi", "ylo")) / columns + EPS)
-    w_gate_up, w_down, qkv_parts = lax.optimization_barrier((w_gate_up, w_down, qkv_parts))
-    cached_own, qkv_parts = lax.optimization_barrier((cached_own, qkv_parts))
-    cached_parts = [cached_own, shift(cached_own, "core", 1)]
-
-    dn_a, gu_b, dn_b = beside(w_down), beyond(w_gate_up), beyond(w_down)
-
+
+    group_from = jnp.stack(
+        [(core * n_x + x_at) * n_z + (z_at - g) % n_z for g in range(n_z)]
+    ).astype(jnp.int32)
+    segments = jnp.take(leaf_segment, group_from, axis=0)
+    middle, root, _ = tree_info(
+        segments, jnp.take(leaf_node, group_from, axis=0), node_parent, node_length
+    )
     slots = slot_from.shape[0]
     slot_nodes = jnp.take(slot_node, slot_from)
     slot_lengths = jnp.take(node_length, slot_nodes)
@@ -385,10 +386,29 @@
     )
     counts = jnp.sum(needed.astype(jnp.int32), axis=2)
     row_info = jnp.stack([middle, root, segments], axis=-1)
+
+    terms = jnp.stack([part[3 * rows : 3 * rows + term_rows] for part in qkv_parts]).astype(F32)
+    squares = jnp.sum(terms.reshape(n_z, 3, 2, rows), axis=1).transpose(0, 2, 1)
+    factors = lax.rsqrt(squares / columns + EPS)
+    w_gate_up, w_down, qkv_parts = lax.optimization_barrier((w_gate_up, w_down, qkv_parts))
+    cached_own, qkv_parts, slot_nodes, slot_lengths, lists, counts, row_info, factors = (
+        lax.optimization_barrier(
+            (cached_own, qkv_parts, slot_nodes, slot_lengths, lists, counts, row_info, factors)
+        )
+    )
+    cached_parts = [cached_own, shift(cached_own, "core", 1)]
+
+    gu_a = beside(w_gate_up)
+
     attended = attention(
         slot_nodes, slot_lengths, lists, counts, qkv_parts, row_info, segments[:, None, :],
         factors, factors[:, None, :, 1], cached_parts,
     )
+
+    attended, gu_a, w_gate_up, w_down = lax.optimization_barrier(
+        (attended, gu_a, w_gate_up, w_down)
+    )
+    gu_b = beyond(w_gate_up)
 
     def back(values, s):
         pairs = [
@@ -398,7 +418,6 @@
         return lax.ppermute(values, corner, pairs)
 
     attended = jnp.concatenate([back(attended[s], s) for s in range(n_z)], axis=1)
-    attended, dn_a, gu_b, dn_b = lax.optimization_barrier((attended, dn_a, gu_b, dn_b))
     attn_part = jnp.dot(attended, w_out, preferred_element_type=F32)
     attn_part = attn_part.reshape(2, 2, rows // 4, -1)
 
@@ -406,6 +425,7 @@
         return lax.dynamic_index_in_dim(attn_part, c, 1, keepdims=False)
 
     attn_part = of_core(core) + shift(of_core(1 - core).astype(BF), "core", 1).astype(F32)
+    attn_part, gu_b, w_down = lax.optimization_barrier((attn_part, gu_b, w_down))
     attn_proj = select_row(attn_part, ylo) + shift(
         select_row(attn_part, 1 - ylo).astype(BF), "ylo", 1
     ).astype(F32)
@@ -414,10 +434,13 @@
     mid_state = (state_rows.astype(F32) + rms_norm(attn_proj, post_gain[0])).astype(BF)
 
     plane = ("yhi", "x")
+    mid_state, w_down = lax.optimization_barrier((mid_state, w_down))
+    dn_a, dn_b = beside(w_down), beyond(w_down)
+    tokens = spread(mid_state, plane)
+    tokens, dn_a, dn_b = lax.optimization_barrier((tokens, dn_a, dn_b))
     weights = (
         gu_a, dn_a, jnp.where(core == 0, w_gate_up, gu_b), jnp.where(core == 0, w_down, dn_b)
     )
-    tokens = spread(mid_state, plane)
     flat = tokens.reshape(-1, tokens.shape[2])
     other = feed_forward(shift(flat, "core", 1), weights)
     total = feed_forward(flat, weights).astype(F32) + shift(other, "core", 1).astype(F32)

time: 221 us -> 231 us (1.045)
  blocking collectives: 74.6 us -> 35.7 us
  starting transfers between devices: 42 us -> 63.1 us
  waiting for transfers between devices: 34.5 us -> 49.4 us
  other arithmetic: 11.7 us -> 20.5 us
  local copies, waits for them, and re-layouts: 15 us -> 19.5 us
    all_to_all x1 -> x0, blocking collectives: 34.7 us -> none  [spread(): return lax.all_to_all(copies, axes, 0, 0, tiled=True)]
    all_to_all x1 -> x2, starting transfers between devices: 4.29 us -> 26.5 us  [spread(): return lax.all_to_all(copies, axes, 0, 0, tiled=True)]
    ppermute x2, waiting for transfers between devices: 8.58 us -> 26.8 us  [beside(): lax.ppermute(weights, ('z', 'core'), [(z * 2 + c, (z + 1 - 2 * c) % n_z *...]
    all_to_all x1 -> x2, waiting for transfers between devices: 0.01 us -> 9.26 us  [spread(): return lax.all_to_all(copies, axes, 0, 0, tiled=True)]
    psum x1 -> x0, blocking collectives: 8.52 us -> none  [on_device(): factors = lax.rsqrt(lax.psum(squares, ('yhi', 'ylo')) / columns + EPS)]
    ppermute x4, waiting for transfers between devices: 11.7 us -> 3.7 us  [back(): return lax.ppermute(values, corner, pairs)]
    all_to_all x1, blocking collectives: 31.4 us -> 35.7 us  [on_device(): lax.all_to_all(total.astype(BF).reshape(tokens.shape), plane, 0, 0, tiled...]
    ppermute x8, waiting for transfers between devices: 4.9 us -> 0.65 us  [across(): return lax.ppermute(values, corner, pairs)]
  transfers between devices with their start and end apart: 22 -> 25, of which waited for: 9 -> 9; matrix products, arithmetic and copies ran while one was open for 11% -> 14% of each run, Pallas kernels for 12% -> 12%
where the time goes in v7:
time: 231 us; the launch traced here: 230 us
  starting transfers between devices  63.1 us (27%)
  waiting for transfers between devices  49.4 us (21%)
  blocking collectives  35.7 us (15%)
  Pallas kernels  33.4 us (14%)
  other arithmetic  20.5 us (9%)
  local copies, waits for them, and re-layouts  19.5 us (8%)
  matrix products  7.51 us (3%)
    all_to_all x1, blocking collectives, on_device(): lax.all_to_all(total.astype(BF).reshape(tokens.shape), plane, 0, 0, tiled...  35.7 us
    ppermute x2, waiting for transfers between devices, beside(): lax.ppermute(weights, ('z', 'core'), [(z * 2 + c, (z + 1 - 2 * c) % n_z *...  26.8 us
    all_to_all x2, starting transfers between devices, spread(): return lax.all_to_all(copies, axes, 0, 0, tiled=True)  26.5 us
    pallas_call x1, Pallas kernels, attention(): pl.pallas_call(attention_body, out_shape=jax.ShapeDtypeStruct((groups, ro...  20.8 us
    ppermute x7, starting transfers between devices, shift(): return lax.ppermute(values, axis, [(i, (i + by) % n) for i in range(n)])  16.1 us
    pallas_call x2, Pallas kernels, feed_forward(): pl.pallas_call(feed_forward_body, out_shape=jax.ShapeDtypeStruct((rows, w...  12.6 us
    ppermute x8, starting transfers between devices, across(): return lax.ppermute(values, corner, pairs)  11.3 us
    all_to_all x2, waiting for transfers between devices, spread(): return lax.all_to_all(copies, axes, 0, 0, tiled=True)  9.26 us
  transfers between devices with their start and end apart: 25, of which 9 were waited for; matrix products, arithmetic and copies ran while one was open for 14% of the time, Pallas kernels for 12%

profile of v7, /device:TPU:0, one launch (start us, length us, event | category | flops | bytes accessed | tf_op | source)
XLA Modules:
  0.0 229.7 jit_solution(1267967995461542763)
XLA Ops:
  0.0 1.2 constant_dynamic-slice_fusion.8
  1.2 4.0 %collective-permute-start.2 = (bf16[2,256,128]{2,1,0:T(8,128)(2,1)S(1)}, bf16[2,256,128]{2,1,0:T(8,128)(2,1)}, u32[]{:S(2)}, u32[]{:S(2)}) collective-permute-start(bf16[2,256,128]{2,1,0:T(8,128)(2,1)S(1)} %pad_maximum_fusion.4), channel_id=1, source_target_pairs={{0,8},{1,72},{4,12},{5,76},{8,0},{9,64},{12,4},{13,68},{64,9},{65,... | collective-permute-start | bytes 393224 | tf_op jit(solution)/shard_map/ppermute | solution.py:292
  6.1 1.4 collective-permute-start.1
  7.5 1.3 collective-permute-start
  8.8 4.7 %convolution_bitcast_fusion = f32[3,256,512]{1,2,0:T(8,128)S(1)} fusion(bf16[3,2048,512]{2,1,0:T(8,128)(2,1)} %param.17, bf16[256,2048]{1,0:T(8,128)(2,1)S(1)} %copy-done.10), kind=kOutput, calls=%fused_computation.11 | convolution fusion | flops 1610612736 | bytes 8912896 | tf_op jit(solution)/shard_map/td,cdw->ctw/dot_general | solution.py:321
  13.7 5.6 %collective-permute-start.4 = (f32[2,256]{1,0:T(2,128)S(1)}, f32[2,256]{1,0:T(2,128)S(1)}, u32[]{:S(2)}, u32[]{:S(2)}) collective-permute-start(f32[2,256]{1,0:T(2,128)S(1)} %fusion.3), channel_id=1, source_target_pairs={{0,1},{1,0},{2,3},{3,2},{4,5},{5,4},{6,7},{7,6},{8,9},{9,8},{10,11... | collective-permute-start | bytes 6152 | tf_op jit(solution)/shard_map/ppermute | solution.py:23
  21.2 1.4 collective-permute-start.5
  23.2 1.8 collective-permute-done.5
  27.9 1.2 pad_maximum_fusion.1
  29.1 1.8 broadcast_in_dim.141
  30.9 4.3 %all-to-all-start = ((bf16[4,4,2,256,128]{4,3,2,1,0:T(8,128)(2,1)}), bf16[4,4,2,256,128]{4,3,2,1,0:T(8,128)(2,1)S(1)}, u32[]{:S(2)}, u32[]{:S(2)}) async-start(bf16[4,4,2,256,128]{4,3,2,1,0:T(8,128)(2,1)} %broadcast_in_dim.141), calls=%async_computation | async-start | bytes 4194304 | tf_op jit(solution)/shard_map/all_to_all | solution.py:31
  37.4 1.9 collective-permute-start.9
  39.3 1.1 collective-permute-start.8
  41.1 1.2 pad_clamp_fusion.1
  42.4 1.3 gather_fusion.3
  45.0 1.4 convert_reduce_fusion.3
  46.4 1.8 select_reduce_fusion.2
  51.6 9.3 %all-to-all-done = bf16[4,4,2,256,128]{4,3,2,1,0:T(8,128)(2,1)S(1)} async-done(((bf16[4,4,2,256,128]{4,3,2,1,0:T(8,128)(2,1)}), bf16[4,4,2,256,128]{4,3,2,1,0:T(8,128)(2,1)S(1)}, u32[]{:S(2)}, u32[]{:S(2)}) %all-to-all-start) | async-done | bytes 2097184 | tf_op jit(solution)/shard_map/all_to_all | solution.py:31
  60.8 1.0 collective-permute-start.11
  63.3 0.8 copy.51.lists_ref
  64.3 0.9 copy.53.rest_4_
  65.3 0.9 copy-done.2
  66.2 0.9 copy-done.4
  67.1 0.9 copy-done.6
  68.0 20.8 %shard_map.136 = bf16[4,256,128]{2,1,0:T(8,128)(2,1)S(1)} custom-call(s32[32]{0:T(128)S(1)} %get-tuple-element.51.nodes_ref, s32[32]{0:T(128)S(1)} %and_select_fusion.lengths_ref, s32[4,2,12]{2,1,0:T(2,128)S(1)} %copy.51.lists_ref, s32[4,2]{1,0:T(4,128)S(1)} %copy.52.counts_ref, bf16[784,128]{1,0:T(8,128)(2,1)S(1)} %copy-done.6, ...), custom_call_target="tpu_custom_call" | custom-call | flops 2000000000 | bytes 6000000 | tf_op jit(solution)/shard_map/pallas_call | solution.py:169
  90.4 0.9 collective-permute-start.15
  91.3 2.8 %collective-permute-start.14 = (bf16[256,128]{1,0:T(8,128)(2,1)S(1)}, bf16[256,128]{1,0:T(8,128)(2,1)S(1)}, u32[]{:S(2)}, u32[]{:S(2)}) collective-permute-start(bf16[256,128]{1,0:T(8,128)(2,1)S(1)} %get-tuple-element.96), channel_id=1, source_target_pairs={{0,8},{1,72},{4,12},{5,76},{8,0},{9,64},{12,4},{13,68},{64,9},{65,... | collective-permute-start | bytes 196616 | tf_op jit(solution)/shard_map/ppermute | solution.py:418
  94.1 1.3 collective-permute-start.13
  95.4 1.6 collective-permute-done.15
  97.0 1.4 collective-permute-done.14
  99.1 2.8 %fusion.1 = f32[256,2048]{1,0:T(8,128)S(1)} fusion(s32[]{:T(128)S(6)} %select_n.352, bf16[512,2048]{1,0:T(8,128)(2,1)} %param.19, bf16[256,128]{1,0:T(8,128)(2,1)S(1)} %collective-permute-done.15, bf16[256,128]{1,0:T(8,128)(2,1)S(1)} %collective-permute-done.14, bf16[256,128]{1,0:T(8,128)(2,1)S(1)} %collective-permute-done.13, ...), kind=kOutput, calls=%fused_computation.9 | convolution fusion | flops 542113792 | bytes 4456452 | tf_op jit(solution)/shard_map/dot_general | solution.py:421
  102.0 1.3 copy-done.9
  103.3 8.1 %collective-permute-start.16 = (bf16[2,64,2048]{2,1,0:T(8,128)(2,1)S(1)}, bf16[2,64,2048]{2,1,0:T(8,128)(2,1)S(1)}, u32[]{:S(2)}, u32[]{:S(2)}) collective-permute-start(bf16[2,64,2048]{2,1,0:T(8,128)(2,1)S(1)} %fusion.5), channel_id=1, source_target_pairs={{0,1},{1,0},{2,3},{3,2},{4,5},{5,4},{6,7},{7,6},{8,9},{9,8},{10,11... | collective-permute-start | bytes 1572872 | tf_op jit(solution)/shard_map/ppermute | solution.py:23
  111.4 1.5 collective-permute-done.16
  113.0 1.3 bitcast_add_fusion
  115.1 5.7 %collective-permute-done.18 = bf16[64,2048]{1,0:T(8,128)(2,1)S(1)} collective-permute-done((bf16[64,2048]{1,0:T(8,128)(2,1)S(1)}, bf16[64,2048]{1,0:T(8,128)(2,1)S(1)}, u32[]{:S(2)}, u32[]{:S(2)}) %collective-permute-start.18) | collective-permute-done | bytes 262176 | tf_op jit(solution)/shard_map/ppermute | solution.py:23
  121.0 1.1 add_convert_fusion.2
  122.1 1.6 broadcast_in_dim.164
  123.7 22.2 %all-to-all-start.1 = ((bf16[8,64,2048]{2,1,0:T(8,128)(2,1)}), bf16[8,64,2048]{2,1,0:T(8,128)(2,1)}, u32[]{:S(2)}, u32[]{:S(2)}) async-start(bf16[8,64,2048]{2,1,0:T(8,128)(2,1)} %broadcast_in_dim.164), calls=%async_computation.1 | async-start | bytes 4194304 | tf_op jit(solution)/shard_map/all_to_all | solution.py:31
  145.9 1.7 collective-permute-start.20
  147.6 26.8 %collective-permute-done.19.dn_a = bf16[256,2048]{1,0:T(8,128)(2,1)S(1)} collective-permute-done((bf16[256,2048]{1,0:T(8,128)(2,1)}, bf16[256,2048]{1,0:T(8,128)(2,1)S(1)}, u32[]{:S(2)}, u32[]{:S(2)}) %collective-permute-start.19) | collective-permute-done | bytes 1048608 | tf_op jit(solution)/shard_map/ppermute | solution.py:311
  174.4 3.1 %broadcast_select_fusion.gu_b = bf16[2,2048,256]{2,1,0:T(8,128)(2,1)} fusion(bf16[2,2048,256]{2,1,0:T(8,128)(2,1)} %param.21, bf16[2,2048,256]{2,1,0:T(8,128)(2,1)S(1)} %collective-permute-done.17, pred[]{:T(512)S(6)} %eq.236), kind=kLoop, calls=%fused_computation.10 | loop fusion | flops 1048576 | bytes 6291457 | tf_op jit(solution)/shard_map/jit(_where)/select_n | solution.py:442
  177.5 1.3 broadcast_select_fusion.1.dn_b
  178.9 6.3 %shard_map.138 = bf16[512,2048]{1,0:T(8,128)(2,1)S(1)} custom-call(bf16[512,2048]{1,0:T(8,128)(2,1)} %collective-permute-done.21.tokens_ref, bf16[2,2048,256]{2,1,0:T(8,128)(2,1)} %collective-permute-done.11.gu_a, bf16[256,2048]{1,0:T(8,128)(2,1)S(1)} %collective-permute-done.19.dn_a, bf16[2,2048,256]{2,1,0:T(8,128)(2,1)} %broadcast_select_fusion.gu_b, ...), custom_call_target="tpu_custom_call" | custom-call | flops 3221225472 | bytes 10485760 | tf_op jit(solution)/shard_map/pallas_call | solution.py:240
  185.4 6.3 %shard_map.137 = bf16[512,2048]{1,0:T(8,128)(2,1)S(1)} custom-call(bf16[512,2048]{1,0:T(8,128)(2,1)} %bitcast.82.tokens_ref, bf16[2,2048,256]{2,1,0:T(8,128)(2,1)} %collective-permute-done.11.gu_a, bf16[256,2048]{1,0:T(8,128)(2,1)S(1)} %collective-permute-done.19.dn_a, bf16[2,2048,256]{2,1,0:T(8,128)(2,1)} %broadcast_select_fusion.gu_b, ...), custom_call_target="tpu_custom_call" | custom-call | flops 3221225472 | bytes 10485760 | tf_op jit(solution)/shard_map/pallas_call | solution.py:240
  191.7 0.9 add_convert_fusion
  192.6 35.7 %all_to_all.15 = bf16[8,64,2048]{2,1,0:T(8,128)(2,1)S(1)} all-to-all(bf16[8,64,2048]{2,1,0:T(8,128)(2,1)S(1)} %bitcast.123), channel_id=1, replica_groups=mesh['yhi'=2,'x'=4,'z'=4,'ylo'=2,'core'=2] {'yhi','x'}, dimensions={0} | all-to-all | bytes 4194304 | tf_op jit(solution)/shard_map/all_to_all | solution.py:447
  228.8 0.9 add_convert_fusion.1
  (136 shorter events, 19.4 us)
Async XLA Ops:
  0.0 19.6 %copy-start = (s32[32,256]{1,0:T(8,128)S(1)}, s32[32,256]{1,0:T(8,128)}, u32[]{:S(2)}) copy-start(s32[32,256]{1,0:T(8,128)} %param.28) | copy-start | bytes 98308
  0.0 8.8 %copy-start.10 = (bf16[256,2048]{1,0:T(8,128)(2,1)S(1)}, bf16[256,2048]{1,0:T(8,128)(2,1)}, u32[]{:S(2)}) copy-start(bf16[256,2048]{1,0:T(8,128)(2,1)} %param.16) | copy-start | bytes 3145732
  1.2 26.7 %collective-permute-start.2 = (bf16[2,256,128]{2,1,0:T(8,128)(2,1)S(1)}, bf16[2,256,128]{2,1,0:T(8,128)(2,1)}, u32[]{:S(2)}, u32[]{:S(2)}) collective-permute-start(bf16[2,256,128]{2,1,0:T(8,128)(2,1)S(1)} %pad_maximum_fusion.4), channel_id=1, source_target_pairs={{0,8},{1,72},{4,12},{5,76},{8,0},{9,64},{12,4},{13,68},{64,9},{65,... | collective-permute-start | bytes 393224 | tf_op jit(solution)/shard_map/ppermute | solution.py:292
  5.3 22.6 %collective-permute-start.3 = (bf16[2,256,128]{2,1,0:T(8,128)(2,1)S(1)}, bf16[2,256,128]{2,1,0:T(8,128)(2,1)}, u32[]{:S(2)}, u32[]{:S(2)}) collective-permute-start(bf16[2,256,128]{2,1,0:T(8,128)(2,1)S(1)} %pad_maximum_fusion.5), channel_id=1, source_target_pairs={{0,12},{1,76},{4,0},{5,64},{8,4},{9,68},{12,8},{13,72},{64,13},{65... | collective-permute-start | bytes 393224 | tf_op jit(solution)/shard_map/ppermute | solution.py:292
  6.1 21.8 %collective-permute-start.1 = (bf16[2,256,128]{2,1,0:T(8,128)(2,1)S(1)}, bf16[2,256,128]{2,1,0:T(8,128)(2,1)}, u32[]{:S(2)}, u32[]{:S(2)}) collective-permute-start(bf16[2,256,128]{2,1,0:T(8,128)(2,1)S(1)} %pad_maximum_fusion.3), channel_id=1, source_target_pairs={{0,4},{1,68},{4,8},{5,72},{8,12},{9,76},{12,0},{13,64},{64,5},{65,... | collective-permute-start | bytes 393224 | tf_op jit(solution)/shard_map/ppermute | solution.py:292
  7.5 20.4 %collective-permute-start = (bf16[2,256,128]{2,1,0:T(8,128)(2,1)S(1)}, bf16[2,256,128]{2,1,0:T(8,128)(2,1)}, u32[]{:S(2)}, u32[]{:S(2)}) collective-permute-start(bf16[2,256,128]{2,1,0:T(8,128)(2,1)S(1)} %pad_maximum_fusion.2), channel_id=1, source_target_pairs={{0,0},{1,64},{4,4},{5,68},{8,8},{9,72},{12,12},{13,76},{64,1},{65,... | collective-permute-start | bytes 393224 | tf_op jit(solution)/shard_map/ppermute | solution.py:292
  13.5 5.9 %copy-start.12 = (s32[32,8]{0,1:T(8,128)S(1)}, s32[32,8]{0,1:T(8,128)}, u32[]{:S(2)}) copy-start(s32[32,8]{0,1:T(8,128)} %param.29) | copy-start | bytes 3076
  13.5 6.6 %copy-start.15 = (f32[2,512]{1,0:T(2,128)S(1)}, f32[2,512]{1,0:T(2,128)}, u32[]{:S(2)}) copy-start(f32[2,512]{1,0:T(2,128)} %param.18) | copy-start | bytes 12292
  13.5 6.7 %copy-start.16 = (s32[28]{0:T(128)S(1)}, s32[28]{0:T(128)}, u32[]{:S(2)}) copy-start(s32[28]{0:T(128)} %param.27) | copy-start | bytes 340
  13.5 6.8 %copy-start.7 = (s32[32]{0:T(128)S(1)}, s32[32]{0:T(128)}, u32[]{:S(2)}) copy-start(s32[32]{0:T(128)} %param.26) | copy-start | bytes 388
  13.7 7.6 %collective-permute-start.4 = (f32[2,256]{1,0:T(2,128)S(1)}, f32[2,256]{1,0:T(2,128)S(1)}, u32[]{:S(2)}, u32[]{:S(2)}) collective-permute-start(f32[2,256]{1,0:T(2,128)S(1)} %fusion.3), channel_id=1, source_target_pairs={{0,1},{1,0},{2,3},{3,2},{4,5},{5,4},{6,7},{7,6},{8,9},{9,8},{10,11... | collective-permute-start | bytes 6152 | tf_op jit(solution)/shard_map/ppermute | solution.py:23
  21.1 5.5 %copy-start.8 = (s32[32]{0:T(128)S(1)}, s32[32]{0:T(128)}, u32[]{:S(2)}) copy-start(s32[32]{0:T(128)} %param.25) | copy-start | bytes 388
  21.2 3.7 %collective-permute-start.5 = (f32[2,256]{1,0:T(2,128)S(1)}, f32[2,256]{1,0:T(2,128)S(1)}, u32[]{:S(2)}, u32[]{:S(2)}) collective-permute-start(f32[2,256]{1,0:T(2,128)S(1)} %add.413), channel_id=1, source_target_pairs={{0,2},{2,0},{1,3},{3,1},{4,6},{6,4},{5,7},{7,5},{8,10},{10,8},{9,1... | collective-permute-start | bytes 6152 | tf_op jit(solution)/shard_map/ppermute | solution.py:23
  22.7 3.7 %copy-start.14 = (pred[4]{0:T(512)(128)(4,1)}, pred[4]{0:T(512)(128)(4,1)S(1)}, u32[]{:S(2)}) copy-start(pred[4]{0:T(512)(128)(4,1)S(1)} %compare_and_fusion) | copy-start | bytes 16
  30.9 29.9 %all-to-all-start = ((bf16[4,4,2,256,128]{4,3,2,1,0:T(8,128)(2,1)}), bf16[4,4,2,256,128]{4,3,2,1,0:T(8,128)(2,1)S(1)}, u32[]{:S(2)}, u32[]{:S(2)}) async-start(bf16[4,4,2,256,128]{4,3,2,1,0:T(8,128)(2,1)} %broadcast_in_dim.141), calls=%async_computation | async-start | bytes 4194304 | tf_op jit(solution)/shard_map/all_to_all | solution.py:31
  35.5 0.6 copy-start.11
  37.4 12.0 %collective-permute-start.9 = (bf16[784,128]{1,0:T(8,128)(2,1)}, bf16[784,128]{1,0:T(8,128)(2,1)S(1)}, u32[]{:S(2)}, u32[]{:S(2)}) collective-permute-start(bf16[784,128]{1,0:T(8,128)(2,1)} %get-tuple-element.86), channel_id=1, source_target_pairs={{0,12},{1,76},{4,0},{5,64},{8,4},{9,68},{12,8},{13,72},{64,13},{65... | collective-permute-start | bytes 602120 | tf_op jit(solution)/shard_map/ppermute | solution.py:292
  39.3 10.1 %collective-permute-start.8 = (bf16[784,128]{1,0:T(8,128)(2,1)S(1)}, bf16[784,128]{1,0:T(8,128)(2,1)S(1)}, u32[]{:S(2)}, u32[]{:S(2)}) collective-permute-start(bf16[784,128]{1,0:T(8,128)(2,1)S(1)} %get-tuple-element.87), channel_id=1, source_target_pairs={{0,8},{1,72},{4,12},{5,76},{8,0},{9,64},{12,4},{13,68},{64,9},{65,... | collective-permute-start | bytes 602120 | tf_op jit(solution)/shard_map/ppermute | solution.py:292
  40.5 9.6 %collective-permute-start.7 = (bf16[784,128]{1,0:T(8,128)(2,1)S(1)}, bf16[784,128]{1,0:T(8,128)(2,1)S(1)}, u32[]{:S(2)}, u32[]{:S(2)}) collective-permute-start(bf16[784,128]{1,0:T(8,128)(2,1)S(1)} %get-tuple-element.88), channel_id=1, source_target_pairs={{0,4},{1,68},{4,8},{5,72},{8,12},{9,76},{12,0},{13,64},{64,5},{65,... | collective-permute-start | bytes 602120 | tf_op jit(solution)/shard_map/ppermute | solution.py:292
  40.5 10.3 %collective-permute-start.6 = (bf16[784,128]{1,0:T(8,128)(2,1)S(1)}, bf16[784,128]{1,0:T(8,128)(2,1)S(1)}, u32[]{:S(2)}, u32[]{:S(2)}) collective-permute-start(bf16[784,128]{1,0:T(8,128)(2,1)S(1)} %get-tuple-element.89), channel_id=1, source_target_pairs={{0,0},{1,64},{4,4},{5,68},{8,8},{9,72},{12,12},{13,76},{64,1},{65,... | collective-permute-start | bytes 602120 | tf_op jit(solution)/shard_map/ppermute | solution.py:292
  49.4 0.7 copy-start.1
  50.1 0.7 copy-start.3
  50.8 0.7 copy-start.5
  60.8 4.4 %collective-permute-start.10 = (bf16[16,2,256,128]{3,2,1,0:T(8,128)(2,1)S(1)}, bf16[16,2,256,128]{3,2,1,0:T(8,128)(2,1)}, u32[]{:S(2)}, u32[]{:S(2)}) collective-permute-start(bf16[16,2,256,128]{3,2,1,0:T(8,128)(2,1)S(1)} %bitcast.121), channel_id=1, source_target_pairs={{0,1},{1,0},{2,3},{3,2},{4,5},{5,4},{6,7},{7,6},{8,9},{9,8},{10,11... | collective-permute-start | bytes 6291464 | tf_op jit(solution)/shard_map/ppermute | solution.py:23
  60.8 28.0 %collective-permute-start.11 = (bf16[2,2048,256]{2,1,0:T(8,128)(2,1)}, bf16[2,2048,256]{2,1,0:T(8,128)(2,1)}, u32[]{:S(2)}, u32[]{:S(2)}) collective-permute-start(bf16[2,2048,256]{2,1,0:T(8,128)(2,1)} %param.21), channel_id=1, source_target_pairs={{0,4},{1,13},{4,8},{5,1},{8,12},{9,5},{12,0},{13,9},{2,6},{3,15},{... | collective-permute-start | bytes 6291464 | tf_op jit(solution)/shard_map/ppermute | solution.py:311
  65.3 0.9 copy-start.2
  66.2 0.9 copy-start.4
  67.1 0.9 copy-start.6
  88.9 25.4 %collective-permute-start.17 = (bf16[2,2048,256]{2,1,0:T(8,128)(2,1)}, bf16[2,2048,256]{2,1,0:T(8,128)(2,1)S(1)}, u32[]{:S(2)}, u32[]{:S(2)}) collective-permute-start(bf16[2,2048,256]{2,1,0:T(8,128)(2,1)} %param.21), channel_id=1, source_target_pairs={{1,9},{5,13},{9,1},{13,5},{3,11},{7,15},{11,3},{15,7},{17,25},{21,... | collective-permute-start | bytes 6291464 | tf_op jit(solution)/shard_map/ppermute | solution.py:317
  89.7 5.8 %collective-permute-start.12 = (bf16[256,128]{1,0:T(8,128)(2,1)S(1)}, bf16[256,128]{1,0:T(8,128)(2,1)S(1)}, u32[]{:S(2)}, u32[]{:S(2)}) collective-permute-start(bf16[256,128]{1,0:T(8,128)(2,1)S(1)} %get-tuple-element.94), channel_id=1, source_target_pairs={{0,0},{1,64},{4,4},{5,68},{8,8},{9,72},{12,12},{13,76},{64,1},{65,... | collective-permute-start | bytes 196616 | tf_op jit(solution)/shard_map/ppermute | solution.py:418
  90.4 6.6 %collective-permute-start.15 = (bf16[256,128]{1,0:T(8,128)(2,1)S(1)}, bf16[256,128]{1,0:T(8,128)(2,1)S(1)}, u32[]{:S(2)}, u32[]{:S(2)}) collective-permute-start(bf16[256,128]{1,0:T(8,128)(2,1)S(1)} %get-tuple-element.95), channel_id=1, source_target_pairs={{0,4},{1,68},{4,8},{5,72},{8,12},{9,76},{12,0},{13,64},{64,5},{65,... | collective-permute-start | bytes 196616 | tf_op jit(solution)/shard_map/ppermute | solution.py:418
  91.3 7.1 %collective-permute-start.14 = (bf16[256,128]{1,0:T(8,128)(2,1)S(1)}, bf16[256,128]{1,0:T(8,128)(2,1)S(1)}, u32[]{:S(2)}, u32[]{:S(2)}) collective-permute-start(bf16[256,128]{1,0:T(8,128)(2,1)S(1)} %get-tuple-element.96), channel_id=1, source_target_pairs={{0,8},{1,72},{4,12},{5,76},{8,0},{9,64},{12,4},{13,68},{64,9},{65,... | collective-permute-start | bytes 196616 | tf_op jit(solution)/shard_map/ppermute | solution.py:418
  94.1 5.0 %collective-permute-start.13 = (bf16[256,128]{1,0:T(8,128)(2,1)S(1)}, bf16[256,128]{1,0:T(8,128)(2,1)S(1)}, u32[]{:S(2)}, u32[]{:S(2)}) collective-permute-start(bf16[256,128]{1,0:T(8,128)(2,1)S(1)} %get-tuple-element.97), channel_id=1, source_target_pairs={{0,12},{1,76},{4,0},{5,64},{8,4},{9,68},{12,8},{13,72},{64,13},{65... | collective-permute-start | bytes 196616 | tf_op jit(solution)/shard_map/ppermute | solution.py:418
  102.0 1.3 copy-start.9
  103.3 11.8 %copy-start.13 = (f32[2,2048]{1,0:T(2,128)S(1)}, f32[2,2048]{1,0:T(2,128)}, u32[]{:S(2)}) copy-start(f32[2,2048]{1,0:T(2,128)} %param.20) | copy-start | bytes 49156
  103.3 9.6 %collective-permute-start.16 = (bf16[2,64,2048]{2,1,0:T(8,128)(2,1)S(1)}, bf16[2,64,2048]{2,1,0:T(8,128)(2,1)S(1)}, u32[]{:S(2)}, u32[]{:S(2)}) collective-permute-start(bf16[2,64,2048]{2,1,0:T(8,128)(2,1)S(1)} %fusion.5), channel_id=1, source_target_pairs={{0,1},{1,0},{2,3},{3,2},{4,5},{5,4},{6,7},{7,6},{8,9},{9,8},{10,11... | collective-permute-start | bytes 1572872 | tf_op jit(solution)/shard_map/ppermute | solution.py:23
  114.3 6.5 %collective-permute-start.18 = (bf16[64,2048]{1,0:T(8,128)(2,1)S(1)}, bf16[64,2048]{1,0:T(8,128)(2,1)S(1)}, u32[]{:S(2)}, u32[]{:S(2)}) collective-permute-start(bf16[64,2048]{1,0:T(8,128)(2,1)S(1)} %fusion.6), channel_id=1, source_target_pairs={{0,2},{2,0},{1,3},{3,1},{4,6},{6,4},{5,7},{7,5},{8,10},{10,8},{9,1... | collective-permute-start | bytes 786440 | tf_op jit(solution)/shard_map/ppermute | solution.py:23
  123.7 50.7 %all-to-all-start.1 = ((bf16[8,64,2048]{2,1,0:T(8,128)(2,1)}), bf16[8,64,2048]{2,1,0:T(8,128)(2,1)}, u32[]{:S(2)}, u32[]{:S(2)}) async-start(bf16[8,64,2048]{2,1,0:T(8,128)(2,1)} %broadcast_in_dim.164), calls=%async_computation.1 | async-start | bytes 4194304 | tf_op jit(solution)/shard_map/all_to_all | solution.py:31
  145.9 1.7 collective-permute-start.20
  147.6 26.8 %collective-permute-start.19 = (bf16[256,2048]{1,0:T(8,128)(2,1)}, bf16[256,2048]{1,0:T(8,128)(2,1)S(1)}, u32[]{:S(2)}, u32[]{:S(2)}) collective-permute-start(bf16[256,2048]{1,0:T(8,128)(2,1)} %param.22), channel_id=1, source_target_pairs={{0,4},{1,13},{4,8},{5,1},{8,12},{9,5},{12,0},{13,9},{2,6},{3,15},{... | collective-permute-start | bytes 3145736 | tf_op jit(solution)/shard_map/ppermute | solution.py:311
  174.4 4.5 %collective-permute-start.21 = (bf16[512,2048]{1,0:T(8,128)(2,1)}, bf16[512,2048]{1,0:T(8,128)(2,1)}, u32[]{:S(2)}, u32[]{:S(2)}) collective-permute-start(bf16[512,2048]{1,0:T(8,128)(2,1)} %bitcast.82.tokens_ref), channel_id=1, source_target_pairs={{0,1},{1,0},{2,3},{3,2},{4,5},{5,4},{6,7},{7,6},{8,9},{9,8},{10,11... | collective-permute-start | bytes 6291464 | tf_op jit(solution)/shard_map/ppermute | solution.py:23
  185.2 6.5 %collective-permute-start.22 = (bf16[512,2048]{1,0:T(8,128)(2,1)S(1)}, bf16[512,2048]{1,0:T(8,128)(2,1)S(1)}, u32[]{:S(2)}, u32[]{:S(2)}) collective-permute-start(bf16[512,2048]{1,0:T(8,128)(2,1)S(1)} %shard_map.138), channel_id=1, source_target_pairs={{0,1},{1,0},{2,3},{3,2},{4,5},{5,4},{6,7},{7,6},{8,9},{9,8},{10,11... | collective-permute-start | bytes 6291464 | tf_op jit(solution)/shard_map/ppermute | solution.py:23

commit v8 on v7

--- a/solution.py
+++ b/solution.py
@@ -318,10 +318,11 @@
             weights, ("z", "core"), [(z * 2 + 1, (z + 2) % n_z * 2 + 1) for z in range(n_z)]
         )
 
+    gu_a = beside(w_gate_up)
+
     qkv_raw = jnp.einsum("td,cdw->ctw", states_in, w_qkv, preferred_element_type=F32)
     squares = jnp.sum(qkv_raw[:2] * qkv_raw[:2], axis=2)
-    for axis in ("core", "ylo"):
-        squares = squares + shift(squares, axis, 1)
+    squares = jnp.sum(spread(squares, HEAD), axis=0)
     cached_own = spread(cached, "x").reshape((n_x * n_z,) + cached.shape[1:])
     def own_group(table):
         return lax.dynamic_slice_in_dim(table, blk, 1, 0)
@@ -352,9 +353,9 @@
         [turned(0), turned(1), qkv_raw[2].astype(BF).reshape(rows, heads_here, HD)]
     ).transpose(2, 0, 1, 3).reshape(heads_here, 3 * rows, HD)
     qkv = jnp.concatenate([qkv, jnp.broadcast_to(terms, (heads_here,) + terms.shape)], axis=1)
-    qkv, slot_node, node_length, node_parent, leaf_segment, leaf_node = (
+    qkv, gu_a, slot_node, node_length, node_parent, leaf_segment, leaf_node = (
         lax.optimization_barrier(
-            (qkv, slot_node, node_length, node_parent, leaf_segment, leaf_node)
+            (qkv, gu_a, slot_node, node_length, node_parent, leaf_segment, leaf_node)
         )
     )
     qkv_parts = [across(select_row(qkv, (z_at + s) % n_z), s) for s in range(n_z)]
@@ -398,17 +399,13 @@
     )
     cached_parts = [cached_own, shift(cached_own, "core", 1)]
 
-    gu_a = beside(w_gate_up)
+
+    gu_b, dn_b = beyond(w_gate_up), beyond(w_down)
 
     attended = attention(
         slot_nodes, slot_lengths, lists, counts, qkv_parts, row_info, segments[:, None, :],
         factors, factors[:, None, :, 1], cached_parts,
     )
-
-    attended, gu_a, w_gate_up, w_down = lax.optimization_barrier(
-        (attended, gu_a, w_gate_up, w_down)
-    )
-    gu_b = beyond(w_gate_up)
 
     def back(values, s):
         pairs = [
@@ -418,6 +415,7 @@
         return lax.ppermute(values, corner, pairs)
 
     attended = jnp.concatenate([back(attended[s], s) for s in range(n_z)], axis=1)
+    attended, gu_b, dn_b = lax.optimization_barrier((attended, gu_b, dn_b))
     attn_part = jnp.dot(attended, w_out, preferred_element_type=F32)
     attn_part = attn_part.reshape(2, 2, rows // 4, -1)
 
@@ -425,7 +423,6 @@
         return lax.dynamic_index_in_dim(attn_part, c, 1, keepdims=False)
 
     attn_part = of_core(core) + shift(of_core(1 - core).astype(BF), "core", 1).astype(F32)
-    attn_part, gu_b, w_down = lax.optimization_barrier((attn_part, gu_b, w_down))
     attn_proj = select_row(attn_part, ylo) + shift(
         select_row(attn_part, 1 - ylo).astype(BF), "ylo", 1
     ).astype(F32)
@@ -435,9 +432,9 @@
 
     plane = ("yhi", "x")
     mid_state, w_down = lax.optimization_barrier((mid_state, w_down))
-    dn_a, dn_b = beside(w_down), beyond(w_down)
+    dn_a = beside(w_down)
     tokens = spread(mid_state, plane)
-    tokens, dn_a, dn_b = lax.optimization_barrier((tokens, dn_a, dn_b))
+    tokens, dn_a = lax.optimization_barrier((tokens, dn_a))
     weights = (
         gu_a, dn_a, jnp.where(core == 0, w_gate_up, gu_b), jnp.where(core == 0, w_down, dn_b)
     )

time: 231 us -> 230 us (level)
  waiting for transfers between devices: 49.4 us -> 60.2 us
  other arithmetic: 20.5 us -> 15.5 us
  starting transfers between devices: 63.1 us -> 59.8 us
  blocking collectives: 35.7 us -> 33 us
    ppermute x2, waiting for transfers between devices: 26.8 us -> 33.3 us  [beside(): lax.ppermute(weights, ('z', 'core'), [(z * 2 + c, (z + 1 - 2 * c) % n_z *...]
    all_to_all x2 -> x3, starting transfers between devices: 26.5 us -> 20.8 us  [spread(): return lax.all_to_all(copies, axes, 0, 0, tiled=True)]
    all_to_all x2 -> x3, waiting for transfers between devices: 9.26 us -> 12.3 us  [spread(): return lax.all_to_all(copies, axes, 0, 0, tiled=True)]
    all_to_all x1, blocking collectives: 35.7 us -> 33 us  [on_device(): lax.all_to_all(total.astype(BF).reshape(tokens.shape), plane, 0, 0, tiled...]
    ppermute x7 -> x5, waiting for transfers between devices: 9 us -> 11.6 us  [shift(): return lax.ppermute(values, axis, [(i, (i + by) % n) for i in range(n)])]
    ppermute x7 -> x5, starting transfers between devices: 16.1 us -> 17.5 us  [shift(): return lax.ppermute(values, axis, [(i, (i + by) % n) for i in range(n)])]
    unnamed x34 -> x36, local copies, waits for them, and re-layouts: 6.58 us -> 5.3 us
  transfers between devices with their start and end apart: 25 -> 24, of which waited for: 9 -> 10; matrix products, arithmetic and copies ran while one was open for 14% -> 12% of each run, Pallas kernels for 12% -> 12%
where the time goes in v8:
time: 230 us; the launch traced here: 229 us
  waiting for transfers between devices  60.2 us (26%)
  starting transfers between devices  59.8 us (26%)
  Pallas kernels  33.3 us (14%)
  blocking collectives  33 us (14%)
  local copies, waits for them, and re-layouts  18.8 us (8%)
  other arithmetic  15.5 us (7%)
  matrix products  7.54 us (3%)
    ppermute x2, waiting for transfers between devices, beside(): lax.ppermute(weights, ('z', 'core'), [(z * 2 + c, (z + 1 - 2 * c) % n_z *...  33.3 us
    all_to_all x1, blocking collectives, on_device(): lax.all_to_all(total.astype(BF).reshape(tokens.shape), plane, 0, 0, tiled...  33 us
    all_to_all x3, starting transfers between devices, spread(): return lax.all_to_all(copies, axes, 0, 0, tiled=True)  20.8 us
    pallas_call x1, Pallas kernels, attention(): pl.pallas_call(attention_body, out_shape=jax.ShapeDtypeStruct((groups, ro...  20.8 us
    ppermute x5, starting transfers between devices, shift(): return lax.ppermute(values, axis, [(i, (i + by) % n) for i in range(n)])  17.5 us
    pallas_call x2, Pallas kernels, feed_forward(): pl.pallas_call(feed_forward_body, out_shape=jax.ShapeDtypeStruct((rows, w...  12.5 us
    all_to_all x3, waiting for transfers between devices, spread(): return lax.all_to_all(copies, axes, 0, 0, tiled=True)  12.3 us
    ppermute x5, waiting for transfers between devices, shift(): return lax.ppermute(values, axis, [(i, (i + by) % n) for i in range(n)])  11.6 us
  transfers between devices with their start and end apart: 24, of which 10 were waited for; matrix products, arithmetic and copies ran while one was open for 12% of the time, Pallas kernels for 12%

profile of v8, /device:TPU:0, one launch (start us, length us, event | category | flops | bytes accessed | tf_op | source)
XLA Modules:
  0.0 228.9 jit_solution(6461747292312497333)
XLA Ops:
  0.0 1.2 constant_dynamic-slice_fusion.8
  1.2 4.0 %collective-permute-start.2 = (bf16[2,256,128]{2,1,0:T(8,128)(2,1)S(1)}, bf16[2,256,128]{2,1,0:T(8,128)(2,1)S(1)}, u32[]{:S(2)}, u32[]{:S(2)}) collective-permute-start(bf16[2,256,128]{2,1,0:T(8,128)(2,1)S(1)} %pad_maximum_fusion.5), channel_id=1, source_target_pairs={{0,8},{1,72},{4,12},{5,76},{8,0},{9,64},{12,4},{13,68},{64,9},{65,... | collective-permute-start | bytes 393224 | tf_op jit(solution)/shard_map/ppermute | solution.py:292
  5.3 0.8 collective-permute-start.3
  6.1 1.4 collective-permute-start.1
  7.5 0.8 collective-permute-start
  8.4 4.7 %convolution_bitcast_fusion = f32[3,256,512]{1,2,0:T(8,128)S(1)} fusion(bf16[3,2048,512]{2,1,0:T(8,128)(2,1)} %param.17, bf16[256,2048]{1,0:T(8,128)(2,1)S(1)} %copy-done.11), kind=kOutput, calls=%fused_computation.11 | convolution fusion | flops 1610612736 | bytes 8912896 | tf_op jit(solution)/shard_map/td,cdw->ctw/dot_general | solution.py:323
  13.8 8.3 %all-to-all-start.1 = ((f32[4,2,256]{2,1,0:T(2,128)}), f32[4,2,256]{2,1,0:T(2,128)S(1)}, u32[]{:S(2)}, u32[]{:S(2)}) async-start(f32[4,2,256]{2,1,0:T(2,128)} %broadcast_in_dim.151), calls=%async_computation.1 | async-start | bytes 16384 | tf_op jit(solution)/shard_map/all_to_all | solution.py:31
  22.1 1.0 collective-permute-start.4
  26.2 1.8 broadcast_in_dim.144
  28.0 4.4 %all-to-all-start = ((bf16[4,4,2,256,128]{4,3,2,1,0:T(8,128)(2,1)}), bf16[4,4,2,256,128]{4,3,2,1,0:T(8,128)(2,1)S(1)}, u32[]{:S(2)}, u32[]{:S(2)}) async-start(bf16[4,4,2,256,128]{4,3,2,1,0:T(8,128)(2,1)} %broadcast_in_dim.144), calls=%async_computation | async-start | bytes 4194304 | tf_op jit(solution)/shard_map/all_to_all | solution.py:31
  32.4 17.3 %collective-permute-done.4.gu_a = bf16[2,2048,256]{2,1,0:T(8,128)(2,1)} collective-permute-done((bf16[2,2048,256]{2,1,0:T(8,128)(2,1)}, bf16[2,2048,256]{2,1,0:T(8,128)(2,1)}, u32[]{:S(2)}, u32[]{:S(2)}) %collective-permute-start.4) | collective-permute-done | bytes 2097184 | tf_op jit(solution)/shard_map/ppermute | solution.py:311
  55.4 1.2 collective-permute-start.7
  57.4 1.2 pad_clamp_fusion.1
  58.6 1.3 gather_fusion.3
  61.3 1.4 convert_reduce_fusion.3
  62.7 1.8 select_reduce_fusion.2
  67.2 7.8 %collective-permute-start.9 = (bf16[16,2,256,128]{3,2,1,0:T(8,128)(2,1)S(1)}, bf16[16,2,256,128]{3,2,1,0:T(8,128)(2,1)}, u32[]{:S(2)}, u32[]{:S(2)}) collective-permute-start(bf16[16,2,256,128]{3,2,1,0:T(8,128)(2,1)S(1)} %bitcast.123), channel_id=1, source_target_pairs={{0,1},{1,0},{2,3},{3,2},{4,5},{5,4},{6,7},{7,6},{8,9},{9,8},{10,11... | collective-permute-start | bytes 6291464 | tf_op jit(solution)/shard_map/ppermute | solution.py:23
  75.0 2.0 collective-permute-start.14
  77.0 1.6 collective-permute-start.15
  79.4 0.8 copy.65.counts_ref
  80.1 0.8 copy.64.lists_ref
  81.1 0.9 copy.66.rest_4_
  82.1 0.9 copy-done.2
  83.0 0.9 copy-done.4
  84.0 0.9 copy-done.6
  84.9 20.8 %shard_map.136 = bf16[4,256,128]{2,1,0:T(8,128)(2,1)S(1)} custom-call(s32[32]{0:T(128)S(1)} %get-tuple-element.47.nodes_ref, s32[32]{0:T(128)S(1)} %and_select_fusion.lengths_ref, s32[4,2,12]{2,1,0:T(2,128)S(1)} %copy.64.lists_ref, s32[4,2]{1,0:T(4,128)S(1)} %copy.65.counts_ref, bf16[784,128]{1,0:T(8,128)(2,1)S(1)} %copy-done.6, ...), custom_call_target="tpu_custom_call" | custom-call | flops 2000000000 | bytes 6000000 | tf_op jit(solution)/shard_map/pallas_call | solution.py:169
  106.4 2.0 collective-permute-start.13
  108.4 2.3 collective-permute-start.12
  110.6 2.1 collective-permute-start.11
  112.7 0.9 collective-permute-done.13
  113.6 1.4 collective-permute-done.12
  115.7 2.8 %fusion.1 = f32[256,2048]{1,0:T(8,128)S(1)} fusion(bf16[256,512]{1,0:T(8,128)(2,1)S(1)} %pad_maximum_fusion.2, s32[]{:T(128)S(6)} %select_n.352, bf16[512,2048]{1,0:T(8,128)(2,1)} %param.19), kind=kOutput, calls=%fused_computation.9 | convolution fusion | flops 541065216 | bytes 4456452 | tf_op jit(solution)/shard_map/dot_general | solution.py:419
  118.6 7.6 %collective-permute-start.16 = (bf16[2,64,2048]{2,1,0:T(8,128)(2,1)S(1)}, bf16[2,64,2048]{2,1,0:T(8,128)(2,1)S(1)}, u32[]{:S(2)}, u32[]{:S(2)}) collective-permute-start(bf16[2,64,2048]{2,1,0:T(8,128)(2,1)S(1)} %fusion.5), channel_id=1, source_target_pairs={{0,1},{1,0},{2,3},{3,2},{4,5},{5,4},{6,7},{7,6},{8,9},{9,8},{10,11... | collective-permute-start | bytes 1572872 | tf_op jit(solution)/shard_map/ppermute | solution.py:23
  126.3 1.5 collective-permute-done.16
  128.0 1.4 collective-permute-start.17
  129.4 7.2 %collective-permute-done.17 = bf16[64,2048]{1,0:T(8,128)(2,1)S(1)} collective-permute-done((bf16[64,2048]{1,0:T(8,128)(2,1)S(1)}, bf16[64,2048]{1,0:T(8,128)(2,1)S(1)}, u32[]{:S(2)}, u32[]{:S(2)}) %collective-permute-start.17) | collective-permute-done | bytes 262176 | tf_op jit(solution)/shard_map/ppermute | solution.py:23
  136.8 1.1 add_convert_fusion.2
  137.9 1.6 broadcast_in_dim.168
  139.5 8.0 %all-to-all-start.2 = ((bf16[8,64,2048]{2,1,0:T(8,128)(2,1)}), bf16[8,64,2048]{2,1,0:T(8,128)(2,1)}, u32[]{:S(2)}, u32[]{:S(2)}) async-start(bf16[8,64,2048]{2,1,0:T(8,128)(2,1)} %broadcast_in_dim.168), calls=%async_computation.2 | async-start | bytes 4194304 | tf_op jit(solution)/shard_map/all_to_all | solution.py:31
  147.8 16.0 %collective-permute-done.18.dn_a = bf16[256,2048]{1,0:T(8,128)(2,1)S(1)} collective-permute-done((bf16[256,2048]{1,0:T(8,128)(2,1)}, bf16[256,2048]{1,0:T(8,128)(2,1)S(1)}, u32[]{:S(2)}, u32[]{:S(2)}) %collective-permute-start.18) | collective-permute-done | bytes 1048608 | tf_op jit(solution)/shard_map/ppermute | solution.py:311
  163.8 12.0 %all-to-all-done.2 = bf16[8,64,2048]{2,1,0:T(8,128)(2,1)} async-done(((bf16[8,64,2048]{2,1,0:T(8,128)(2,1)}), bf16[8,64,2048]{2,1,0:T(8,128)(2,1)}, u32[]{:S(2)}, u32[]{:S(2)}) %all-to-all-start.2) | async-done | bytes 2097184 | tf_op jit(solution)/shard_map/all_to_all | solution.py:31
  175.8 1.6 broadcast_select_fusion.gu_b
  177.5 2.8 %collective-permute-done.19.tokens_ref = bf16[512,2048]{1,0:T(8,128)(2,1)} collective-permute-done((bf16[512,2048]{1,0:T(8,128)(2,1)}, bf16[512,2048]{1,0:T(8,128)(2,1)}, u32[]{:S(2)}, u32[]{:S(2)}) %collective-permute-start.19) | collective-permute-done | bytes 2097184 | tf_op jit(solution)/shard_map/ppermute | solution.py:23
  180.3 6.3 %shard_map.138 = bf16[512,2048]{1,0:T(8,128)(2,1)S(1)} custom-call(bf16[512,2048]{1,0:T(8,128)(2,1)} %collective-permute-done.19.tokens_ref, bf16[2,2048,256]{2,1,0:T(8,128)(2,1)} %collective-permute-done.4.gu_a, bf16[256,2048]{1,0:T(8,128)(2,1)S(1)} %collective-permute-done.18.dn_a, bf16[2,2048,256]{2,1,0:T(8,128)(2,1)} %broadcast_select_fusion.gu_b, ...), custom_call_target="tpu_custom_call" | custom-call | flops 3221225472 | bytes 10485760 | tf_op jit(solution)/shard_map/pallas_call | solution.py:240
  187.3 6.3 %shard_map.137 = bf16[512,2048]{1,0:T(8,128)(2,1)S(1)} custom-call(bf16[512,2048]{1,0:T(8,128)(2,1)} %bitcast.80.tokens_ref, bf16[2,2048,256]{2,1,0:T(8,128)(2,1)} %collective-permute-done.4.gu_a, bf16[256,2048]{1,0:T(8,128)(2,1)S(1)} %collective-permute-done.18.dn_a, bf16[2,2048,256]{2,1,0:T(8,128)(2,1)} %broadcast_select_fusion.gu_b, ...), custom_call_target="tpu_custom_call" | custom-call | flops 3221225472 | bytes 10485760 | tf_op jit(solution)/shard_map/pallas_call | solution.py:240
  193.6 0.9 add_convert_fusion
  194.5 33.0 %all_to_all.20 = bf16[8,64,2048]{2,1,0:T(8,128)(2,1)S(1)} all-to-all(bf16[8,64,2048]{2,1,0:T(8,128)(2,1)S(1)} %bitcast.125), channel_id=1, replica_groups=mesh['yhi'=2,'x'=4,'z'=4,'ylo'=2,'core'=2] {'yhi','x'}, dimensions={0} | all-to-all | bytes 4194304 | tf_op jit(solution)/shard_map/all_to_all | solution.py:444
  228.0 0.9 add_convert_fusion.1
  (138 shorter events, 18.5 us)
Async XLA Ops:
  0.0 23.4 %copy-start = (s32[32,256]{1,0:T(8,128)S(1)}, s32[32,256]{1,0:T(8,128)}, u32[]{:S(2)}) copy-start(s32[32,256]{1,0:T(8,128)} %param.28) | copy-start | bytes 98308
  0.0 8.3 %copy-start.11 = (bf16[256,2048]{1,0:T(8,128)(2,1)S(1)}, bf16[256,2048]{1,0:T(8,128)(2,1)}, u32[]{:S(2)}) copy-start(bf16[256,2048]{1,0:T(8,128)(2,1)} %param.16) | copy-start | bytes 3145732
  1.2 24.9 %collective-permute-start.2 = (bf16[2,256,128]{2,1,0:T(8,128)(2,1)S(1)}, bf16[2,256,128]{2,1,0:T(8,128)(2,1)S(1)}, u32[]{:S(2)}, u32[]{:S(2)}) collective-permute-start(bf16[2,256,128]{2,1,0:T(8,128)(2,1)S(1)} %pad_maximum_fusion.5), channel_id=1, source_target_pairs={{0,8},{1,72},{4,12},{5,76},{8,0},{9,64},{12,4},{13,68},{64,9},{65,... | collective-permute-start | bytes 393224 | tf_op jit(solution)/shard_map/ppermute | solution.py:292
  5.3 20.8 %collective-permute-start.3 = (bf16[2,256,128]{2,1,0:T(8,128)(2,1)S(1)}, bf16[2,256,128]{2,1,0:T(8,128)(2,1)S(1)}, u32[]{:S(2)}, u32[]{:S(2)}) collective-permute-start(bf16[2,256,128]{2,1,0:T(8,128)(2,1)S(1)} %pad_maximum_fusion.6), channel_id=1, source_target_pairs={{0,12},{1,76},{4,0},{5,64},{8,4},{9,68},{12,8},{13,72},{64,13},{65... | collective-permute-start | bytes 393224 | tf_op jit(solution)/shard_map/ppermute | solution.py:292
  6.1 20.0 %collective-permute-start.1 = (bf16[2,256,128]{2,1,0:T(8,128)(2,1)S(1)}, bf16[2,256,128]{2,1,0:T(8,128)(2,1)S(1)}, u32[]{:S(2)}, u32[]{:S(2)}) collective-permute-start(bf16[2,256,128]{2,1,0:T(8,128)(2,1)S(1)} %pad_maximum_fusion.4), channel_id=1, source_target_pairs={{0,4},{1,68},{4,8},{5,72},{8,12},{9,76},{12,0},{13,64},{64,5},{65,... | collective-permute-start | bytes 393224 | tf_op jit(solution)/shard_map/ppermute | solution.py:292
  7.5 15.7 %copy-start.13 = (s32[32,8]{0,1:T(8,128)S(1)}, s32[32,8]{0,1:T(8,128)}, u32[]{:S(2)}) copy-start(s32[32,8]{0,1:T(8,128)} %param.29) | copy-start | bytes 3076
  7.5 16.4 %copy-start.17 = (s32[28]{0:T(128)S(1)}, s32[28]{0:T(128)}, u32[]{:S(2)}) copy-start(s32[28]{0:T(128)} %param.27) | copy-start | bytes 340
  7.5 16.6 %copy-start.7 = (s32[32]{0:T(128)S(1)}, s32[32]{0:T(128)}, u32[]{:S(2)}) copy-start(s32[32]{0:T(128)} %param.26) | copy-start | bytes 388
  7.5 16.7 %copy-start.16 = (f32[2,512]{1,0:T(2,128)S(1)}, f32[2,512]{1,0:T(2,128)}, u32[]{:S(2)}) copy-start(f32[2,512]{1,0:T(2,128)} %param.18) | copy-start | bytes 12292
  7.5 18.6 %collective-permute-start = (bf16[2,256,128]{2,1,0:T(8,128)(2,1)S(1)}, bf16[2,256,128]{2,1,0:T(8,128)(2,1)S(1)}, u32[]{:S(2)}, u32[]{:S(2)}) collective-permute-start(bf16[2,256,128]{2,1,0:T(8,128)(2,1)S(1)} %pad_maximum_fusion.3), channel_id=1, source_target_pairs={{0,0},{1,64},{4,4},{5,68},{8,8},{9,72},{12,12},{13,76},{64,1},{65,... | collective-permute-start | bytes 393224 | tf_op jit(solution)/shard_map/ppermute | solution.py:292
  13.8 12.1 %all-to-all-start.1 = ((f32[4,2,256]{2,1,0:T(2,128)}), f32[4,2,256]{2,1,0:T(2,128)S(1)}, u32[]{:S(2)}, u32[]{:S(2)}) async-start(f32[4,2,256]{2,1,0:T(2,128)} %broadcast_in_dim.151), calls=%async_computation.1 | async-start | bytes 16384 | tf_op jit(solution)/shard_map/all_to_all | solution.py:31
  22.1 27.6 %collective-permute-start.4 = (bf16[2,2048,256]{2,1,0:T(8,128)(2,1)}, bf16[2,2048,256]{2,1,0:T(8,128)(2,1)}, u32[]{:S(2)}, u32[]{:S(2)}) collective-permute-start(bf16[2,2048,256]{2,1,0:T(8,128)(2,1)} %param.21), channel_id=1, source_target_pairs={{0,4},{1,13},{4,8},{5,1},{8,12},{9,5},{12,0},{13,9},{2,6},{3,15},{... | collective-permute-start | bytes 6291464 | tf_op jit(solution)/shard_map/ppermute | solution.py:311
  25.2 27.0 %copy-start.15 = (pred[4]{0:T(512)(128)(4,1)}, pred[4]{0:T(512)(128)(4,1)S(1)}, u32[]{:S(2)}) copy-start(pred[4]{0:T(512)(128)(4,1)S(1)} %compare_and_fusion) | copy-start | bytes 16
  28.0 21.7 %copy-start.8 = (s32[32]{0:T(128)S(1)}, s32[32]{0:T(128)}, u32[]{:S(2)}) copy-start(s32[32]{0:T(128)} %param.25) | copy-start | bytes 388
  28.0 39.3 %all-to-all-start = ((bf16[4,4,2,256,128]{4,3,2,1,0:T(8,128)(2,1)}), bf16[4,4,2,256,128]{4,3,2,1,0:T(8,128)(2,1)S(1)}, u32[]{:S(2)}, u32[]{:S(2)}) async-start(bf16[4,4,2,256,128]{4,3,2,1,0:T(8,128)(2,1)} %broadcast_in_dim.144), calls=%async_computation | async-start | bytes 4194304 | tf_op jit(solution)/shard_map/all_to_all | solution.py:31
  52.8 0.6 copy-start.12
  54.7 10.3 %collective-permute-start.8 = (bf16[784,128]{1,0:T(8,128)(2,1)}, bf16[784,128]{1,0:T(8,128)(2,1)S(1)}, u32[]{:S(2)}, u32[]{:S(2)}) collective-permute-start(bf16[784,128]{1,0:T(8,128)(2,1)} %get-tuple-element.78), channel_id=1, source_target_pairs={{0,12},{1,76},{4,0},{5,64},{8,4},{9,68},{12,8},{13,72},{64,13},{65... | collective-permute-start | bytes 602120 | tf_op jit(solution)/shard_map/ppermute | solution.py:292
  55.4 9.6 %collective-permute-start.7 = (bf16[784,128]{1,0:T(8,128)(2,1)S(1)}, bf16[784,128]{1,0:T(8,128)(2,1)S(1)}, u32[]{:S(2)}, u32[]{:S(2)}) collective-permute-start(bf16[784,128]{1,0:T(8,128)(2,1)S(1)} %get-tuple-element.79), channel_id=1, source_target_pairs={{0,8},{1,72},{4,12},{5,76},{8,0},{9,64},{12,4},{13,68},{64,9},{65,... | collective-permute-start | bytes 602120 | tf_op jit(solution)/shard_map/ppermute | solution.py:292
  56.6 9.2 %collective-permute-start.6 = (bf16[784,128]{1,0:T(8,128)(2,1)S(1)}, bf16[784,128]{1,0:T(8,128)(2,1)S(1)}, u32[]{:S(2)}, u32[]{:S(2)}) collective-permute-start(bf16[784,128]{1,0:T(8,128)(2,1)S(1)} %get-tuple-element.80), channel_id=1, source_target_pairs={{0,4},{1,68},{4,8},{5,72},{8,12},{9,76},{12,0},{13,64},{64,5},{65,... | collective-permute-start | bytes 602120 | tf_op jit(solution)/shard_map/ppermute | solution.py:292
  56.7 9.7 %collective-permute-start.5 = (bf16[784,128]{1,0:T(8,128)(2,1)S(1)}, bf16[784,128]{1,0:T(8,128)(2,1)S(1)}, u32[]{:S(2)}, u32[]{:S(2)}) collective-permute-start(bf16[784,128]{1,0:T(8,128)(2,1)S(1)} %get-tuple-element.81), channel_id=1, source_target_pairs={{0,0},{1,64},{4,4},{5,68},{8,8},{9,72},{12,12},{13,76},{64,1},{65,... | collective-permute-start | bytes 602120 | tf_op jit(solution)/shard_map/ppermute | solution.py:292
  65.1 0.7 copy-start.1
  65.8 0.7 copy-start.3
  66.5 0.7 copy-start.5
  67.2 14.8 %collective-permute-start.9 = (bf16[16,2,256,128]{3,2,1,0:T(8,128)(2,1)S(1)}, bf16[16,2,256,128]{3,2,1,0:T(8,128)(2,1)}, u32[]{:S(2)}, u32[]{:S(2)}) collective-permute-start(bf16[16,2,256,128]{3,2,1,0:T(8,128)(2,1)S(1)} %bitcast.123), channel_id=1, source_target_pairs={{0,1},{1,0},{2,3},{3,2},{4,5},{5,4},{6,7},{7,6},{8,9},{9,8},{10,11... | collective-permute-start | bytes 6291464 | tf_op jit(solution)/shard_map/ppermute | solution.py:23
  75.0 40.7 %collective-permute-start.14 = (bf16[2,2048,256]{2,1,0:T(8,128)(2,1)}, bf16[2,2048,256]{2,1,0:T(8,128)(2,1)}, u32[]{:S(2)}, u32[]{:S(2)}) collective-permute-start(bf16[2,2048,256]{2,1,0:T(8,128)(2,1)} %param.21), channel_id=1, source_target_pairs={{1,9},{5,13},{9,1},{13,5},{3,11},{7,15},{11,3},{15,7},{17,25},{21,... | collective-permute-start | bytes 6291464 | tf_op jit(solution)/shard_map/ppermute | solution.py:317
  77.0 38.7 %collective-permute-start.15 = (bf16[256,2048]{1,0:T(8,128)(2,1)}, bf16[256,2048]{1,0:T(8,128)(2,1)}, u32[]{:S(2)}, u32[]{:S(2)}) collective-permute-start(bf16[256,2048]{1,0:T(8,128)(2,1)} %param.22), channel_id=1, source_target_pairs={{1,9},{5,13},{9,1},{13,5},{3,11},{7,15},{11,3},{15,7},{17,25},{21,... | collective-permute-start | bytes 3145736 | tf_op jit(solution)/shard_map/ppermute | solution.py:317
  82.1 0.9 copy-start.2
  83.0 0.9 copy-start.4
  84.0 0.9 copy-start.6
  105.7 4.9 %collective-permute-start.10 = (bf16[256,128]{1,0:T(8,128)(2,1)S(1)}, bf16[256,128]{1,0:T(8,128)(2,1)S(1)}, u32[]{:S(2)}, u32[]{:S(2)}) collective-permute-start(bf16[256,128]{1,0:T(8,128)(2,1)S(1)} %get-tuple-element.86), channel_id=1, source_target_pairs={{0,0},{1,64},{4,4},{5,68},{8,8},{9,72},{12,12},{13,76},{64,1},{65,... | collective-permute-start | bytes 196616 | tf_op jit(solution)/shard_map/ppermute | solution.py:415
  106.4 7.2 %collective-permute-start.13 = (bf16[256,128]{1,0:T(8,128)(2,1)S(1)}, bf16[256,128]{1,0:T(8,128)(2,1)S(1)}, u32[]{:S(2)}, u32[]{:S(2)}) collective-permute-start(bf16[256,128]{1,0:T(8,128)(2,1)S(1)} %get-tuple-element.87), channel_id=1, source_target_pairs={{0,4},{1,68},{4,8},{5,72},{8,12},{9,76},{12,0},{13,64},{64,5},{65,... | collective-permute-start | bytes 196616 | tf_op jit(solution)/shard_map/ppermute | solution.py:415
  108.4 6.7 %collective-permute-start.12 = (bf16[256,128]{1,0:T(8,128)(2,1)S(1)}, bf16[256,128]{1,0:T(8,128)(2,1)S(1)}, u32[]{:S(2)}, u32[]{:S(2)}) collective-permute-start(bf16[256,128]{1,0:T(8,128)(2,1)S(1)} %get-tuple-element.88), channel_id=1, source_target_pairs={{0,8},{1,72},{4,12},{5,76},{8,0},{9,64},{12,4},{13,68},{64,9},{65,... | collective-permute-start | bytes 196616 | tf_op jit(solution)/shard_map/ppermute | solution.py:415
  110.6 5.0 %collective-permute-start.11 = (bf16[256,128]{1,0:T(8,128)(2,1)S(1)}, bf16[256,128]{1,0:T(8,128)(2,1)S(1)}, u32[]{:S(2)}, u32[]{:S(2)}) collective-permute-start(bf16[256,128]{1,0:T(8,128)(2,1)S(1)} %get-tuple-element.89), channel_id=1, source_target_pairs={{0,12},{1,76},{4,0},{5,64},{8,4},{9,68},{12,8},{13,72},{64,13},{65... | collective-permute-start | bytes 196616 | tf_op jit(solution)/shard_map/ppermute | solution.py:415
  118.5 10.8 %copy-start.14 = (f32[2,2048]{1,0:T(2,128)S(1)}, f32[2,2048]{1,0:T(2,128)}, u32[]{:S(2)}) copy-start(f32[2,2048]{1,0:T(2,128)} %param.20) | copy-start | bytes 49156
  118.6 9.2 %collective-permute-start.16 = (bf16[2,64,2048]{2,1,0:T(8,128)(2,1)S(1)}, bf16[2,64,2048]{2,1,0:T(8,128)(2,1)S(1)}, u32[]{:S(2)}, u32[]{:S(2)}) collective-permute-start(bf16[2,64,2048]{2,1,0:T(8,128)(2,1)S(1)} %fusion.5), channel_id=1, source_target_pairs={{0,1},{1,0},{2,3},{3,2},{4,5},{5,4},{6,7},{7,6},{8,9},{9,8},{10,11... | collective-permute-start | bytes 1572872 | tf_op jit(solution)/shard_map/ppermute | solution.py:23
  128.0 8.7 %collective-permute-start.17 = (bf16[64,2048]{1,0:T(8,128)(2,1)S(1)}, bf16[64,2048]{1,0:T(8,128)(2,1)S(1)}, u32[]{:S(2)}, u32[]{:S(2)}) collective-permute-start(bf16[64,2048]{1,0:T(8,128)(2,1)S(1)} %fusion.6), channel_id=1, source_target_pairs={{0,2},{2,0},{1,3},{3,1},{4,6},{6,4},{5,7},{7,5},{8,10},{10,8},{9,1... | collective-permute-start | bytes 786440 | tf_op jit(solution)/shard_map/ppermute | solution.py:23
  139.5 36.3 %copy-start.9 = (bf16[2,2048,256]{2,1,0:T(8,128)(2,1)S(1)}, bf16[2,2048,256]{2,1,0:T(8,128)(2,1)}, u32[]{:S(2)}) copy-start(bf16[2,2048,256]{2,1,0:T(8,128)(2,1)} %param.21) | copy-start | bytes 6291460
  139.5 36.3 %all-to-all-start.2 = ((bf16[8,64,2048]{2,1,0:T(8,128)(2,1)}), bf16[8,64,2048]{2,1,0:T(8,128)(2,1)}, u32[]{:S(2)}, u32[]{:S(2)}) async-start(bf16[8,64,2048]{2,1,0:T(8,128)(2,1)} %broadcast_in_dim.168), calls=%async_computation.2 | async-start | bytes 4194304 | tf_op jit(solution)/shard_map/all_to_all | solution.py:31
  147.6 16.3 %collective-permute-start.18 = (bf16[256,2048]{1,0:T(8,128)(2,1)}, bf16[256,2048]{1,0:T(8,128)(2,1)S(1)}, u32[]{:S(2)}, u32[]{:S(2)}) collective-permute-start(bf16[256,2048]{1,0:T(8,128)(2,1)} %param.22), channel_id=1, source_target_pairs={{0,4},{1,13},{4,8},{5,1},{8,12},{9,5},{12,0},{13,9},{2,6},{3,15},{... | collective-permute-start | bytes 3145736 | tf_op jit(solution)/shard_map/ppermute | solution.py:311
  175.8 4.5 %collective-permute-start.19 = (bf16[512,2048]{1,0:T(8,128)(2,1)}, bf16[512,2048]{1,0:T(8,128)(2,1)}, u32[]{:S(2)}, u32[]{:S(2)}) collective-permute-start(bf16[512,2048]{1,0:T(8,128)(2,1)} %bitcast.80.tokens_ref), channel_id=1, source_target_pairs={{0,1},{1,0},{2,3},{3,2},{4,5},{5,4},{6,7},{7,6},{8,9},{9,8},{10,11... | collective-permute-start | bytes 6291464 | tf_op jit(solution)/shard_map/ppermute | solution.py:23
  175.8 1.6 copy-start.10
  186.6 7.0 %collective-permute-start.20 = (bf16[512,2048]{1,0:T(8,128)(2,1)S(1)}, bf16[512,2048]{1,0:T(8,128)(2,1)S(1)}, u32[]{:S(2)}, u32[]{:S(2)}) collective-permute-start(bf16[512,2048]{1,0:T(8,128)(2,1)S(1)} %shard_map.138), channel_id=1, source_target_pairs={{0,1},{1,0},{2,3},{3,2},{4,5},{5,4},{6,7},{7,6},{8,9},{9,8},{10,11... | collective-permute-start | bytes 6291464 | tf_op jit(solution)/shard_map/ppermute | solution.py:23

commit v9 on v8

--- a/solution.py
+++ b/solution.py
@@ -322,7 +322,6 @@
 
     qkv_raw = jnp.einsum("td,cdw->ctw", states_in, w_qkv, preferred_element_type=F32)
     squares = jnp.sum(qkv_raw[:2] * qkv_raw[:2], axis=2)
-    squares = jnp.sum(spread(squares, HEAD), axis=0)
     cached_own = spread(cached, "x").reshape((n_x * n_z,) + cached.shape[1:])
     def own_group(table):
         return lax.dynamic_slice_in_dim(table, blk, 1, 0)
@@ -353,12 +352,24 @@
         [turned(0), turned(1), qkv_raw[2].astype(BF).reshape(rows, heads_here, HD)]
     ).transpose(2, 0, 1, 3).reshape(heads_here, 3 * rows, HD)
     qkv = jnp.concatenate([qkv, jnp.broadcast_to(terms, (heads_here,) + terms.shape)], axis=1)
-    qkv, gu_a, slot_node, node_length, node_parent, leaf_segment, leaf_node = (
+    qkv, gu_a = lax.optimization_barrier((qkv, gu_a))
+    qkv_parts = [across(select_row(qkv, (z_at + s) % n_z), s) for s in range(n_z)]
+
+    terms = jnp.stack([part[3 * rows : 3 * rows + term_rows] for part in qkv_parts]).astype(F32)
+    squares = jnp.sum(terms.reshape(n_z, 3, 2, rows), axis=1).transpose(0, 2, 1)
+    for axis in ("yhi", "ylo"):
+        squares = squares + shift(squares, axis, 1)
+    factors = lax.rsqrt(squares / columns + EPS)
+    w_gate_up, w_down, qkv_parts = lax.optimization_barrier((w_gate_up, w_down, qkv_parts))
+    cached_own, qkv_parts, slot_node, node_length, node_parent, leaf_segment, leaf_node = (
         lax.optimization_barrier(
-            (qkv, gu_a, slot_node, node_length, node_parent, leaf_segment, leaf_node)
+            (cached_own, qkv_parts, slot_node, node_length, node_parent, leaf_segment, leaf_node)
         )
     )
-    qkv_parts = [across(select_row(qkv, (z_at + s) % n_z), s) for s in range(n_z)]
+    cached_parts = [cached_own, shift(cached_own, "core", 1)]
+
+
+    gu_b, dn_b = beyond(w_gate_up), beyond(w_down)
 
     group_from = jnp.stack(
         [(core * n_x + x_at) * n_z + (z_at - g) % n_z for g in range(n_z)]
@@ -388,20 +399,6 @@
     counts = jnp.sum(needed.astype(jnp.int32), axis=2)
     row_info = jnp.stack([middle, root, segments], axis=-1)
 
-    terms = jnp.stack([part[3 * rows : 3 * rows + term_rows] for part in qkv_parts]).astype(F32)
-    squares = jnp.sum(terms.reshape(n_z, 3, 2, rows), axis=1).transpose(0, 2, 1)
-    factors = lax.rsqrt(squares / columns + EPS)
-    w_gate_up, w_down, qkv_parts = lax.optimization_barrier((w_gate_up, w_down, qkv_parts))
-    cached_own, qkv_parts, slot_nodes, slot_lengths, lists, counts, row_info, factors = (
-        lax.optimization_barrier(
-            (cached_own, qkv_parts, slot_nodes, slot_lengths, lists, counts, row_info, factors)
-        )
-    )
-    cached_parts = [cached_own, shift(cached_own, "core", 1)]
-
-
-    gu_b, dn_b = beyond(w_gate_up), beyond(w_down)
-
     attended = attention(
         slot_nodes, slot_lengths, lists, counts, qkv_parts, row_info, segments[:, None, :],
         factors, factors[:, None, :, 1], cached_parts,

time: 230 us -> 225 us (0.978)
  other arithmetic: 15.5 us -> 23.1 us
  local copies, waits for them, and re-layouts: 18.8 us -> 14.7 us
  waiting for transfers between devices: 60.2 us -> 56.5 us
  starting transfers between devices: 59.8 us -> 56.8 us
    all_to_all x3 -> x2, starting transfers between devices: 20.8 us -> 10.5 us  [spread(): return lax.all_to_all(copies, axes, 0, 0, tiled=True)]
    ppermute x2, waiting for transfers between devices: 33.3 us -> 24.8 us  [beside(): lax.ppermute(weights, ('z', 'core'), [(z * 2 + c, (z + 1 - 2 * c) % n_z *...]
    ppermute x8, waiting for transfers between devices: 0.02 us -> 5.54 us  [across(): return lax.ppermute(values, corner, pairs)]
    ppermute x5 -> x7, starting transfers between devices: 17.5 us -> 22 us  [shift(): return lax.ppermute(values, axis, [(i, (i + by) % n) for i in range(n)])]
    optimization_barrier x5 -> x1, local copies, waits for them, and re-layouts: 2.78 us -> 0.08 us  [on_device(): lax.optimization_barrier((cached_own, qkv_parts, slot_node, node_length,...]
    another operation x4, other arithmetic: 0.06 us -> 2.69 us  [head_piece(): jnp.stack([lax.dynamic_slice_in_dim(c[0], cut, HD, 1) for c in (cache_key...]
    unnamed x36, local copies, waits for them, and re-layouts: 5.3 us -> 2.85 us
    select_n x1, other arithmetic: 1.57 us -> 3.95 us  [on_device(): jnp.where(core == 0, w_gate_up, gu_b)]
  transfers between devices with their start and end apart: 24 -> 25, of which waited for: 10 -> 14; matrix products, arithmetic and copies ran while one was open for 12% -> 12% of each run, Pallas kernels for 12% -> 12%
where the time goes in v9:
time: 225 us; the launch traced here: 224 us
  starting transfers between devices  56.8 us (25%)
  waiting for transfers between devices  56.5 us (25%)
  blocking collectives  33.1 us (15%)
  Pallas kernels  32.2 us (14%)
  other arithmetic  23.1 us (10%)
  local copies, waits for them, and re-layouts  14.7 us (7%)
  matrix products  7.56 us (3%)
    all_to_all x1, blocking collectives, on_device(): lax.all_to_all(total.astype(BF).reshape(tokens.shape), plane, 0, 0, tiled...  33.1 us
    ppermute x2, waiting for transfers between devices, beside(): lax.ppermute(weights, ('z', 'core'), [(z * 2 + c, (z + 1 - 2 * c) % n_z *...  24.8 us
    ppermute x7, starting transfers between devices, shift(): return lax.ppermute(values, axis, [(i, (i + by) % n) for i in range(n)])  22 us
    pallas_call x1, Pallas kernels, attention(): pl.pallas_call(attention_body, out_shape=jax.ShapeDtypeStruct((groups, ro...  19.6 us
    pallas_call x2, Pallas kernels, feed_forward(): pl.pallas_call(feed_forward_body, out_shape=jax.ShapeDtypeStruct((rows, w...  12.6 us
    ppermute x7, waiting for transfers between devices, shift(): return lax.ppermute(values, axis, [(i, (i + by) % n) for i in range(n)])  12.4 us
    all_to_all x2, waiting for transfers between devices, spread(): return lax.all_to_all(copies, axes, 0, 0, tiled=True)  11.8 us
    ppermute x8, starting transfers between devices, across(): return lax.ppermute(values, corner, pairs)  10.9 us
  transfers between devices with their start and end apart: 25, of which 14 were waited for; matrix products, arithmetic and copies ran while one was open for 12% of the time, Pallas kernels for 12%

profile of v9, /device:TPU:0, one launch (start us, length us, event | category | flops | bytes accessed | tf_op | source)
XLA Modules:
  0.0 224.5 jit_solution(2638320675848408721)
XLA Ops:
  0.0 1.2 constant_dynamic-slice_fusion.8
  1.9 4.0 %collective-permute-start.2 = (bf16[2,256,128]{2,1,0:T(8,128)(2,1)}, bf16[2,256,128]{2,1,0:T(8,128)(2,1)}, u32[]{:S(2)}, u32[]{:S(2)}) collective-permute-start(bf16[2,256,128]{2,1,0:T(8,128)(2,1)} %pad_maximum_fusion.5), channel_id=1, source_target_pairs={{0,8},{1,72},{4,12},{5,76},{8,0},{9,64},{12,4},{13,68},{64,9},{65,... | collective-permute-start | bytes 393224 | tf_op jit(solution)/shard_map/ppermute | solution.py:292
  7.9 1.3 collective-permute-start.1
  9.9 2.2 collective-permute-start
  12.0 1.0 collective-permute-start.4
  13.1 4.7 %convolution_bitcast_fusion = f32[3,256,512]{1,2,0:T(8,128)S(1)} fusion(bf16[3,2048,512]{2,1,0:T(8,128)(2,1)} %param.17, bf16[256,2048]{1,0:T(8,128)(2,1)S(1)} %copy-done.11), kind=kOutput, calls=%fused_computation.11 | convolution fusion | flops 1610612736 | bytes 8912896 | tf_op jit(solution)/shard_map/td,cdw->ctw/dot_general | solution.py:323
  19.7 1.2 broadcast_multiply_fusion
  21.1 1.2 pad_maximum_fusion.1
  22.3 1.8 broadcast_in_dim.141
  24.1 4.3 %all-to-all-start = ((bf16[4,4,2,256,128]{4,3,2,1,0:T(8,128)(2,1)}), bf16[4,4,2,256,128]{4,3,2,1,0:T(8,128)(2,1)S(1)}, u32[]{:S(2)}, u32[]{:S(2)}) async-start(bf16[4,4,2,256,128]{4,3,2,1,0:T(8,128)(2,1)} %broadcast_in_dim.141), calls=%async_computation | async-start | bytes 4194304 | tf_op jit(solution)/shard_map/all_to_all | solution.py:31
  28.9 0.9 maximum_bitcast_fusion
  29.8 1.5 copy.46
  32.3 8.7 %collective-permute-done.4.gu_a = bf16[2,2048,256]{2,1,0:T(8,128)(2,1)} collective-permute-done((bf16[2,2048,256]{2,1,0:T(8,128)(2,1)}, bf16[2,2048,256]{2,1,0:T(8,128)(2,1)}, u32[]{:S(2)}, u32[]{:S(2)}) %collective-permute-start.4) | collective-permute-done | bytes 2097184 | tf_op jit(solution)/shard_map/ppermute | solution.py:311
  41.8 1.2 collective-permute-start.7
  45.1 1.8 collective-permute-done.8.rest_3_
  47.5 1.7 collective-permute-done.7.rest_2_
  49.2 2.0 collective-permute-done.6.rest_1_
  57.3 10.8 %collective-permute-start.11 = (bf16[16,2,256,128]{3,2,1,0:T(8,128)(2,1)S(1)}, bf16[16,2,256,128]{3,2,1,0:T(8,128)(2,1)}, u32[]{:S(2)}, u32[]{:S(2)}) collective-permute-start(bf16[16,2,256,128]{3,2,1,0:T(8,128)(2,1)S(1)} %bitcast.123), channel_id=1, source_target_pairs={{0,1},{1,0},{2,3},{3,2},{4,5},{5,4},{6,7},{7,6},{8,9},{9,8},{10,11... | collective-permute-start | bytes 6291464 | tf_op jit(solution)/shard_map/ppermute | solution.py:23
  68.1 2.0 collective-permute-start.16
  74.8 2.5 %collective-permute-done.9 = f32[4,256,2]{1,2,0:T(2,128)S(1)} collective-permute-done((f32[4,256,2]{1,2,0:T(2,128)S(1)}, f32[4,256,2]{1,2,0:T(2,128)S(1)}, u32[]{:S(2)}, u32[]{:S(2)}) %collective-permute-start.9) | collective-permute-done | bytes 8224 | tf_op jit(solution)/shard_map/ppermute | solution.py:23
  78.4 1.6 collective-permute-start.17
  80.0 0.9 collective-permute-done.10
  81.2 0.9 copy-done.2
  82.1 0.9 copy-done.4
  83.1 0.9 copy-done.6
  84.0 19.6 %shard_map.136 = bf16[4,256,128]{2,1,0:T(8,128)(2,1)S(1)} custom-call(s32[32]{0:T(128)S(1)} %get-tuple-element.63.nodes_ref, s32[32]{0:T(128)S(1)} %and_select_fusion.lengths_ref, s32[4,2,12]{2,1,0:T(2,128)S(1)} %copy.51.lists_ref, s32[4,2]{1,0:T(4,128)S(1)} %copy.52.counts_ref, bf16[784,128]{1,0:T(8,128)(2,1)S(1)} %copy-done.6, ...), custom_call_target="tpu_custom_call" | custom-call | flops 2000000000 | bytes 6000000 | tf_op jit(solution)/shard_map/pallas_call | solution.py:169
  104.3 1.3 collective-permute-start.15
  105.6 3.5 %collective-permute-start.14 = (bf16[256,128]{1,0:T(8,128)(2,1)S(1)}, bf16[256,128]{1,0:T(8,128)(2,1)S(1)}, u32[]{:S(2)}, u32[]{:S(2)}) collective-permute-start(bf16[256,128]{1,0:T(8,128)(2,1)S(1)} %get-tuple-element.76), channel_id=1, source_target_pairs={{0,8},{1,72},{4,12},{5,76},{8,0},{9,64},{12,4},{13,68},{64,9},{65,... | collective-permute-start | bytes 196616 | tf_op jit(solution)/shard_map/ppermute | solution.py:412
  109.0 2.4 %collective-permute-start.13 = (bf16[256,128]{1,0:T(8,128)(2,1)S(1)}, bf16[256,128]{1,0:T(8,128)(2,1)S(1)}, u32[]{:S(2)}, u32[]{:S(2)}) collective-permute-start(bf16[256,128]{1,0:T(8,128)(2,1)S(1)} %get-tuple-element.77), channel_id=1, source_target_pairs={{0,12},{1,76},{4,0},{5,64},{8,4},{9,68},{12,8},{13,72},{64,13},{65... | collective-permute-start | bytes 196616 | tf_op jit(solution)/shard_map/ppermute | solution.py:412
  111.7 1.6 collective-permute-done.13
  113.4 2.8 %fusion.1 = f32[256,2048]{1,0:T(8,128)S(1)} fusion(bf16[256,512]{1,0:T(8,128)(2,1)S(1)} %pad_maximum_fusion.2, s32[]{:T(128)S(6)} %select_n.352, bf16[512,2048]{1,0:T(8,128)(2,1)} %param.19), kind=kOutput, calls=%fused_computation.9 | convolution fusion | flops 541065216 | bytes 4456452 | tf_op jit(solution)/shard_map/dot_general | solution.py:416
  116.3 7.4 %collective-permute-start.18 = (bf16[2,64,2048]{2,1,0:T(8,128)(2,1)S(1)}, bf16[2,64,2048]{2,1,0:T(8,128)(2,1)S(1)}, u32[]{:S(2)}, u32[]{:S(2)}) collective-permute-start(bf16[2,64,2048]{2,1,0:T(8,128)(2,1)S(1)} %fusion.5), channel_id=1, source_target_pairs={{0,1},{1,0},{2,3},{3,2},{4,5},{5,4},{6,7},{7,6},{8,9},{9,8},{10,11... | collective-permute-start | bytes 1572872 | tf_op jit(solution)/shard_map/ppermute | solution.py:23
  123.7 1.5 collective-permute-done.18
  125.4 1.4 collective-permute-start.19
  126.8 7.3 %collective-permute-done.19 = bf16[64,2048]{1,0:T(8,128)(2,1)S(1)} collective-permute-done((bf16[64,2048]{1,0:T(8,128)(2,1)S(1)}, bf16[64,2048]{1,0:T(8,128)(2,1)S(1)}, u32[]{:S(2)}, u32[]{:S(2)}) %collective-permute-start.19) | collective-permute-done | bytes 262176 | tf_op jit(solution)/shard_map/ppermute | solution.py:23
  134.3 1.1 add_convert_fusion.2
  135.4 1.6 broadcast_in_dim.164
  137.0 6.2 %all-to-all-start.1 = ((bf16[8,64,2048]{2,1,0:T(8,128)(2,1)}), bf16[8,64,2048]{2,1,0:T(8,128)(2,1)S(1)}, u32[]{:S(2)}, u32[]{:S(2)}) async-start(bf16[8,64,2048]{2,1,0:T(8,128)(2,1)} %broadcast_in_dim.164), calls=%async_computation.1 | async-start | bytes 4194304 | tf_op jit(solution)/shard_map/all_to_all | solution.py:31
  143.1 1.0 collective-permute-start.20
  144.2 16.1 %collective-permute-done.20.dn_a = bf16[256,2048]{1,0:T(8,128)(2,1)S(1)} collective-permute-done((bf16[256,2048]{1,0:T(8,128)(2,1)}, bf16[256,2048]{1,0:T(8,128)(2,1)S(1)}, u32[]{:S(2)}, u32[]{:S(2)}) %collective-permute-start.20) | collective-permute-done | bytes 1048608 | tf_op jit(solution)/shard_map/ppermute | solution.py:311
  160.2 11.1 %all-to-all-done.1 = bf16[8,64,2048]{2,1,0:T(8,128)(2,1)S(1)} async-done(((bf16[8,64,2048]{2,1,0:T(8,128)(2,1)}), bf16[8,64,2048]{2,1,0:T(8,128)(2,1)S(1)}, u32[]{:S(2)}, u32[]{:S(2)}) %all-to-all-start.1) | async-done | bytes 2097184 | tf_op jit(solution)/shard_map/all_to_all | solution.py:31
  171.3 3.9 %broadcast_select_fusion.gu_b = bf16[2,2048,256]{2,1,0:T(8,128)(2,1)} fusion(bf16[2,2048,256]{2,1,0:T(8,128)(2,1)} %param.21, bf16[2,2048,256]{2,1,0:T(8,128)(2,1)} %collective-permute-done.16, pred[]{:T(512)S(6)} %eq.236), kind=kLoop, calls=%fused_computation.10 | loop fusion | flops 1048576 | bytes 6291457 | tf_op jit(solution)/shard_map/jit(_where)/select_n | solution.py:436
  175.6 6.3 %shard_map.138 = bf16[512,2048]{1,0:T(8,128)(2,1)S(1)} custom-call(bf16[512,2048]{1,0:T(8,128)(2,1)} %collective-permute-done.21.tokens_ref, bf16[2,2048,256]{2,1,0:T(8,128)(2,1)} %collective-permute-done.4.gu_a, bf16[256,2048]{1,0:T(8,128)(2,1)S(1)} %collective-permute-done.20.dn_a, bf16[2,2048,256]{2,1,0:T(8,128)(2,1)} %broadcast_select_fusion.gu_b, ...), custom_call_target="tpu_custom_call" | custom-call | flops 3221225472 | bytes 10485760 | tf_op jit(solution)/shard_map/pallas_call | solution.py:240
  181.9 0.9 collective-permute-start.22
  182.8 6.3 %shard_map.137 = bf16[512,2048]{1,0:T(8,128)(2,1)S(1)} custom-call(bf16[512,2048]{1,0:T(8,128)(2,1)} %bitcast.128, bf16[2,2048,256]{2,1,0:T(8,128)(2,1)} %collective-permute-done.4.gu_a, bf16[256,2048]{1,0:T(8,128)(2,1)S(1)} %collective-permute-done.20.dn_a, bf16[2,2048,256]{2,1,0:T(8,128)(2,1)} %broadcast_select_fusion.gu_b, ...), custom_call_target="tpu_custom_call" | custom-call | flops 3221225472 | bytes 10485760 | tf_op jit(solution)/shard_map/pallas_call | solution.py:240
  189.1 0.9 add_convert_fusion
  190.0 33.1 %all_to_all.15 = bf16[8,64,2048]{2,1,0:T(8,128)(2,1)S(1)} all-to-all(bf16[8,64,2048]{2,1,0:T(8,128)(2,1)S(1)} %bitcast.125), channel_id=1, replica_groups=mesh['yhi'=2,'x'=4,'z'=4,'ylo'=2,'core'=2] {'yhi','x'}, dimensions={0} | all-to-all | bytes 4194304 | tf_op jit(solution)/shard_map/all_to_all | solution.py:441
  223.6 0.9 add_convert_fusion.1
  (139 shorter events, 24.5 us)
Async XLA Ops:
  0.0 19.0 %copy-start = (s32[32,256]{1,0:T(8,128)S(1)}, s32[32,256]{1,0:T(8,128)}, u32[]{:S(2)}) copy-start(s32[32,256]{1,0:T(8,128)} %param.28) | copy-start | bytes 98308
  0.0 13.1 %copy-start.11 = (bf16[256,2048]{1,0:T(8,128)(2,1)S(1)}, bf16[256,2048]{1,0:T(8,128)(2,1)}, u32[]{:S(2)}) copy-start(bf16[256,2048]{1,0:T(8,128)(2,1)} %param.16) | copy-start | bytes 3145732
  1.9 19.2 %collective-permute-start.2 = (bf16[2,256,128]{2,1,0:T(8,128)(2,1)}, bf16[2,256,128]{2,1,0:T(8,128)(2,1)}, u32[]{:S(2)}, u32[]{:S(2)}) collective-permute-start(bf16[2,256,128]{2,1,0:T(8,128)(2,1)} %pad_maximum_fusion.5), channel_id=1, source_target_pairs={{0,8},{1,72},{4,12},{5,76},{8,0},{9,64},{12,4},{13,68},{64,9},{65,... | collective-permute-start | bytes 393224 | tf_op jit(solution)/shard_map/ppermute | solution.py:292
  6.5 14.6 %collective-permute-start.3 = (bf16[2,256,128]{2,1,0:T(8,128)(2,1)}, bf16[2,256,128]{2,1,0:T(8,128)(2,1)}, u32[]{:S(2)}, u32[]{:S(2)}) collective-permute-start(bf16[2,256,128]{2,1,0:T(8,128)(2,1)} %pad_maximum_fusion.6), channel_id=1, source_target_pairs={{0,12},{1,76},{4,0},{5,64},{8,4},{9,68},{12,8},{13,72},{64,13},{65... | collective-permute-start | bytes 393224 | tf_op jit(solution)/shard_map/ppermute | solution.py:292
  7.9 13.2 %collective-permute-start.1 = (bf16[2,256,128]{2,1,0:T(8,128)(2,1)}, bf16[2,256,128]{2,1,0:T(8,128)(2,1)}, u32[]{:S(2)}, u32[]{:S(2)}) collective-permute-start(bf16[2,256,128]{2,1,0:T(8,128)(2,1)} %pad_maximum_fusion.4), channel_id=1, source_target_pairs={{0,4},{1,68},{4,8},{5,72},{8,12},{9,76},{12,0},{13,64},{64,5},{65,... | collective-permute-start | bytes 393224 | tf_op jit(solution)/shard_map/ppermute | solution.py:292
  9.9 11.2 %collective-permute-start = (bf16[2,256,128]{2,1,0:T(8,128)(2,1)}, bf16[2,256,128]{2,1,0:T(8,128)(2,1)}, u32[]{:S(2)}, u32[]{:S(2)}) collective-permute-start(bf16[2,256,128]{2,1,0:T(8,128)(2,1)} %pad_maximum_fusion.3), channel_id=1, source_target_pairs={{0,0},{1,64},{4,4},{5,68},{8,8},{9,72},{12,12},{13,76},{64,1},{65,... | collective-permute-start | bytes 393224 | tf_op jit(solution)/shard_map/ppermute | solution.py:292
  12.0 29.0 %collective-permute-start.4 = (bf16[2,2048,256]{2,1,0:T(8,128)(2,1)}, bf16[2,2048,256]{2,1,0:T(8,128)(2,1)}, u32[]{:S(2)}, u32[]{:S(2)}) collective-permute-start(bf16[2,2048,256]{2,1,0:T(8,128)(2,1)} %param.21), channel_id=1, source_target_pairs={{0,4},{1,13},{4,8},{5,1},{8,12},{9,5},{12,0},{13,9},{2,6},{3,15},{... | collective-permute-start | bytes 6291464 | tf_op jit(solution)/shard_map/ppermute | solution.py:311
  13.1 6.3 %copy-start.16 = (s32[28]{0:T(128)}, s32[28]{0:T(128)S(1)}, u32[]{:S(2)}) copy-start(s32[28]{0:T(128)S(1)} %iota_add_fusion) | copy-start | bytes 340
  17.8 1.0 copy-start.12
  17.8 1.4 copy-start.14
  17.8 1.6 copy-start.15
  17.9 1.7 copy-start.7
  24.1 27.9 %all-to-all-start = ((bf16[4,4,2,256,128]{4,3,2,1,0:T(8,128)(2,1)}), bf16[4,4,2,256,128]{4,3,2,1,0:T(8,128)(2,1)S(1)}, u32[]{:S(2)}, u32[]{:S(2)}) async-start(bf16[4,4,2,256,128]{4,3,2,1,0:T(8,128)(2,1)} %broadcast_in_dim.141), calls=%async_computation | async-start | bytes 4194304 | tf_op jit(solution)/shard_map/all_to_all | solution.py:31
  31.3 20.7 %copy-start.8 = (s32[32]{0:T(128)S(1)}, s32[32]{0:T(128)}, u32[]{:S(2)}) copy-start(s32[32]{0:T(128)} %param.25) | copy-start | bytes 388
  31.5 11.7 %copy-start.17 = (s32[32]{0:T(128)}, s32[32]{0:T(128)S(1)}, u32[]{:S(2)}) copy-start(s32[32]{0:T(128)S(1)} %stack.237) | copy-start | bytes 388
  41.1 5.8 %collective-permute-start.8 = (bf16[784,128]{1,0:T(8,128)(2,1)S(1)}, bf16[784,128]{1,0:T(8,128)(2,1)S(1)}, u32[]{:S(2)}, u32[]{:S(2)}) collective-permute-start(bf16[784,128]{1,0:T(8,128)(2,1)S(1)} %get-tuple-element.66), channel_id=1, source_target_pairs={{0,12},{1,76},{4,0},{5,64},{8,4},{9,68},{12,8},{13,72},{64,13},{65... | collective-permute-start | bytes 602120 | tf_op jit(solution)/shard_map/ppermute | solution.py:292
  41.8 7.3 %collective-permute-start.7 = (bf16[784,128]{1,0:T(8,128)(2,1)S(1)}, bf16[784,128]{1,0:T(8,128)(2,1)S(1)}, u32[]{:S(2)}, u32[]{:S(2)}) collective-permute-start(bf16[784,128]{1,0:T(8,128)(2,1)S(1)} %get-tuple-element.67), channel_id=1, source_target_pairs={{0,8},{1,72},{4,12},{5,76},{8,0},{9,64},{12,4},{13,68},{64,9},{65,... | collective-permute-start | bytes 602120 | tf_op jit(solution)/shard_map/ppermute | solution.py:292
  43.0 8.2 %collective-permute-start.6 = (bf16[784,128]{1,0:T(8,128)(2,1)S(1)}, bf16[784,128]{1,0:T(8,128)(2,1)S(1)}, u32[]{:S(2)}, u32[]{:S(2)}) collective-permute-start(bf16[784,128]{1,0:T(8,128)(2,1)S(1)} %get-tuple-element.68), channel_id=1, source_target_pairs={{0,4},{1,68},{4,8},{5,72},{8,12},{9,76},{12,0},{13,64},{64,5},{65,... | collective-permute-start | bytes 602120 | tf_op jit(solution)/shard_map/ppermute | solution.py:292
  43.2 8.1 %collective-permute-start.5 = (bf16[784,128]{1,0:T(8,128)(2,1)S(1)}, bf16[784,128]{1,0:T(8,128)(2,1)S(1)}, u32[]{:S(2)}, u32[]{:S(2)}) collective-permute-start(bf16[784,128]{1,0:T(8,128)(2,1)S(1)} %get-tuple-element.69), channel_id=1, source_target_pairs={{0,0},{1,64},{4,4},{5,68},{8,8},{9,72},{12,12},{13,76},{64,1},{65,... | collective-permute-start | bytes 602120 | tf_op jit(solution)/shard_map/ppermute | solution.py:292
  49.2 28.9 %copy-start.1 = (bf16[784,128]{1,0:T(8,128)(2,1)}, bf16[784,128]{1,0:T(8,128)(2,1)S(1)}, u32[]{:S(2)}) copy-start(bf16[784,128]{1,0:T(8,128)(2,1)S(1)} %collective-permute-done.7.rest_2_) | copy-start | bytes 602116
  51.2 26.8 %copy-start.3 = (bf16[784,128]{1,0:T(8,128)(2,1)}, bf16[784,128]{1,0:T(8,128)(2,1)S(1)}, u32[]{:S(2)}) copy-start(bf16[784,128]{1,0:T(8,128)(2,1)S(1)} %collective-permute-done.6.rest_1_) | copy-start | bytes 602116
  51.2 26.8 %copy-start.5 = (bf16[784,128]{1,0:T(8,128)(2,1)}, bf16[784,128]{1,0:T(8,128)(2,1)S(1)}, u32[]{:S(2)}) copy-start(bf16[784,128]{1,0:T(8,128)(2,1)S(1)} %collective-permute-done.5.rest_0_) | copy-start | bytes 602116
  57.3 23.9 %collective-permute-start.11 = (bf16[16,2,256,128]{3,2,1,0:T(8,128)(2,1)S(1)}, bf16[16,2,256,128]{3,2,1,0:T(8,128)(2,1)}, u32[]{:S(2)}, u32[]{:S(2)}) collective-permute-start(bf16[16,2,256,128]{3,2,1,0:T(8,128)(2,1)S(1)} %bitcast.123), channel_id=1, source_target_pairs={{0,1},{1,0},{2,3},{3,2},{4,5},{5,4},{6,7},{7,6},{8,9},{9,8},{10,11... | collective-permute-start | bytes 6291464 | tf_op jit(solution)/shard_map/ppermute | solution.py:23
  68.1 45.3 %collective-permute-start.16 = (bf16[2,2048,256]{2,1,0:T(8,128)(2,1)}, bf16[2,2048,256]{2,1,0:T(8,128)(2,1)}, u32[]{:S(2)}, u32[]{:S(2)}) collective-permute-start(bf16[2,2048,256]{2,1,0:T(8,128)(2,1)} %param.21), channel_id=1, source_target_pairs={{1,9},{5,13},{9,1},{13,5},{3,11},{7,15},{11,3},{15,7},{17,25},{21,... | collective-permute-start | bytes 6291464 | tf_op jit(solution)/shard_map/ppermute | solution.py:317
  72.0 5.2 %collective-permute-start.9 = (f32[4,256,2]{1,2,0:T(2,128)S(1)}, f32[4,256,2]{1,2,0:T(2,128)S(1)}, u32[]{:S(2)}, u32[]{:S(2)}) collective-permute-start(f32[4,256,2]{1,2,0:T(2,128)S(1)} %bitcast.138), channel_id=1, source_target_pairs={{0,64},{64,0},{1,65},{65,1},{2,66},{66,2},{3,67},{67,3},{4,68},{68... | collective-permute-start | bytes 24584 | tf_op jit(solution)/shard_map/ppermute | solution.py:23
  77.3 3.7 %collective-permute-start.10 = (f32[4,256,2]{1,2,0:T(2,128)S(1)}, f32[4,256,2]{1,2,0:T(2,128)S(1)}, u32[]{:S(2)}, u32[]{:S(2)}) collective-permute-start(f32[4,256,2]{1,2,0:T(2,128)S(1)} %bitcast_add_fusion.2), channel_id=1, source_target_pairs={{0,2},{2,0},{1,3},{3,1},{4,6},{6,4},{5,7},{7,5},{8,10},{10,8},{9,1... | collective-permute-start | bytes 24584 | tf_op jit(solution)/shard_map/ppermute | solution.py:23
  78.4 35.0 %collective-permute-start.17 = (bf16[256,2048]{1,0:T(8,128)(2,1)}, bf16[256,2048]{1,0:T(8,128)(2,1)}, u32[]{:S(2)}, u32[]{:S(2)}) collective-permute-start(bf16[256,2048]{1,0:T(8,128)(2,1)} %param.22), channel_id=1, source_target_pairs={{1,9},{5,13},{9,1},{13,5},{3,11},{7,15},{11,3},{15,7},{17,25},{21,... | collective-permute-start | bytes 3145736 | tf_op jit(solution)/shard_map/ppermute | solution.py:317
  81.2 0.9 copy-start.2
  82.1 0.9 copy-start.4
  83.1 0.9 copy-start.6
  103.6 5.4 %collective-permute-start.12 = (bf16[256,128]{1,0:T(8,128)(2,1)S(1)}, bf16[256,128]{1,0:T(8,128)(2,1)S(1)}, u32[]{:S(2)}, u32[]{:S(2)}) collective-permute-start(bf16[256,128]{1,0:T(8,128)(2,1)S(1)} %get-tuple-element.74), channel_id=1, source_target_pairs={{0,0},{1,64},{4,4},{5,68},{8,8},{9,72},{12,12},{13,76},{64,1},{65,... | collective-permute-start | bytes 196616 | tf_op jit(solution)/shard_map/ppermute | solution.py:412
  104.3 7.1 %collective-permute-start.15 = (bf16[256,128]{1,0:T(8,128)(2,1)S(1)}, bf16[256,128]{1,0:T(8,128)(2,1)S(1)}, u32[]{:S(2)}, u32[]{:S(2)}) collective-permute-start(bf16[256,128]{1,0:T(8,128)(2,1)S(1)} %get-tuple-element.75), channel_id=1, source_target_pairs={{0,4},{1,68},{4,8},{5,72},{8,12},{9,76},{12,0},{13,64},{64,5},{65,... | collective-permute-start | bytes 196616 | tf_op jit(solution)/shard_map/ppermute | solution.py:412
  105.6 6.1 %collective-permute-start.14 = (bf16[256,128]{1,0:T(8,128)(2,1)S(1)}, bf16[256,128]{1,0:T(8,128)(2,1)S(1)}, u32[]{:S(2)}, u32[]{:S(2)}) collective-permute-start(bf16[256,128]{1,0:T(8,128)(2,1)S(1)} %get-tuple-element.76), channel_id=1, source_target_pairs={{0,8},{1,72},{4,12},{5,76},{8,0},{9,64},{12,4},{13,68},{64,9},{65,... | collective-permute-start | bytes 196616 | tf_op jit(solution)/shard_map/ppermute | solution.py:412
  109.0 4.3 %collective-permute-start.13 = (bf16[256,128]{1,0:T(8,128)(2,1)S(1)}, bf16[256,128]{1,0:T(8,128)(2,1)S(1)}, u32[]{:S(2)}, u32[]{:S(2)}) collective-permute-start(bf16[256,128]{1,0:T(8,128)(2,1)S(1)} %get-tuple-element.77), channel_id=1, source_target_pairs={{0,12},{1,76},{4,0},{5,64},{8,4},{9,68},{12,8},{13,72},{64,13},{65... | collective-permute-start | bytes 196616 | tf_op jit(solution)/shard_map/ppermute | solution.py:412
  116.2 10.6 %copy-start.13 = (f32[2,2048]{1,0:T(2,128)S(1)}, f32[2,2048]{1,0:T(2,128)}, u32[]{:S(2)}) copy-start(f32[2,2048]{1,0:T(2,128)} %param.20) | copy-start | bytes 49156
  116.3 9.0 %collective-permute-start.18 = (bf16[2,64,2048]{2,1,0:T(8,128)(2,1)S(1)}, bf16[2,64,2048]{2,1,0:T(8,128)(2,1)S(1)}, u32[]{:S(2)}, u32[]{:S(2)}) collective-permute-start(bf16[2,64,2048]{2,1,0:T(8,128)(2,1)S(1)} %fusion.5), channel_id=1, source_target_pairs={{0,1},{1,0},{2,3},{3,2},{4,5},{5,4},{6,7},{7,6},{8,9},{9,8},{10,11... | collective-permute-start | bytes 1572872 | tf_op jit(solution)/shard_map/ppermute | solution.py:23
  125.4 8.7 %collective-permute-start.19 = (bf16[64,2048]{1,0:T(8,128)(2,1)S(1)}, bf16[64,2048]{1,0:T(8,128)(2,1)S(1)}, u32[]{:S(2)}, u32[]{:S(2)}) collective-permute-start(bf16[64,2048]{1,0:T(8,128)(2,1)S(1)} %fusion.6), channel_id=1, source_target_pairs={{0,2},{2,0},{1,3},{3,1},{4,6},{6,4},{5,7},{7,5},{8,10},{10,8},{9,1... | collective-permute-start | bytes 786440 | tf_op jit(solution)/shard_map/ppermute | solution.py:23
  137.0 34.3 %all-to-all-start.1 = ((bf16[8,64,2048]{2,1,0:T(8,128)(2,1)}), bf16[8,64,2048]{2,1,0:T(8,128)(2,1)S(1)}, u32[]{:S(2)}, u32[]{:S(2)}) async-start(bf16[8,64,2048]{2,1,0:T(8,128)(2,1)} %broadcast_in_dim.164), calls=%async_computation.1 | async-start | bytes 4194304 | tf_op jit(solution)/shard_map/all_to_all | solution.py:31
  143.1 17.1 %collective-permute-start.20 = (bf16[256,2048]{1,0:T(8,128)(2,1)}, bf16[256,2048]{1,0:T(8,128)(2,1)S(1)}, u32[]{:S(2)}, u32[]{:S(2)}) collective-permute-start(bf16[256,2048]{1,0:T(8,128)(2,1)} %param.22), channel_id=1, source_target_pairs={{0,4},{1,13},{4,8},{5,1},{8,12},{9,5},{12,0},{13,9},{2,6},{3,15},{... | collective-permute-start | bytes 3145736 | tf_op jit(solution)/shard_map/ppermute | solution.py:311
  171.3 4.0 %copy-start.9 = (bf16[8,64,2048]{2,1,0:T(8,128)(2,1)}, bf16[8,64,2048]{2,1,0:T(8,128)(2,1)S(1)}, u32[]{:S(2)}) copy-start(bf16[8,64,2048]{2,1,0:T(8,128)(2,1)S(1)} %all-to-all-done.1) | copy-start | bytes 6291460
  171.3 4.3 %collective-permute-start.21 = (bf16[512,2048]{1,0:T(8,128)(2,1)S(1)}, bf16[512,2048]{1,0:T(8,128)(2,1)}, u32[]{:S(2)}, u32[]{:S(2)}) collective-permute-start(bf16[512,2048]{1,0:T(8,128)(2,1)S(1)} %bitcast.127), channel_id=1, source_target_pairs={{0,1},{1,0},{2,3},{3,2},{4,5},{5,4},{6,7},{7,6},{8,9},{9,8},{10,11... | collective-permute-start | bytes 6291464 | tf_op jit(solution)/shard_map/ppermute | solution.py:23
  171.3 4.0 %copy-start.10 = (bf16[256,2048]{1,0:T(8,128)(2,1)S(1)}, bf16[256,2048]{1,0:T(8,128)(2,1)}, u32[]{:S(2)}) copy-start(bf16[256,2048]{1,0:T(8,128)(2,1)} %param.22) | copy-start | bytes 3145732
  181.9 7.2 %collective-permute-start.22 = (bf16[512,2048]{1,0:T(8,128)(2,1)S(1)}, bf16[512,2048]{1,0:T(8,128)(2,1)S(1)}, u32[]{:S(2)}, u32[]{:S(2)}) collective-permute-start(bf16[512,2048]{1,0:T(8,128)(2,1)S(1)} %shard_map.138), channel_id=1, source_target_pairs={{0,1},{1,0},{2,3},{3,2},{4,5},{5,4},{6,7},{7,6},{8,9},{9,8},{10,11... | collective-permute-start | bytes 6291464 | tf_op jit(solution)/shard_map/ppermute | solution.py:23

commit v10 on v5

--- a/solution.py
+++ b/solution.py
@@ -79,9 +79,11 @@
     per_part = parts[0].shape[0]
     batch = held.shape[2] // node_rows
 
-    def copies():
+    def new_copies():
         for i, part in enumerate(qkv_parts):
             yield pltpu.make_async_copy(part, qkv_ref.at[i], qkv_sems.at[i])
+
+    def cached_copies():
         for i, part in enumerate(parts):
             for j in range(per_part):
                 yield pltpu.make_async_copy(
@@ -93,9 +95,11 @@
 
     @pl.when(step == 0)
     def _():
-        for copy in copies():
+        for copy in new_copies():
             copy.start()
-        for copy in copies():
+        for copy in cached_copies():
+            copy.start()
+        for copy in new_copies():
             copy.wait()
 
     nt = (((1,), (1,)), ((), ()))
@@ -117,6 +121,12 @@
         near = jnp.where((seg_col == seg_row) & (col_at <= row_at), near, NEG)
         top = jnp.max(near, axis=1, keepdims=True)
 
+        if first == 0:
+            @pl.when(step == 0)
+            def _():
+                for copy in cached_copies():
+                    copy.wait()
+
         def score(i, top):
             best = None
             for j in range(batch):
@@ -155,6 +165,10 @@
         @pl.when(tile == t)
         def _(t=t):
             work(t * half_rows)
+
+
+def in_hbm(arrays):
+    return [pltpu.with_memory_space_constraint(a, pltpu.MemorySpace.HBM) for a in arrays]
 
 
 def attention(
@@ -172,9 +186,9 @@
         grid_spec=pltpu.PrefetchScalarGridSpec(
             num_scalar_prefetch=4,
             grid=(groups * 2,),
-            in_specs=[pl.BlockSpec(memory_space=pl.ANY)] * groups
+            in_specs=[pl.BlockSpec(memory_space=pltpu.MemorySpace.HBM)] * groups
             + [one((rows, 3)), one((1, rows)), one((rows, 2)), one((1, rows))]
-            + [pl.BlockSpec(memory_space=pl.ANY)] * len(parts),
+            + [pl.BlockSpec(memory_space=pltpu.MemorySpace.HBM)] * len(parts),
             out_specs=pl.BlockSpec((1, rows // 2, HD), lambda i, *_: (i // 2, i % 2, 0)),
             scratch_shapes=[
                 pltpu.VMEM((groups,) + qkv_parts[0].shape, BF),
@@ -189,7 +203,7 @@
         cost_estimate=pl.CostEstimate(
             flops=2 * 10**9, transcendentals=4 * 10**6, bytes_accessed=6 * 10**6
         ),
-    )(nodes, lengths, lists, counts, *qkv_parts, row_info, seg_row, factors, key_factors, *parts)
+    )(nodes, lengths, lists, counts, *in_hbm(qkv_parts), row_info, seg_row, factors, key_factors, *in_hbm(parts))
 
 
 def feed_forward_body(tokens_ref, gu_a, dn_a, gu_b, dn_b, out_ref, tokens, gu, dn, made, sems):
@@ -240,8 +254,8 @@
     return pl.pallas_call(
         feed_forward_body,
         out_shape=jax.ShapeDtypeStruct((rows, width), BF),
-        in_specs=[pl.BlockSpec(memory_space=pl.ANY)] * 5,
-        out_specs=pl.BlockSpec(memory_space=pl.ANY),
+        in_specs=[pl.BlockSpec(memory_space=pltpu.MemorySpace.HBM)] * 5,
+        out_specs=pl.BlockSpec(memory_space=pltpu.MemorySpace.HBM),
         scratch_shapes=[
             pltpu.VMEM((rows, width), BF),
             pltpu.VMEM((2, 2, width, units), BF),
@@ -363,7 +377,7 @@
     cached_own, qkv_parts = lax.optimization_barrier((cached_own, qkv_parts))
     cached_parts = [cached_own, shift(cached_own, "core", 1)]
 
-    dn_a, gu_b, dn_b = beside(w_down), beyond(w_gate_up), beyond(w_down)
+    gu_b, dn_b = beyond(w_gate_up), beyond(w_down)
 
     slots = slot_from.shape[0]
     slot_nodes = jnp.take(slot_node, slot_from)
@@ -398,7 +412,7 @@
         return lax.ppermute(values, corner, pairs)
 
     attended = jnp.concatenate([back(attended[s], s) for s in range(n_z)], axis=1)
-    attended, dn_a, gu_b, dn_b = lax.optimization_barrier((attended, dn_a, gu_b, dn_b))
+    attended, gu_b, dn_b = lax.optimization_barrier((attended, gu_b, dn_b))
     attn_part = jnp.dot(attended, w_out, preferred_element_type=F32)
     attn_part = attn_part.reshape(2, 2, rows // 4, -1)
 
@@ -414,10 +428,13 @@
     mid_state = (state_rows.astype(F32) + rms_norm(attn_proj, post_gain[0])).astype(BF)
 
     plane = ("yhi", "x")
+    mid_state, w_down = lax.optimization_barrier((mid_state, w_down))
+    dn_a = beside(w_down)
+    tokens = spread(mid_state, plane)
+    tokens, dn_a = lax.optimization_barrier((tokens, dn_a))
     weights = (
         gu_a, dn_a, jnp.where(core == 0, w_gate_up, gu_b), jnp.where(core == 0, w_down, dn_b)
     )
-    tokens = spread(mid_state, plane)
     flat = tokens.reshape(-1, tokens.shape[2])
     other = feed_forward(shift(flat, "core", 1), weights)
     total = feed_forward(flat, weights).astype(F32) + shift(other, "core", 1).astype(F32)

time: 221 us -> 217 us (0.982)
  blocking collectives: 74.6 us -> 40.5 us
  waiting for transfers between devices: 34.5 us -> 57.9 us
  starting transfers between devices: 42 us -> 55.4 us
  local copies, waits for them, and re-layouts: 15 us -> 11.6 us
  Pallas kernels: 33.7 us -> 30.5 us
    all_to_all x1 -> x0, blocking collectives: 34.7 us -> none  [spread(): return lax.all_to_all(copies, axes, 0, 0, tiled=True)]
    ppermute x2, waiting for transfers between devices: 8.58 us -> 28.5 us  [beside(): lax.ppermute(weights, ('z', 'core'), [(z * 2 + c, (z + 1 - 2 * c) % n_z *...]
    all_to_all x1 -> x2, waiting for transfers between devices: 0.01 us -> 11.1 us  [spread(): return lax.all_to_all(copies, axes, 0, 0, tiled=True)]
    ppermute x4, waiting for transfers between devices: 11.7 us -> 2.78 us  [back(): return lax.ppermute(values, corner, pairs)]
    all_to_all x1 -> x2, starting transfers between devices: 4.29 us -> 12.8 us  [spread(): return lax.all_to_all(copies, axes, 0, 0, tiled=True)]
    ppermute x5, starting transfers between devices: 15.8 us -> 20.8 us  [shift(): return lax.ppermute(values, axis, [(i, (i + by) % n) for i in range(n)])]
    ppermute x4, starting transfers between devices: 3.44 us -> 6.55 us  [back(): return lax.ppermute(values, corner, pairs)]
    pallas_call x1, Pallas kernels: 20.8 us -> 17.9 us  [attention(): pl.pallas_call(attention_body, out_shape=jax.ShapeDtypeStruct((groups, ro...]
  transfers between devices with their start and end apart: 22 -> 23, of which waited for: 9 -> 12; matrix products, arithmetic and copies ran while one was open for 11% -> 9% of each run, Pallas kernels for 12% -> 11%
where the time goes in v10:
time: 217 us; the launch traced here: 216 us
  waiting for transfers between devices  57.9 us (27%)
  starting transfers between devices  55.4 us (26%)
  blocking collectives  40.5 us (19%)
  Pallas kernels  30.5 us (14%)
  local copies, waits for them, and re-layouts  11.6 us (5%)
  other arithmetic  11.3 us (5%)
  matrix products  7.82 us (4%)
    all_to_all x1, blocking collectives, on_device(): lax.all_to_all(total.astype(BF).reshape(tokens.shape), plane, 0, 0, tiled...  32.5 us
    ppermute x2, waiting for transfers between devices, beside(): lax.ppermute(weights, ('z', 'core'), [(z * 2 + c, (z + 1 - 2 * c) % n_z *...  28.5 us
    ppermute x5, starting transfers between devices, shift(): return lax.ppermute(values, axis, [(i, (i + by) % n) for i in range(n)])  20.8 us
    pallas_call x1, Pallas kernels, attention(): pl.pallas_call(attention_body, out_shape=jax.ShapeDtypeStruct((groups, ro...  17.9 us
    all_to_all x2, starting transfers between devices, spread(): return lax.all_to_all(copies, axes, 0, 0, tiled=True)  12.8 us
    pallas_call x2, Pallas kernels, feed_forward(): pl.pallas_call(feed_forward_body, out_shape=jax.ShapeDtypeStruct((rows, w...  12.6 us
    all_to_all x2, waiting for transfers between devices, spread(): return lax.all_to_all(copies, axes, 0, 0, tiled=True)  11.1 us
    ppermute x8, starting transfers between devices, across(): return lax.ppermute(values, corner, pairs)  10.8 us
  transfers between devices with their start and end apart: 23, of which 12 were waited for; matrix products, arithmetic and copies ran while one was open for 9% of the time, Pallas kernels for 11%

profile of v10, /device:TPU:0, one launch (start us, length us, event | category | flops | bytes accessed | tf_op | source)
XLA Modules:
  0.0 215.7 jit_solution(291622540732487889)
XLA Ops:
  0.0 1.1 constant_dynamic-slice_fusion.6
  1.2 4.1 %collective-permute-start.2 = (bf16[2,256,128]{2,1,0:T(8,128)(2,1)S(1)}, bf16[2,256,128]{2,1,0:T(8,128)(2,1)S(1)}, u32[]{:S(2)}, u32[]{:S(2)}) collective-permute-start(bf16[2,256,128]{2,1,0:T(8,128)(2,1)S(1)} %pad_maximum_fusion.5), channel_id=1, source_target_pairs={{0,8},{1,72},{4,12},{5,76},{8,0},{9,64},{12,4},{13,68},{64,9},{65,... | collective-permute-start | bytes 393224 | tf_op jit(solution)/shard_map/ppermute | solution.py:306
  5.3 0.8 collective-permute-start.3
  6.1 1.4 collective-permute-start.1
  8.2 1.1 collective-permute-start.4
  11.1 5.0 %convolution_bitcast_fusion = f32[3,256,512]{1,2,0:T(8,128)S(1)} fusion(bf16[3,2048,512]{2,1,0:T(8,128)(2,1)} %param.17, bf16[256,2048]{1,0:T(8,128)(2,1)} %param.16), kind=kOutput, calls=%fused_computation.11 | convolution fusion | flops 1610612736 | bytes 8912896 | tf_op jit(solution)/shard_map/td,cdw->ctw/dot_general | solution.py:337
  17.2 1.8 broadcast_in_dim.132
  19.0 4.4 %all-to-all-start = ((bf16[4,4,2,256,128]{4,3,2,1,0:T(8,128)(2,1)}), bf16[4,4,2,256,128]{4,3,2,1,0:T(8,128)(2,1)}, u32[]{:S(2)}, u32[]{:S(2)}) async-start(bf16[4,4,2,256,128]{4,3,2,1,0:T(8,128)(2,1)} %broadcast_in_dim.132), calls=%async_computation | async-start | bytes 4194304 | tf_op jit(solution)/shard_map/all_to_all | solution.py:31
  24.7 12.5 %collective-permute-done.4.gu_a = bf16[2,2048,256]{2,1,0:T(8,128)(2,1)} collective-permute-done((bf16[2,2048,256]{2,1,0:T(8,128)(2,1)}, bf16[2,2048,256]{2,1,0:T(8,128)(2,1)}, u32[]{:S(2)}, u32[]{:S(2)}) %collective-permute-start.4) | collective-permute-done | bytes 2097184 | tf_op jit(solution)/shard_map/ppermute | solution.py:325
  37.3 0.8 collective-permute-start.8
  38.0 1.6 collective-permute-start.7
  39.7 0.8 collective-permute-start.6
  41.1 0.7 gather_fusion.2
  41.8 1.2 collective-permute-done.8.rest_3_
  43.0 2.3 %collective-permute-done.7.rest_2_ = bf16[784,128]{1,0:T(8,128)(2,1)S(1)} collective-permute-done((bf16[784,128]{1,0:T(8,128)(2,1)S(1)}, bf16[784,128]{1,0:T(8,128)(2,1)S(1)}, u32[]{:S(2)}, u32[]{:S(2)}) %collective-permute-start.7) | collective-permute-done | bytes 200736 | tf_op jit(solution)/shard_map/ppermute | solution.py:306
  45.3 2.1 collective-permute-done.6.rest_1_
  47.4 11.6 %collective-permute-start.9 = (bf16[16,2,256,128]{3,2,1,0:T(8,128)(2,1)}, bf16[16,2,256,128]{3,2,1,0:T(8,128)(2,1)}, u32[]{:S(2)}, u32[]{:S(2)}) collective-permute-start(bf16[16,2,256,128]{3,2,1,0:T(8,128)(2,1)} %bitcast.47.rest_8_), channel_id=1, source_target_pairs={{0,1},{1,0},{2,3},{3,2},{4,5},{5,4},{6,7},{7,6},{8,9},{9,8},{10,11... | collective-permute-start | bytes 6291464 | tf_op jit(solution)/shard_map/ppermute | solution.py:23
  59.0 0.8 collective-permute-start.14
  59.9 0.7 gather_fusion.3
  62.9 0.7 slice.124
  63.6 1.7 collective-permute-start.15
  65.3 8.0 %psum.7 = f32[4,256,2]{1,2,0:T(2,128)S(1)} all-reduce(f32[4,256,2]{1,2,0:T(2,128)S(1)} %bitcast.139), channel_id=1, replica_groups=mesh['yhi'=2,'x'=4,'z'=4,'ylo'=2,'core'=2] {'yhi','ylo'}, use_global_device_ids=true, to_apply=%region_13.15 | all-reduce | flops 2048 | bytes 16384 | tf_op jit(solution)/shard_map/psum | solution.py:375
  73.6 17.9 %shard_map.136 = bf16[4,256,128]{2,1,0:T(8,128)(2,1)S(1)} custom-call(s32[32]{0:T(128)S(1)} %get-tuple-element.53.nodes_ref, s32[32]{0:T(128)S(1)} %and_select_fusion.lengths_ref, s32[4,2,12]{2,1,0:T(2,128)S(1)} %copy.44.lists_ref, s32[4,2]{1,0:T(4,128)S(1)} %copy.45.counts_ref, bf16[784,128]{1,0:T(8,128)(2,1)} %copy-done.12, bf16[784,128]{1,0:T(8,128)(2,1)} %copy-done.11, ...), custom_call_target="tpu_custom_call" | custom-call | flops 2000000000 | bytes 6000000 | tf_op jit(solution)/shard_map/pallas_call | solution.py:183
  92.3 1.2 collective-permute-start.13
  93.5 3.2 %collective-permute-start.12 = (bf16[256,128]{1,0:T(8,128)(2,1)S(1)}, bf16[256,128]{1,0:T(8,128)(2,1)S(1)}, u32[]{:S(2)}, u32[]{:S(2)}) collective-permute-start(bf16[256,128]{1,0:T(8,128)(2,1)S(1)} %get-tuple-element.66), channel_id=1, source_target_pairs={{0,8},{1,72},{4,12},{5,76},{8,0},{9,64},{12,4},{13,68},{64,9},{65,... | collective-permute-start | bytes 196616 | tf_op jit(solution)/shard_map/ppermute | solution.py:412
  96.7 1.5 collective-permute-start.11
  98.2 1.5 collective-permute-done.13
  99.7 0.7 collective-permute-done.12
  101.0 2.8 %fusion.1 = f32[256,2048]{1,0:T(8,128)S(1)} fusion(bf16[256,512]{1,0:T(8,128)(2,1)S(1)} %pad_maximum_fusion.2, s32[]{:T(128)S(6)} %select_n.293, bf16[512,2048]{1,0:T(8,128)(2,1)} %param.19), kind=kOutput, calls=%fused_computation.9 | convolution fusion | flops 541065216 | bytes 4456452 | tf_op jit(solution)/shard_map/dot_general | solution.py:416
  103.8 1.3 copy-done.3
  105.2 7.6 %collective-permute-start.16 = (bf16[2,64,2048]{2,1,0:T(8,128)(2,1)S(1)}, bf16[2,64,2048]{2,1,0:T(8,128)(2,1)S(1)}, u32[]{:S(2)}, u32[]{:S(2)}) collective-permute-start(bf16[2,64,2048]{2,1,0:T(8,128)(2,1)S(1)} %fusion.5), channel_id=1, source_target_pairs={{0,1},{1,0},{2,3},{3,2},{4,5},{5,4},{6,7},{7,6},{8,9},{9,8},{10,11... | collective-permute-start | bytes 1572872 | tf_op jit(solution)/shard_map/ppermute | solution.py:23
  112.8 1.5 collective-permute-done.16
  114.3 1.3 bitcast_add_fusion
  115.8 1.4 collective-permute-start.17
  117.2 7.2 %collective-permute-done.17 = bf16[64,2048]{1,0:T(8,128)(2,1)S(1)} collective-permute-done((bf16[64,2048]{1,0:T(8,128)(2,1)S(1)}, bf16[64,2048]{1,0:T(8,128)(2,1)S(1)}, u32[]{:S(2)}, u32[]{:S(2)}) %collective-permute-start.17) | collective-permute-done | bytes 262176 | tf_op jit(solution)/shard_map/ppermute | solution.py:23
  124.6 1.1 add_convert_fusion.2
  125.7 1.6 broadcast_in_dim.140
  127.3 8.3 %all-to-all-start.1 = ((bf16[8,64,2048]{2,1,0:T(8,128)(2,1)}), bf16[8,64,2048]{2,1,0:T(8,128)(2,1)}, u32[]{:S(2)}, u32[]{:S(2)}) async-start(bf16[8,64,2048]{2,1,0:T(8,128)(2,1)} %broadcast_in_dim.140), calls=%async_computation.1 | async-start | bytes 4194304 | tf_op jit(solution)/shard_map/all_to_all | solution.py:31
  135.6 0.9 collective-permute-start.18
  136.5 16.0 %collective-permute-done.18.dn_a = bf16[256,2048]{1,0:T(8,128)(2,1)S(1)} collective-permute-done((bf16[256,2048]{1,0:T(8,128)(2,1)}, bf16[256,2048]{1,0:T(8,128)(2,1)S(1)}, u32[]{:S(2)}, u32[]{:S(2)}) %collective-permute-start.18) | collective-permute-done | bytes 1048608 | tf_op jit(solution)/shard_map/ppermute | solution.py:325
  152.6 11.1 %all-to-all-done.1 = bf16[8,64,2048]{2,1,0:T(8,128)(2,1)} async-done(((bf16[8,64,2048]{2,1,0:T(8,128)(2,1)}), bf16[8,64,2048]{2,1,0:T(8,128)(2,1)}, u32[]{:S(2)}, u32[]{:S(2)}) %all-to-all-start.1) | async-done | bytes 2097184 | tf_op jit(solution)/shard_map/all_to_all | solution.py:31
  163.6 3.2 %broadcast_select_fusion.gu_b = bf16[2,2048,256]{2,1,0:T(8,128)(2,1)} fusion(bf16[2,2048,256]{2,1,0:T(8,128)(2,1)} %param.21, bf16[2,2048,256]{2,1,0:T(8,128)(2,1)S(1)} %collective-permute-done.14, pred[]{:T(512)S(6)} %eq.164), kind=kLoop, calls=%fused_computation.10 | loop fusion | flops 1048576 | bytes 6291457 | tf_op jit(solution)/shard_map/jit(_where)/select_n | solution.py:436
  167.0 1.2 collective-permute-done.19.tokens_ref
  168.1 6.3 %shard_map.138 = bf16[512,2048]{1,0:T(8,128)(2,1)S(1)} custom-call(bf16[512,2048]{1,0:T(8,128)(2,1)} %collective-permute-done.19.tokens_ref, bf16[2,2048,256]{2,1,0:T(8,128)(2,1)} %collective-permute-done.4.gu_a, bf16[256,2048]{1,0:T(8,128)(2,1)S(1)} %collective-permute-done.18.dn_a, bf16[2,2048,256]{2,1,0:T(8,128)(2,1)} %broadcast_select_fusion.gu_b, ...), custom_call_target="tpu_custom_call" | custom-call | flops 3221225472 | bytes 10485760 | tf_op jit(solution)/shard_map/pallas_call | solution.py:254
  174.7 6.3 %shard_map.137 = bf16[512,2048]{1,0:T(8,128)(2,1)S(1)} custom-call(bf16[512,2048]{1,0:T(8,128)(2,1)} %bitcast.82.tokens_ref, bf16[2,2048,256]{2,1,0:T(8,128)(2,1)} %collective-permute-done.4.gu_a, bf16[256,2048]{1,0:T(8,128)(2,1)S(1)} %collective-permute-done.18.dn_a, bf16[2,2048,256]{2,1,0:T(8,128)(2,1)} %broadcast_select_fusion.gu_b, ...), custom_call_target="tpu_custom_call" | custom-call | flops 3221225472 | bytes 10485760 | tf_op jit(solution)/shard_map/pallas_call | solution.py:254
  180.9 0.9 add_convert_fusion
  181.8 32.5 %all_to_all.15 = bf16[8,64,2048]{2,1,0:T(8,128)(2,1)S(1)} all-to-all(bf16[8,64,2048]{2,1,0:T(8,128)(2,1)S(1)} %bitcast.126), channel_id=1, replica_groups=mesh['yhi'=2,'x'=4,'z'=4,'ylo'=2,'core'=2] {'yhi','x'}, dimensions={0} | all-to-all | bytes 4194304 | tf_op jit(solution)/shard_map/all_to_all | solution.py:441
  214.8 0.9 add_convert_fusion.1
  (125 shorter events, 10.4 us)
Async XLA Ops:
  0.0 9.6 %copy-start = (s32[32,256]{1,0:T(8,128)S(1)}, s32[32,256]{1,0:T(8,128)}, u32[]{:S(2)}) copy-start(s32[32,256]{1,0:T(8,128)} %param.28) | copy-start | bytes 98308
  0.0 9.5 %copy-start.7 = (f32[2,512]{1,0:T(2,128)S(1)}, f32[2,512]{1,0:T(2,128)}, u32[]{:S(2)}) copy-start(f32[2,512]{1,0:T(2,128)} %param.18) | copy-start | bytes 12292
  0.0 10.4 %copy-start.6 = (s32[32,8]{0,1:T(8,128)S(1)}, s32[32,8]{0,1:T(8,128)}, u32[]{:S(2)}) copy-start(s32[32,8]{0,1:T(8,128)} %param.29) | copy-start | bytes 3076
  1.2 15.9 %collective-permute-start.2 = (bf16[2,256,128]{2,1,0:T(8,128)(2,1)S(1)}, bf16[2,256,128]{2,1,0:T(8,128)(2,1)S(1)}, u32[]{:S(2)}, u32[]{:S(2)}) collective-permute-start(bf16[2,256,128]{2,1,0:T(8,128)(2,1)S(1)} %pad_maximum_fusion.5), channel_id=1, source_target_pairs={{0,8},{1,72},{4,12},{5,76},{8,0},{9,64},{12,4},{13,68},{64,9},{65,... | collective-permute-start | bytes 393224 | tf_op jit(solution)/shard_map/ppermute | solution.py:306
  5.3 11.8 %collective-permute-start.3 = (bf16[2,256,128]{2,1,0:T(8,128)(2,1)S(1)}, bf16[2,256,128]{2,1,0:T(8,128)(2,1)S(1)}, u32[]{:S(2)}, u32[]{:S(2)}) collective-permute-start(bf16[2,256,128]{2,1,0:T(8,128)(2,1)S(1)} %pad_maximum_fusion.6), channel_id=1, source_target_pairs={{0,12},{1,76},{4,0},{5,64},{8,4},{9,68},{12,8},{13,72},{64,13},{65... | collective-permute-start | bytes 393224 | tf_op jit(solution)/shard_map/ppermute | solution.py:306
  6.1 11.0 %collective-permute-start.1 = (bf16[2,256,128]{2,1,0:T(8,128)(2,1)S(1)}, bf16[2,256,128]{2,1,0:T(8,128)(2,1)S(1)}, u32[]{:S(2)}, u32[]{:S(2)}) collective-permute-start(bf16[2,256,128]{2,1,0:T(8,128)(2,1)S(1)} %pad_maximum_fusion.4), channel_id=1, source_target_pairs={{0,4},{1,68},{4,8},{5,72},{8,12},{9,76},{12,0},{13,64},{64,5},{65,... | collective-permute-start | bytes 393224 | tf_op jit(solution)/shard_map/ppermute | solution.py:306
  7.5 9.6 %collective-permute-start = (bf16[2,256,128]{2,1,0:T(8,128)(2,1)S(1)}, bf16[2,256,128]{2,1,0:T(8,128)(2,1)S(1)}, u32[]{:S(2)}, u32[]{:S(2)}) collective-permute-start(bf16[2,256,128]{2,1,0:T(8,128)(2,1)S(1)} %pad_maximum_fusion.3), channel_id=1, source_target_pairs={{0,0},{1,64},{4,4},{5,68},{8,8},{9,72},{12,12},{13,76},{64,1},{65,... | collective-permute-start | bytes 393224 | tf_op jit(solution)/shard_map/ppermute | solution.py:306
  8.2 29.0 %collective-permute-start.4 = (bf16[2,2048,256]{2,1,0:T(8,128)(2,1)}, bf16[2,2048,256]{2,1,0:T(8,128)(2,1)}, u32[]{:S(2)}, u32[]{:S(2)}) collective-permute-start(bf16[2,2048,256]{2,1,0:T(8,128)(2,1)} %param.21), channel_id=1, source_target_pairs={{0,4},{1,13},{4,8},{5,1},{8,12},{9,5},{12,0},{13,9},{2,6},{3,15},{... | collective-permute-start | bytes 6291464 | tf_op jit(solution)/shard_map/ppermute | solution.py:325
  11.1 5.4 %copy-start.8 = (s32[28]{0:T(128)S(1)}, s32[28]{0:T(128)}, u32[]{:S(2)}) copy-start(s32[28]{0:T(128)} %param.27) | copy-start | bytes 340
  11.1 5.5 %copy-start.1 = (s32[32]{0:T(128)S(1)}, s32[32]{0:T(128)}, u32[]{:S(2)}) copy-start(s32[32]{0:T(128)} %param.26) | copy-start | bytes 388
  19.0 28.4 %all-to-all-start = ((bf16[4,4,2,256,128]{4,3,2,1,0:T(8,128)(2,1)}), bf16[4,4,2,256,128]{4,3,2,1,0:T(8,128)(2,1)}, u32[]{:S(2)}, u32[]{:S(2)}) async-start(bf16[4,4,2,256,128]{4,3,2,1,0:T(8,128)(2,1)} %broadcast_in_dim.132), calls=%async_computation | async-start | bytes 4194304 | tf_op jit(solution)/shard_map/all_to_all | solution.py:31
  24.1 17.1 %copy-start.2 = (s32[32]{0:T(128)S(1)}, s32[32]{0:T(128)}, u32[]{:S(2)}) copy-start(s32[32]{0:T(128)} %param.25) | copy-start | bytes 388
  37.3 5.8 %collective-permute-start.8 = (bf16[784,128]{1,0:T(8,128)(2,1)S(1)}, bf16[784,128]{1,0:T(8,128)(2,1)S(1)}, u32[]{:S(2)}, u32[]{:S(2)}) collective-permute-start(bf16[784,128]{1,0:T(8,128)(2,1)S(1)} %get-tuple-element.56), channel_id=1, source_target_pairs={{0,12},{1,76},{4,0},{5,64},{8,4},{9,68},{12,8},{13,72},{64,13},{65... | collective-permute-start | bytes 602120 | tf_op jit(solution)/shard_map/ppermute | solution.py:306
  38.0 7.3 %collective-permute-start.7 = (bf16[784,128]{1,0:T(8,128)(2,1)S(1)}, bf16[784,128]{1,0:T(8,128)(2,1)S(1)}, u32[]{:S(2)}, u32[]{:S(2)}) collective-permute-start(bf16[784,128]{1,0:T(8,128)(2,1)S(1)} %get-tuple-element.57), channel_id=1, source_target_pairs={{0,8},{1,72},{4,12},{5,76},{8,0},{9,64},{12,4},{13,68},{64,9},{65,... | collective-permute-start | bytes 602120 | tf_op jit(solution)/shard_map/ppermute | solution.py:306
  39.7 7.7 %collective-permute-start.6 = (bf16[784,128]{1,0:T(8,128)(2,1)S(1)}, bf16[784,128]{1,0:T(8,128)(2,1)S(1)}, u32[]{:S(2)}, u32[]{:S(2)}) collective-permute-start(bf16[784,128]{1,0:T(8,128)(2,1)S(1)} %get-tuple-element.58), channel_id=1, source_target_pairs={{0,4},{1,68},{4,8},{5,72},{8,12},{9,76},{12,0},{13,64},{64,5},{65,... | collective-permute-start | bytes 602120 | tf_op jit(solution)/shard_map/ppermute | solution.py:306
  40.4 7.0 %collective-permute-start.5 = (bf16[784,128]{1,0:T(8,128)(2,1)S(1)}, bf16[784,128]{1,0:T(8,128)(2,1)S(1)}, u32[]{:S(2)}, u32[]{:S(2)}) collective-permute-start(bf16[784,128]{1,0:T(8,128)(2,1)S(1)} %get-tuple-element.59), channel_id=1, source_target_pairs={{0,0},{1,64},{4,4},{5,68},{8,8},{9,72},{12,12},{13,76},{64,1},{65,... | collective-permute-start | bytes 602120 | tf_op jit(solution)/shard_map/ppermute | solution.py:306
  43.0 30.6 %copy-start.9 = (bf16[784,128]{1,0:T(8,128)(2,1)}, bf16[784,128]{1,0:T(8,128)(2,1)S(1)}, u32[]{:S(2)}) copy-start(bf16[784,128]{1,0:T(8,128)(2,1)S(1)} %collective-permute-done.8.rest_3_) | copy-start | bytes 602116
  45.3 28.0 %copy-start.10 = (bf16[784,128]{1,0:T(8,128)(2,1)}, bf16[784,128]{1,0:T(8,128)(2,1)S(1)}, u32[]{:S(2)}) copy-start(bf16[784,128]{1,0:T(8,128)(2,1)S(1)} %collective-permute-done.7.rest_2_) | copy-start | bytes 602116
  47.4 13.5 %copy-start.11 = (bf16[784,128]{1,0:T(8,128)(2,1)}, bf16[784,128]{1,0:T(8,128)(2,1)S(1)}, u32[]{:S(2)}) copy-start(bf16[784,128]{1,0:T(8,128)(2,1)S(1)} %collective-permute-done.6.rest_1_) | copy-start | bytes 602116
  47.4 14.5 %copy-start.12 = (bf16[784,128]{1,0:T(8,128)(2,1)}, bf16[784,128]{1,0:T(8,128)(2,1)S(1)}, u32[]{:S(2)}) copy-start(bf16[784,128]{1,0:T(8,128)(2,1)S(1)} %collective-permute-done.5.rest_0_) | copy-start | bytes 602116
  47.4 26.2 %collective-permute-start.9 = (bf16[16,2,256,128]{3,2,1,0:T(8,128)(2,1)}, bf16[16,2,256,128]{3,2,1,0:T(8,128)(2,1)}, u32[]{:S(2)}, u32[]{:S(2)}) collective-permute-start(bf16[16,2,256,128]{3,2,1,0:T(8,128)(2,1)} %bitcast.47.rest_8_), channel_id=1, source_target_pairs={{0,1},{1,0},{2,3},{3,2},{4,5},{5,4},{6,7},{7,6},{8,9},{9,8},{10,11... | collective-permute-start | bytes 6291464 | tf_op jit(solution)/shard_map/ppermute | solution.py:23
  59.0 42.0 %collective-permute-start.14 = (bf16[2,2048,256]{2,1,0:T(8,128)(2,1)}, bf16[2,2048,256]{2,1,0:T(8,128)(2,1)S(1)}, u32[]{:S(2)}, u32[]{:S(2)}) collective-permute-start(bf16[2,2048,256]{2,1,0:T(8,128)(2,1)} %param.21), channel_id=1, source_target_pairs={{1,9},{5,13},{9,1},{13,5},{3,11},{7,15},{11,3},{15,7},{17,25},{21,... | collective-permute-start | bytes 6291464 | tf_op jit(solution)/shard_map/ppermute | solution.py:331
  63.6 37.4 %collective-permute-start.15 = (bf16[256,2048]{1,0:T(8,128)(2,1)}, bf16[256,2048]{1,0:T(8,128)(2,1)}, u32[]{:S(2)}, u32[]{:S(2)}) collective-permute-start(bf16[256,2048]{1,0:T(8,128)(2,1)} %param.22), channel_id=1, source_target_pairs={{1,9},{5,13},{9,1},{13,5},{3,11},{7,15},{11,3},{15,7},{17,25},{21,... | collective-permute-start | bytes 3145736 | tf_op jit(solution)/shard_map/ppermute | solution.py:331
  91.6 5.1 %collective-permute-start.10 = (bf16[256,128]{1,0:T(8,128)(2,1)S(1)}, bf16[256,128]{1,0:T(8,128)(2,1)S(1)}, u32[]{:S(2)}, u32[]{:S(2)}) collective-permute-start(bf16[256,128]{1,0:T(8,128)(2,1)S(1)} %get-tuple-element.64), channel_id=1, source_target_pairs={{0,0},{1,64},{4,4},{5,68},{8,8},{9,72},{12,12},{13,76},{64,1},{65,... | collective-permute-start | bytes 196616 | tf_op jit(solution)/shard_map/ppermute | solution.py:412
  92.3 7.4 %collective-permute-start.13 = (bf16[256,128]{1,0:T(8,128)(2,1)S(1)}, bf16[256,128]{1,0:T(8,128)(2,1)S(1)}, u32[]{:S(2)}, u32[]{:S(2)}) collective-permute-start(bf16[256,128]{1,0:T(8,128)(2,1)S(1)} %get-tuple-element.65), channel_id=1, source_target_pairs={{0,4},{1,68},{4,8},{5,72},{8,12},{9,76},{12,0},{13,64},{64,5},{65,... | collective-permute-start | bytes 196616 | tf_op jit(solution)/shard_map/ppermute | solution.py:412
  93.5 6.9 %collective-permute-start.12 = (bf16[256,128]{1,0:T(8,128)(2,1)S(1)}, bf16[256,128]{1,0:T(8,128)(2,1)S(1)}, u32[]{:S(2)}, u32[]{:S(2)}) collective-permute-start(bf16[256,128]{1,0:T(8,128)(2,1)S(1)} %get-tuple-element.66), channel_id=1, source_target_pairs={{0,8},{1,72},{4,12},{5,76},{8,0},{9,64},{12,4},{13,68},{64,9},{65,... | collective-permute-start | bytes 196616 | tf_op jit(solution)/shard_map/ppermute | solution.py:412
  96.7 4.3 %collective-permute-start.11 = (bf16[256,128]{1,0:T(8,128)(2,1)S(1)}, bf16[256,128]{1,0:T(8,128)(2,1)S(1)}, u32[]{:S(2)}, u32[]{:S(2)}) collective-permute-start(bf16[256,128]{1,0:T(8,128)(2,1)S(1)} %get-tuple-element.67), channel_id=1, source_target_pairs={{0,12},{1,76},{4,0},{5,64},{8,4},{9,68},{12,8},{13,72},{64,13},{65... | collective-permute-start | bytes 196616 | tf_op jit(solution)/shard_map/ppermute | solution.py:412
  103.8 1.3 copy-start.3
  105.1 12.0 %copy-start.5 = (f32[2,2048]{1,0:T(2,128)S(1)}, f32[2,2048]{1,0:T(2,128)}, u32[]{:S(2)}) copy-start(f32[2,2048]{1,0:T(2,128)} %param.20) | copy-start | bytes 49156
  105.2 9.1 %collective-permute-start.16 = (bf16[2,64,2048]{2,1,0:T(8,128)(2,1)S(1)}, bf16[2,64,2048]{2,1,0:T(8,128)(2,1)S(1)}, u32[]{:S(2)}, u32[]{:S(2)}) collective-permute-start(bf16[2,64,2048]{2,1,0:T(8,128)(2,1)S(1)} %fusion.5), channel_id=1, source_target_pairs={{0,1},{1,0},{2,3},{3,2},{4,5},{5,4},{6,7},{7,6},{8,9},{9,8},{10,11... | collective-permute-start | bytes 1572872 | tf_op jit(solution)/shard_map/ppermute | solution.py:23
  115.8 8.7 %collective-permute-start.17 = (bf16[64,2048]{1,0:T(8,128)(2,1)S(1)}, bf16[64,2048]{1,0:T(8,128)(2,1)S(1)}, u32[]{:S(2)}, u32[]{:S(2)}) collective-permute-start(bf16[64,2048]{1,0:T(8,128)(2,1)S(1)} %fusion.6), channel_id=1, source_target_pairs={{0,2},{2,0},{1,3},{3,1},{4,6},{6,4},{5,7},{7,5},{8,10},{10,8},{9,1... | collective-permute-start | bytes 786440 | tf_op jit(solution)/shard_map/ppermute | solution.py:23
  127.3 36.4 %all-to-all-start.1 = ((bf16[8,64,2048]{2,1,0:T(8,128)(2,1)}), bf16[8,64,2048]{2,1,0:T(8,128)(2,1)}, u32[]{:S(2)}, u32[]{:S(2)}) async-start(bf16[8,64,2048]{2,1,0:T(8,128)(2,1)} %broadcast_in_dim.140), calls=%async_computation.1 | async-start | bytes 4194304 | tf_op jit(solution)/shard_map/all_to_all | solution.py:31
  135.6 16.9 %collective-permute-start.18 = (bf16[256,2048]{1,0:T(8,128)(2,1)}, bf16[256,2048]{1,0:T(8,128)(2,1)S(1)}, u32[]{:S(2)}, u32[]{:S(2)}) collective-permute-start(bf16[256,2048]{1,0:T(8,128)(2,1)} %param.22), channel_id=1, source_target_pairs={{0,4},{1,13},{4,8},{5,1},{8,12},{9,5},{12,0},{13,9},{2,6},{3,15},{... | collective-permute-start | bytes 3145736 | tf_op jit(solution)/shard_map/ppermute | solution.py:325
  163.6 4.5 %collective-permute-start.19 = (bf16[512,2048]{1,0:T(8,128)(2,1)}, bf16[512,2048]{1,0:T(8,128)(2,1)}, u32[]{:S(2)}, u32[]{:S(2)}) collective-permute-start(bf16[512,2048]{1,0:T(8,128)(2,1)} %bitcast.82.tokens_ref), channel_id=1, source_target_pairs={{0,1},{1,0},{2,3},{3,2},{4,5},{5,4},{6,7},{7,6},{8,9},{9,8},{10,11... | collective-permute-start | bytes 6291464 | tf_op jit(solution)/shard_map/ppermute | solution.py:23
  163.6 3.2 %copy-start.4 = (bf16[256,2048]{1,0:T(8,128)(2,1)S(1)}, bf16[256,2048]{1,0:T(8,128)(2,1)}, u32[]{:S(2)}) copy-start(bf16[256,2048]{1,0:T(8,128)(2,1)} %param.22) | copy-start | bytes 3145732
  174.4 6.5 %collective-permute-start.20 = (bf16[512,2048]{1,0:T(8,128)(2,1)S(1)}, bf16[512,2048]{1,0:T(8,128)(2,1)S(1)}, u32[]{:S(2)}, u32[]{:S(2)}) collective-permute-start(bf16[512,2048]{1,0:T(8,128)(2,1)S(1)} %shard_map.138), channel_id=1, source_target_pairs={{0,1},{1,0},{2,3},{3,2},{4,5},{5,4},{6,7},{7,6},{8,9},{9,8},{10,11... | collective-permute-start | bytes 6291464 | tf_op jit(solution)/shard_map/ppermute | solution.py:23

commit v11 on v10

--- a/solution.py
+++ b/solution.py
@@ -206,7 +206,9 @@
     )(nodes, lengths, lists, counts, *in_hbm(qkv_parts), row_info, seg_row, factors, key_factors, *in_hbm(parts))
 
 
-def feed_forward_body(tokens_ref, gu_a, dn_a, gu_b, dn_b, out_ref, tokens, gu, dn, made, sems):
+def feed_forward_body(
+    tokens_ref, gate_a, up_a, dn_a, gu_b, dn_b, out_ref, tokens, gu, dn, made, sems
+):
     rows = 256
     blocks = tokens.shape[0] // rows
 
@@ -221,8 +223,8 @@
 
     loads = [
         pltpu.make_async_copy(source, target, sems.at[2 + j, k])
-        for k, pair in enumerate(((gu_a, dn_a), (gu_b, dn_b)))
-        for j, (source, target) in enumerate(((pair[0], gu.at[k]), (pair[1], dn.at[k])))
+        for k, parts in enumerate(((gate_a, up_a, dn_a), (gu_b.at[0], gu_b.at[1], dn_b)))
+        for j, (source, target) in enumerate(zip(parts, (gu.at[k, 0], gu.at[k, 1], dn.at[k])))
     ]
     fetch(0).start()
     for load in loads:
@@ -234,13 +236,14 @@
         part = 0.0
         for k in range(2):
             if i == 0:
-                loads[2 * k].wait()
+                loads[3 * k].wait()
+                loads[3 * k + 1].wait()
             values = tokens[i * rows : (i + 1) * rows, :]
             gate = jnp.dot(values, gu[k, 0], preferred_element_type=F32)
             up = jnp.dot(values, gu[k, 1], preferred_element_type=F32)
             hidden = (gate / (1.0 + jnp.exp(-gate)) * up).astype(BF)
             if i == 0:
-                loads[2 * k + 1].wait()
+                loads[3 * k + 2].wait()
             part = part + jnp.dot(hidden, dn[k], preferred_element_type=F32)
         made[i * rows : (i + 1) * rows, :] = part.astype(BF)
         store(i).start()
@@ -250,18 +253,18 @@
 
 def feed_forward(tokens, weights):
     rows, width = tokens.shape
-    units = weights[1].shape[0]
+    units = weights[2].shape[0]
     return pl.pallas_call(
         feed_forward_body,
         out_shape=jax.ShapeDtypeStruct((rows, width), BF),
-        in_specs=[pl.BlockSpec(memory_space=pltpu.MemorySpace.HBM)] * 5,
+        in_specs=[pl.BlockSpec(memory_space=pltpu.MemorySpace.HBM)] * 6,
         out_specs=pl.BlockSpec(memory_space=pltpu.MemorySpace.HBM),
         scratch_shapes=[
             pltpu.VMEM((rows, width), BF),
             pltpu.VMEM((2, 2, width, units), BF),
             pltpu.VMEM((2, units, width), BF),
             pltpu.VMEM((rows, width), BF),
-            pltpu.SemaphoreType.DMA((4, 2)),
+            pltpu.SemaphoreType.DMA((5, 2)),
         ],
         compiler_params=pltpu.CompilerParams(vmem_limit_bytes=48 << 20),
         cost_estimate=pl.CostEstimate(
@@ -332,7 +335,7 @@
             weights, ("z", "core"), [(z * 2 + 1, (z + 2) % n_z * 2 + 1) for z in range(n_z)]
         )
 
-    gu_a = beside(w_gate_up)
+    gate_a = beside(w_gate_up[0])
 
     qkv_raw = jnp.einsum("td,cdw->ctw", states_in, w_qkv, preferred_element_type=F32)
     squares = jnp.sum(qkv_raw[:2] * qkv_raw[:2], axis=2)
@@ -368,7 +371,7 @@
         [turned(0), turned(1), qkv_raw[2].astype(BF).reshape(rows, heads_here, HD)]
     ).transpose(2, 0, 1, 3).reshape(heads_here, 3 * rows, HD)
     qkv = jnp.concatenate([qkv, jnp.broadcast_to(terms, (heads_here,) + terms.shape)], axis=1)
-    qkv, gu_a = lax.optimization_barrier((qkv, gu_a))
+    qkv, gate_a = lax.optimization_barrier((qkv, gate_a))
     qkv_parts = [across(select_row(qkv, (z_at + s) % n_z), s) for s in range(n_z)]
     terms = jnp.stack([part[3 * rows : 3 * rows + term_rows] for part in qkv_parts]).astype(F32)
     squares = jnp.sum(terms.reshape(n_z, 3, 2, rows), axis=1).transpose(0, 2, 1)
@@ -428,12 +431,12 @@
     mid_state = (state_rows.astype(F32) + rms_norm(attn_proj, post_gain[0])).astype(BF)
 
     plane = ("yhi", "x")
-    mid_state, w_down = lax.optimization_barrier((mid_state, w_down))
-    dn_a = beside(w_down)
+    mid_state, w_down, w_gate_up = lax.optimization_barrier((mid_state, w_down, w_gate_up))
+    up_a, dn_a = beside(w_gate_up[1]), beside(w_down)
     tokens = spread(mid_state, plane)
-    tokens, dn_a = lax.optimization_barrier((tokens, dn_a))
+    tokens, up_a, dn_a = lax.optimization_barrier((tokens, up_a, dn_a))
     weights = (
-        gu_a, dn_a, jnp.where(core == 0, w_gate_up, gu_b), jnp.where(core == 0, w_down, dn_b)
+        gate_a, up_a, dn_a, jnp.where(core == 0, w_gate_up, gu_b), jnp.where(core == 0, w_down, dn_b)
     )
     flat = tokens.reshape(-1, tokens.shape[2])
     other = feed_forward(shift(flat, "core", 1), weights)

time: 217 us -> 215 us (level)
  starting transfers between devices: 55.4 us -> 47.7 us
  blocking collectives: 40.5 us -> 45.3 us
  other arithmetic: 11.3 us -> 14.8 us
  waiting for transfers between devices: 57.9 us -> 54.6 us
  local copies, waits for them, and re-layouts: 11.6 us -> 14.8 us
    ppermute x5, starting transfers between devices: 20.8 us -> 13.1 us  [shift(): return lax.ppermute(values, axis, [(i, (i + by) % n) for i in range(n)])]
    squeeze x0 -> x2, local copies, waits for them, and re-layouts: none -> 3.65 us  [the longest x1 2.27 us: on_device(): gate_a = beside(w_gate_up[0])]
    all_to_all x1, blocking collectives: 32.5 us -> 35.6 us  [on_device(): lax.all_to_all(total.astype(BF).reshape(tokens.shape), plane, 0, 0, tiled...]
    ppermute x2 -> x3, waiting for transfers between devices: 28.5 us -> 26 us  [beside(): lax.ppermute(weights, ('z', 'core'), [(z * 2 + c, (z + 1 - 2 * c) % n_z *...]
    all_to_all x2, starting transfers between devices: 12.8 us -> 10.4 us  [spread(): return lax.all_to_all(copies, axes, 0, 0, tiled=True)]
  transfers between devices with their start and end apart: 23 -> 24, of which waited for: 12 -> 11; matrix products, arithmetic and copies ran while one was open for 9% -> 11% of each run, Pallas kernels for 11% -> 10%
where the time goes in v11:
time: 215 us
  waiting for transfers between devices  54.6 us (25%)
  starting transfers between devices  47.7 us (22%)
  blocking collectives  45.3 us (21%)
  Pallas kernels  28.9 us (13%)
  local copies, waits for them, and re-layouts  14.8 us (7%)
  other arithmetic  14.8 us (7%)
  matrix products  7.82 us (4%)
    all_to_all x1, blocking collectives, on_device(): lax.all_to_all(total.astype(BF).reshape(tokens.shape), plane, 0, 0, tiled...  35.6 us
    ppermute x3, waiting for transfers between devices, beside(): lax.ppermute(weights, ('z', 'core'), [(z * 2 + c, (z + 1 - 2 * c) % n_z *...  26 us
    pallas_call x1, Pallas kernels, attention(): pl.pallas_call(attention_body, out_shape=jax.ShapeDtypeStruct((groups, ro...  16.1 us
    ppermute x5, starting transfers between devices, shift(): return lax.ppermute(values, axis, [(i, (i + by) % n) for i in range(n)])  13.1 us
    pallas_call x2, Pallas kernels, feed_forward(): pl.pallas_call(feed_forward_body, out_shape=jax.ShapeDtypeStruct((rows, w...  12.9 us
    ppermute x8, starting transfers between devices, across(): return lax.ppermute(values, corner, pairs)  12.7 us
    ppermute x5, waiting for transfers between devices, shift(): return lax.ppermute(values, axis, [(i, (i + by) % n) for i in range(n)])  10.4 us
    all_to_all x2, starting transfers between devices, spread(): return lax.all_to_all(copies, axes, 0, 0, tiled=True)  10.4 us
  transfers between devices with their start and end apart: 24, of which 11 were waited for; matrix products, arithmetic and copies ran while one was open for 11% of the time, Pallas kernels for 10%

profile of v11, /device:TPU:0, one launch (start us, length us, event | category | flops | bytes accessed | tf_op | source)
XLA Modules:
  0.0 214.8 jit_solution(11239856844719852283)
XLA Ops:
  0.0 1.1 constant_dynamic-slice_fusion.6
  1.2 4.0 %collective-permute-start.2 = (bf16[2,256,128]{2,1,0:T(8,128)(2,1)S(1)}, bf16[2,256,128]{2,1,0:T(8,128)(2,1)S(1)}, u32[]{:S(2)}, u32[]{:S(2)}) collective-permute-start(bf16[2,256,128]{2,1,0:T(8,128)(2,1)S(1)} %pad_maximum_fusion.5), channel_id=1, source_target_pairs={{0,8},{1,72},{4,12},{5,76},{8,0},{9,64},{12,4},{13,68},{64,9},{65,... | collective-permute-start | bytes 393224 | tf_op jit(solution)/shard_map/ppermute | solution.py:309
  5.2 0.8 collective-permute-start.3
  6.0 1.4 collective-permute-start.1
  7.4 1.3 collective-permute-start
  8.8 2.3 %slice_bitcast_fusion.1 = bf16[2048,256]{1,0:T(8,128)(2,1)} fusion(bf16[2,2048,256]{2,1,0:T(8,128)(2,1)} %param.21), kind=kLoop, calls=%fused_computation.18 | loop fusion | bytes 2097152 | tf_op jit(solution)/shard_map/squeeze | solution.py:338
  11.0 1.0 collective-permute-start.4
  13.9 5.0 %convolution_bitcast_fusion = f32[3,256,512]{1,2,0:T(8,128)S(1)} fusion(bf16[3,2048,512]{2,1,0:T(8,128)(2,1)} %param.17, bf16[256,2048]{1,0:T(8,128)(2,1)} %param.16), kind=kOutput, calls=%fused_computation.11 | convolution fusion | flops 1610612736 | bytes 8912896 | tf_op jit(solution)/shard_map/td,cdw->ctw/dot_general | solution.py:340
  19.9 1.1 pad_maximum_fusion.1
  21.0 1.8 broadcast_in_dim.132
  22.8 4.4 %all-to-all-start = ((bf16[4,4,2,256,128]{4,3,2,1,0:T(8,128)(2,1)}), bf16[4,4,2,256,128]{4,3,2,1,0:T(8,128)(2,1)}, u32[]{:S(2)}, u32[]{:S(2)}) async-start(bf16[4,4,2,256,128]{4,3,2,1,0:T(8,128)(2,1)} %broadcast_in_dim.132), calls=%async_computation | async-start | bytes 4194304 | tf_op jit(solution)/shard_map/all_to_all | solution.py:31
  28.7 2.3 %collective-permute-start.8 = (bf16[784,128]{1,0:T(8,128)(2,1)S(1)}, bf16[784,128]{1,0:T(8,128)(2,1)S(1)}, u32[]{:S(2)}, u32[]{:S(2)}) collective-permute-start(bf16[784,128]{1,0:T(8,128)(2,1)S(1)} %get-tuple-element.60), channel_id=1, source_target_pairs={{0,12},{1,76},{4,0},{5,64},{8,4},{9,68},{12,8},{13,72},{64,13},{65... | collective-permute-start | bytes 602120 | tf_op jit(solution)/shard_map/ppermute | solution.py:309
  31.2 1.3 collective-permute-start.6
  32.5 1.3 collective-permute-start.5
  33.9 0.7 gather_fusion.2
  34.6 1.8 collective-permute-done.8.rest_3_
  36.4 1.9 collective-permute-done.7.rest_2_
  38.3 2.1 collective-permute-done.6.rest_1_
  40.4 9.5 %all-to-all-done = bf16[4,4,2,256,128]{4,3,2,1,0:T(8,128)(2,1)} async-done(((bf16[4,4,2,256,128]{4,3,2,1,0:T(8,128)(2,1)}), bf16[4,4,2,256,128]{4,3,2,1,0:T(8,128)(2,1)}, u32[]{:S(2)}, u32[]{:S(2)}) %all-to-all-start) | async-done | bytes 2097184 | tf_op jit(solution)/shard_map/all_to_all | solution.py:31
  49.9 5.0 %collective-permute-start.9 = (bf16[16,2,256,128]{3,2,1,0:T(8,128)(2,1)}, bf16[16,2,256,128]{3,2,1,0:T(8,128)(2,1)}, u32[]{:S(2)}, u32[]{:S(2)}) collective-permute-start(bf16[16,2,256,128]{3,2,1,0:T(8,128)(2,1)} %bitcast.47.rest_8_), channel_id=1, source_target_pairs={{0,1},{1,0},{2,3},{3,2},{4,5},{5,4},{6,7},{7,6},{8,9},{9,8},{10,11... | collective-permute-start | bytes 6291464 | tf_op jit(solution)/shard_map/ppermute | solution.py:23
  54.9 2.0 collective-permute-start.14
  60.6 1.7 collective-permute-start.15
  62.4 9.7 %psum.7 = f32[4,256,2]{1,2,0:T(2,128)S(1)} all-reduce(f32[4,256,2]{1,2,0:T(2,128)S(1)} %bitcast.140), channel_id=1, replica_groups=mesh['yhi'=2,'x'=4,'z'=4,'ylo'=2,'core'=2] {'yhi','ylo'}, use_global_device_ids=true, to_apply=%region_13.15 | all-reduce | flops 2048 | bytes 16384 | tf_op jit(solution)/shard_map/psum | solution.py:378
  72.4 16.1 %shard_map.136 = bf16[4,256,128]{2,1,0:T(8,128)(2,1)S(1)} custom-call(s32[32]{0:T(128)S(1)} %get-tuple-element.57.nodes_ref, s32[32]{0:T(128)S(1)} %and_select_fusion.lengths_ref, s32[4,2,12]{2,1,0:T(2,128)S(1)} %copy.44.lists_ref, s32[4,2]{1,0:T(4,128)S(1)} %copy.45.counts_ref, bf16[784,128]{1,0:T(8,128)(2,1)} %collective-permute-done.5.rest_0_, ...), custom_call_target="tpu_custom_call" | custom-call | flops 2000000000 | bytes 6000000 | tf_op jit(solution)/shard_map/pallas_call | solution.py:183
  89.3 3.3 %collective-permute-start.12 = (bf16[256,128]{1,0:T(8,128)(2,1)S(1)}, bf16[256,128]{1,0:T(8,128)(2,1)S(1)}, u32[]{:S(2)}, u32[]{:S(2)}) collective-permute-start(bf16[256,128]{1,0:T(8,128)(2,1)S(1)} %get-tuple-element.70), channel_id=1, source_target_pairs={{0,8},{1,72},{4,12},{5,76},{8,0},{9,64},{12,4},{13,68},{64,9},{65,... | collective-permute-start | bytes 196616 | tf_op jit(solution)/shard_map/ppermute | solution.py:415
  92.6 1.3 collective-permute-start.11
  94.0 1.6 collective-permute-done.13
  95.6 0.7 collective-permute-done.12
  97.0 2.8 %fusion.1 = f32[256,2048]{1,0:T(8,128)S(1)} fusion(bf16[256,512]{1,0:T(8,128)(2,1)S(1)} %pad_maximum_fusion.2, s32[]{:T(128)S(6)} %select_n.293, bf16[512,2048]{1,0:T(8,128)(2,1)} %param.19), kind=kOutput, calls=%fused_computation.9 | convolution fusion | flops 541065216 | bytes 4456452 | tf_op jit(solution)/shard_map/dot_general | solution.py:419
  99.8 0.9 fusion.5
  100.7 7.3 %collective-permute-start.16 = (bf16[2,64,2048]{2,1,0:T(8,128)(2,1)}, bf16[2,64,2048]{2,1,0:T(8,128)(2,1)}, u32[]{:S(2)}, u32[]{:S(2)}) collective-permute-start(bf16[2,64,2048]{2,1,0:T(8,128)(2,1)} %fusion.5), channel_id=1, source_target_pairs={{0,1},{1,0},{2,3},{3,2},{4,5},{5,4},{6,7},{7,6},{8,9},{9,8},{10,11... | collective-permute-start | bytes 1572872 | tf_op jit(solution)/shard_map/ppermute | solution.py:23
  108.0 1.9 collective-permute-done.16
  109.9 1.1 bitcast_add_fusion
  111.2 8.5 %collective-permute-done.17 = bf16[64,2048]{1,0:T(8,128)(2,1)S(1)} collective-permute-done((bf16[64,2048]{1,0:T(8,128)(2,1)S(1)}, bf16[64,2048]{1,0:T(8,128)(2,1)S(1)}, u32[]{:S(2)}, u32[]{:S(2)}) %collective-permute-start.17) | collective-permute-done | bytes 262176 | tf_op jit(solution)/shard_map/ppermute | solution.py:23
  120.0 1.1 add_convert_fusion.2
  121.1 1.6 broadcast_in_dim.140
  122.6 5.9 %all-to-all-start.1 = ((bf16[8,64,2048]{2,1,0:T(8,128)(2,1)}), bf16[8,64,2048]{2,1,0:T(8,128)(2,1)}, u32[]{:S(2)}, u32[]{:S(2)}) async-start(bf16[8,64,2048]{2,1,0:T(8,128)(2,1)} %broadcast_in_dim.140), calls=%async_computation.1 | async-start | bytes 4194304 | tf_op jit(solution)/shard_map/all_to_all | solution.py:31
  128.6 1.4 slice_bitcast_fusion
  130.0 1.2 collective-permute-start.18
  131.3 14.7 %collective-permute-done.18.up_a = bf16[2048,256]{1,0:T(8,128)(2,1)S(1)} collective-permute-done((bf16[2048,256]{1,0:T(8,128)(2,1)S(1)}, bf16[2048,256]{1,0:T(8,128)(2,1)S(1)}, u32[]{:S(2)}, u32[]{:S(2)}) %collective-permute-start.18) | collective-permute-done | bytes 1048608 | tf_op jit(solution)/shard_map/ppermute | solution.py:328
  146.1 11.2 %collective-permute-done.19.dn_a = bf16[256,2048]{1,0:T(8,128)(2,1)S(1)} collective-permute-done((bf16[256,2048]{1,0:T(8,128)(2,1)S(1)}, bf16[256,2048]{1,0:T(8,128)(2,1)S(1)}, u32[]{:S(2)}, u32[]{:S(2)}) %collective-permute-start.19) | collective-permute-done | bytes 1048608 | tf_op jit(solution)/shard_map/ppermute | solution.py:328
  157.3 1.3 broadcast_select_fusion.1.dn_b
  158.6 3.1 %broadcast_select_fusion.gu_b = bf16[2,2048,256]{2,1,0:T(8,128)(2,1)} fusion(bf16[2,2048,256]{2,1,0:T(8,128)(2,1)} %param.21, bf16[2,2048,256]{2,1,0:T(8,128)(2,1)} %collective-permute-done.14, pred[]{:T(512)S(6)} %eq.164), kind=kLoop, calls=%fused_computation.10 | loop fusion | flops 1048576 | bytes 6291457 | tf_op jit(solution)/shard_map/jit(_where)/select_n | solution.py:439
  161.8 6.4 %shard_map.138 = bf16[512,2048]{1,0:T(8,128)(2,1)} custom-call(bf16[512,2048]{1,0:T(8,128)(2,1)} %collective-permute-done.20.tokens_ref, bf16[2048,256]{1,0:T(8,128)(2,1)S(1)} %collective-permute-done.4.gate_a, bf16[2048,256]{1,0:T(8,128)(2,1)S(1)} %collective-permute-done.18.up_a, bf16[256,2048]{1,0:T(8,128)(2,1)S(1)} %collective-permute-done.19.dn_a, ...), custom_call_target="tpu_custom_call" | custom-call | flops 3221225472 | bytes 10485760 | tf_op jit(solution)/shard_map/pallas_call | solution.py:257
  168.8 6.4 %shard_map.137 = bf16[512,2048]{1,0:T(8,128)(2,1)} custom-call(bf16[512,2048]{1,0:T(8,128)(2,1)} %bitcast.84.tokens_ref, bf16[2048,256]{1,0:T(8,128)(2,1)S(1)} %collective-permute-done.4.gate_a, bf16[2048,256]{1,0:T(8,128)(2,1)S(1)} %collective-permute-done.18.up_a, bf16[256,2048]{1,0:T(8,128)(2,1)S(1)} %collective-permute-done.19.dn_a, ...), custom_call_target="tpu_custom_call" | custom-call | flops 3221225472 | bytes 10485760 | tf_op jit(solution)/shard_map/pallas_call | solution.py:257
  175.3 2.5 %add_convert_fusion = bf16[512,2048]{1,0:T(8,128)(2,1)S(1)} fusion(bf16[512,2048]{1,0:T(8,128)(2,1)S(1)} %collective-permute-done.21, bf16[512,2048]{1,0:T(8,128)(2,1)} %shard_map.137), kind=kLoop, calls=%fused_computation.7 | loop fusion | flops 4194304 | bytes 6291456 | tf_op jit(solution)/shard_map/convert_element_type | solution.py:444
  177.8 35.6 %all_to_all.15 = bf16[8,64,2048]{2,1,0:T(8,128)(2,1)S(1)} all-to-all(bf16[8,64,2048]{2,1,0:T(8,128)(2,1)S(1)} %bitcast.130), channel_id=1, replica_groups=mesh['yhi'=2,'x'=4,'z'=4,'ylo'=2,'core'=2] {'yhi','x'}, dimensions={0} | all-to-all | bytes 4194304 | tf_op jit(solution)/shard_map/all_to_all | solution.py:444
  213.9 0.9 add_convert_fusion.1
  (125 shorter events, 11.3 us)
Async XLA Ops:
  0.0 12.4 %copy-start = (s32[32,256]{1,0:T(8,128)S(1)}, s32[32,256]{1,0:T(8,128)}, u32[]{:S(2)}) copy-start(s32[32,256]{1,0:T(8,128)} %param.28) | copy-start | bytes 98308
  0.0 12.3 %copy-start.7 = (f32[2,512]{1,0:T(2,128)S(1)}, f32[2,512]{1,0:T(2,128)}, u32[]{:S(2)}) copy-start(f32[2,512]{1,0:T(2,128)} %param.18) | copy-start | bytes 12292
  0.0 13.2 %copy-start.6 = (s32[32,8]{0,1:T(8,128)S(1)}, s32[32,8]{0,1:T(8,128)}, u32[]{:S(2)}) copy-start(s32[32,8]{0,1:T(8,128)} %param.29) | copy-start | bytes 3076
  1.2 18.7 %collective-permute-start.2 = (bf16[2,256,128]{2,1,0:T(8,128)(2,1)S(1)}, bf16[2,256,128]{2,1,0:T(8,128)(2,1)S(1)}, u32[]{:S(2)}, u32[]{:S(2)}) collective-permute-start(bf16[2,256,128]{2,1,0:T(8,128)(2,1)S(1)} %pad_maximum_fusion.5), channel_id=1, source_target_pairs={{0,8},{1,72},{4,12},{5,76},{8,0},{9,64},{12,4},{13,68},{64,9},{65,... | collective-permute-start | bytes 393224 | tf_op jit(solution)/shard_map/ppermute | solution.py:309
  5.2 14.7 %collective-permute-start.3 = (bf16[2,256,128]{2,1,0:T(8,128)(2,1)S(1)}, bf16[2,256,128]{2,1,0:T(8,128)(2,1)}, u32[]{:S(2)}, u32[]{:S(2)}) collective-permute-start(bf16[2,256,128]{2,1,0:T(8,128)(2,1)S(1)} %pad_maximum_fusion.6), channel_id=1, source_target_pairs={{0,12},{1,76},{4,0},{5,64},{8,4},{9,68},{12,8},{13,72},{64,13},{65... | collective-permute-start | bytes 393224 | tf_op jit(solution)/shard_map/ppermute | solution.py:309
  6.0 13.9 %collective-permute-start.1 = (bf16[2,256,128]{2,1,0:T(8,128)(2,1)S(1)}, bf16[2,256,128]{2,1,0:T(8,128)(2,1)}, u32[]{:S(2)}, u32[]{:S(2)}) collective-permute-start(bf16[2,256,128]{2,1,0:T(8,128)(2,1)S(1)} %pad_maximum_fusion.4), channel_id=1, source_target_pairs={{0,4},{1,68},{4,8},{5,72},{8,12},{9,76},{12,0},{13,64},{64,5},{65,... | collective-permute-start | bytes 393224 | tf_op jit(solution)/shard_map/ppermute | solution.py:309
  7.4 12.5 %collective-permute-start = (bf16[2,256,128]{2,1,0:T(8,128)(2,1)S(1)}, bf16[2,256,128]{2,1,0:T(8,128)(2,1)}, u32[]{:S(2)}, u32[]{:S(2)}) collective-permute-start(bf16[2,256,128]{2,1,0:T(8,128)(2,1)S(1)} %pad_maximum_fusion.3), channel_id=1, source_target_pairs={{0,0},{1,64},{4,4},{5,68},{8,8},{9,72},{12,12},{13,76},{64,1},{65,... | collective-permute-start | bytes 393224 | tf_op jit(solution)/shard_map/ppermute | solution.py:309
  11.0 17.6 %collective-permute-start.4 = (bf16[2048,256]{1,0:T(8,128)(2,1)}, bf16[2048,256]{1,0:T(8,128)(2,1)S(1)}, u32[]{:S(2)}, u32[]{:S(2)}) collective-permute-start(bf16[2048,256]{1,0:T(8,128)(2,1)} %slice_bitcast_fusion.1), channel_id=1, source_target_pairs={{0,4},{1,13},{4,8},{5,1},{8,12},{9,5},{12,0},{13,9},{2,6},{3,15},{... | collective-permute-start | bytes 3145736 | tf_op jit(solution)/shard_map/ppermute | solution.py:328
  13.9 5.4 %copy-start.8 = (s32[28]{0:T(128)S(1)}, s32[28]{0:T(128)}, u32[]{:S(2)}) copy-start(s32[28]{0:T(128)} %param.27) | copy-start | bytes 340
  13.9 5.5 %copy-start.1 = (s32[32]{0:T(128)S(1)}, s32[32]{0:T(128)}, u32[]{:S(2)}) copy-start(s32[32]{0:T(128)} %param.26) | copy-start | bytes 388
  22.8 27.0 %all-to-all-start = ((bf16[4,4,2,256,128]{4,3,2,1,0:T(8,128)(2,1)}), bf16[4,4,2,256,128]{4,3,2,1,0:T(8,128)(2,1)}, u32[]{:S(2)}, u32[]{:S(2)}) async-start(bf16[4,4,2,256,128]{4,3,2,1,0:T(8,128)(2,1)} %broadcast_in_dim.132), calls=%async_computation | async-start | bytes 4194304 | tf_op jit(solution)/shard_map/all_to_all | solution.py:31
  27.9 6.0 %copy-start.2 = (s32[32]{0:T(128)S(1)}, s32[32]{0:T(128)}, u32[]{:S(2)}) copy-start(s32[32]{0:T(128)} %param.25) | copy-start | bytes 388
  28.6 32.1 %copy-start.3 = (bf16[256,2048]{1,0:T(8,128)(2,1)S(1)}, bf16[256,2048]{1,0:T(8,128)(2,1)}, u32[]{:S(2)}) copy-start(bf16[256,2048]{1,0:T(8,128)(2,1)} %param.22) | copy-start | bytes 3145732
  28.7 7.7 %collective-permute-start.8 = (bf16[784,128]{1,0:T(8,128)(2,1)S(1)}, bf16[784,128]{1,0:T(8,128)(2,1)S(1)}, u32[]{:S(2)}, u32[]{:S(2)}) collective-permute-start(bf16[784,128]{1,0:T(8,128)(2,1)S(1)} %get-tuple-element.60), channel_id=1, source_target_pairs={{0,12},{1,76},{4,0},{5,64},{8,4},{9,68},{12,8},{13,72},{64,13},{65... | collective-permute-start | bytes 602120 | tf_op jit(solution)/shard_map/ppermute | solution.py:309
  31.0 7.3 %collective-permute-start.7 = (bf16[784,128]{1,0:T(8,128)(2,1)S(1)}, bf16[784,128]{1,0:T(8,128)(2,1)S(1)}, u32[]{:S(2)}, u32[]{:S(2)}) collective-permute-start(bf16[784,128]{1,0:T(8,128)(2,1)S(1)} %get-tuple-element.61), channel_id=1, source_target_pairs={{0,8},{1,72},{4,12},{5,76},{8,0},{9,64},{12,4},{13,68},{64,9},{65,... | collective-permute-start | bytes 602120 | tf_op jit(solution)/shard_map/ppermute | solution.py:309
  31.2 9.2 %collective-permute-start.6 = (bf16[784,128]{1,0:T(8,128)(2,1)S(1)}, bf16[784,128]{1,0:T(8,128)(2,1)}, u32[]{:S(2)}, u32[]{:S(2)}) collective-permute-start(bf16[784,128]{1,0:T(8,128)(2,1)S(1)} %get-tuple-element.62), channel_id=1, source_target_pairs={{0,4},{1,68},{4,8},{5,72},{8,12},{9,76},{12,0},{13,64},{64,5},{65,... | collective-permute-start | bytes 602120 | tf_op jit(solution)/shard_map/ppermute | solution.py:309
  32.5 7.9 %collective-permute-start.5 = (bf16[784,128]{1,0:T(8,128)(2,1)S(1)}, bf16[784,128]{1,0:T(8,128)(2,1)}, u32[]{:S(2)}, u32[]{:S(2)}) collective-permute-start(bf16[784,128]{1,0:T(8,128)(2,1)S(1)} %get-tuple-element.63), channel_id=1, source_target_pairs={{0,0},{1,64},{4,4},{5,68},{8,8},{9,72},{12,12},{13,76},{64,1},{65,... | collective-permute-start | bytes 602120 | tf_op jit(solution)/shard_map/ppermute | solution.py:309
  36.4 36.0 %copy-start.9 = (bf16[784,128]{1,0:T(8,128)(2,1)}, bf16[784,128]{1,0:T(8,128)(2,1)S(1)}, u32[]{:S(2)}) copy-start(bf16[784,128]{1,0:T(8,128)(2,1)S(1)} %collective-permute-done.8.rest_3_) | copy-start | bytes 602116
  38.3 33.8 %copy-start.10 = (bf16[784,128]{1,0:T(8,128)(2,1)}, bf16[784,128]{1,0:T(8,128)(2,1)S(1)}, u32[]{:S(2)}) copy-start(bf16[784,128]{1,0:T(8,128)(2,1)S(1)} %collective-permute-done.7.rest_2_) | copy-start | bytes 602116
  49.9 22.5 %collective-permute-start.9 = (bf16[16,2,256,128]{3,2,1,0:T(8,128)(2,1)}, bf16[16,2,256,128]{3,2,1,0:T(8,128)(2,1)}, u32[]{:S(2)}, u32[]{:S(2)}) collective-permute-start(bf16[16,2,256,128]{3,2,1,0:T(8,128)(2,1)} %bitcast.47.rest_8_), channel_id=1, source_target_pairs={{0,1},{1,0},{2,3},{3,2},{4,5},{5,4},{6,7},{7,6},{8,9},{9,8},{10,11... | collective-permute-start | bytes 6291464 | tf_op jit(solution)/shard_map/ppermute | solution.py:23
  54.9 42.0 %collective-permute-start.14 = (bf16[2,2048,256]{2,1,0:T(8,128)(2,1)}, bf16[2,2048,256]{2,1,0:T(8,128)(2,1)}, u32[]{:S(2)}, u32[]{:S(2)}) collective-permute-start(bf16[2,2048,256]{2,1,0:T(8,128)(2,1)} %param.21), channel_id=1, source_target_pairs={{1,9},{5,13},{9,1},{13,5},{3,11},{7,15},{11,3},{15,7},{17,25},{21,... | collective-permute-start | bytes 6291464 | tf_op jit(solution)/shard_map/ppermute | solution.py:334
  60.6 36.3 %collective-permute-start.15 = (bf16[256,2048]{1,0:T(8,128)(2,1)S(1)}, bf16[256,2048]{1,0:T(8,128)(2,1)}, u32[]{:S(2)}, u32[]{:S(2)}) collective-permute-start(bf16[256,2048]{1,0:T(8,128)(2,1)S(1)} %copy-done.3), channel_id=1, source_target_pairs={{1,9},{5,13},{9,1},{13,5},{3,11},{7,15},{11,3},{15,7},{17,25},{21,... | collective-permute-start | bytes 3145736 | tf_op jit(solution)/shard_map/ppermute | solution.py:334
  88.5 4.2 %collective-permute-start.10 = (bf16[256,128]{1,0:T(8,128)(2,1)S(1)}, bf16[256,128]{1,0:T(8,128)(2,1)S(1)}, u32[]{:S(2)}, u32[]{:S(2)}) collective-permute-start(bf16[256,128]{1,0:T(8,128)(2,1)S(1)} %get-tuple-element.68), channel_id=1, source_target_pairs={{0,0},{1,64},{4,4},{5,68},{8,8},{9,72},{12,12},{13,76},{64,1},{65,... | collective-permute-start | bytes 196616 | tf_op jit(solution)/shard_map/ppermute | solution.py:415
  89.2 6.4 %collective-permute-start.13 = (bf16[256,128]{1,0:T(8,128)(2,1)S(1)}, bf16[256,128]{1,0:T(8,128)(2,1)S(1)}, u32[]{:S(2)}, u32[]{:S(2)}) collective-permute-start(bf16[256,128]{1,0:T(8,128)(2,1)S(1)} %get-tuple-element.69), channel_id=1, source_target_pairs={{0,4},{1,68},{4,8},{5,72},{8,12},{9,76},{12,0},{13,64},{64,5},{65,... | collective-permute-start | bytes 196616 | tf_op jit(solution)/shard_map/ppermute | solution.py:415
  89.3 6.9 %collective-permute-start.12 = (bf16[256,128]{1,0:T(8,128)(2,1)S(1)}, bf16[256,128]{1,0:T(8,128)(2,1)S(1)}, u32[]{:S(2)}, u32[]{:S(2)}) collective-permute-start(bf16[256,128]{1,0:T(8,128)(2,1)S(1)} %get-tuple-element.70), channel_id=1, source_target_pairs={{0,8},{1,72},{4,12},{5,76},{8,0},{9,64},{12,4},{13,68},{64,9},{65,... | collective-permute-start | bytes 196616 | tf_op jit(solution)/shard_map/ppermute | solution.py:415
  92.6 4.3 %collective-permute-start.11 = (bf16[256,128]{1,0:T(8,128)(2,1)S(1)}, bf16[256,128]{1,0:T(8,128)(2,1)S(1)}, u32[]{:S(2)}, u32[]{:S(2)}) collective-permute-start(bf16[256,128]{1,0:T(8,128)(2,1)S(1)} %get-tuple-element.71), channel_id=1, source_target_pairs={{0,12},{1,76},{4,0},{5,64},{8,4},{9,68},{12,8},{13,72},{64,13},{65... | collective-permute-start | bytes 196616 | tf_op jit(solution)/shard_map/ppermute | solution.py:415
  99.8 11.4 %copy-start.5 = (f32[2,2048]{1,0:T(2,128)S(1)}, f32[2,2048]{1,0:T(2,128)}, u32[]{:S(2)}) copy-start(f32[2,2048]{1,0:T(2,128)} %param.20) | copy-start | bytes 49156
  100.7 9.2 %collective-permute-start.16 = (bf16[2,64,2048]{2,1,0:T(8,128)(2,1)}, bf16[2,64,2048]{2,1,0:T(8,128)(2,1)}, u32[]{:S(2)}, u32[]{:S(2)}) collective-permute-start(bf16[2,64,2048]{2,1,0:T(8,128)(2,1)} %fusion.5), channel_id=1, source_target_pairs={{0,1},{1,0},{2,3},{3,2},{4,5},{5,4},{6,7},{7,6},{8,9},{9,8},{10,11... | collective-permute-start | bytes 1572872 | tf_op jit(solution)/shard_map/ppermute | solution.py:23
  111.1 8.7 %collective-permute-start.17 = (bf16[64,2048]{1,0:T(8,128)(2,1)S(1)}, bf16[64,2048]{1,0:T(8,128)(2,1)S(1)}, u32[]{:S(2)}, u32[]{:S(2)}) collective-permute-start(bf16[64,2048]{1,0:T(8,128)(2,1)S(1)} %fusion.6), channel_id=1, source_target_pairs={{0,2},{2,0},{1,3},{3,1},{4,6},{6,4},{5,7},{7,5},{8,10},{10,8},{9,1... | collective-permute-start | bytes 786440 | tf_op jit(solution)/shard_map/ppermute | solution.py:23
  122.6 34.7 %all-to-all-start.1 = ((bf16[8,64,2048]{2,1,0:T(8,128)(2,1)}), bf16[8,64,2048]{2,1,0:T(8,128)(2,1)}, u32[]{:S(2)}, u32[]{:S(2)}) async-start(bf16[8,64,2048]{2,1,0:T(8,128)(2,1)} %broadcast_in_dim.140), calls=%async_computation.1 | async-start | bytes 4194304 | tf_op jit(solution)/shard_map/all_to_all | solution.py:31
  128.6 2.6 %copy-start.4 = (bf16[256,2048]{1,0:T(8,128)(2,1)S(1)}, bf16[256,2048]{1,0:T(8,128)(2,1)}, u32[]{:S(2)}) copy-start(bf16[256,2048]{1,0:T(8,128)(2,1)} %param.22) | copy-start | bytes 3145732
  130.0 16.1 %collective-permute-start.18 = (bf16[2048,256]{1,0:T(8,128)(2,1)S(1)}, bf16[2048,256]{1,0:T(8,128)(2,1)S(1)}, u32[]{:S(2)}, u32[]{:S(2)}) collective-permute-start(bf16[2048,256]{1,0:T(8,128)(2,1)S(1)} %slice_bitcast_fusion), channel_id=1, source_target_pairs={{0,4},{1,13},{4,8},{5,1},{8,12},{9,5},{12,0},{13,9},{2,6},{3,15},{... | collective-permute-start | bytes 3145736 | tf_op jit(solution)/shard_map/ppermute | solution.py:328
  131.2 26.1 %collective-permute-start.19 = (bf16[256,2048]{1,0:T(8,128)(2,1)S(1)}, bf16[256,2048]{1,0:T(8,128)(2,1)S(1)}, u32[]{:S(2)}, u32[]{:S(2)}) collective-permute-start(bf16[256,2048]{1,0:T(8,128)(2,1)S(1)} %copy-done.4), channel_id=1, source_target_pairs={{0,4},{1,13},{4,8},{5,1},{8,12},{9,5},{12,0},{13,9},{2,6},{3,15},{... | collective-permute-start | bytes 3145736 | tf_op jit(solution)/shard_map/ppermute | solution.py:328
  157.3 4.5 %collective-permute-start.20 = (bf16[512,2048]{1,0:T(8,128)(2,1)}, bf16[512,2048]{1,0:T(8,128)(2,1)}, u32[]{:S(2)}, u32[]{:S(2)}) collective-permute-start(bf16[512,2048]{1,0:T(8,128)(2,1)} %bitcast.84.tokens_ref), channel_id=1, source_target_pairs={{0,1},{1,0},{2,3},{3,2},{4,5},{5,4},{6,7},{7,6},{8,9},{9,8},{10,11... | collective-permute-start | bytes 6291464 | tf_op jit(solution)/shard_map/ppermute | solution.py:23
  168.2 7.0 %collective-permute-start.21 = (bf16[512,2048]{1,0:T(8,128)(2,1)}, bf16[512,2048]{1,0:T(8,128)(2,1)S(1)}, u32[]{:S(2)}, u32[]{:S(2)}) collective-permute-start(bf16[512,2048]{1,0:T(8,128)(2,1)} %shard_map.138), channel_id=1, source_target_pairs={{0,1},{1,0},{2,3},{3,2},{4,5},{5,4},{6,7},{7,6},{8,9},{9,8},{10,11... | collective-permute-start | bytes 6291464 | tf_op jit(solution)/shard_map/ppermute | solution.py:23

commit v12 on v10

--- a/solution.py
+++ b/solution.py
@@ -332,7 +332,7 @@
             weights, ("z", "core"), [(z * 2 + 1, (z + 2) % n_z * 2 + 1) for z in range(n_z)]
         )
 
-    gu_a = beside(w_gate_up)
+    dn_a = beside(w_down)
 
     qkv_raw = jnp.einsum("td,cdw->ctw", states_in, w_qkv, preferred_element_type=F32)
     squares = jnp.sum(qkv_raw[:2] * qkv_raw[:2], axis=2)
@@ -368,13 +368,13 @@
         [turned(0), turned(1), qkv_raw[2].astype(BF).reshape(rows, heads_here, HD)]
     ).transpose(2, 0, 1, 3).reshape(heads_here, 3 * rows, HD)
     qkv = jnp.concatenate([qkv, jnp.broadcast_to(terms, (heads_here,) + terms.shape)], axis=1)
-    qkv, gu_a = lax.optimization_barrier((qkv, gu_a))
+    qkv, dn_a = lax.optimization_barrier((qkv, dn_a))
     qkv_parts = [across(select_row(qkv, (z_at + s) % n_z), s) for s in range(n_z)]
     terms = jnp.stack([part[3 * rows : 3 * rows + term_rows] for part in qkv_parts]).astype(F32)
     squares = jnp.sum(terms.reshape(n_z, 3, 2, rows), axis=1).transpose(0, 2, 1)
     factors = lax.rsqrt(lax.psum(squares, ("yhi", "ylo")) / columns + EPS)
     w_gate_up, w_down, qkv_parts = lax.optimization_barrier((w_gate_up, w_down, qkv_parts))
-    cached_own, qkv_parts = lax.optimization_barrier((cached_own, qkv_parts))
+    cached_own, factors = lax.optimization_barrier((cached_own, factors))
     cached_parts = [cached_own, shift(cached_own, "core", 1)]
 
     gu_b, dn_b = beyond(w_gate_up), beyond(w_down)
@@ -428,10 +428,10 @@
     mid_state = (state_rows.astype(F32) + rms_norm(attn_proj, post_gain[0])).astype(BF)
 
     plane = ("yhi", "x")
-    mid_state, w_down = lax.optimization_barrier((mid_state, w_down))
-    dn_a = beside(w_down)
+    mid_state, w_gate_up = lax.optimization_barrier((mid_state, w_gate_up))
+    gu_a = beside(w_gate_up)
     tokens = spread(mid_state, plane)
-    tokens, dn_a = lax.optimization_barrier((tokens, dn_a))
+    tokens, gu_a = lax.optimization_barrier((tokens, gu_a))
     weights = (
         gu_a, dn_a, jnp.where(core == 0, w_gate_up, gu_b), jnp.where(core == 0, w_down, dn_b)
     )

time: 217 us -> 209 us (0.963)
  blocking collectives: 40.5 us -> 84.3 us
  waiting for transfers between devices: 57.9 us -> 21 us
  starting transfers between devices: 55.4 us -> 39.6 us
    all_to_all x0 -> x1, blocking collectives: none -> 33.4 us  [spread(): return lax.all_to_all(copies, axes, 0, 0, tiled=True)]
    ppermute x2, waiting for transfers between devices: 28.5 us -> 0.49 us  [beside(): lax.ppermute(weights, ('z', 'core'), [(z * 2 + c, (z + 1 - 2 * c) % n_z *...]
    psum x1, blocking collectives: 8 us -> 19.5 us  [on_device(): factors = lax.rsqrt(lax.psum(squares, ('yhi', 'ylo')) / columns + EPS)]
    all_to_all x2 -> x1, waiting for transfers between devices: 11.1 us -> 0.01 us  [spread(): return lax.all_to_all(copies, axes, 0, 0, tiled=True)]
    ppermute x5, starting transfers between devices: 20.8 us -> 11.9 us  [shift(): return lax.ppermute(values, axis, [(i, (i + by) % n) for i in range(n)])]
    all_to_all x2 -> x1, starting transfers between devices: 12.8 us -> 4.57 us  [spread(): return lax.all_to_all(copies, axes, 0, 0, tiled=True)]
  transfers between devices with their start and end apart: 23 -> 22, of which waited for: 12 -> 9; matrix products, arithmetic and copies ran while one was open for 9% -> 9% of each run, Pallas kernels for 11% -> 12%
where the time goes in v12:
time: 209 us; the launch traced here: 208 us
  blocking collectives  84.3 us (40%)
  starting transfers between devices  39.6 us (19%)
  Pallas kernels  30.5 us (15%)
  waiting for transfers between devices  21 us (10%)
  other arithmetic  13.2 us (6%)
  local copies, waits for them, and re-layouts  10.8 us (5%)
  matrix products  7.5 us (4%)
    all_to_all x1, blocking collectives, spread(): return lax.all_to_all(copies, axes, 0, 0, tiled=True)  33.4 us
    all_to_all x1, blocking collectives, on_device(): lax.all_to_all(total.astype(BF).reshape(tokens.shape), plane, 0, 0, tiled...  31.4 us
    psum x1, blocking collectives, on_device(): factors = lax.rsqrt(lax.psum(squares, ('yhi', 'ylo')) / columns + EPS)  19.5 us
    pallas_call x1, Pallas kernels, attention(): pl.pallas_call(attention_body, out_shape=jax.ShapeDtypeStruct((groups, ro...  17.9 us
    pallas_call x2, Pallas kernels, feed_forward(): pl.pallas_call(feed_forward_body, out_shape=jax.ShapeDtypeStruct((rows, w...  12.6 us
    ppermute x5, starting transfers between devices, shift(): return lax.ppermute(values, axis, [(i, (i + by) % n) for i in range(n)])  11.9 us
    ppermute x8, starting transfers between devices, across(): return lax.ppermute(values, corner, pairs)  11.6 us
    ppermute x5, waiting for transfers between devices, shift(): return lax.ppermute(values, axis, [(i, (i + by) % n) for i in range(n)])  10.4 us
  transfers between devices with their start and end apart: 22, of which 9 were waited for; matrix products, arithmetic and copies ran while one was open for 9% of the time, Pallas kernels for 12%

profile of v12, /device:TPU:0, one launch (start us, length us, event | category | flops | bytes accessed | tf_op | source)
XLA Modules:
  0.0 207.6 jit_solution(6900598094928294089)
XLA Ops:
  0.0 1.2 constant_dynamic-slice_fusion.6
  1.2 4.0 %collective-permute-start.7 = (bf16[2,256,128]{2,1,0:T(8,128)(2,1)S(1)}, bf16[2,256,128]{2,1,0:T(8,128)(2,1)S(1)}, u32[]{:S(2)}, u32[]{:S(2)}) collective-permute-start(bf16[2,256,128]{2,1,0:T(8,128)(2,1)S(1)} %pad_maximum_fusion.5), channel_id=1, source_target_pairs={{0,8},{1,72},{4,12},{5,76},{8,0},{9,64},{12,4},{13,68},{64,9},{65,... | collective-permute-start | bytes 393224 | tf_op jit(solution)/shard_map/ppermute | solution.py:306
  5.3 0.8 collective-permute-start.8
  6.1 1.4 collective-permute-start.6
  7.5 1.3 collective-permute-start.5
  8.8 1.0 collective-permute-start
  9.8 4.7 %convolution_bitcast_fusion = f32[3,256,512]{1,2,0:T(8,128)S(1)} fusion(bf16[3,2048,512]{2,1,0:T(8,128)(2,1)} %param.17, bf16[256,2048]{1,0:T(8,128)(2,1)S(1)} %copy-done.5), kind=kOutput, calls=%fused_computation.11 | convolution fusion | flops 1610612736 | bytes 8912896 | tf_op jit(solution)/shard_map/td,cdw->ctw/dot_general | solution.py:337
  15.0 0.6 gather_fusion
  17.5 1.0 pad_maximum_fusion.1
  18.5 1.8 broadcast_in_dim.139
  20.3 4.6 %all-to-all-start = ((bf16[4,4,2,256,128]{4,3,2,1,0:T(8,128)(2,1)}), bf16[4,4,2,256,128]{4,3,2,1,0:T(8,128)(2,1)}, u32[]{:S(2)}, u32[]{:S(2)}) async-start(bf16[4,4,2,256,128]{4,3,2,1,0:T(8,128)(2,1)} %broadcast_in_dim.139), calls=%async_computation | async-start | bytes 4194304 | tf_op jit(solution)/shard_map/all_to_all | solution.py:31
  26.5 1.8 collective-permute-start.4
  28.5 1.3 collective-permute-start.2
  29.9 0.7 collective-permute-start.1
  30.6 3.2 %collective-permute-done.4.rest_3_ = bf16[784,128]{1,0:T(8,128)(2,1)S(1)} collective-permute-done((bf16[784,128]{1,0:T(8,128)(2,1)S(1)}, bf16[784,128]{1,0:T(8,128)(2,1)S(1)}, u32[]{:S(2)}, u32[]{:S(2)}) %collective-permute-start.4) | collective-permute-done | bytes 200736 | tf_op jit(solution)/shard_map/ppermute | solution.py:306
  33.7 1.9 collective-permute-done.3.rest_2_
  35.7 2.0 collective-permute-done.2.rest_1_
  37.7 19.5 %psum.7 = f32[4,256,2]{1,2,0:T(2,128)S(1)} all-reduce(f32[4,256,2]{1,2,0:T(2,128)S(1)} %bitcast.140), channel_id=1, replica_groups=mesh['yhi'=2,'x'=4,'z'=4,'ylo'=2,'core'=2] {'yhi','ylo'}, use_global_device_ids=true, to_apply=%region_13.15 | all-reduce | flops 2048 | bytes 16384 | tf_op jit(solution)/shard_map/psum | solution.py:375
  57.4 0.7 gather_fusion.2
  58.1 0.7 gather_fusion.3
  58.8 2.0 collective-permute-start.14
  62.4 0.7 collective-permute-start.15
  63.4 17.9 %shard_map.136 = bf16[4,256,128]{2,1,0:T(8,128)(2,1)S(1)} custom-call(s32[32]{0:T(128)S(1)} %get-tuple-element.47.nodes_ref, s32[32]{0:T(128)S(1)} %and_select_fusion.lengths_ref, s32[4,2,12]{2,1,0:T(2,128)S(1)} %copy.44.lists_ref, s32[4,2]{1,0:T(4,128)S(1)} %copy.45.counts_ref, bf16[784,128]{1,0:T(8,128)(2,1)} %copy-done.13, bf16[784,128]{1,0:T(8,128)(2,1)} %copy-done.12, ...), custom_call_target="tpu_custom_call" | custom-call | flops 2000000000 | bytes 6000000 | tf_op jit(solution)/shard_map/pallas_call | solution.py:183
  81.3 0.7 collective-permute-start.10
  82.0 1.4 collective-permute-start.13
  83.4 2.2 %collective-permute-start.12 = (bf16[256,128]{1,0:T(8,128)(2,1)S(1)}, bf16[256,128]{1,0:T(8,128)(2,1)S(1)}, u32[]{:S(2)}, u32[]{:S(2)}) collective-permute-start(bf16[256,128]{1,0:T(8,128)(2,1)S(1)} %get-tuple-element.60), channel_id=1, source_target_pairs={{0,8},{1,72},{4,12},{5,76},{8,0},{9,64},{12,4},{13,68},{64,9},{65,... | collective-permute-start | bytes 196616 | tf_op jit(solution)/shard_map/ppermute | solution.py:412
  85.6 1.9 collective-permute-start.11
  87.5 1.1 collective-permute-done.13
  88.6 1.4 collective-permute-done.12
  90.0 0.6 collective-permute-done.11
  90.6 1.0 copy-done.4
  91.6 2.8 %fusion.1 = f32[256,2048]{1,0:T(8,128)S(1)} fusion(bf16[256,512]{1,0:T(8,128)(2,1)S(1)} %pad_maximum_fusion.2, s32[]{:T(128)S(6)} %select_n.293, bf16[512,2048]{1,0:T(8,128)(2,1)} %param.19), kind=kOutput, calls=%fused_computation.9 | convolution fusion | flops 541065216 | bytes 4456452 | tf_op jit(solution)/shard_map/dot_general | solution.py:416
  94.5 0.9 fusion.5
  95.4 11.2 %collective-permute-start.16 = (bf16[2,64,2048]{2,1,0:T(8,128)(2,1)}, bf16[2,64,2048]{2,1,0:T(8,128)(2,1)}, u32[]{:S(2)}, u32[]{:S(2)}) collective-permute-start(bf16[2,64,2048]{2,1,0:T(8,128)(2,1)} %fusion.5), channel_id=1, source_target_pairs={{0,1},{1,0},{2,3},{3,2},{4,5},{5,4},{6,7},{7,6},{8,9},{9,8},{10,11... | collective-permute-start | bytes 1572872 | tf_op jit(solution)/shard_map/ppermute | solution.py:23
  106.6 1.9 collective-permute-done.16
  108.4 1.1 bitcast_add_fusion
  109.8 8.5 %collective-permute-done.17 = bf16[64,2048]{1,0:T(8,128)(2,1)S(1)} collective-permute-done((bf16[64,2048]{1,0:T(8,128)(2,1)S(1)}, bf16[64,2048]{1,0:T(8,128)(2,1)S(1)}, u32[]{:S(2)}, u32[]{:S(2)}) %collective-permute-start.17) | collective-permute-done | bytes 262176 | tf_op jit(solution)/shard_map/ppermute | solution.py:23
  118.5 1.1 add_convert_fusion.2
  119.6 1.6 collective-permute-start.18
  121.5 33.4 %all_to_all.15 = bf16[8,64,2048]{2,1,0:T(8,128)(2,1)S(1)} all-to-all(bf16[8,64,2048]{2,1,0:T(8,128)(2,1)S(1)} %broadcast_in_dim.140), channel_id=1, replica_groups=mesh['yhi'=2,'x'=4,'z'=4,'ylo'=2,'core'=2] {'yhi','x'}, dimensions={0} | all-to-all | bytes 4194304 | tf_op jit(solution)/shard_map/all_to_all | solution.py:31
  154.9 1.4 copy-done.14
  156.2 1.4 broadcast_select_fusion.1.dn_b
  157.6 3.2 %broadcast_select_fusion.gu_b = bf16[2,2048,256]{2,1,0:T(8,128)(2,1)} fusion(bf16[2,2048,256]{2,1,0:T(8,128)(2,1)} %param.21, bf16[2,2048,256]{2,1,0:T(8,128)(2,1)} %collective-permute-done.14, pred[]{:T(512)S(6)} %eq.164), kind=kLoop, calls=%fused_computation.10 | loop fusion | flops 1048576 | bytes 6291457 | tf_op jit(solution)/shard_map/jit(_where)/select_n | solution.py:436
  160.8 6.3 %shard_map.138 = bf16[512,2048]{1,0:T(8,128)(2,1)S(1)} custom-call(bf16[512,2048]{1,0:T(8,128)(2,1)} %collective-permute-done.19.tokens_ref, bf16[2,2048,256]{2,1,0:T(8,128)(2,1)} %copy-done.14, bf16[256,2048]{1,0:T(8,128)(2,1)S(1)} %collective-permute-done.dn_a, bf16[2,2048,256]{2,1,0:T(8,128)(2,1)} %broadcast_select_fusion.gu_b, ...), custom_call_target="tpu_custom_call" | custom-call | flops 3221225472 | bytes 10485760 | tf_op jit(solution)/shard_map/pallas_call | solution.py:254
  167.6 6.3 %shard_map.137 = bf16[512,2048]{1,0:T(8,128)(2,1)S(1)} custom-call(bf16[512,2048]{1,0:T(8,128)(2,1)} %bitcast.129, bf16[2,2048,256]{2,1,0:T(8,128)(2,1)} %copy-done.14, bf16[256,2048]{1,0:T(8,128)(2,1)S(1)} %collective-permute-done.dn_a, bf16[2,2048,256]{2,1,0:T(8,128)(2,1)} %broadcast_select_fusion.gu_b, bf16[256,2048]{1,0:T(8,128)(2,1)S(1)} %broadcast_select_fusion.1.dn_b), custom_call_target="tpu_custom_call" | custom-call | flops 3221225472 | bytes 10485760 | tf_op jit(solution)/shard_map/pallas_call | solution.py:254
  173.9 0.9 add_convert_fusion
  174.8 31.4 %all_to_all.16 = bf16[8,64,2048]{2,1,0:T(8,128)(2,1)S(1)} all-to-all(bf16[8,64,2048]{2,1,0:T(8,128)(2,1)S(1)} %bitcast.126), channel_id=1, replica_groups=mesh['yhi'=2,'x'=4,'z'=4,'ylo'=2,'core'=2] {'yhi','x'}, dimensions={0} | all-to-all | bytes 4194304 | tf_op jit(solution)/shard_map/all_to_all | solution.py:441
  206.7 0.9 add_convert_fusion.1
  (128 shorter events, 7.8 us)
Async XLA Ops:
  0.0 15.0 %copy-start = (s32[32,256]{1,0:T(8,128)S(1)}, s32[32,256]{1,0:T(8,128)}, u32[]{:S(2)}) copy-start(s32[32,256]{1,0:T(8,128)} %param.28) | copy-start | bytes 98308
  0.0 9.8 %copy-start.5 = (bf16[256,2048]{1,0:T(8,128)(2,1)S(1)}, bf16[256,2048]{1,0:T(8,128)(2,1)}, u32[]{:S(2)}) copy-start(bf16[256,2048]{1,0:T(8,128)(2,1)} %param.16) | copy-start | bytes 3145732
  1.2 16.2 %collective-permute-start.7 = (bf16[2,256,128]{2,1,0:T(8,128)(2,1)S(1)}, bf16[2,256,128]{2,1,0:T(8,128)(2,1)S(1)}, u32[]{:S(2)}, u32[]{:S(2)}) collective-permute-start(bf16[2,256,128]{2,1,0:T(8,128)(2,1)S(1)} %pad_maximum_fusion.5), channel_id=1, source_target_pairs={{0,8},{1,72},{4,12},{5,76},{8,0},{9,64},{12,4},{13,68},{64,9},{65,... | collective-permute-start | bytes 393224 | tf_op jit(solution)/shard_map/ppermute | solution.py:306
  5.3 12.2 %collective-permute-start.8 = (bf16[2,256,128]{2,1,0:T(8,128)(2,1)S(1)}, bf16[2,256,128]{2,1,0:T(8,128)(2,1)S(1)}, u32[]{:S(2)}, u32[]{:S(2)}) collective-permute-start(bf16[2,256,128]{2,1,0:T(8,128)(2,1)S(1)} %pad_maximum_fusion.6), channel_id=1, source_target_pairs={{0,12},{1,76},{4,0},{5,64},{8,4},{9,68},{12,8},{13,72},{64,13},{65... | collective-permute-start | bytes 393224 | tf_op jit(solution)/shard_map/ppermute | solution.py:306
  6.1 11.4 %collective-permute-start.6 = (bf16[2,256,128]{2,1,0:T(8,128)(2,1)S(1)}, bf16[2,256,128]{2,1,0:T(8,128)(2,1)S(1)}, u32[]{:S(2)}, u32[]{:S(2)}) collective-permute-start(bf16[2,256,128]{2,1,0:T(8,128)(2,1)S(1)} %pad_maximum_fusion.4), channel_id=1, source_target_pairs={{0,4},{1,68},{4,8},{5,72},{8,12},{9,76},{12,0},{13,64},{64,5},{65,... | collective-permute-start | bytes 393224 | tf_op jit(solution)/shard_map/ppermute | solution.py:306
  7.5 10.0 %collective-permute-start.5 = (bf16[2,256,128]{2,1,0:T(8,128)(2,1)S(1)}, bf16[2,256,128]{2,1,0:T(8,128)(2,1)}, u32[]{:S(2)}, u32[]{:S(2)}) collective-permute-start(bf16[2,256,128]{2,1,0:T(8,128)(2,1)S(1)} %pad_maximum_fusion.3), channel_id=1, source_target_pairs={{0,0},{1,64},{4,4},{5,68},{8,8},{9,72},{12,12},{13,76},{64,1},{65,... | collective-permute-start | bytes 393224 | tf_op jit(solution)/shard_map/ppermute | solution.py:306
  8.8 17.6 %collective-permute-start = (bf16[256,2048]{1,0:T(8,128)(2,1)}, bf16[256,2048]{1,0:T(8,128)(2,1)S(1)}, u32[]{:S(2)}, u32[]{:S(2)}) collective-permute-start(bf16[256,2048]{1,0:T(8,128)(2,1)} %param.22), channel_id=1, source_target_pairs={{0,4},{1,13},{4,8},{5,1},{8,12},{9,5},{12,0},{13,9},{2,6},{3,15},{... | collective-permute-start | bytes 3145736 | tf_op jit(solution)/shard_map/ppermute | solution.py:325
  14.5 1.3 copy-start.7
  14.5 2.3 %copy-start.9 = (s32[28]{0:T(128)S(1)}, s32[28]{0:T(128)}, u32[]{:S(2)}) copy-start(s32[28]{0:T(128)} %param.27) | copy-start | bytes 340
  14.6 2.4 %copy-start.1 = (s32[32]{0:T(128)S(1)}, s32[32]{0:T(128)}, u32[]{:S(2)}) copy-start(s32[32]{0:T(128)} %param.26) | copy-start | bytes 388
  20.3 4.6 %copy-start.8 = (f32[2,512]{1,0:T(2,128)S(1)}, f32[2,512]{1,0:T(2,128)}, u32[]{:S(2)}) copy-start(f32[2,512]{1,0:T(2,128)} %param.18) | copy-start | bytes 12292
  20.3 37.0 %all-to-all-start = ((bf16[4,4,2,256,128]{4,3,2,1,0:T(8,128)(2,1)}), bf16[4,4,2,256,128]{4,3,2,1,0:T(8,128)(2,1)}, u32[]{:S(2)}, u32[]{:S(2)}) async-start(bf16[4,4,2,256,128]{4,3,2,1,0:T(8,128)(2,1)} %broadcast_in_dim.139), calls=%async_computation | async-start | bytes 4194304 | tf_op jit(solution)/shard_map/all_to_all | solution.py:31
  25.7 31.7 %copy-start.2 = (s32[32]{0:T(128)S(1)}, s32[32]{0:T(128)}, u32[]{:S(2)}) copy-start(s32[32]{0:T(128)} %param.25) | copy-start | bytes 388
  26.5 7.2 %collective-permute-start.4 = (bf16[784,128]{1,0:T(8,128)(2,1)S(1)}, bf16[784,128]{1,0:T(8,128)(2,1)S(1)}, u32[]{:S(2)}, u32[]{:S(2)}) collective-permute-start(bf16[784,128]{1,0:T(8,128)(2,1)S(1)} %get-tuple-element.50), channel_id=1, source_target_pairs={{0,12},{1,76},{4,0},{5,64},{8,4},{9,68},{12,8},{13,72},{64,13},{65... | collective-permute-start | bytes 602120 | tf_op jit(solution)/shard_map/ppermute | solution.py:306
  28.3 7.3 %collective-permute-start.3 = (bf16[784,128]{1,0:T(8,128)(2,1)S(1)}, bf16[784,128]{1,0:T(8,128)(2,1)S(1)}, u32[]{:S(2)}, u32[]{:S(2)}) collective-permute-start(bf16[784,128]{1,0:T(8,128)(2,1)S(1)} %get-tuple-element.51), channel_id=1, source_target_pairs={{0,8},{1,72},{4,12},{5,76},{8,0},{9,64},{12,4},{13,68},{64,9},{65,... | collective-permute-start | bytes 602120 | tf_op jit(solution)/shard_map/ppermute | solution.py:306
  28.5 9.1 %collective-permute-start.2 = (bf16[784,128]{1,0:T(8,128)(2,1)S(1)}, bf16[784,128]{1,0:T(8,128)(2,1)S(1)}, u32[]{:S(2)}, u32[]{:S(2)}) collective-permute-start(bf16[784,128]{1,0:T(8,128)(2,1)S(1)} %get-tuple-element.52), channel_id=1, source_target_pairs={{0,4},{1,68},{4,8},{5,72},{8,12},{9,76},{12,0},{13,64},{64,5},{65,... | collective-permute-start | bytes 602120 | tf_op jit(solution)/shard_map/ppermute | solution.py:306
  29.9 7.8 %collective-permute-start.1 = (bf16[784,128]{1,0:T(8,128)(2,1)S(1)}, bf16[784,128]{1,0:T(8,128)(2,1)S(1)}, u32[]{:S(2)}, u32[]{:S(2)}) collective-permute-start(bf16[784,128]{1,0:T(8,128)(2,1)S(1)} %get-tuple-element.53), channel_id=1, source_target_pairs={{0,0},{1,64},{4,4},{5,68},{8,8},{9,72},{12,12},{13,76},{64,1},{65,... | collective-permute-start | bytes 602120 | tf_op jit(solution)/shard_map/ppermute | solution.py:306
  33.7 29.7 %copy-start.10 = (bf16[784,128]{1,0:T(8,128)(2,1)}, bf16[784,128]{1,0:T(8,128)(2,1)S(1)}, u32[]{:S(2)}) copy-start(bf16[784,128]{1,0:T(8,128)(2,1)S(1)} %collective-permute-done.4.rest_3_) | copy-start | bytes 602116
  35.6 27.5 %copy-start.11 = (bf16[784,128]{1,0:T(8,128)(2,1)}, bf16[784,128]{1,0:T(8,128)(2,1)S(1)}, u32[]{:S(2)}) copy-start(bf16[784,128]{1,0:T(8,128)(2,1)S(1)} %collective-permute-done.3.rest_2_) | copy-start | bytes 602116
  37.6 25.5 %copy-start.12 = (bf16[784,128]{1,0:T(8,128)(2,1)}, bf16[784,128]{1,0:T(8,128)(2,1)S(1)}, u32[]{:S(2)}) copy-start(bf16[784,128]{1,0:T(8,128)(2,1)S(1)} %collective-permute-done.2.rest_1_) | copy-start | bytes 602116
  37.7 24.5 %copy-start.13 = (bf16[784,128]{1,0:T(8,128)(2,1)}, bf16[784,128]{1,0:T(8,128)(2,1)S(1)}, u32[]{:S(2)}) copy-start(bf16[784,128]{1,0:T(8,128)(2,1)S(1)} %collective-permute-done.1.rest_0_) | copy-start | bytes 602116
  57.3 6.1 %collective-permute-start.9 = (bf16[16,2,256,128]{3,2,1,0:T(8,128)(2,1)}, bf16[16,2,256,128]{3,2,1,0:T(8,128)(2,1)}, u32[]{:S(2)}, u32[]{:S(2)}) collective-permute-start(bf16[16,2,256,128]{3,2,1,0:T(8,128)(2,1)} %bitcast.69.rest_8_), channel_id=1, source_target_pairs={{0,1},{1,0},{2,3},{3,2},{4,5},{5,4},{6,7},{7,6},{8,9},{9,8},{10,11... | collective-permute-start | bytes 6291464 | tf_op jit(solution)/shard_map/ppermute | solution.py:23
  58.8 32.8 %collective-permute-start.14 = (bf16[2,2048,256]{2,1,0:T(8,128)(2,1)}, bf16[2,2048,256]{2,1,0:T(8,128)(2,1)}, u32[]{:S(2)}, u32[]{:S(2)}) collective-permute-start(bf16[2,2048,256]{2,1,0:T(8,128)(2,1)} %param.21), channel_id=1, source_target_pairs={{1,9},{5,13},{9,1},{13,5},{3,11},{7,15},{11,3},{15,7},{17,25},{21,... | collective-permute-start | bytes 6291464 | tf_op jit(solution)/shard_map/ppermute | solution.py:331
  62.4 28.3 %collective-permute-start.15 = (bf16[256,2048]{1,0:T(8,128)(2,1)}, bf16[256,2048]{1,0:T(8,128)(2,1)S(1)}, u32[]{:S(2)}, u32[]{:S(2)}) collective-permute-start(bf16[256,2048]{1,0:T(8,128)(2,1)} %param.22), channel_id=1, source_target_pairs={{1,9},{5,13},{9,1},{13,5},{3,11},{7,15},{11,3},{15,7},{17,25},{21,... | collective-permute-start | bytes 3145736 | tf_op jit(solution)/shard_map/ppermute | solution.py:331
  81.3 4.3 %collective-permute-start.10 = (bf16[256,128]{1,0:T(8,128)(2,1)S(1)}, bf16[256,128]{1,0:T(8,128)(2,1)S(1)}, u32[]{:S(2)}, u32[]{:S(2)}) collective-permute-start(bf16[256,128]{1,0:T(8,128)(2,1)S(1)} %get-tuple-element.58), channel_id=1, source_target_pairs={{0,0},{1,64},{4,4},{5,68},{8,8},{9,72},{12,12},{13,76},{64,1},{65,... | collective-permute-start | bytes 196616 | tf_op jit(solution)/shard_map/ppermute | solution.py:412
  82.0 6.6 %collective-permute-start.13 = (bf16[256,128]{1,0:T(8,128)(2,1)S(1)}, bf16[256,128]{1,0:T(8,128)(2,1)S(1)}, u32[]{:S(2)}, u32[]{:S(2)}) collective-permute-start(bf16[256,128]{1,0:T(8,128)(2,1)S(1)} %get-tuple-element.59), channel_id=1, source_target_pairs={{0,4},{1,68},{4,8},{5,72},{8,12},{9,76},{12,0},{13,64},{64,5},{65,... | collective-permute-start | bytes 196616 | tf_op jit(solution)/shard_map/ppermute | solution.py:412
  83.4 6.6 %collective-permute-start.12 = (bf16[256,128]{1,0:T(8,128)(2,1)S(1)}, bf16[256,128]{1,0:T(8,128)(2,1)S(1)}, u32[]{:S(2)}, u32[]{:S(2)}) collective-permute-start(bf16[256,128]{1,0:T(8,128)(2,1)S(1)} %get-tuple-element.60), channel_id=1, source_target_pairs={{0,8},{1,72},{4,12},{5,76},{8,0},{9,64},{12,4},{13,68},{64,9},{65,... | collective-permute-start | bytes 196616 | tf_op jit(solution)/shard_map/ppermute | solution.py:412
  85.6 5.0 %collective-permute-start.11 = (bf16[256,128]{1,0:T(8,128)(2,1)S(1)}, bf16[256,128]{1,0:T(8,128)(2,1)S(1)}, u32[]{:S(2)}, u32[]{:S(2)}) collective-permute-start(bf16[256,128]{1,0:T(8,128)(2,1)S(1)} %get-tuple-element.61), channel_id=1, source_target_pairs={{0,12},{1,76},{4,0},{5,64},{8,4},{9,68},{12,8},{13,72},{64,13},{65... | collective-permute-start | bytes 196616 | tf_op jit(solution)/shard_map/ppermute | solution.py:412
  90.6 1.0 copy-start.4
  94.5 15.3 %copy-start.6 = (f32[2,2048]{1,0:T(2,128)S(1)}, f32[2,2048]{1,0:T(2,128)}, u32[]{:S(2)}) copy-start(f32[2,2048]{1,0:T(2,128)} %param.20) | copy-start | bytes 49156
  95.4 13.1 %collective-permute-start.16 = (bf16[2,64,2048]{2,1,0:T(8,128)(2,1)}, bf16[2,64,2048]{2,1,0:T(8,128)(2,1)}, u32[]{:S(2)}, u32[]{:S(2)}) collective-permute-start(bf16[2,64,2048]{2,1,0:T(8,128)(2,1)} %fusion.5), channel_id=1, source_target_pairs={{0,1},{1,0},{2,3},{3,2},{4,5},{5,4},{6,7},{7,6},{8,9},{9,8},{10,11... | collective-permute-start | bytes 1572872 | tf_op jit(solution)/shard_map/ppermute | solution.py:23
  109.6 8.7 %collective-permute-start.17 = (bf16[64,2048]{1,0:T(8,128)(2,1)S(1)}, bf16[64,2048]{1,0:T(8,128)(2,1)S(1)}, u32[]{:S(2)}, u32[]{:S(2)}) collective-permute-start(bf16[64,2048]{1,0:T(8,128)(2,1)S(1)} %fusion.6), channel_id=1, source_target_pairs={{0,2},{2,0},{1,3},{3,1},{4,6},{6,4},{5,7},{7,5},{8,10},{10,8},{9,1... | collective-permute-start | bytes 786440 | tf_op jit(solution)/shard_map/ppermute | solution.py:23
  119.6 35.3 %collective-permute-start.18 = (bf16[2,2048,256]{2,1,0:T(8,128)(2,1)}, bf16[2,2048,256]{2,1,0:T(8,128)(2,1)S(1)}, u32[]{:S(2)}, u32[]{:S(2)}) collective-permute-start(bf16[2,2048,256]{2,1,0:T(8,128)(2,1)} %param.21), channel_id=1, source_target_pairs={{0,4},{1,13},{4,8},{5,1},{8,12},{9,5},{12,0},{13,9},{2,6},{3,15},{... | collective-permute-start | bytes 6291464 | tf_op jit(solution)/shard_map/ppermute | solution.py:325
  154.9 5.9 %copy-start.3 = (bf16[8,64,2048]{2,1,0:T(8,128)(2,1)}, bf16[8,64,2048]{2,1,0:T(8,128)(2,1)S(1)}, u32[]{:S(2)}) copy-start(bf16[8,64,2048]{2,1,0:T(8,128)(2,1)S(1)} %all_to_all.15) | copy-start | bytes 6291460
  154.9 1.4 copy-start.14
  156.2 4.5 %collective-permute-start.19 = (bf16[512,2048]{1,0:T(8,128)(2,1)S(1)}, bf16[512,2048]{1,0:T(8,128)(2,1)}, u32[]{:S(2)}, u32[]{:S(2)}) collective-permute-start(bf16[512,2048]{1,0:T(8,128)(2,1)S(1)} %bitcast.128), channel_id=1, source_target_pairs={{0,1},{1,0},{2,3},{3,2},{4,5},{5,4},{6,7},{7,6},{8,9},{9,8},{10,11... | collective-permute-start | bytes 6291464 | tf_op jit(solution)/shard_map/ppermute | solution.py:23
  167.1 6.8 %collective-permute-start.20 = (bf16[512,2048]{1,0:T(8,128)(2,1)S(1)}, bf16[512,2048]{1,0:T(8,128)(2,1)S(1)}, u32[]{:S(2)}, u32[]{:S(2)}) collective-permute-start(bf16[512,2048]{1,0:T(8,128)(2,1)S(1)} %shard_map.138), channel_id=1, source_target_pairs={{0,1},{1,0},{2,3},{3,2},{4,5},{5,4},{6,7},{7,6},{8,9},{9,8},{10,11... | collective-permute-start | bytes 6291464 | tf_op jit(solution)/shard_map/ppermute | solution.py:23

commit v13 on v12

--- a/solution.py
+++ b/solution.py
@@ -206,7 +206,10 @@
     )(nodes, lengths, lists, counts, *in_hbm(qkv_parts), row_info, seg_row, factors, key_factors, *in_hbm(parts))
 
 
-def feed_forward_body(tokens_ref, gu_a, dn_a, gu_b, dn_b, out_ref, tokens, gu, dn, made, sems):
+def feed_forward_body(
+    core_ref, tokens_ref, gu_a, dn_a, gu_own, dn_own, gu_far, dn_far, out_ref,
+    tokens, gu, dn, made, sems,
+):
     rows = 256
     blocks = tokens.shape[0] // rows
 
@@ -219,14 +222,27 @@
     def store(i):
         return pltpu.make_async_copy(block(made, i), block(out_ref, i), sems.at[1, i])
 
-    loads = [
-        pltpu.make_async_copy(source, target, sems.at[2 + j, k])
-        for k, pair in enumerate(((gu_a, dn_a), (gu_b, dn_b)))
-        for j, (source, target) in enumerate(((pair[0], gu.at[k]), (pair[1], dn.at[k])))
-    ]
+    def share(k, gu_ref, dn_ref):
+        return [
+            pltpu.make_async_copy(gu_ref, gu.at[k], sems.at[2, k]),
+            pltpu.make_async_copy(dn_ref, dn.at[k], sems.at[3, k]),
+        ]
+
+    loads = share(0, gu_a, dn_a) + share(1, gu_far, dn_far)
     fetch(0).start()
-    for load in loads:
+    for load in share(0, gu_a, dn_a):
         load.start()
+
+    @pl.when(core_ref[0] == 0)
+    def _():
+        for load in share(1, gu_own, dn_own):
+            load.start()
+
+    @pl.when(core_ref[0] != 0)
+    def _():
+        for load in share(1, gu_far, dn_far):
+            load.start()
+
     for i in range(1, blocks):
         fetch(i).start()
     for i in range(blocks):
@@ -248,13 +264,14 @@
         store(i).wait()
 
 
-def feed_forward(tokens, weights):
+def feed_forward(core, tokens, weights):
     rows, width = tokens.shape
     units = weights[1].shape[0]
     return pl.pallas_call(
         feed_forward_body,
         out_shape=jax.ShapeDtypeStruct((rows, width), BF),
-        in_specs=[pl.BlockSpec(memory_space=pltpu.MemorySpace.HBM)] * 5,
+        in_specs=[pl.BlockSpec(memory_space=pltpu.MemorySpace.SMEM)]
+        + [pl.BlockSpec(memory_space=pltpu.MemorySpace.HBM)] * 7,
         out_specs=pl.BlockSpec(memory_space=pltpu.MemorySpace.HBM),
         scratch_shapes=[
             pltpu.VMEM((rows, width), BF),
@@ -269,7 +286,7 @@
             transcendentals=2 * rows * units,
             bytes_accessed=(2 * rows * width + 6 * width * units) * 2,
         ),
-    )(tokens, *weights)
+    )(core, tokens, *weights)
 
 
 def on_device(
@@ -432,12 +449,11 @@
     gu_a = beside(w_gate_up)
     tokens = spread(mid_state, plane)
     tokens, gu_a = lax.optimization_barrier((tokens, gu_a))
-    weights = (
-        gu_a, dn_a, jnp.where(core == 0, w_gate_up, gu_b), jnp.where(core == 0, w_down, dn_b)
-    )
+    weights = (gu_a, dn_a, w_gate_up, w_down, gu_b, dn_b)
+    core_at = core.astype(jnp.int32).reshape(1)
     flat = tokens.reshape(-1, tokens.shape[2])
-    other = feed_forward(shift(flat, "core", 1), weights)
-    total = feed_forward(flat, weights).astype(F32) + shift(other, "core", 1).astype(F32)
+    other = feed_forward(core_at, shift(flat, "core", 1), weights)
+    total = feed_forward(core_at, flat, weights).astype(F32) + shift(other, "core", 1).astype(F32)
     total = lax.all_to_all(total.astype(BF).reshape(tokens.shape), plane, 0, 0, tiled=True)
     mlp_proj = jnp.sum(total.astype(F32), axis=0)
     return (mid_state.astype(F32) + rms_norm(mlp_proj, post_gain[1])).astype(BF)

time: 209 us -> 221 us (1.057)
  local copies, waits for them, and re-layouts: 10.8 us -> 17.4 us
  waiting for transfers between devices: 21 us -> 24 us
  blocking collectives: 84.3 us -> 87 us
    select_n x2 -> x0, other arithmetic: 4.54 us -> none  [the longest x1 3.16 us: on_device(): jnp.where(core == 0, w_gate_up, gu_b)]
    ppermute x5, waiting for transfers between devices: 10.4 us -> 14.5 us  [shift(): return lax.ppermute(values, axis, [(i, (i + by) % n) for i in range(n)])]
    all_to_all x1, blocking collectives: 33.4 us -> 36.4 us  [spread(): return lax.all_to_all(copies, axes, 0, 0, tiled=True)]
    unnamed x31 -> x41, local copies, waits for them, and re-layouts: 2.49 us -> 5.52 us
    ppermute x5, starting transfers between devices: 11.9 us -> 9.02 us  [shift(): return lax.ppermute(values, axis, [(i, (i + by) % n) for i in range(n)])]
    another operation x4, other arithmetic: 0.06 us -> 2.68 us  [head_piece(): jnp.stack([lax.dynamic_slice_in_dim(c[0], cut, HD, 1) for c in (cache_key...]
  transfers between devices with their start and end apart: 22 -> 22, of which waited for: 9 -> 9; matrix products, arithmetic and copies ran while one was open for 9% -> 10% of each run, Pallas kernels for 12% -> 11%
where the time goes in v13:
time: 221 us; the launch traced here: 220 us
  blocking collectives  87 us (39%)
  starting transfers between devices  38.4 us (17%)
  Pallas kernels  30.5 us (14%)
  waiting for transfers between devices  24 us (11%)
  local copies, waits for them, and re-layouts  17.4 us (8%)
  other arithmetic  14.2 us (6%)
  matrix products  7.51 us (3%)
    all_to_all x1, blocking collectives, spread(): return lax.all_to_all(copies, axes, 0, 0, tiled=True)  36.4 us
    all_to_all x1, blocking collectives, on_device(): lax.all_to_all(total.astype(BF).reshape(tokens.shape), plane, 0, 0, tiled...  31.8 us
    psum x1, blocking collectives, on_device(): factors = lax.rsqrt(lax.psum(squares, ('yhi', 'ylo')) / columns + EPS)  18.8 us
    pallas_call x1, Pallas kernels, attention(): pl.pallas_call(attention_body, out_shape=jax.ShapeDtypeStruct((groups, ro...  17.9 us
    ppermute x5, waiting for transfers between devices, shift(): return lax.ppermute(values, axis, [(i, (i + by) % n) for i in range(n)])  14.5 us
    ppermute x8, starting transfers between devices, across(): return lax.ppermute(values, corner, pairs)  13.4 us
    pallas_call x2, Pallas kernels, feed_forward(): pl.pallas_call(feed_forward_body, out_shape=jax.ShapeDtypeStruct((rows, w...  12.6 us
    ppermute x5, starting transfers between devices, shift(): return lax.ppermute(values, axis, [(i, (i + by) % n) for i in range(n)])  9.02 us
  transfers between devices with their start and end apart: 22, of which 9 were waited for; matrix products, arithmetic and copies ran while one was open for 10% of the time, Pallas kernels for 11%

profile of v13, /device:TPU:0, one launch (start us, length us, event | category | flops | bytes accessed | tf_op | source)
XLA Modules:
  0.0 219.6 jit_solution(11612378616574240251)
XLA Ops:
  0.0 1.3 constant_dynamic-slice_fusion.6
  1.9 4.0 %collective-permute-start.7 = (bf16[2,256,128]{2,1,0:T(8,128)(2,1)}, bf16[2,256,128]{2,1,0:T(8,128)(2,1)}, u32[]{:S(2)}, u32[]{:S(2)}) collective-permute-start(bf16[2,256,128]{2,1,0:T(8,128)(2,1)} %pad_maximum_fusion.5), channel_id=1, source_target_pairs={{0,8},{1,72},{4,12},{5,76},{8,0},{9,64},{12,4},{13,68},{64,9},{65,... | collective-permute-start | bytes 393224 | tf_op jit(solution)/shard_map/ppermute | solution.py:323
  8.0 1.3 collective-permute-start.6
  10.0 2.2 collective-permute-start.5
  12.2 1.0 collective-permute-start
  13.2 4.7 %convolution_bitcast_fusion = f32[3,256,512]{1,2,0:T(8,128)S(1)} fusion(bf16[3,2048,512]{2,1,0:T(8,128)(2,1)} %param.17, bf16[256,2048]{1,0:T(8,128)(2,1)S(1)} %copy-done.12), kind=kOutput, calls=%fused_computation.10 | convolution fusion | flops 1610612736 | bytes 8912896 | tf_op jit(solution)/shard_map/td,cdw->ctw/dot_general | solution.py:354
  20.5 0.9 multiply_cosine_fusion
  21.5 1.2 pad_maximum_fusion.1
  22.6 1.8 broadcast_in_dim.139
  24.4 4.6 %all-to-all-start = ((bf16[4,4,2,256,128]{4,3,2,1,0:T(8,128)(2,1)}), bf16[4,4,2,256,128]{4,3,2,1,0:T(8,128)(2,1)}, u32[]{:S(2)}, u32[]{:S(2)}) async-start(bf16[4,4,2,256,128]{4,3,2,1,0:T(8,128)(2,1)} %broadcast_in_dim.139), calls=%async_computation | async-start | bytes 4194304 | tf_op jit(solution)/shard_map/all_to_all | solution.py:31
  30.0 0.9 maximum_bitcast_fusion
  31.0 1.5 copy.43
  32.8 2.3 %collective-permute-start.4 = (bf16[784,128]{1,0:T(8,128)(2,1)S(1)}, bf16[784,128]{1,0:T(8,128)(2,1)S(1)}, u32[]{:S(2)}, u32[]{:S(2)}) collective-permute-start(bf16[784,128]{1,0:T(8,128)(2,1)S(1)} %get-tuple-element.50), channel_id=1, source_target_pairs={{0,12},{1,76},{4,0},{5,64},{8,4},{9,68},{12,8},{13,72},{64,13},{65... | collective-permute-start | bytes 602120 | tf_op jit(solution)/shard_map/ppermute | solution.py:323
  35.3 1.3 collective-permute-start.2
  36.7 1.3 collective-permute-start.1
  38.0 2.5 %collective-permute-done.4.rest_3_ = bf16[784,128]{1,0:T(8,128)(2,1)S(1)} collective-permute-done((bf16[784,128]{1,0:T(8,128)(2,1)S(1)}, bf16[784,128]{1,0:T(8,128)(2,1)S(1)}, u32[]{:S(2)}, u32[]{:S(2)}) %collective-permute-start.4) | collective-permute-done | bytes 200736 | tf_op jit(solution)/shard_map/ppermute | solution.py:323
  40.5 1.9 collective-permute-done.3.rest_2_
  42.4 2.0 collective-permute-done.2.rest_1_
  45.2 18.8 %psum.7 = f32[4,256,2]{1,2,0:T(2,128)S(1)} all-reduce(f32[4,256,2]{1,2,0:T(2,128)S(1)} %bitcast.138), channel_id=1, replica_groups=mesh['yhi'=2,'x'=4,'z'=4,'ylo'=2,'core'=2] {'yhi','ylo'}, use_global_device_ids=true, to_apply=%region_13.15 | all-reduce | flops 2048 | bytes 16384 | tf_op jit(solution)/shard_map/psum | solution.py:392
  65.5 2.0 collective-permute-start.14
  68.8 1.0 copy.46.rest_4_
  70.6 1.0 copy.47.rest_6_
  71.7 1.0 copy-done.2
  72.7 1.0 copy-done.3
  73.8 17.9 %shard_map.136 = bf16[4,256,128]{2,1,0:T(8,128)(2,1)S(1)} custom-call(s32[32]{0:T(128)S(1)} %get-tuple-element.47.nodes_ref, s32[32]{0:T(128)S(1)} %and_select_fusion.lengths_ref, s32[4,2,12]{2,1,0:T(2,128)S(1)} %copy.44.lists_ref, s32[4,2]{1,0:T(4,128)S(1)} %copy.45.counts_ref, bf16[784,128]{1,0:T(8,128)(2,1)} %collective-permute-done.1.rest_0_, ...), custom_call_target="tpu_custom_call" | custom-call | flops 2000000000 | bytes 6000000 | tf_op jit(solution)/shard_map/pallas_call | solution.py:183
  92.4 1.4 collective-permute-start.13
  93.8 2.2 collective-permute-start.12
  96.0 1.9 collective-permute-start.11
  97.9 1.1 collective-permute-done.13
  99.0 1.5 collective-permute-done.12
  101.1 0.9 pad_maximum_fusion.2
  102.0 2.8 %fusion.1 = f32[256,2048]{1,0:T(8,128)S(1)} fusion(bf16[256,512]{1,0:T(8,128)(2,1)S(1)} %pad_maximum_fusion.2, s32[]{:T(128)S(6)} %select_n.277, bf16[512,2048]{1,0:T(8,128)(2,1)} %param.19), kind=kOutput, calls=%fused_computation.9 | convolution fusion | flops 541065216 | bytes 4456452 | tf_op jit(solution)/shard_map/dot_general | solution.py:433
  104.8 1.3 copy-done.10
  106.2 0.9 fusion.5
  107.0 8.5 %collective-permute-start.16 = (bf16[2,64,2048]{2,1,0:T(8,128)(2,1)}, bf16[2,64,2048]{2,1,0:T(8,128)(2,1)}, u32[]{:S(2)}, u32[]{:S(2)}) collective-permute-start(bf16[2,64,2048]{2,1,0:T(8,128)(2,1)} %fusion.5), channel_id=1, source_target_pairs={{0,1},{1,0},{2,3},{3,2},{4,5},{5,4},{6,7},{7,6},{8,9},{9,8},{10,11... | collective-permute-start | bytes 1572872 | tf_op jit(solution)/shard_map/ppermute | solution.py:23
  115.5 1.9 collective-permute-done.16
  117.4 1.5 bitcast_add_fusion
  119.0 8.5 %collective-permute-done.17 = bf16[64,2048]{1,0:T(8,128)(2,1)S(1)} collective-permute-done((bf16[64,2048]{1,0:T(8,128)(2,1)S(1)}, bf16[64,2048]{1,0:T(8,128)(2,1)S(1)}, u32[]{:S(2)}, u32[]{:S(2)}) %collective-permute-start.17) | collective-permute-done | bytes 262176 | tf_op jit(solution)/shard_map/ppermute | solution.py:23
  127.8 1.1 add_convert_fusion.2
  128.9 1.5 collective-permute-start.18
  130.6 36.4 %all_to_all.15 = bf16[8,64,2048]{2,1,0:T(8,128)(2,1)S(1)} all-to-all(bf16[8,64,2048]{2,1,0:T(8,128)(2,1)S(1)} %broadcast_in_dim.140), channel_id=1, replica_groups=mesh['yhi'=2,'x'=4,'z'=4,'ylo'=2,'core'=2] {'yhi','x'}, dimensions={0} | all-to-all | bytes 4194304 | tf_op jit(solution)/shard_map/all_to_all | solution.py:31
  167.2 4.0 %collective-permute-done.19.tokens_ref = bf16[512,2048]{1,0:T(8,128)(2,1)S(1)} collective-permute-done((bf16[512,2048]{1,0:T(8,128)(2,1)S(1)}, bf16[512,2048]{1,0:T(8,128)(2,1)S(1)}, u32[]{:S(2)}, u32[]{:S(2)}) %collective-permute-start.19) | collective-permute-done | bytes 2097184 | tf_op jit(solution)/shard_map/ppermute | solution.py:23
  171.3 1.4 copy-done.9
  172.7 6.3 %shard_map.138 = bf16[512,2048]{1,0:T(8,128)(2,1)S(1)} custom-call(s32[1]{0:T(128)} %bitcast.82.core_ref, bf16[512,2048]{1,0:T(8,128)(2,1)} %copy-done.9, bf16[2,2048,256]{2,1,0:T(8,128)(2,1)} %copy-done.8, bf16[256,2048]{1,0:T(8,128)(2,1)S(1)} %collective-permute-done.dn_a, bf16[2,2048,256]{2,1,0:T(8,128)(2,1)} %gu_own.1, bf16[256,2048]{1,0:T(8,128)(2,1)S(1)} %copy-done.1, ...), custom_call_target="tpu_custom_call" | custom-call | flops 3221225472 | bytes 10485760 | tf_op jit(solution)/shard_map/pallas_call | solution.py:270
  179.2 6.3 %shard_map.137 = bf16[512,2048]{1,0:T(8,128)(2,1)S(1)} custom-call(s32[1]{0:T(128)} %bitcast.82.core_ref, bf16[512,2048]{1,0:T(8,128)(2,1)} %bitcast.129, bf16[2,2048,256]{2,1,0:T(8,128)(2,1)} %copy-done.8, bf16[256,2048]{1,0:T(8,128)(2,1)S(1)} %collective-permute-done.dn_a, bf16[2,2048,256]{2,1,0:T(8,128)(2,1)} %gu_own.1, bf16[256,2048]{1,0:T(8,128)(2,1)S(1)} %copy-done.1, ...), custom_call_target="tpu_custom_call" | custom-call | flops 3221225472 | bytes 10485760 | tf_op jit(solution)/shard_map/pallas_call | solution.py:270
  185.5 0.9 add_convert_fusion
  186.4 31.8 %all_to_all.16 = bf16[8,64,2048]{2,1,0:T(8,128)(2,1)S(1)} all-to-all(bf16[8,64,2048]{2,1,0:T(8,128)(2,1)S(1)} %bitcast.127), channel_id=1, replica_groups=mesh['yhi'=2,'x'=4,'z'=4,'ylo'=2,'core'=2] {'yhi','x'}, dimensions={0} | all-to-all | bytes 4194304 | tf_op jit(solution)/shard_map/all_to_all | solution.py:457
  218.7 0.9 add_convert_fusion.1
  (136 shorter events, 14.5 us)
Async XLA Ops:
  0.0 18.4 %copy-start = (s32[32,256]{1,0:T(8,128)S(1)}, s32[32,256]{1,0:T(8,128)}, u32[]{:S(2)}) copy-start(s32[32,256]{1,0:T(8,128)} %param.28) | copy-start | bytes 98308
  0.0 12.2 %copy-start.1 = (bf16[256,2048]{1,0:T(8,128)(2,1)S(1)}, bf16[256,2048]{1,0:T(8,128)(2,1)}, u32[]{:S(2)}) copy-start(bf16[256,2048]{1,0:T(8,128)(2,1)} %dn_own.1) | copy-start | bytes 3145732
  0.0 13.2 %copy-start.12 = (bf16[256,2048]{1,0:T(8,128)(2,1)S(1)}, bf16[256,2048]{1,0:T(8,128)(2,1)}, u32[]{:S(2)}) copy-start(bf16[256,2048]{1,0:T(8,128)(2,1)} %param.16) | copy-start | bytes 3145732
  1.9 19.5 %collective-permute-start.7 = (bf16[2,256,128]{2,1,0:T(8,128)(2,1)}, bf16[2,256,128]{2,1,0:T(8,128)(2,1)}, u32[]{:S(2)}, u32[]{:S(2)}) collective-permute-start(bf16[2,256,128]{2,1,0:T(8,128)(2,1)} %pad_maximum_fusion.5), channel_id=1, source_target_pairs={{0,8},{1,72},{4,12},{5,76},{8,0},{9,64},{12,4},{13,68},{64,9},{65,... | collective-permute-start | bytes 393224 | tf_op jit(solution)/shard_map/ppermute | solution.py:323
  6.6 14.8 %collective-permute-start.8 = (bf16[2,256,128]{2,1,0:T(8,128)(2,1)}, bf16[2,256,128]{2,1,0:T(8,128)(2,1)}, u32[]{:S(2)}, u32[]{:S(2)}) collective-permute-start(bf16[2,256,128]{2,1,0:T(8,128)(2,1)} %pad_maximum_fusion.6), channel_id=1, source_target_pairs={{0,12},{1,76},{4,0},{5,64},{8,4},{9,68},{12,8},{13,72},{64,13},{65... | collective-permute-start | bytes 393224 | tf_op jit(solution)/shard_map/ppermute | solution.py:323
  8.0 13.4 %collective-permute-start.6 = (bf16[2,256,128]{2,1,0:T(8,128)(2,1)}, bf16[2,256,128]{2,1,0:T(8,128)(2,1)}, u32[]{:S(2)}, u32[]{:S(2)}) collective-permute-start(bf16[2,256,128]{2,1,0:T(8,128)(2,1)} %pad_maximum_fusion.4), channel_id=1, source_target_pairs={{0,4},{1,68},{4,8},{5,72},{8,12},{9,76},{12,0},{13,64},{64,5},{65,... | collective-permute-start | bytes 393224 | tf_op jit(solution)/shard_map/ppermute | solution.py:323
  10.0 11.5 %collective-permute-start.5 = (bf16[2,256,128]{2,1,0:T(8,128)(2,1)}, bf16[2,256,128]{2,1,0:T(8,128)(2,1)}, u32[]{:S(2)}, u32[]{:S(2)}) collective-permute-start(bf16[2,256,128]{2,1,0:T(8,128)(2,1)} %pad_maximum_fusion.3), channel_id=1, source_target_pairs={{0,0},{1,64},{4,4},{5,68},{8,8},{9,72},{12,12},{13,76},{64,1},{65,... | collective-permute-start | bytes 393224 | tf_op jit(solution)/shard_map/ppermute | solution.py:323
  12.2 20.6 %collective-permute-start = (bf16[256,2048]{1,0:T(8,128)(2,1)S(1)}, bf16[256,2048]{1,0:T(8,128)(2,1)S(1)}, u32[]{:S(2)}, u32[]{:S(2)}) collective-permute-start(bf16[256,2048]{1,0:T(8,128)(2,1)S(1)} %copy-done.1), channel_id=1, source_target_pairs={{0,4},{1,13},{4,8},{5,1},{8,12},{9,5},{12,0},{13,9},{2,6},{3,15},{... | collective-permute-start | bytes 3145736 | tf_op jit(solution)/shard_map/ppermute | solution.py:342
  17.9 1.3 copy-start.14
  17.9 2.3 %copy-start.16 = (s32[28]{0:T(128)S(1)}, s32[28]{0:T(128)}, u32[]{:S(2)}) copy-start(s32[28]{0:T(128)} %param.27) | copy-start | bytes 340
  17.9 2.4 %copy-start.4 = (s32[32]{0:T(128)S(1)}, s32[32]{0:T(128)}, u32[]{:S(2)}) copy-start(s32[32]{0:T(128)} %param.26) | copy-start | bytes 388
  24.4 4.6 %copy-start.15 = (f32[2,512]{1,0:T(2,128)S(1)}, f32[2,512]{1,0:T(2,128)}, u32[]{:S(2)}) copy-start(f32[2,512]{1,0:T(2,128)} %param.18) | copy-start | bytes 12292
  24.4 39.6 %all-to-all-start = ((bf16[4,4,2,256,128]{4,3,2,1,0:T(8,128)(2,1)}), bf16[4,4,2,256,128]{4,3,2,1,0:T(8,128)(2,1)}, u32[]{:S(2)}, u32[]{:S(2)}) async-start(bf16[4,4,2,256,128]{4,3,2,1,0:T(8,128)(2,1)} %broadcast_in_dim.139), calls=%async_computation | async-start | bytes 4194304 | tf_op jit(solution)/shard_map/all_to_all | solution.py:31
  29.0 0.8 copy-start.11
  32.5 31.6 %copy-start.5 = (s32[32]{0:T(128)S(1)}, s32[32]{0:T(128)}, u32[]{:S(2)}) copy-start(s32[32]{0:T(128)} %param.25) | copy-start | bytes 388
  32.8 7.7 %collective-permute-start.4 = (bf16[784,128]{1,0:T(8,128)(2,1)S(1)}, bf16[784,128]{1,0:T(8,128)(2,1)S(1)}, u32[]{:S(2)}, u32[]{:S(2)}) collective-permute-start(bf16[784,128]{1,0:T(8,128)(2,1)S(1)} %get-tuple-element.50), channel_id=1, source_target_pairs={{0,12},{1,76},{4,0},{5,64},{8,4},{9,68},{12,8},{13,72},{64,13},{65... | collective-permute-start | bytes 602120 | tf_op jit(solution)/shard_map/ppermute | solution.py:323
  35.1 7.3 %collective-permute-start.3 = (bf16[784,128]{1,0:T(8,128)(2,1)S(1)}, bf16[784,128]{1,0:T(8,128)(2,1)S(1)}, u32[]{:S(2)}, u32[]{:S(2)}) collective-permute-start(bf16[784,128]{1,0:T(8,128)(2,1)S(1)} %get-tuple-element.51), channel_id=1, source_target_pairs={{0,8},{1,72},{4,12},{5,76},{8,0},{9,64},{12,4},{13,68},{64,9},{65,... | collective-permute-start | bytes 602120 | tf_op jit(solution)/shard_map/ppermute | solution.py:323
  35.3 9.1 %collective-permute-start.2 = (bf16[784,128]{1,0:T(8,128)(2,1)S(1)}, bf16[784,128]{1,0:T(8,128)(2,1)S(1)}, u32[]{:S(2)}, u32[]{:S(2)}) collective-permute-start(bf16[784,128]{1,0:T(8,128)(2,1)S(1)} %get-tuple-element.52), channel_id=1, source_target_pairs={{0,4},{1,68},{4,8},{5,72},{8,12},{9,76},{12,0},{13,64},{64,5},{65,... | collective-permute-start | bytes 602120 | tf_op jit(solution)/shard_map/ppermute | solution.py:323
  36.7 7.8 %collective-permute-start.1 = (bf16[784,128]{1,0:T(8,128)(2,1)S(1)}, bf16[784,128]{1,0:T(8,128)(2,1)}, u32[]{:S(2)}, u32[]{:S(2)}) collective-permute-start(bf16[784,128]{1,0:T(8,128)(2,1)S(1)} %get-tuple-element.53), channel_id=1, source_target_pairs={{0,0},{1,64},{4,4},{5,68},{8,8},{9,72},{12,12},{13,76},{64,1},{65,... | collective-permute-start | bytes 602120 | tf_op jit(solution)/shard_map/ppermute | solution.py:323
  40.5 31.2 %copy-start.17 = (bf16[784,128]{1,0:T(8,128)(2,1)}, bf16[784,128]{1,0:T(8,128)(2,1)S(1)}, u32[]{:S(2)}) copy-start(bf16[784,128]{1,0:T(8,128)(2,1)S(1)} %collective-permute-done.4.rest_3_) | copy-start | bytes 602116
  42.4 26.4 %copy-start.18 = (bf16[784,128]{1,0:T(8,128)(2,1)}, bf16[784,128]{1,0:T(8,128)(2,1)S(1)}, u32[]{:S(2)}) copy-start(bf16[784,128]{1,0:T(8,128)(2,1)S(1)} %collective-permute-done.3.rest_2_) | copy-start | bytes 602116
  44.4 24.4 %copy-start.19 = (bf16[784,128]{1,0:T(8,128)(2,1)}, bf16[784,128]{1,0:T(8,128)(2,1)S(1)}, u32[]{:S(2)}) copy-start(bf16[784,128]{1,0:T(8,128)(2,1)S(1)} %collective-permute-done.2.rest_1_) | copy-start | bytes 602116
  64.0 7.7 %collective-permute-start.9 = (bf16[16,2,256,128]{3,2,1,0:T(8,128)(2,1)}, bf16[16,2,256,128]{3,2,1,0:T(8,128)(2,1)}, u32[]{:S(2)}, u32[]{:S(2)}) collective-permute-start(bf16[16,2,256,128]{3,2,1,0:T(8,128)(2,1)} %bitcast.69.rest_8_), channel_id=1, source_target_pairs={{0,1},{1,0},{2,3},{3,2},{4,5},{5,4},{6,7},{7,6},{8,9},{9,8},{10,11... | collective-permute-start | bytes 6291464 | tf_op jit(solution)/shard_map/ppermute | solution.py:23
  65.5 36.4 %collective-permute-start.14 = (bf16[2,2048,256]{2,1,0:T(8,128)(2,1)}, bf16[2,2048,256]{2,1,0:T(8,128)(2,1)}, u32[]{:S(2)}, u32[]{:S(2)}) collective-permute-start(bf16[2,2048,256]{2,1,0:T(8,128)(2,1)} %gu_own.1), channel_id=1, source_target_pairs={{1,9},{5,13},{9,1},{13,5},{3,11},{7,15},{11,3},{15,7},{17,25},{21,... | collective-permute-start | bytes 6291464 | tf_op jit(solution)/shard_map/ppermute | solution.py:348
  69.9 32.1 %collective-permute-start.15 = (bf16[256,2048]{1,0:T(8,128)(2,1)S(1)}, bf16[256,2048]{1,0:T(8,128)(2,1)S(1)}, u32[]{:S(2)}, u32[]{:S(2)}) collective-permute-start(bf16[256,2048]{1,0:T(8,128)(2,1)S(1)} %copy-done.1), channel_id=1, source_target_pairs={{1,9},{5,13},{9,1},{13,5},{3,11},{7,15},{11,3},{15,7},{17,25},{21,... | collective-permute-start | bytes 3145736 | tf_op jit(solution)/shard_map/ppermute | solution.py:348
  71.7 1.0 copy-start.2
  72.7 1.0 copy-start.3
  91.7 4.2 %collective-permute-start.10 = (bf16[256,128]{1,0:T(8,128)(2,1)S(1)}, bf16[256,128]{1,0:T(8,128)(2,1)S(1)}, u32[]{:S(2)}, u32[]{:S(2)}) collective-permute-start(bf16[256,128]{1,0:T(8,128)(2,1)S(1)} %get-tuple-element.58), channel_id=1, source_target_pairs={{0,0},{1,64},{4,4},{5,68},{8,8},{9,72},{12,12},{13,76},{64,1},{65,... | collective-permute-start | bytes 196616 | tf_op jit(solution)/shard_map/ppermute | solution.py:429
  92.4 6.6 %collective-permute-start.13 = (bf16[256,128]{1,0:T(8,128)(2,1)S(1)}, bf16[256,128]{1,0:T(8,128)(2,1)S(1)}, u32[]{:S(2)}, u32[]{:S(2)}) collective-permute-start(bf16[256,128]{1,0:T(8,128)(2,1)S(1)} %get-tuple-element.59), channel_id=1, source_target_pairs={{0,4},{1,68},{4,8},{5,72},{8,12},{9,76},{12,0},{13,64},{64,5},{65,... | collective-permute-start | bytes 196616 | tf_op jit(solution)/shard_map/ppermute | solution.py:429
  93.8 6.7 %collective-permute-start.12 = (bf16[256,128]{1,0:T(8,128)(2,1)S(1)}, bf16[256,128]{1,0:T(8,128)(2,1)}, u32[]{:S(2)}, u32[]{:S(2)}) collective-permute-start(bf16[256,128]{1,0:T(8,128)(2,1)S(1)} %get-tuple-element.60), channel_id=1, source_target_pairs={{0,8},{1,72},{4,12},{5,76},{8,0},{9,64},{12,4},{13,68},{64,9},{65,... | collective-permute-start | bytes 196616 | tf_op jit(solution)/shard_map/ppermute | solution.py:429
  96.0 5.1 %collective-permute-start.11 = (bf16[256,128]{1,0:T(8,128)(2,1)S(1)}, bf16[256,128]{1,0:T(8,128)(2,1)}, u32[]{:S(2)}, u32[]{:S(2)}) collective-permute-start(bf16[256,128]{1,0:T(8,128)(2,1)S(1)} %get-tuple-element.61), channel_id=1, source_target_pairs={{0,12},{1,76},{4,0},{5,64},{8,4},{9,68},{12,8},{13,72},{64,13},{65... | collective-permute-start | bytes 196616 | tf_op jit(solution)/shard_map/ppermute | solution.py:429
  104.8 1.3 copy-start.10
  106.2 12.8 %copy-start.13 = (f32[2,2048]{1,0:T(2,128)S(1)}, f32[2,2048]{1,0:T(2,128)}, u32[]{:S(2)}) copy-start(f32[2,2048]{1,0:T(2,128)} %param.20) | copy-start | bytes 49156
  107.0 10.3 %collective-permute-start.16 = (bf16[2,64,2048]{2,1,0:T(8,128)(2,1)}, bf16[2,64,2048]{2,1,0:T(8,128)(2,1)}, u32[]{:S(2)}, u32[]{:S(2)}) collective-permute-start(bf16[2,64,2048]{2,1,0:T(8,128)(2,1)} %fusion.5), channel_id=1, source_target_pairs={{0,1},{1,0},{2,3},{3,2},{4,5},{5,4},{6,7},{7,6},{8,9},{9,8},{10,11... | collective-permute-start | bytes 1572872 | tf_op jit(solution)/shard_map/ppermute | solution.py:23
  115.5 13.4 %copy-start.7 = (bf16[2,2048,256]{2,1,0:T(8,128)(2,1)S(1)}, bf16[2,2048,256]{2,1,0:T(8,128)(2,1)}, u32[]{:S(2)}) copy-start(bf16[2,2048,256]{2,1,0:T(8,128)(2,1)} %gu_own.1) | copy-start | bytes 6291460
  118.9 8.7 %collective-permute-start.17 = (bf16[64,2048]{1,0:T(8,128)(2,1)S(1)}, bf16[64,2048]{1,0:T(8,128)(2,1)S(1)}, u32[]{:S(2)}, u32[]{:S(2)}) collective-permute-start(bf16[64,2048]{1,0:T(8,128)(2,1)S(1)} %fusion.6), channel_id=1, source_target_pairs={{0,2},{2,0},{1,3},{3,1},{4,6},{6,4},{5,7},{7,5},{8,10},{10,8},{9,1... | collective-permute-start | bytes 786440 | tf_op jit(solution)/shard_map/ppermute | solution.py:23
  128.9 38.2 %collective-permute-start.18 = (bf16[2,2048,256]{2,1,0:T(8,128)(2,1)S(1)}, bf16[2,2048,256]{2,1,0:T(8,128)(2,1)S(1)}, u32[]{:S(2)}, u32[]{:S(2)}) collective-permute-start(bf16[2,2048,256]{2,1,0:T(8,128)(2,1)S(1)} %copy-done.7), channel_id=1, source_target_pairs={{0,4},{1,13},{4,8},{5,1},{8,12},{9,5},{12,0},{13,9},{2,6},{3,15},{... | collective-permute-start | bytes 6291464 | tf_op jit(solution)/shard_map/ppermute | solution.py:342
  167.1 11.9 %copy-start.6 = (bf16[8,64,2048]{2,1,0:T(8,128)(2,1)}, bf16[8,64,2048]{2,1,0:T(8,128)(2,1)S(1)}, u32[]{:S(2)}) copy-start(bf16[8,64,2048]{2,1,0:T(8,128)(2,1)S(1)} %all_to_all.15) | copy-start | bytes 6291460
  167.1 4.2 %copy-start.8 = (bf16[2,2048,256]{2,1,0:T(8,128)(2,1)}, bf16[2,2048,256]{2,1,0:T(8,128)(2,1)S(1)}, u32[]{:S(2)}) copy-start(bf16[2,2048,256]{2,1,0:T(8,128)(2,1)S(1)} %collective-permute-done.18.gu_a) | copy-start | bytes 6291460
  167.1 4.2 %collective-permute-start.19 = (bf16[512,2048]{1,0:T(8,128)(2,1)S(1)}, bf16[512,2048]{1,0:T(8,128)(2,1)S(1)}, u32[]{:S(2)}, u32[]{:S(2)}) collective-permute-start(bf16[512,2048]{1,0:T(8,128)(2,1)S(1)} %bitcast.128), channel_id=1, source_target_pairs={{0,1},{1,0},{2,3},{3,2},{4,5},{5,4},{6,7},{7,6},{8,9},{9,8},{10,11... | collective-permute-start | bytes 6291464 | tf_op jit(solution)/shard_map/ppermute | solution.py:23
  171.3 1.4 copy-start.9
  179.0 6.5 %collective-permute-start.20 = (bf16[512,2048]{1,0:T(8,128)(2,1)S(1)}, bf16[512,2048]{1,0:T(8,128)(2,1)S(1)}, u32[]{:S(2)}, u32[]{:S(2)}) collective-permute-start(bf16[512,2048]{1,0:T(8,128)(2,1)S(1)} %shard_map.138), channel_id=1, source_target_pairs={{0,1},{1,0},{2,3},{3,2},{4,5},{5,4},{6,7},{7,6},{8,9},{9,8},{10,11... | collective-permute-start | bytes 6291464 | tf_op jit(solution)/shard_map/ppermute | solution.py:23
